TPU v7x, 256 devices: a whole 4x4x8 slice. The times are simulated.
256 devices in a mesh: layer: 32 (over x, z), dp: 8 (over y, core).
Axes of the slice: x: 4, y: 4, z: 8, core: 2. Of those that a mesh axis runs over, the one named last changes fastest.
Arguments:
- coarse_guess: float32 [32, 8, 64, 512], P('layer', 'dp'), may hold values from -6 to 6
- adjoint_guess: float32 [32, 8, 64, 512], P('layer', 'dp'), may hold values from -6 to 6
- weights: float32 [64, 64, 576], P('layer'), may hold values from -0.25 to 0.25
- biases: float32 [64, 64], P('layer'), may hold values from -3 to 3
Outputs:
- states: float32 [64, 8, 64, 512], P('layer', 'dp')
- adjoints: float32 [64, 8, 64, 512], P('layer', 'dp')
- grad_weight: float32 [64, 64, 576], P('layer')
- grad_bias: float32 [64, 64], P('layer')
All inputs are finite; a program needn't handle non-finite values.
Results may differ from a plain program's by a relative error of at most 0.0003.
Values sent between devices are 32-bit elements; how exact they have to be, the bound alone decides.
No kernel may reach another device: no remote copies, remote signals or barrier semaphores. Data moves between devices by JAX's collectives and lax.ppermute only.
A program may use at most 64 MiB of HBM per device.

v0:
```python
import jax
import jax.numpy as jnp
from jax import lax
from jax.sharding import PartitionSpec as P

COLS = 32


step_size = 0.125


def shifted_2(value, axis, steps):
    count = lax.axis_size(axis)
    first, last = (max(0, -steps), min(count, count - steps))
    return lax.ppermute(value, axis, [(source, source + steps) for source in range(first, last)])


def patches(state_field, orient):
    cell_count = state_field.shape[-1]
    padded = jnp.pad(state_field, ((0, 0), (0, 0), (COLS + 1, COLS + 1)))
    col_index = jnp.arange(cell_count, dtype=jnp.int32) % COLS
    tap_fields = []
    for row_step in (-1, 0, 1):
        for col_step in (-1, 0, 1):
            offset = orient * (row_step * COLS + col_step)
            shifted = lax.slice_in_dim(
                padded, COLS + 1 + offset, COLS + 1 + offset + cell_count, axis=2
            )
            target = col_index + orient * col_step
            inside = (target >= 0) & (target < COLS)
            tap_fields.append(jnp.where(inside, shifted, 0.0))
    return jnp.concatenate(tap_fields, axis=1)


def convolve(matrix, state_field, orient):
    return jnp.einsum(
        "ok,bkc->boc", matrix, patches(state_field, orient), precision=lax.Precision.HIGHEST
    )


def flipped(matrix):
    channel_count = matrix.shape[0]
    return (
        matrix.reshape(channel_count, 9, channel_count)
        .transpose(2, 1, 0)
        .reshape(channel_count, 9 * channel_count)
    )


def tangent(matrix, bias_row, state_field):
    return jnp.tanh(convolve(matrix, state_field, 1) + bias_row[:, None])


def advance(matrix, bias_row, state_field, step_scale):
    return state_field + step_scale * tangent(matrix, bias_row, state_field)


def pull_back(matrix, slope_field, cotangent, step_scale):
    return cotangent + step_scale * convolve(flipped(matrix), slope_field * cotangent, -1)


def weight_term(term_field, state_field):
    return jnp.einsum(
        "boc,bkc->ok", term_field, patches(state_field, 1), precision=lax.Precision.HIGHEST
    )


def body(coarse_guess, adjoint_guess, weights, biases):
    slice_index = lax.axis_index("layer")
    slice_count = lax.axis_size("layer")
    last_place = slice_count - 1
    start_field = coarse_guess[0]
    terminal_side = adjoint_guess[0]
    even_matrix = weights[0]
    odd_matrix = weights[1]
    even_bias = biases[0]
    odd_bias = biases[1]
    double_step = 2.0 * step_size
    fine_first = advance(even_matrix, even_bias, start_field, step_size)
    fine_second = advance(odd_matrix, odd_bias, fine_first, step_size)
    forward_tau = fine_second - advance(even_matrix, even_bias, start_field, double_step)

    def forward_turn(turn_index, loop_state):
        current, finished = loop_state
        produced = advance(even_matrix, even_bias, current, double_step) + forward_tau
        produced = jnp.where(slice_index == 0, fine_second, produced)
        finished = jnp.where(slice_index == turn_index, produced, finished)
        arrived = shifted_2(produced, "layer", 1)
        current = jnp.where(slice_index == turn_index + 1, arrived, current)
        return (current, finished)

    begin_field, finished = lax.fori_loop(0, last_place, forward_turn, (start_field, fine_second))
    last_step = advance(even_matrix, even_bias, begin_field, double_step) + forward_tau
    end_field = jnp.where(slice_index == last_place, last_step, finished)
    even_tangent = tangent(even_matrix, even_bias, begin_field)
    mid_field = begin_field + step_size * even_tangent
    even_slope = 1.0 - even_tangent * even_tangent
    odd_tangent = tangent(odd_matrix, odd_bias, mid_field)
    odd_slope = 1.0 - odd_tangent * odd_tangent
    relaxed = pull_back(odd_matrix, odd_slope, terminal_side, step_size)
    fine_adjoint = pull_back(even_matrix, even_slope, relaxed, step_size)
    adjoint_tau = fine_adjoint - pull_back(even_matrix, even_slope, terminal_side, double_step)

    def backward_turn(turn_index, loop_state):
        current, finished = loop_state
        active = last_place - turn_index
        produced = pull_back(even_matrix, even_slope, current, double_step) + adjoint_tau
        produced = jnp.where(slice_index == last_place, fine_adjoint, produced)
        finished = jnp.where(slice_index == active, produced, finished)
        arrived = shifted_2(produced, "layer", -1)
        current = jnp.where(slice_index == active - 1, arrived, current)
        return (current, finished)

    received_adjoint, finished = lax.fori_loop(
        0, last_place, backward_turn, (terminal_side, fine_adjoint)
    )
    first_step = pull_back(even_matrix, even_slope, received_adjoint, double_step) + adjoint_tau
    even_adjoint = jnp.where(slice_index == 0, first_step, finished)
    odd_adjoint = pull_back(odd_matrix, odd_slope, received_adjoint, step_size)
    even_term = step_size * even_slope * odd_adjoint
    odd_term = step_size * odd_slope * received_adjoint
    grad_parts = jnp.stack([weight_term(even_term, begin_field), weight_term(odd_term, mid_field)])
    bias_parts = jnp.stack([jnp.sum(even_term, axis=(0, 2)), jnp.sum(odd_term, axis=(0, 2))])
    grad_total, bias_total = lax.psum((grad_parts, bias_parts), "dp")
    inverse = 1.0 / (start_field.shape[0] * lax.axis_size("dp"))
    states = jnp.stack([mid_field, end_field])
    adjoints = jnp.stack([even_adjoint, odd_adjoint])
    return (states, adjoints, grad_total * inverse, bias_total * inverse)


def solution(mesh):
    return jax.shard_map(
        body,
        mesh=mesh,
        in_specs=(
            P("layer", "dp", None, None),
            P("layer", "dp", None, None),
            P("layer", None, None),
            P("layer", None),
        ),
        out_specs=(
            P("layer", "dp", None, None),
            P("layer", "dp", None, None),
            P("layer", None, None),
            P("layer", None),
        ),
        check_vma=False,
    )
```

profile of v0, /device:TPU:1, one launch (start us, length us, event | category | flops | bytes accessed | tf_op | source)
XLA Modules:
  0.0 797.9 jit_solution(14104022900156034072)
XLA Ops:
  12.8 288.2 %while.36 = (s32[]{:T(128)}, f32[1,64,512]{2,1,0:T(8,128)S(1)}, f32[1,64,512]{2,1,0:T(8,128)S(1)}, s32[]{:T(128)}, pred[]{:T(512)}, /*index=5*/f32[64,576]{1,0:T...) while((s32[]{:T(128)}, f32[1,64,512]{2,1,0:T(8,128)S(1)}, ...), condition=%wide.region_1.2_spmd, body=%wide.region_0.1_spmd.sunk | while | flops 227031552 | bytes 5396898 | solution.py:92
  46.7 5.3 collective-permute-start
  120.0 5.3 collective-permute-start
  129.2 5.3 collective-permute-start
  204.3 5.7 collective-permute-start
  214.5 5.4 collective-permute-start
  223.8 6.3 collective-permute-start
  234.0 5.4 collective-permute-start
  243.3 5.9 collective-permute-start
  253.1 6.1 collective-permute-start
  263.1 6.0 collective-permute-start
  273.0 6.2 collective-permute-start
  283.0 5.9 collective-permute-start
  292.8 5.9 collective-permute-start
  313.6 320.0 %while.37 = (s32[]{:T(128)}, f32[1,64,512]{2,1,0:T(8,128)S(1)}, f32[1,64,512]{2,1,0:T(8,128)S(1)}, s32[]{:T(128)}, pred[]{:T(512)}, /*index=5*/f32[1,64,512]{2,1...) while((s32[]{:T(128)}, f32[1,64,512]{2,1,0:T(8,128)S(1)}, ...), condition=%wide.region_3.4_spmd, body=%wide.region_2.3_spmd.sunk | while | flops 227031552 | bytes 6084810 | solution.py:114
  317.0 7.2 collective-permute-done.1
  327.6 7.4 collective-permute-done.1
  338.5 7.6 collective-permute-done.1
  349.5 6.9 collective-permute-done.1
  359.9 7.2 collective-permute-done.1
  370.5 7.0 collective-permute-done.1
  381.0 7.1 collective-permute-done.1
  391.5 7.3 collective-permute-done.1
  402.2 6.5 collective-permute-done.1
  412.1 6.5 collective-permute-done.1
  422.1 6.8 collective-permute-done.1
  432.3 8.5 %collective-permute-done.1 = f32[1,64,512]{2,1,0:T(8,128)S(1)} collective-permute-done((f32[1,64,512]{2,1,0:T(8,128)S(1)}, f32[1,64,512]{2,1,0:T(8,128)S(1)}, u32[]{:S(2)}, u32[]{:S(2)}) %collective-permute-start.1) | collective-permute-done | bytes 131104 | tf_op jit(solution)/shard_map/while/body/eval_jaxpr/ppermute | solution.py:15
  444.3 7.6 collective-permute-done.1
  455.3 6.7 collective-permute-done.1
  465.5 6.0 collective-permute-done.1
  474.9 6.8 collective-permute-done.1
  485.2 6.7 collective-permute-done.1
  495.3 5.7 collective-permute-done.1
  504.4 6.5 collective-permute-done.1
  514.4 6.5 collective-permute-done.1
  524.3 7.0 collective-permute-done.1
  534.8 8.2 %collective-permute-done.1 = f32[1,64,512]{2,1,0:T(8,128)S(1)} collective-permute-done((f32[1,64,512]{2,1,0:T(8,128)S(1)}, f32[1,64,512]{2,1,0:T(8,128)S(1)}, u32[]{:S(2)}, u32[]{:S(2)}) %collective-permute-start.1) | collective-permute-done | bytes 131104 | tf_op jit(solution)/shard_map/while/body/eval_jaxpr/ppermute | solution.py:15
  546.5 7.3 collective-permute-done.1
  557.2 7.5 collective-permute-done.1
  568.2 5.4 collective-permute-done.1
  577.0 6.6 collective-permute-done.1
  587.1 7.0 collective-permute-done.1
  597.5 5.6 collective-permute-done.1
  606.6 6.5 collective-permute-done.1
  616.5 6.5 collective-permute-done.1
  626.4 6.9 collective-permute-done.1
  640.2 80.0 %psum.15 = f32[2,64]{1,0:T(2,128)S(1)} all-reduce(f32[2,64]{1,0:T(2,128)S(1)} %pad_maximum_fusion.3), channel_id=1, replica_groups=mesh['layer'=32,'dp'=8] {'dp'}, use_global_device_ids=true, to_apply=%region_7.8 | all-reduce | flops 128 | bytes 1024 | tf_op jit(solution)/shard_map/psum | solution.py:124
  723.5 65.9 %all-reduce.13.cloned.1.call-done = f32[2,64,576]{2,1,0:T(8,128)} async-done(((f32[2,64,576]{2,1,0:T(8,128)}), f32[2,64,576]{2,1,0:T(8,128)}) %all-reduce.13.cloned.1.call-update) | async-done | bytes 294928 | tf_op jit(solution)/shard_map/psum | solution.py:124
  (1136 shorter events, 340.1 us)
Async XLA Ops:
  7.2 782.2 %all-reduce.13.cloned.1.call-start = ((), (), s32[]{:S(2)}) async-start(), calls=%async_computation | async-start | bytes 655360 | tf_op jit(solution)/shard_map/psum | solution.py:124
  46.7 7.3 collective-permute-start
  82.4 7.5 collective-permute-start
  91.8 8.3 %collective-permute-start = (f32[1,64,512]{2,1,0:T(8,128)S(1)}, f32[1,64,512]{2,1,0:T(8,128)S(1)}, u32[]{:S(2)}, u32[]{:S(2)}) collective-permute-start(f32[1,64,512]{2,1,0:T(8,128)S(1)} %get-tuple-element.673), channel_id=1, source_target_pairs={{0,8},{8,16},{16,24},{24,32},{32,40},{40,48},{48,56},{56,64},{64,7... | collective-permute-start | bytes 393224 | tf_op jit(solution)/shard_map/while/body/eval_jaxpr/ppermute | solution.py:15
  102.0 7.3 collective-permute-start
  120.0 7.3 collective-permute-start
  129.2 7.3 collective-permute-start
  174.1 8.6 %collective-permute-start = (f32[1,64,512]{2,1,0:T(8,128)S(1)}, f32[1,64,512]{2,1,0:T(8,128)S(1)}, u32[]{:S(2)}, u32[]{:S(2)}) collective-permute-start(f32[1,64,512]{2,1,0:T(8,128)S(1)} %get-tuple-element.673), channel_id=1, source_target_pairs={{0,8},{8,16},{16,24},{24,32},{32,40},{40,48},{48,56},{56,64},{64,7... | collective-permute-start | bytes 393224 | tf_op jit(solution)/shard_map/while/body/eval_jaxpr/ppermute | solution.py:15
  184.6 7.8 collective-permute-start
  194.3 8.0 %collective-permute-start = (f32[1,64,512]{2,1,0:T(8,128)S(1)}, f32[1,64,512]{2,1,0:T(8,128)S(1)}, u32[]{:S(2)}, u32[]{:S(2)}) collective-permute-start(f32[1,64,512]{2,1,0:T(8,128)S(1)} %get-tuple-element.673), channel_id=1, source_target_pairs={{0,8},{8,16},{16,24},{24,32},{32,40},{40,48},{48,56},{56,64},{64,7... | collective-permute-start | bytes 393224 | tf_op jit(solution)/shard_map/while/body/eval_jaxpr/ppermute | solution.py:15
  204.3 8.3 %collective-permute-start = (f32[1,64,512]{2,1,0:T(8,128)S(1)}, f32[1,64,512]{2,1,0:T(8,128)S(1)}, u32[]{:S(2)}, u32[]{:S(2)}) collective-permute-start(f32[1,64,512]{2,1,0:T(8,128)S(1)} %get-tuple-element.673), channel_id=1, source_target_pairs={{0,8},{8,16},{16,24},{24,32},{32,40},{40,48},{48,56},{56,64},{64,7... | collective-permute-start | bytes 393224 | tf_op jit(solution)/shard_map/while/body/eval_jaxpr/ppermute | solution.py:15
  214.5 7.4 collective-permute-start
  223.8 8.2 %collective-permute-start = (f32[1,64,512]{2,1,0:T(8,128)S(1)}, f32[1,64,512]{2,1,0:T(8,128)S(1)}, u32[]{:S(2)}, u32[]{:S(2)}) collective-permute-start(f32[1,64,512]{2,1,0:T(8,128)S(1)} %get-tuple-element.673), channel_id=1, source_target_pairs={{0,8},{8,16},{16,24},{24,32},{32,40},{40,48},{48,56},{56,64},{64,7... | collective-permute-start | bytes 393224 | tf_op jit(solution)/shard_map/while/body/eval_jaxpr/ppermute | solution.py:15
  234.0 7.4 collective-permute-start
  243.3 7.8 collective-permute-start
  253.1 8.0 %collective-permute-start = (f32[1,64,512]{2,1,0:T(8,128)S(1)}, f32[1,64,512]{2,1,0:T(8,128)S(1)}, u32[]{:S(2)}, u32[]{:S(2)}) collective-permute-start(f32[1,64,512]{2,1,0:T(8,128)S(1)} %get-tuple-element.673), channel_id=1, source_target_pairs={{0,8},{8,16},{16,24},{24,32},{32,40},{40,48},{48,56},{56,64},{64,7... | collective-permute-start | bytes 393224 | tf_op jit(solution)/shard_map/while/body/eval_jaxpr/ppermute | solution.py:15
  263.1 8.0 collective-permute-start
  273.0 8.1 %collective-permute-start = (f32[1,64,512]{2,1,0:T(8,128)S(1)}, f32[1,64,512]{2,1,0:T(8,128)S(1)}, u32[]{:S(2)}, u32[]{:S(2)}) collective-permute-start(f32[1,64,512]{2,1,0:T(8,128)S(1)} %get-tuple-element.673), channel_id=1, source_target_pairs={{0,8},{8,16},{16,24},{24,32},{32,40},{40,48},{48,56},{56,64},{64,7... | collective-permute-start | bytes 393224 | tf_op jit(solution)/shard_map/while/body/eval_jaxpr/ppermute | solution.py:15
  283.0 7.8 collective-permute-start
  292.8 8.3 %collective-permute-start = (f32[1,64,512]{2,1,0:T(8,128)S(1)}, f32[1,64,512]{2,1,0:T(8,128)S(1)}, u32[]{:S(2)}, u32[]{:S(2)}) collective-permute-start(f32[1,64,512]{2,1,0:T(8,128)S(1)} %get-tuple-element.673), channel_id=1, source_target_pairs={{0,8},{8,16},{16,24},{24,32},{32,40},{40,48},{48,56},{56,64},{64,7... | collective-permute-start | bytes 393224 | tf_op jit(solution)/shard_map/while/body/eval_jaxpr/ppermute | solution.py:15
  315.7 8.5 %collective-permute-start.1 = (f32[1,64,512]{2,1,0:T(8,128)S(1)}, f32[1,64,512]{2,1,0:T(8,128)S(1)}, u32[]{:S(2)}, u32[]{:S(2)}) collective-permute-start(f32[1,64,512]{2,1,0:T(8,128)S(1)} %get-tuple-element.684), channel_id=1, source_target_pairs={{8,0},{16,8},{24,16},{32,24},{40,32},{48,40},{56,48},{64,56},{72,6... | collective-permute-start | bytes 393224 | tf_op jit(solution)/shard_map/while/body/eval_jaxpr/ppermute | solution.py:15
  326.3 8.7 %collective-permute-start.1 = (f32[1,64,512]{2,1,0:T(8,128)S(1)}, f32[1,64,512]{2,1,0:T(8,128)S(1)}, u32[]{:S(2)}, u32[]{:S(2)}) collective-permute-start(f32[1,64,512]{2,1,0:T(8,128)S(1)} %get-tuple-element.684), channel_id=1, source_target_pairs={{8,0},{16,8},{24,16},{32,24},{40,32},{48,40},{56,48},{64,56},{72,6... | collective-permute-start | bytes 393224 | tf_op jit(solution)/shard_map/while/body/eval_jaxpr/ppermute | solution.py:15
  337.1 8.9 %collective-permute-start.1 = (f32[1,64,512]{2,1,0:T(8,128)S(1)}, f32[1,64,512]{2,1,0:T(8,128)S(1)}, u32[]{:S(2)}, u32[]{:S(2)}) collective-permute-start(f32[1,64,512]{2,1,0:T(8,128)S(1)} %get-tuple-element.684), channel_id=1, source_target_pairs={{8,0},{16,8},{24,16},{32,24},{40,32},{48,40},{56,48},{64,56},{72,6... | collective-permute-start | bytes 393224 | tf_op jit(solution)/shard_map/while/body/eval_jaxpr/ppermute | solution.py:15
  348.2 8.2 %collective-permute-start.1 = (f32[1,64,512]{2,1,0:T(8,128)S(1)}, f32[1,64,512]{2,1,0:T(8,128)S(1)}, u32[]{:S(2)}, u32[]{:S(2)}) collective-permute-start(f32[1,64,512]{2,1,0:T(8,128)S(1)} %get-tuple-element.684), channel_id=1, source_target_pairs={{8,0},{16,8},{24,16},{32,24},{40,32},{48,40},{56,48},{64,56},{72,6... | collective-permute-start | bytes 393224 | tf_op jit(solution)/shard_map/while/body/eval_jaxpr/ppermute | solution.py:15
  358.5 8.5 %collective-permute-start.1 = (f32[1,64,512]{2,1,0:T(8,128)S(1)}, f32[1,64,512]{2,1,0:T(8,128)S(1)}, u32[]{:S(2)}, u32[]{:S(2)}) collective-permute-start(f32[1,64,512]{2,1,0:T(8,128)S(1)} %get-tuple-element.684), channel_id=1, source_target_pairs={{8,0},{16,8},{24,16},{32,24},{40,32},{48,40},{56,48},{64,56},{72,6... | collective-permute-start | bytes 393224 | tf_op jit(solution)/shard_map/while/body/eval_jaxpr/ppermute | solution.py:15
  369.2 8.3 %collective-permute-start.1 = (f32[1,64,512]{2,1,0:T(8,128)S(1)}, f32[1,64,512]{2,1,0:T(8,128)S(1)}, u32[]{:S(2)}, u32[]{:S(2)}) collective-permute-start(f32[1,64,512]{2,1,0:T(8,128)S(1)} %get-tuple-element.684), channel_id=1, source_target_pairs={{8,0},{16,8},{24,16},{32,24},{40,32},{48,40},{56,48},{64,56},{72,6... | collective-permute-start | bytes 393224 | tf_op jit(solution)/shard_map/while/body/eval_jaxpr/ppermute | solution.py:15
  379.7 8.4 %collective-permute-start.1 = (f32[1,64,512]{2,1,0:T(8,128)S(1)}, f32[1,64,512]{2,1,0:T(8,128)S(1)}, u32[]{:S(2)}, u32[]{:S(2)}) collective-permute-start(f32[1,64,512]{2,1,0:T(8,128)S(1)} %get-tuple-element.684), channel_id=1, source_target_pairs={{8,0},{16,8},{24,16},{32,24},{40,32},{48,40},{56,48},{64,56},{72,6... | collective-permute-start | bytes 393224 | tf_op jit(solution)/shard_map/while/body/eval_jaxpr/ppermute | solution.py:15
  390.2 8.6 %collective-permute-start.1 = (f32[1,64,512]{2,1,0:T(8,128)S(1)}, f32[1,64,512]{2,1,0:T(8,128)S(1)}, u32[]{:S(2)}, u32[]{:S(2)}) collective-permute-start(f32[1,64,512]{2,1,0:T(8,128)S(1)} %get-tuple-element.684), channel_id=1, source_target_pairs={{8,0},{16,8},{24,16},{32,24},{40,32},{48,40},{56,48},{64,56},{72,6... | collective-permute-start | bytes 393224 | tf_op jit(solution)/shard_map/while/body/eval_jaxpr/ppermute | solution.py:15
  400.9 7.8 collective-permute-start.1
  410.8 7.8 collective-permute-start.1
  420.8 8.1 %collective-permute-start.1 = (f32[1,64,512]{2,1,0:T(8,128)S(1)}, f32[1,64,512]{2,1,0:T(8,128)S(1)}, u32[]{:S(2)}, u32[]{:S(2)}) collective-permute-start(f32[1,64,512]{2,1,0:T(8,128)S(1)} %get-tuple-element.684), channel_id=1, source_target_pairs={{8,0},{16,8},{24,16},{32,24},{40,32},{48,40},{56,48},{64,56},{72,6... | collective-permute-start | bytes 393224 | tf_op jit(solution)/shard_map/while/body/eval_jaxpr/ppermute | solution.py:15
  431.0 9.9 %collective-permute-start.1 = (f32[1,64,512]{2,1,0:T(8,128)S(1)}, f32[1,64,512]{2,1,0:T(8,128)S(1)}, u32[]{:S(2)}, u32[]{:S(2)}) collective-permute-start(f32[1,64,512]{2,1,0:T(8,128)S(1)} %get-tuple-element.684), channel_id=1, source_target_pairs={{8,0},{16,8},{24,16},{32,24},{40,32},{48,40},{56,48},{64,56},{72,6... | collective-permute-start | bytes 393224 | tf_op jit(solution)/shard_map/while/body/eval_jaxpr/ppermute | solution.py:15
  443.0 8.9 %collective-permute-start.1 = (f32[1,64,512]{2,1,0:T(8,128)S(1)}, f32[1,64,512]{2,1,0:T(8,128)S(1)}, u32[]{:S(2)}, u32[]{:S(2)}) collective-permute-start(f32[1,64,512]{2,1,0:T(8,128)S(1)} %get-tuple-element.684), channel_id=1, source_target_pairs={{8,0},{16,8},{24,16},{32,24},{40,32},{48,40},{56,48},{64,56},{72,6... | collective-permute-start | bytes 393224 | tf_op jit(solution)/shard_map/while/body/eval_jaxpr/ppermute | solution.py:15
  454.0 8.0 %collective-permute-start.1 = (f32[1,64,512]{2,1,0:T(8,128)S(1)}, f32[1,64,512]{2,1,0:T(8,128)S(1)}, u32[]{:S(2)}, u32[]{:S(2)}) collective-permute-start(f32[1,64,512]{2,1,0:T(8,128)S(1)} %get-tuple-element.684), channel_id=1, source_target_pairs={{8,0},{16,8},{24,16},{32,24},{40,32},{48,40},{56,48},{64,56},{72,6... | collective-permute-start | bytes 393224 | tf_op jit(solution)/shard_map/while/body/eval_jaxpr/ppermute | solution.py:15
  464.2 7.3 collective-permute-start.1
  473.6 8.1 %collective-permute-start.1 = (f32[1,64,512]{2,1,0:T(8,128)S(1)}, f32[1,64,512]{2,1,0:T(8,128)S(1)}, u32[]{:S(2)}, u32[]{:S(2)}) collective-permute-start(f32[1,64,512]{2,1,0:T(8,128)S(1)} %get-tuple-element.684), channel_id=1, source_target_pairs={{8,0},{16,8},{24,16},{32,24},{40,32},{48,40},{56,48},{64,56},{72,6... | collective-permute-start | bytes 393224 | tf_op jit(solution)/shard_map/while/body/eval_jaxpr/ppermute | solution.py:15
  483.9 8.0 collective-permute-start.1
  503.1 7.8 collective-permute-start.1
  513.1 7.8 collective-permute-start.1
  523.0 8.3 %collective-permute-start.1 = (f32[1,64,512]{2,1,0:T(8,128)S(1)}, f32[1,64,512]{2,1,0:T(8,128)S(1)}, u32[]{:S(2)}, u32[]{:S(2)}) collective-permute-start(f32[1,64,512]{2,1,0:T(8,128)S(1)} %get-tuple-element.684), channel_id=1, source_target_pairs={{8,0},{16,8},{24,16},{32,24},{40,32},{48,40},{56,48},{64,56},{72,6... | collective-permute-start | bytes 393224 | tf_op jit(solution)/shard_map/while/body/eval_jaxpr/ppermute | solution.py:15
  533.5 9.5 %collective-permute-start.1 = (f32[1,64,512]{2,1,0:T(8,128)S(1)}, f32[1,64,512]{2,1,0:T(8,128)S(1)}, u32[]{:S(2)}, u32[]{:S(2)}) collective-permute-start(f32[1,64,512]{2,1,0:T(8,128)S(1)} %get-tuple-element.684), channel_id=1, source_target_pairs={{8,0},{16,8},{24,16},{32,24},{40,32},{48,40},{56,48},{64,56},{72,6... | collective-permute-start | bytes 393224 | tf_op jit(solution)/shard_map/while/body/eval_jaxpr/ppermute | solution.py:15
  545.2 8.6 %collective-permute-start.1 = (f32[1,64,512]{2,1,0:T(8,128)S(1)}, f32[1,64,512]{2,1,0:T(8,128)S(1)}, u32[]{:S(2)}, u32[]{:S(2)}) collective-permute-start(f32[1,64,512]{2,1,0:T(8,128)S(1)} %get-tuple-element.684), channel_id=1, source_target_pairs={{8,0},{16,8},{24,16},{32,24},{40,32},{48,40},{56,48},{64,56},{72,6... | collective-permute-start | bytes 393224 | tf_op jit(solution)/shard_map/while/body/eval_jaxpr/ppermute | solution.py:15
  555.9 8.8 %collective-permute-start.1 = (f32[1,64,512]{2,1,0:T(8,128)S(1)}, f32[1,64,512]{2,1,0:T(8,128)S(1)}, u32[]{:S(2)}, u32[]{:S(2)}) collective-permute-start(f32[1,64,512]{2,1,0:T(8,128)S(1)} %get-tuple-element.684), channel_id=1, source_target_pairs={{8,0},{16,8},{24,16},{32,24},{40,32},{48,40},{56,48},{64,56},{72,6... | collective-permute-start | bytes 393224 | tf_op jit(solution)/shard_map/while/body/eval_jaxpr/ppermute | solution.py:15
  575.7 7.9 collective-permute-start.1
  585.8 8.3 %collective-permute-start.1 = (f32[1,64,512]{2,1,0:T(8,128)S(1)}, f32[1,64,512]{2,1,0:T(8,128)S(1)}, u32[]{:S(2)}, u32[]{:S(2)}) collective-permute-start(f32[1,64,512]{2,1,0:T(8,128)S(1)} %get-tuple-element.684), channel_id=1, source_target_pairs={{8,0},{16,8},{24,16},{32,24},{40,32},{48,40},{56,48},{64,56},{72,6... | collective-permute-start | bytes 393224 | tf_op jit(solution)/shard_map/while/body/eval_jaxpr/ppermute | solution.py:15
  605.3 7.8 collective-permute-start.1
  615.2 7.8 collective-permute-start.1
  625.1 8.2 %collective-permute-start.1 = (f32[1,64,512]{2,1,0:T(8,128)S(1)}, f32[1,64,512]{2,1,0:T(8,128)S(1)}, u32[]{:S(2)}, u32[]{:S(2)}) collective-permute-start(f32[1,64,512]{2,1,0:T(8,128)S(1)} %get-tuple-element.684), channel_id=1, source_target_pairs={{8,0},{16,8},{24,16},{32,24},{40,32},{48,40},{56,48},{64,56},{72,6... | collective-permute-start | bytes 393224 | tf_op jit(solution)/shard_map/while/body/eval_jaxpr/ppermute | solution.py:15
  (22 other events, 108.6 us)
Sparse Core Ops, SparseCore 0:
  640.3 148.9 all-reduce.12
where the time goes:
time: 801 us; the launch traced here: 798 us
  waiting for transfers between devices  345 us (43%)
  starting transfers between devices  202 us (25%)
  blocking collectives  80 us (10%)
  matrix products  74.1 us (9%)
  other arithmetic  65 us (8%)
  between operations  14.9 us (2%)
  loops' own time  8.89 us (1%)
  local copies, waits for them, and re-layouts  8.22 us (1%)
    ppermute x62, waiting for transfers between devices, shifted_2(): lax.ppermute(value, axis, [(source, source + steps) for source in range(f...  279 us
    ppermute x62, starting transfers between devices, shifted_2(): lax.ppermute(value, axis, [(source, source + steps) for source in range(f...  202 us
    psum x1, blocking collectives, body(): grad_total, bias_total = lax.psum((grad_parts, bias_parts), 'dp')  80 us
    dot_general x71, matrix products, convolve(): jnp.einsum('ok,bkc->boc', matrix, patches(state_field, orient), precision...  70.4 us
    psum x1, waiting for transfers between devices, body(): grad_total, bias_total = lax.psum((grad_parts, bias_parts), 'dp')  65.9 us
    while x496, other arithmetic  43.2 us
  transfers between devices with their start and end apart: 63, of which 63 were waited for; matrix products, arithmetic and copies ran while one was open for 0% of the time, Pallas kernels for 0%

commit v1 on v0

v1 whole, which is shorter than its diff:
```python
import jax
import jax.numpy as jnp
from jax import lax
from jax.experimental import pallas as pl
from jax.experimental.pallas import tpu as pltpu
from jax.sharding import PartitionSpec as P

F32 = jnp.float32
BF16 = jnp.bfloat16
H = 0.125
CH, CELLS = 64, 512
WPAD = 640
BLK = WPAD + CELLS
RING = 8
AXES = ("layer", "dp")
ANY = pl.BlockSpec(memory_space=pl.ANY)
SMEM = pl.BlockSpec(memory_space=pltpu.SMEM)
VMEM = pl.BlockSpec(memory_space=pltpu.VMEM)
PARAMS = pltpu.CompilerParams(vmem_limit_bytes=40 << 20)


def split(x):
    hi = x.astype(BF16)
    return hi, (x - hi.astype(F32)).astype(BF16)


def lane_index():
    return lax.broadcasted_iota(jnp.int32, (CH, 128), 1)


def columns(x):
    return [x[:, 128 * a : 128 * (a + 1)] for a in range(4)]


def swap(x):
    parts, lane, out = columns(x), lane_index(), []
    for a in range(4):
        acc = None
        for b in range(4):
            shift = ((b - a) * 32) % 128
            part = parts[b] if shift == 0 else pltpu.roll(parts[b], shift, 1)
            acc = part if acc is None else jnp.where(lane >= 32 * b, part, acc)
        out.append(acc)
    return jnp.concatenate(out, 1)


def lhs_forward(w):
    hi = w.astype(BF16).astype(F32)
    lo = w - hi
    rows = []
    for t in range(9):
        a, b = hi[:, 64 * t : 64 * t + 64], lo[:, 64 * t : 64 * t + 64]
        rows.append(jnp.concatenate([a, a, b], 1).astype(BF16))
    return jnp.concatenate(rows, 0)


def lhs_backward(w):
    wt = w.T
    hi = wt.astype(BF16).astype(F32)
    lo = wt - hi
    return jnp.concatenate([hi, hi, lo], 1).astype(BF16)


def conv(lhs, x, sign):
    hi, lo = split(x)
    z = jnp.dot(lhs, jnp.concatenate([hi, lo, hi], 0), preferred_element_type=F32)
    lane = lane_index()
    q = lane % 32
    lower, upper, right, left = lane < 96, lane >= 32, q < 31, q > 0

    def tap(a, e, col):
        t = 3 * (sign * a + 1) + (sign * e + 1)
        return z[64 * t : 64 * t + 64, 128 * col : 128 * col + 128]

    out = []
    for col in range(4):
        s = []
        for e in (-1, 0, 1):
            if col < 3:
                up = tap(1, e, col + 1)
            else:
                up = jnp.where(lower, pltpu.roll(tap(1, e, 0), 96, 1), 0.0)
            if col > 0:
                down = tap(-1, e, col - 1)
            else:
                down = jnp.where(upper, pltpu.roll(tap(-1, e, 3), 32, 1), 0.0)
            s.append(tap(0, e, col) + up + down)
        out.append(
            s[1]
            + jnp.where(right, pltpu.roll(s[2], 127, 1), 0.0)
            + jnp.where(left, pltpu.roll(s[0], 1, 1), 0.0)
        )
    return jnp.concatenate(out, 1)


def patches(x):
    lane = lane_index()
    q = lane % 32
    lower, upper, right, left = lane < 96, lane >= 32, q < 31, q > 0
    mid = columns(x)
    base = {
        0: mid,
        1: [jnp.where(right, pltpu.roll(c, 127, 1), 0.0) for c in mid],
        -1: [jnp.where(left, pltpu.roll(c, 1, 1), 0.0) for c in mid],
    }
    hi, lo = [], []
    for a in (-1, 0, 1):
        for e in (-1, 0, 1):
            c = base[e]
            if a == 1:
                c = c[1:] + [jnp.where(lower, pltpu.roll(c[0], 96, 1), 0.0)]
            elif a == -1:
                c = [jnp.where(upper, pltpu.roll(c[3], 32, 1), 0.0)] + c[:3]
            h, l = split(jnp.concatenate(c, 1))
            hi.append(h)
            lo.append(l)
    return jnp.concatenate(hi, 0), jnp.concatenate(lo, 0)


def dot_t(a, b):
    return lax.dot_general(a, b, (((1,), (1,)), ((), ())), preferred_element_type=F32)


def correlate(term, x):
    t_hi, t_lo = split(term)
    p_hi, p_lo = patches(x)
    return dot_t(t_hi, p_hi) + dot_t(t_hi, p_lo) + dot_t(t_lo, p_hi)


def as_column(row):
    r = lax.broadcasted_iota(jnp.int32, (CH, CH), 0)
    c = lax.broadcasted_iota(jnp.int32, (CH, CH), 1)
    spread = jnp.broadcast_to(row, (CH, CH))
    return jnp.sum(jnp.where(r == c, spread, 0.0), axis=1, keepdims=True)


def relax_kernel(c_ref, a_ref, w_ref, b_ref, one_ref, two_ref):
    c = swap(c_ref[...])
    w0, w1 = w_ref[0], w_ref[1]
    b0, b1 = as_column(b_ref[0:1]), as_column(b_ref[1:2])
    t0 = jnp.tanh(conv(lhs_forward(w0), c, 1) + b0)
    t1 = jnp.tanh(conv(lhs_forward(w1), c + H * t0, 1) + b1)
    pad = WPAD - 576
    one_ref[:, 0:576] = w0
    one_ref[:, 576:WPAD] = jnp.broadcast_to(b0, (CH, pad))
    one_ref[:, WPAD:BLK] = H * (t1 - t0)
    two_ref[:, 0:576] = w1
    two_ref[:, 576:WPAD] = jnp.broadcast_to(b1, (CH, pad))
    two_ref[:, WPAD:BLK] = swap(a_ref[...])


def relax(c, a, w, b):
    shape = jax.ShapeDtypeStruct((CH, BLK), F32)
    return pl.pallas_call(
        relax_kernel, out_shape=(shape, shape), compiler_params=PARAMS, name="relax"
    )(c, a, w, b)


def chain_kernel(stage, *refs):
    info_ref, refs = refs[0], refs[1:]
    g_refs, v_ref = refs[:RING], refs[RING]
    vt_ref, out_ref, g, vt, lhs, sems = refs[-6:]

    @pl.when((info_ref[0] == stage) & (info_ref[1] == 1))
    def _():
        copies = [pltpu.make_async_copy(g_refs[j], g.at[j], sems.at[j]) for j in range(RING)]
        for copy in copies:
            copy.start()
        for copy in copies:
            copy.wait()
        start = v_ref[...]
        if stage == 0:
            start = swap(start)

        def prepare(j, carry):
            lhs[j] = lhs_forward(g[j][:, 0:576])
            return carry

        lax.fori_loop(0, RING, prepare, 0)

        def step(j, v):
            t = jnp.tanh(conv(lhs[j], v, 1) + g[j][:, 576:577])
            vt[j, :, 0:CELLS] = v
            vt[j, :, CELLS:] = t
            return v + 2 * H * t + g[j][:, WPAD:BLK]

        out_ref[...] = lax.fori_loop(0, RING, step, start)
        copy = pltpu.make_async_copy(vt, vt_ref, sems.at[0])
        copy.start()
        copy.wait()


def chain(stage, info, blocks, v, previous):
    args = [info, *blocks, v]
    specs = [SMEM] + [ANY] * RING + [VMEM]
    aliases = {}
    if previous is not None:
        aliases = {len(args): 0}
        args.append(previous)
        specs.append(ANY)
    return pl.pallas_call(
        lambda *refs: chain_kernel(stage, *refs),
        out_shape=(
            jax.ShapeDtypeStruct((RING, CH, 2 * CELLS), F32),
            jax.ShapeDtypeStruct((CH, CELLS), F32),
        ),
        in_specs=specs,
        out_specs=(ANY, VMEM),
        scratch_shapes=[
            pltpu.VMEM((RING, CH, BLK), F32),
            pltpu.VMEM((RING, CH, 2 * CELLS), F32),
            pltpu.VMEM((RING, 9 * CH, 3 * CH), BF16),
            pltpu.SemaphoreType.DMA((RING,)),
        ],
        input_output_aliases=aliases,
        compiler_params=PARAMS,
        name=f"chain_{stage}",
    )(*args)


def middle_kernel(*refs):
    info_ref, refs = refs[0], refs[1:]
    one_refs, two_refs, vt_ref = refs[:RING], refs[RING : 2 * RING], refs[2 * RING]
    outs = refs[2 * RING + 1 : 3 * RING + 1]
    slope_ref, back_ref, one, two, vt, vs, slope, back, sems = refs[3 * RING + 1 :]

    @pl.when(info_ref[1] == 1)
    def _():
        copies = [pltpu.make_async_copy(one_refs[j], one.at[j], sems.at[j]) for j in range(RING)]
        copies += [
            pltpu.make_async_copy(two_refs[j], two.at[j], sems.at[RING + j]) for j in range(RING)
        ]
        copies.append(pltpu.make_async_copy(vt_ref, vt, sems.at[2 * RING]))
        for copy in copies:
            copy.start()
        for copy in copies:
            copy.wait()

        def step(j, carry):
            v, t0 = vt[j, :, 0:CELLS], vt[j, :, CELLS:]
            w0, w1 = one[j][:, 0:576], two[j][:, 0:576]
            b1, a = two[j][:, 576:577], two[j][:, WPAD:BLK]
            s0 = 1.0 - t0 * t0
            t1 = jnp.tanh(conv(lhs_forward(w1), v + H * t0, 1) + b1)
            s1 = 1.0 - t1 * t1
            shift = H * conv(lhs_backward(w1), s1 * a, -1)
            lhs = lhs_backward(w0)
            back[j] = lhs
            slope[j] = s0
            vs[j, :, 0:CELLS] = v
            vs[j, :, CELLS:] = shift + conv(lhs, s0 * (H * (a + shift) - 2 * H * a), -1)
            return carry

        lax.fori_loop(0, RING, step, 0)
        copies = [pltpu.make_async_copy(vs.at[j], outs[j], sems.at[j]) for j in range(RING)]
        copies.append(pltpu.make_async_copy(slope, slope_ref, sems.at[RING]))
        copies.append(pltpu.make_async_copy(back, back_ref, sems.at[RING + 1]))
        for copy in copies:
            copy.start()
        for copy in copies:
            copy.wait()


def middle(info, ones, twos, vt):
    vs_shape = jax.ShapeDtypeStruct((CH, 2 * CELLS), F32)
    out = pl.pallas_call(
        middle_kernel,
        out_shape=(vs_shape,) * RING
        + (
            jax.ShapeDtypeStruct((RING, CH, CELLS), F32),
            jax.ShapeDtypeStruct((RING, 9 * CH, 3 * CH), BF16),
        ),
        in_specs=[SMEM] + [ANY] * (2 * RING + 1),
        out_specs=(ANY,) * (RING + 2),
        scratch_shapes=[
            pltpu.VMEM((RING, CH, BLK), F32),
            pltpu.VMEM((RING, CH, BLK), F32),
            pltpu.VMEM((RING, CH, 2 * CELLS), F32),
            pltpu.VMEM((RING, CH, 2 * CELLS), F32),
            pltpu.VMEM((RING, CH, CELLS), F32),
            pltpu.VMEM((RING, 9 * CH, 3 * CH), BF16),
            pltpu.SemaphoreType.DMA((2 * RING + 1,)),
        ],
        compiler_params=PARAMS,
        name="middle",
    )(info, *ones, *twos, vt)
    return out[:RING], out[RING], out[RING + 1]


def back_kernel(stage, last, *refs):
    info_ref, slope_ref, back_ref, refs = refs[0], refs[1], refs[2], refs[3:]
    vs_refs, mu_ref = refs[:RING], refs[RING]
    outs = refs[-(RING + 6) : -6]
    out_ref, sigma, slope, back, mus, sems = refs[-6:]

    @pl.when((info_ref[0] == stage) & (info_ref[1] == 1))
    def _():
        copies = [
            pltpu.make_async_copy(vs_refs[j].at[:, pl.ds(CELLS, CELLS)], sigma.at[j], sems.at[j])
            for j in range(RING)
        ]
        copies.append(pltpu.make_async_copy(slope_ref, slope, sems.at[RING]))
        copies.append(pltpu.make_async_copy(back_ref, back, sems.at[RING + 1]))
        for copy in copies:
            copy.start()
        for copy in copies:
            copy.wait()
        start = mu_ref[:, WPAD:BLK] if stage == last else mu_ref[...]

        def step(k, mu):
            j = RING - 1 - k
            mus[j] = mu
            return mu + 2 * H * conv(back[j], slope[j] * mu, -1) + sigma[j]

        out_ref[...] = lax.fori_loop(0, RING, step, start)
        copies = [pltpu.make_async_copy(mus.at[j], outs[j], sems.at[j]) for j in range(RING)]
        for copy in copies:
            copy.start()
        for copy in copies:
            copy.wait()


def back_chain(stage, last, info, slope, back, vs, mu, previous):
    args = [info, slope, back, *vs, mu]
    specs = [SMEM, ANY, ANY] + [ANY] * RING + [VMEM]
    aliases = {}
    if previous is not None:
        aliases = {len(args) + j: j for j in range(RING)}
        args += list(previous)
        specs += [ANY] * RING
    shape = jax.ShapeDtypeStruct((CH, CELLS), F32)
    out = pl.pallas_call(
        lambda *refs: back_kernel(stage, last, *refs),
        out_shape=(shape,) * (RING + 1),
        in_specs=specs,
        out_specs=(ANY,) * RING + (VMEM,),
        scratch_shapes=[
            pltpu.VMEM((RING, CH, CELLS), F32),
            pltpu.VMEM((RING, CH, CELLS), F32),
            pltpu.VMEM((RING, 9 * CH, 3 * CH), BF16),
            pltpu.VMEM((RING, CH, CELLS), F32),
            pltpu.SemaphoreType.DMA((RING + 2,)),
        ],
        input_output_aliases=aliases,
        compiler_params=PARAMS,
        name=f"back_{stage}",
    )(*args)
    return out[:RING], out[RING]


def fetch(place, refs, target, sem):
    for m in range(RING):

        @pl.when(place == m)
        def _():
            copy = pltpu.make_async_copy(refs[m], target, sem)
            copy.start()
            copy.wait()


def early_kernel(*refs):
    info_ref, one_ref, w_ref, b_ref, refs = refs[0], refs[1], refs[2], refs[3], refs[4:]
    vs_refs = refs[:RING]
    states_ref, m_ref, s0_ref, s1_ref, vs_ref, sem = refs[RING:]
    fetch(info_ref[2], vs_refs, vs_ref, sem)
    v = vs_ref[:, 0:CELLS]
    t0 = jnp.tanh(conv(lhs_forward(w_ref[0]), v, 1) + as_column(b_ref[0:1]))
    m = v + H * t0
    t1 = jnp.tanh(conv(lhs_forward(w_ref[1]), m, 1) + as_column(b_ref[1:2]))
    m_ref[...] = m
    states_ref[0] = swap(m)
    states_ref[1] = swap(v + 2 * H * t0 + one_ref[:, WPAD:BLK])
    s0_ref[...] = 1.0 - t0 * t0
    s1_ref[...] = 1.0 - t1 * t1


def early(info, one, w, b, vs):
    shape = jax.ShapeDtypeStruct((CH, CELLS), F32)
    return pl.pallas_call(
        early_kernel,
        out_shape=(
            jax.ShapeDtypeStruct((2, CH, CELLS), F32),
            shape,
            shape,
            shape,
            jax.ShapeDtypeStruct((CH, 2 * CELLS), F32),
        ),
        in_specs=[SMEM, VMEM, VMEM, VMEM] + [ANY] * RING,
        scratch_shapes=[pltpu.SemaphoreType.DMA],
        compiler_params=PARAMS,
        name="early",
    )(info, one, w, b, *vs)


def late_kernel(*refs):
    info_ref, w_ref, m_ref, s0_ref, s1_ref, vs_ref = refs[:6]
    mu_refs = refs[6 : 6 + RING]
    adjoints_ref, mine_ref, other_ref, mu_scratch, sem = refs[6 + RING :]
    fetch(info_ref[2], mu_refs, mu_scratch, sem)
    mu = mu_scratch[...]
    v, sigma = vs_ref[:, 0:CELLS], vs_ref[:, CELLS:]
    s0 = s0_ref[...]
    odd_product = s1_ref[...] * mu
    odd = mu + H * conv(lhs_backward(w_ref[1]), odd_product, -1)
    even = mu + 2 * H * conv(lhs_backward(w_ref[0]), s0 * mu, -1) + sigma
    adjoints_ref[0] = swap(even)
    adjoints_ref[1] = swap(odd)
    even_term = (H / 8) * (s0 * odd)
    odd_term = (H / 8) * odd_product
    even_grad, odd_grad = correlate(even_term, v), correlate(odd_term, m_ref[...])
    pad = (CH, WPAD - 576)
    even_bias = jnp.broadcast_to(jnp.sum(even_term, axis=1, keepdims=True), pad)
    odd_bias = jnp.broadcast_to(jnp.sum(odd_term, axis=1, keepdims=True), pad)

    def write(ref, grad, bias):
        ref[:, 0:576] = grad
        ref[:, 576:WPAD] = bias

    @pl.when(info_ref[3] == 0)
    def _():
        write(mine_ref, even_grad, even_bias)
        write(other_ref, odd_grad, odd_bias)

    @pl.when(info_ref[3] == 1)
    def _():
        write(mine_ref, odd_grad, odd_bias)
        write(other_ref, even_grad, even_bias)


def late(info, w, m, s0, s1, vs, mus):
    grad = jax.ShapeDtypeStruct((CH, WPAD), F32)
    return pl.pallas_call(
        late_kernel,
        out_shape=(jax.ShapeDtypeStruct((2, CH, CELLS), F32), grad, grad),
        in_specs=[SMEM] + [VMEM] * 5 + [ANY] * RING,
        scratch_shapes=[pltpu.VMEM((CH, CELLS), F32), pltpu.SemaphoreType.DMA],
        compiler_params=PARAMS,
        name="late",
    )(info, w, m, s0, s1, vs, *mus)


def after(first, *others):
    return lax.optimization_barrier((first, *others))[1:]


def body(coarse_guess, adjoint_guess, weights, biases):
    images = lax.axis_size("dp")
    groups = lax.axis_size("layer") // RING
    layer, image = lax.axis_index("layer"), lax.axis_index("dp")

    def device(x, z, d):
        return (RING * x + z) * images + d

    def lead(d):
        return (RING // 2) * (d % 2)

    def gather(value, m):
        pairs = [
            (device(x, m, d), device(x, lead(d), d)) for x in range(groups) for d in range(images)
        ]
        return lax.ppermute(value, AXES, pairs)

    def scatter(value, m):
        pairs = [
            (device(x, lead(d), d), device(x, m, d)) for x in range(groups) for d in range(images)
        ]
        return lax.ppermute(value, AXES, pairs)

    def hop(value, source, target):
        pairs = [
            (device(source, lead(d), d), device(target, lead(d), d)) for d in range(images)
        ]
        return lax.ppermute(value, AXES, pairs)

    place = layer % RING
    info = jnp.stack(
        [layer // RING, (place == lead(image)).astype(jnp.int32), place, image % 2]
    ).astype(jnp.int32)
    c, a = coarse_guess[0, 0], adjoint_guess[0, 0]
    v = lax.ppermute(c, AXES, [(device(0, 0, d), device(0, lead(d), d)) for d in range(images)])
    one, two = relax(c, a, weights, biases)
    ones = [gather(one, m) for m in range(RING)]
    twos, waiting = [], list(range(RING))
    vt = None
    for stage in range(groups):
        vt, end = chain(stage, info, ones, v, vt)
        if stage < groups - 1:
            v = hop(end, stage, stage + 1)
            for m in waiting[: 3 if stage < groups - 2 else RING]:
                (operand,) = after(end, two)
                twos.append(gather(operand, m))
                waiting = waiting[1:]
    vs, slope, back = middle(info, ones, twos, vt)
    mus, mu = None, twos[RING - 1]
    own, waiting = [], list(range(RING))
    for stage in range(groups - 1, -1, -1):
        mus, end = back_chain(stage, groups - 1, info, slope, back, vs, mu, mus)
        if stage > 0:
            mu = hop(end, stage, stage - 1)
            for m in waiting[: 3 if stage > 1 else RING]:
                (operand,) = after(end, vs[m])
                own.append(scatter(operand, m))
                waiting = waiting[1:]
        if stage == 1:
            states, mid, s0, s1, own_vs = early(info, one, weights, biases, own)
            (mu,) = after(s1, mu)
    own_mu = [scatter(mus[m], m) for m in range(RING)]
    adjoints, mine, other = late(info, weights, mid, s0, s1, own_vs, own_mu)
    mine = mine + lax.ppermute(other, "dp", [(i, i ^ 1) for i in range(images)])
    for flip in (2, 6):
        mine = mine + lax.ppermute(mine, "dp", [(i, i ^ flip) for i in range(images)])
    other = lax.ppermute(mine, "dp", [(i, i ^ 1) for i in range(images)])
    first = image % 2 == 0
    even, odd = jnp.where(first, mine, other), jnp.where(first, other, mine)
    grad = jnp.stack([even[:, :576], odd[:, :576]])
    bias = jnp.stack([even[:, 576], odd[:, 576]])
    return states[:, None], adjoints[:, None], grad, bias


def solution(mesh):
    return jax.shard_map(
        body,
        mesh=mesh,
        in_specs=(
            P("layer", "dp", None, None),
            P("layer", "dp", None, None),
            P("layer", None, None),
            P("layer", None),
        ),
        out_specs=(
            P("layer", "dp", None, None),
            P("layer", "dp", None, None),
            P("layer", None, None),
            P("layer", None),
        ),
        check_vma=False,
    )
```

time: 801 us -> 187 us (0.23)
  waiting for transfers between devices: 345 us -> 80.9 us
  starting transfers between devices: 202 us -> 84.3 us
  blocking collectives: 80 us -> 0 us
  matrix products: 74.1 us -> 0 us
  other arithmetic: 65 us -> 1.47 us
  Pallas kernels: 0 us -> 14 us
  between operations: 14.9 us -> 1.4 us
  loops' own time: 8.89 us -> 0 us
    ppermute x62 -> x43, waiting for transfers between devices: 279 us -> 80.9 us  [the longest x16 66.8 us: scatter(): return lax.ppermute(value, AXES, pairs)]
    ppermute x62 -> x43, starting transfers between devices: 202 us -> 84.3 us  [the longest x16 36.9 us: gather(): return lax.ppermute(value, AXES, pairs)]
    psum x1 -> x0, blocking collectives: 80 us -> none  [body(): grad_total, bias_total = lax.psum((grad_parts, bias_parts), 'dp')]
    dot_general x73 -> x0, matrix products: 74.1 us -> none  [the longest x71 70.4 us: convolve(): jnp.einsum('ok,bkc->boc', matrix, patches(state_field, orient), precision...]
    psum x1 -> x0, waiting for transfers between devices: 65.9 us -> none  [body(): grad_total, bias_total = lax.psum((grad_parts, bias_parts), 'dp')]
    while x496 -> x0, other arithmetic: 43.2 us -> none
    pallas_call x0 -> x12, Pallas kernels: none -> 14 us  [the longest x4 3.45 us: back_chain(): pl.pallas_call(lambda *refs: back_kernel(stage, last, *refs), out_shape=(...]
    another operation x2 -> x0, loops' own time: 8.89 us -> none  [the longest x1 4.78 us: body(): lax.fori_loop(0, last_place, backward_turn, (terminal_side, fine_adjoint))]
  transfers between devices with their start and end apart: 63 -> 43, of which waited for: 63 -> 8; matrix products, arithmetic and copies ran while one was open for 0% -> 0% of each run, Pallas kernels for 0% -> 3%
where the time goes in v1:
time: 187 us; the launch traced here: 186 us
  starting transfers between devices  84.3 us (45%)
  waiting for transfers between devices  80.9 us (43%)
  Pallas kernels  14 us (7%)
  local copies, waits for them, and re-layouts  3.67 us (2%)
    ppermute x16, waiting for transfers between devices, scatter(): return lax.ppermute(value, AXES, pairs)  66.8 us
    ppermute x16, starting transfers between devices, gather(): return lax.ppermute(value, AXES, pairs)  36.9 us
    ppermute x1, starting transfers between devices, body(): mine = mine + lax.ppermute(other, 'dp', [(i, i ^ 1) for i in range(images)])  13.5 us
    ppermute x16, starting transfers between devices, scatter(): return lax.ppermute(value, AXES, pairs)  12 us
    ppermute x1, starting transfers between devices, body(): lax.ppermute(c, AXES, [(device(0, 0, d), device(0, lead(d), d)) for d in...  11.5 us
    ppermute x2, waiting for transfers between devices, body(): lax.ppermute(mine, 'dp', [(i, i ^ flip) for i in range(images)])  7.2 us
    ppermute x2, starting transfers between devices, body(): lax.ppermute(mine, 'dp', [(i, i ^ flip) for i in range(images)])  4.17 us
    ppermute x6, starting transfers between devices, hop(): return lax.ppermute(value, AXES, pairs)  4.01 us
  transfers between devices with their start and end apart: 43, of which 8 were waited for; matrix products, arithmetic and copies ran while one was open for 0% of the time, Pallas kernels for 3%

profile of v1, /device:TPU:1, one launch (start us, length us, event | category | flops | bytes accessed | tf_op | source)
XLA Modules:
  0.0 185.7 jit_solution(5469708499239692571)
XLA Ops:
  0.6 1.0 copy-done
  1.6 0.9 copy-done.2
  2.5 0.9 copy-done.3
  3.4 0.7 copy-done.4
  4.1 1.1 relax.1
  5.2 0.7 collective-permute-start.7
  5.8 0.7 collective-permute-start.6
  6.5 0.7 collective-permute-start.5
  7.2 11.5 %collective-permute-start.8 = (f32[64,512]{1,0:T(8,128)S(1)}, f32[64,512]{1,0:T(8,128)S(1)}, u32[]{:S(2)}, u32[]{:S(2)}) collective-permute-start(f32[64,512]{1,0:T(8,128)S(1)} %bitcast.20), channel_id=1, source_target_pairs={{0,0},{1,33},{2,2},{3,35},{4,4},{5,37},{6,6},{7,39}} | collective-permute-start | bytes 393224 | tf_op jit(solution)/shard_map/ppermute | solution.py:480
  18.7 0.7 collective-permute-start.4
  19.4 1.2 collective-permute-done.8.refs_9_
  21.3 0.7 collective-permute-start.2
  22.0 0.7 collective-permute-start.1
  22.7 9.5 %collective-permute-start = (f32[64,1152]{1,0:T(8,128)S(1)}, f32[64,1152]{1,0:T(8,128)S(1)}, u32[]{:S(2)}, u32[]{:S(2)}) collective-permute-start(f32[64,1152]{1,0:T(8,128)S(1)} %get-tuple-element.78.refs_1_), channel_id=1, source_target_pairs={{0,0},{1,33},{2,2},{3,35},{4,4},{5,37},{6,6},{7,39},{64,64},{65,97... | collective-permute-start | bytes 884744 | tf_op jit(solution)/shard_map/ppermute | solution.py:461
  32.4 3.5 %collective-permute-done.refs_1_ = f32[64,1152]{1,0:T(8,128)S(1)} collective-permute-done((f32[64,1152]{1,0:T(8,128)S(1)}, f32[64,1152]{1,0:T(8,128)S(1)}, u32[]{:S(2)}, u32[]{:S(2)}) %collective-permute-start) | collective-permute-done | bytes 294944 | tf_op jit(solution)/shard_map/ppermute | solution.py:461
  37.2 0.7 collective-permute-start.11
  37.9 0.7 collective-permute-start.10
  38.6 17.9 %collective-permute-start.9 = (f32[64,1152]{1,0:T(8,128)S(1)}, f32[64,1152]{1,0:T(8,128)S(1)}, u32[]{:S(2)}, u32[]{:S(2)}) collective-permute-start(f32[64,1152]{1,0:T(8,128)S(1)} %get-tuple-element.87), channel_id=1, source_target_pairs={{0,0},{1,33},{2,2},{3,35},{4,4},{5,37},{6,6},{7,39},{64,64},{65,97... | collective-permute-start | bytes 884744 | tf_op jit(solution)/shard_map/ppermute | solution.py:461
  58.5 0.7 collective-permute-start.19
  59.2 0.7 collective-permute-start.15
  59.9 0.7 collective-permute-start.14
  60.6 0.7 collective-permute-start.13
  61.3 0.7 collective-permute-start.18
  61.9 0.7 collective-permute-start.17
  62.6 1.3 chain_3.1
  64.0 0.7 middle.1
  66.0 1.3 collective-permute-start.20
  67.3 0.7 collective-permute-start.21
  68.0 0.7 collective-permute-start.22
  70.1 0.7 collective-permute-start.24
  70.8 0.7 collective-permute-start.25
  72.1 34.9 %collective-permute-done.20.refs_4_ = f32[64,1024]{1,0:T(8,128)S(1)} collective-permute-done((f32[64,1024]{1,0:T(8,128)S(1)}, f32[64,1024]{1,0:T(8,128)S(1)}, u32[]{:S(2)}, u32[]{:S(2)}) %collective-permute-start.20) | collective-permute-done | bytes 262176 | tf_op jit(solution)/shard_map/ppermute | solution.py:467
  107.7 0.7 collective-permute-start.28
  108.4 0.7 collective-permute-start.29
  109.8 2.3 %early.1 = (f32[2,64,512]{2,1,0:T(8,128)}, f32[64,512]{1,0:T(8,128)S(1)}, f32[64,512]{1,0:T(8,128)S(1)}, f32[64,512]{1,0:T(8,128)S(1)}, f32[64,1024]{1,0:T(8,128)S(1)}) custom-call(s32[4]{0:T(128)S(1)} %pad_add_fusion.refs_0_, f32[64,1152]{1,0:T(8,128)S(1)} %get-tuple-element.78.refs_1_, f32[2,64,576]{2,1,0:T(8,128)S(1)} %copy-done.1, ...), custom_call_target="tpu_custom_call" | custom-call | tf_op jit(solution)/shard_map/early/pallas_call | solution.py:379
  112.1 1.5 back_0.1
  113.6 1.3 collective-permute-start.31
  117.6 31.9 %collective-permute-done.31.refs_6_ = f32[64,512]{1,0:T(8,128)S(1)} collective-permute-done((f32[64,512]{1,0:T(8,128)S(1)}, f32[64,512]{1,0:T(8,128)S(1)}, u32[]{:S(2)}, u32[]{:S(2)}) %collective-permute-start.31) | collective-permute-done | bytes 131104 | tf_op jit(solution)/shard_map/ppermute | solution.py:467
  151.6 3.4 %late.1 = (f32[2,64,512]{2,1,0:T(8,128)}, f32[64,640]{1,0:T(8,128)S(1)}, f32[64,640]{1,0:T(8,128)S(1)}) custom-call(s32[4]{0:T(128)S(1)} %pad_add_fusion.refs_0_, f32[2,64,576]{2,1,0:T(8,128)S(1)} %copy-done.1, f32[64,512]{1,0:T(8,128)S(1)} %get-tuple-element.128.refs_2_, f32[64,512]{1,0:T(8,128)S(1)} %get-tuple-element.129.refs_3_, ...), custom_call_target="tpu_custom_call" | custom-call | tf_op jit(solution)/shard_map/late/pallas_call | solution.py:432
  155.0 13.5 %collective-permute-start.39 = (f32[64,640]{1,0:T(8,128)S(1)}, f32[64,640]{1,0:T(8,128)S(1)}, u32[]{:S(2)}, u32[]{:S(2)}) collective-permute-start(f32[64,640]{1,0:T(8,128)S(1)} %get-tuple-element.151), channel_id=1, source_target_pairs={{0,1},{1,0},{2,3},{3,2},{4,5},{5,4},{6,7},{7,6},{8,9},{9,8},{10,11... | collective-permute-start | bytes 491528 | tf_op jit(solution)/shard_map/ppermute | solution.py:509
  168.5 1.0 collective-permute-done.39
  169.5 1.4 collective-permute-start.40
  170.9 4.1 %collective-permute-done.40 = f32[64,640]{1,0:T(8,128)S(1)} collective-permute-done((f32[64,640]{1,0:T(8,128)S(1)}, f32[64,640]{1,0:T(8,128)S(1)}, u32[]{:S(2)}, u32[]{:S(2)}) %collective-permute-start.40) | collective-permute-done | bytes 163872 | tf_op jit(solution)/shard_map/ppermute | solution.py:511
  175.1 2.8 %collective-permute-start.41 = (f32[64,640]{1,0:T(8,128)S(1)}, f32[64,640]{1,0:T(8,128)S(1)}, u32[]{:S(2)}, u32[]{:S(2)}) collective-permute-start(f32[64,640]{1,0:T(8,128)S(1)} %add.22), channel_id=1, source_target_pairs={{0,6},{1,7},{2,4},{3,5},{4,2},{5,3},{6,0},{7,1},{8,14},{9,15},{10,... | collective-permute-start | bytes 491528 | tf_op jit(solution)/shard_map/ppermute | solution.py:511
  177.9 3.1 %collective-permute-done.41 = f32[64,640]{1,0:T(8,128)S(1)} collective-permute-done((f32[64,640]{1,0:T(8,128)S(1)}, f32[64,640]{1,0:T(8,128)S(1)}, u32[]{:S(2)}, u32[]{:S(2)}) %collective-permute-start.41) | collective-permute-done | bytes 163872 | tf_op jit(solution)/shard_map/ppermute | solution.py:511
  181.0 2.2 %collective-permute-start.42 = (f32[64,640]{1,0:T(8,128)S(1)}, f32[64,640]{1,0:T(8,128)S(1)}, u32[]{:S(2)}, u32[]{:S(2)}) collective-permute-start(f32[64,640]{1,0:T(8,128)S(1)} %add.23), channel_id=1, source_target_pairs={{0,1},{1,0},{2,3},{3,2},{4,5},{5,4},{6,7},{7,6},{8,9},{9,8},{10,11... | collective-permute-start | bytes 491528 | tf_op jit(solution)/shard_map/ppermute | solution.py:512
  183.1 1.0 collective-permute-done.42
  185.0 0.7 pad_maximum_fusion
  (71 shorter events, 14.2 us)
Async XLA Ops:
  0.6 1.0 copy-start
  1.6 0.9 copy-start.2
  2.5 0.9 copy-start.3
  5.2 16.2 %collective-permute-start.7 = (f32[64,1152]{1,0:T(8,128)S(1)}, f32[64,1152]{1,0:T(8,128)S(1)}, u32[]{:S(2)}, u32[]{:S(2)}) collective-permute-start(f32[64,1152]{1,0:T(8,128)S(1)} %get-tuple-element.78.refs_1_), channel_id=1, source_target_pairs={{56,0},{57,33},{58,2},{59,35},{60,4},{61,37},{62,6},{63,39},{120,6... | collective-permute-start | bytes 884744 | tf_op jit(solution)/shard_map/ppermute | solution.py:461
  5.8 16.2 %collective-permute-start.6 = (f32[64,1152]{1,0:T(8,128)S(1)}, f32[64,1152]{1,0:T(8,128)S(1)}, u32[]{:S(2)}, u32[]{:S(2)}) collective-permute-start(f32[64,1152]{1,0:T(8,128)S(1)} %get-tuple-element.78.refs_1_), channel_id=1, source_target_pairs={{48,0},{49,33},{50,2},{51,35},{52,4},{53,37},{54,6},{55,39},{112,6... | collective-permute-start | bytes 884744 | tf_op jit(solution)/shard_map/ppermute | solution.py:461
  6.5 16.2 %collective-permute-start.5 = (f32[64,1152]{1,0:T(8,128)S(1)}, f32[64,1152]{1,0:T(8,128)S(1)}, u32[]{:S(2)}, u32[]{:S(2)}) collective-permute-start(f32[64,1152]{1,0:T(8,128)S(1)} %get-tuple-element.78.refs_1_), channel_id=1, source_target_pairs={{40,0},{41,33},{42,2},{43,35},{44,4},{45,37},{46,6},{47,39},{104,6... | collective-permute-start | bytes 884744 | tf_op jit(solution)/shard_map/ppermute | solution.py:461
  7.2 13.4 %collective-permute-start.8 = (f32[64,512]{1,0:T(8,128)S(1)}, f32[64,512]{1,0:T(8,128)S(1)}, u32[]{:S(2)}, u32[]{:S(2)}) collective-permute-start(f32[64,512]{1,0:T(8,128)S(1)} %bitcast.20), channel_id=1, source_target_pairs={{0,0},{1,33},{2,2},{3,35},{4,4},{5,37},{6,6},{7,39}} | collective-permute-start | bytes 393224 | tf_op jit(solution)/shard_map/ppermute | solution.py:480
  18.7 13.7 %collective-permute-start.4 = (f32[64,1152]{1,0:T(8,128)S(1)}, f32[64,1152]{1,0:T(8,128)S(1)}, u32[]{:S(2)}, u32[]{:S(2)}) collective-permute-start(f32[64,1152]{1,0:T(8,128)S(1)} %get-tuple-element.78.refs_1_), channel_id=1, source_target_pairs={{32,0},{33,33},{34,2},{35,35},{36,4},{37,37},{38,6},{39,39},{96,64... | collective-permute-start | bytes 884744 | tf_op jit(solution)/shard_map/ppermute | solution.py:461
  20.6 11.7 %collective-permute-start.3 = (f32[64,1152]{1,0:T(8,128)S(1)}, f32[64,1152]{1,0:T(8,128)S(1)}, u32[]{:S(2)}, u32[]{:S(2)}) collective-permute-start(f32[64,1152]{1,0:T(8,128)S(1)} %get-tuple-element.78.refs_1_), channel_id=1, source_target_pairs={{24,0},{25,33},{26,2},{27,35},{28,4},{29,37},{30,6},{31,39},{88,64... | collective-permute-start | bytes 884744 | tf_op jit(solution)/shard_map/ppermute | solution.py:461
  21.3 11.1 %collective-permute-start.2 = (f32[64,1152]{1,0:T(8,128)S(1)}, f32[64,1152]{1,0:T(8,128)S(1)}, u32[]{:S(2)}, u32[]{:S(2)}) collective-permute-start(f32[64,1152]{1,0:T(8,128)S(1)} %get-tuple-element.78.refs_1_), channel_id=1, source_target_pairs={{16,0},{17,33},{18,2},{19,35},{20,4},{21,37},{22,6},{23,39},{80,64... | collective-permute-start | bytes 884744 | tf_op jit(solution)/shard_map/ppermute | solution.py:461
  22.0 10.4 %collective-permute-start.1 = (f32[64,1152]{1,0:T(8,128)S(1)}, f32[64,1152]{1,0:T(8,128)S(1)}, u32[]{:S(2)}, u32[]{:S(2)}) collective-permute-start(f32[64,1152]{1,0:T(8,128)S(1)} %get-tuple-element.78.refs_1_), channel_id=1, source_target_pairs={{8,0},{9,33},{10,2},{11,35},{12,4},{13,37},{14,6},{15,39},{72,64},... | collective-permute-start | bytes 884744 | tf_op jit(solution)/shard_map/ppermute | solution.py:461
  22.7 13.2 %collective-permute-start = (f32[64,1152]{1,0:T(8,128)S(1)}, f32[64,1152]{1,0:T(8,128)S(1)}, u32[]{:S(2)}, u32[]{:S(2)}) collective-permute-start(f32[64,1152]{1,0:T(8,128)S(1)} %get-tuple-element.78.refs_1_), channel_id=1, source_target_pairs={{0,0},{1,33},{2,2},{3,35},{4,4},{5,37},{6,6},{7,39},{64,64},{65,97... | collective-permute-start | bytes 884744 | tf_op jit(solution)/shard_map/ppermute | solution.py:461
  36.6 20.0 %collective-permute-start.12 = (f32[64,512]{1,0:T(8,128)S(1)}, f32[64,512]{1,0:T(8,128)S(1)}, u32[]{:S(2)}, u32[]{:S(2)}) collective-permute-start(f32[64,512]{1,0:T(8,128)S(1)} %get-tuple-element.79), channel_id=1, source_target_pairs={{0,64},{33,97},{2,66},{35,99},{4,68},{37,101},{6,70},{39,103}} | collective-permute-start | bytes 393224 | tf_op jit(solution)/shard_map/ppermute | solution.py:473
  37.2 22.6 %collective-permute-start.11 = (f32[64,1152]{1,0:T(8,128)S(1)}, f32[64,1152]{1,0:T(8,128)S(1)}, u32[]{:S(2)}, u32[]{:S(2)}) collective-permute-start(f32[64,1152]{1,0:T(8,128)S(1)} %get-tuple-element.87), channel_id=1, source_target_pairs={{16,0},{17,33},{18,2},{19,35},{20,4},{21,37},{22,6},{23,39},{80,64... | collective-permute-start | bytes 884744 | tf_op jit(solution)/shard_map/ppermute | solution.py:461
  37.9 22.6 %collective-permute-start.10 = (f32[64,1152]{1,0:T(8,128)S(1)}, f32[64,1152]{1,0:T(8,128)S(1)}, u32[]{:S(2)}, u32[]{:S(2)}) collective-permute-start(f32[64,1152]{1,0:T(8,128)S(1)} %get-tuple-element.87), channel_id=1, source_target_pairs={{8,0},{9,33},{10,2},{11,35},{12,4},{13,37},{14,6},{15,39},{72,64},... | collective-permute-start | bytes 884744 | tf_op jit(solution)/shard_map/ppermute | solution.py:461
  38.6 22.6 %collective-permute-start.9 = (f32[64,1152]{1,0:T(8,128)S(1)}, f32[64,1152]{1,0:T(8,128)S(1)}, u32[]{:S(2)}, u32[]{:S(2)}) collective-permute-start(f32[64,1152]{1,0:T(8,128)S(1)} %get-tuple-element.87), channel_id=1, source_target_pairs={{0,0},{1,33},{2,2},{3,35},{4,4},{5,37},{6,6},{7,39},{64,64},{65,97... | collective-permute-start | bytes 884744 | tf_op jit(solution)/shard_map/ppermute | solution.py:461
  57.2 0.7 collective-permute-start.16
  58.5 3.5 %collective-permute-start.19 = (f32[64,512]{1,0:T(8,128)S(1)}, f32[64,512]{1,0:T(8,128)S(1)}, u32[]{:S(2)}, u32[]{:S(2)}) collective-permute-start(f32[64,512]{1,0:T(8,128)S(1)} %get-tuple-element.86), channel_id=1, source_target_pairs={{128,192},{161,225},{130,194},{163,227},{132,196},{165,229},{134,1... | collective-permute-start | bytes 393224 | tf_op jit(solution)/shard_map/ppermute | solution.py:473
  59.2 4.8 %collective-permute-start.15 = (f32[64,1152]{1,0:T(8,128)S(1)}, f32[64,1152]{1,0:T(8,128)S(1)}, u32[]{:S(2)}, u32[]{:S(2)}) collective-permute-start(f32[64,1152]{1,0:T(8,128)S(1)} %get-tuple-element.87), channel_id=1, source_target_pairs={{40,0},{41,33},{42,2},{43,35},{44,4},{45,37},{46,6},{47,39},{104,6... | collective-permute-start | bytes 884744 | tf_op jit(solution)/shard_map/ppermute | solution.py:461
  59.9 4.1 %collective-permute-start.14 = (f32[64,1152]{1,0:T(8,128)S(1)}, f32[64,1152]{1,0:T(8,128)S(1)}, u32[]{:S(2)}, u32[]{:S(2)}) collective-permute-start(f32[64,1152]{1,0:T(8,128)S(1)} %get-tuple-element.87), channel_id=1, source_target_pairs={{32,0},{33,33},{34,2},{35,35},{36,4},{37,37},{38,6},{39,39},{96,64... | collective-permute-start | bytes 884744 | tf_op jit(solution)/shard_map/ppermute | solution.py:461
  60.6 3.4 %collective-permute-start.13 = (f32[64,1152]{1,0:T(8,128)S(1)}, f32[64,1152]{1,0:T(8,128)S(1)}, u32[]{:S(2)}, u32[]{:S(2)}) collective-permute-start(f32[64,1152]{1,0:T(8,128)S(1)} %get-tuple-element.87), channel_id=1, source_target_pairs={{24,0},{25,33},{26,2},{27,35},{28,4},{29,37},{30,6},{31,39},{88,64... | collective-permute-start | bytes 884744 | tf_op jit(solution)/shard_map/ppermute | solution.py:461
  61.3 2.7 %collective-permute-start.18 = (f32[64,1152]{1,0:T(8,128)S(1)}, f32[64,1152]{1,0:T(8,128)S(1)}, u32[]{:S(2)}, u32[]{:S(2)}) collective-permute-start(f32[64,1152]{1,0:T(8,128)S(1)} %get-tuple-element.87), channel_id=1, source_target_pairs={{56,0},{57,33},{58,2},{59,35},{60,4},{61,37},{62,6},{63,39},{120,6... | collective-permute-start | bytes 884744 | tf_op jit(solution)/shard_map/ppermute | solution.py:461
  61.9 2.0 %collective-permute-start.17 = (f32[64,1152]{1,0:T(8,128)S(1)}, f32[64,1152]{1,0:T(8,128)S(1)}, u32[]{:S(2)}, u32[]{:S(2)}) collective-permute-start(f32[64,1152]{1,0:T(8,128)S(1)} %get-tuple-element.87), channel_id=1, source_target_pairs={{48,0},{49,33},{50,2},{51,35},{52,4},{53,37},{54,6},{55,39},{112,6... | collective-permute-start | bytes 884744 | tf_op jit(solution)/shard_map/ppermute | solution.py:461
  65.4 3.4 %collective-permute-start.23 = (f32[64,512]{1,0:T(8,128)S(1)}, f32[64,512]{1,0:T(8,128)S(1)}, u32[]{:S(2)}, u32[]{:S(2)}) collective-permute-start(f32[64,512]{1,0:T(8,128)S(1)} %get-tuple-element.100), channel_id=1, source_target_pairs={{192,128},{225,161},{194,130},{227,163},{196,132},{229,165},{198,1... | collective-permute-start | bytes 393224 | tf_op jit(solution)/shard_map/ppermute | solution.py:473
  66.0 41.0 %collective-permute-start.20 = (f32[64,1024]{1,0:T(8,128)S(1)}, f32[64,1024]{1,0:T(8,128)S(1)}, u32[]{:S(2)}, u32[]{:S(2)}) collective-permute-start(f32[64,1024]{1,0:T(8,128)S(1)} %get-tuple-element.101.refs_3_), channel_id=1, source_target_pairs={{0,0},{33,1},{2,2},{35,3},{4,4},{37,5},{6,6},{39,7},{64,64},{97,65... | collective-permute-start | bytes 786440 | tf_op jit(solution)/shard_map/ppermute | solution.py:467
  67.3 40.4 %collective-permute-start.21 = (f32[64,1024]{1,0:T(8,128)S(1)}, f32[64,1024]{1,0:T(8,128)S(1)}, u32[]{:S(2)}, u32[]{:S(2)}) collective-permute-start(f32[64,1024]{1,0:T(8,128)S(1)} %get-tuple-element.102.refs_4_), channel_id=1, source_target_pairs={{0,8},{33,9},{2,10},{35,11},{4,12},{37,13},{6,14},{39,15},{64,72},... | collective-permute-start | bytes 786440 | tf_op jit(solution)/shard_map/ppermute | solution.py:467
  68.0 40.4 %collective-permute-start.22 = (f32[64,1024]{1,0:T(8,128)S(1)}, f32[64,1024]{1,0:T(8,128)S(1)}, u32[]{:S(2)}, u32[]{:S(2)}) collective-permute-start(f32[64,1024]{1,0:T(8,128)S(1)} %get-tuple-element.103.refs_5_), channel_id=1, source_target_pairs={{0,16},{33,17},{2,18},{35,19},{4,20},{37,21},{6,22},{39,23},{64,80... | collective-permute-start | bytes 786440 | tf_op jit(solution)/shard_map/ppermute | solution.py:467
  69.4 1.4 collective-permute-start.27
  70.1 39.0 %collective-permute-start.24 = (f32[64,1024]{1,0:T(8,128)S(1)}, f32[64,1024]{1,0:T(8,128)S(1)}, u32[]{:S(2)}, u32[]{:S(2)}) collective-permute-start(f32[64,1024]{1,0:T(8,128)S(1)} %get-tuple-element.113.refs_6_), channel_id=1, source_target_pairs={{0,24},{33,25},{2,26},{35,27},{4,28},{37,29},{6,30},{39,31},{64,88... | collective-permute-start | bytes 786440 | tf_op jit(solution)/shard_map/ppermute | solution.py:467
  70.8 39.0 %collective-permute-start.25 = (f32[64,1024]{1,0:T(8,128)S(1)}, f32[64,1024]{1,0:T(8,128)S(1)}, u32[]{:S(2)}, u32[]{:S(2)}) collective-permute-start(f32[64,1024]{1,0:T(8,128)S(1)} %get-tuple-element.114.refs_7_), channel_id=1, source_target_pairs={{0,32},{33,33},{2,34},{35,35},{4,36},{37,37},{6,38},{39,39},{64,96... | collective-permute-start | bytes 786440 | tf_op jit(solution)/shard_map/ppermute | solution.py:467
  71.4 38.4 %copy-start.1 = (f32[2,64,576]{2,1,0:T(8,128)S(1)}, f32[2,64,576]{2,1,0:T(8,128)}, u32[]{:S(2)}) copy-start(f32[2,64,576]{2,1,0:T(8,128)} %refs_1_.1) | copy-start | bytes 884740
  71.5 38.4 %copy-start.5 = (f32[2,64]{1,0:T(2,128)S(1)}, f32[2,64]{1,0:T(2,128)}, u32[]{:S(2)}) copy-start(f32[2,64]{1,0:T(2,128)} %refs_3_.1) | copy-start | bytes 1540
  107.0 2.8 %collective-permute-start.26 = (f32[64,1024]{1,0:T(8,128)S(1)}, f32[64,1024]{1,0:T(8,128)S(1)}, u32[]{:S(2)}, u32[]{:S(2)}) collective-permute-start(f32[64,1024]{1,0:T(8,128)S(1)} %get-tuple-element.115.refs_8_), channel_id=1, source_target_pairs={{0,40},{33,41},{2,42},{35,43},{4,44},{37,45},{6,46},{39,47},{64,10... | collective-permute-start | bytes 786440 | tf_op jit(solution)/shard_map/ppermute | solution.py:467
  107.7 2.1 %collective-permute-start.28 = (f32[64,1024]{1,0:T(8,128)S(1)}, f32[64,1024]{1,0:T(8,128)S(1)}, u32[]{:S(2)}, u32[]{:S(2)}) collective-permute-start(f32[64,1024]{1,0:T(8,128)S(1)} %get-tuple-element.125.refs_9_), channel_id=1, source_target_pairs={{0,48},{33,49},{2,50},{35,51},{4,52},{37,53},{6,54},{39,55},{64,11... | collective-permute-start | bytes 786440 | tf_op jit(solution)/shard_map/ppermute | solution.py:467
  108.4 1.4 collective-permute-start.29
  109.1 3.0 %collective-permute-start.30 = (f32[64,512]{1,0:T(8,128)S(1)}, f32[64,512]{1,0:T(8,128)S(1)}, u32[]{:S(2)}, u32[]{:S(2)}) collective-permute-start(f32[64,512]{1,0:T(8,128)S(1)} %get-tuple-element.124), channel_id=1, source_target_pairs={{64,0},{97,33},{66,2},{99,35},{68,4},{101,37},{70,6},{103,39}} | collective-permute-start | bytes 393224 | tf_op jit(solution)/shard_map/ppermute | solution.py:473
  113.6 35.9 %collective-permute-start.31 = (f32[64,512]{1,0:T(8,128)S(1)}, f32[64,512]{1,0:T(8,128)S(1)}, u32[]{:S(2)}, u32[]{:S(2)}) collective-permute-start(f32[64,512]{1,0:T(8,128)S(1)} %get-tuple-element.141), channel_id=1, source_target_pairs={{0,0},{33,1},{2,2},{35,3},{4,4},{37,5},{6,6},{39,7},{64,64},{97,65... | collective-permute-start | bytes 393224 | tf_op jit(solution)/shard_map/ppermute | solution.py:467
  114.9 35.3 %collective-permute-start.32 = (f32[64,512]{1,0:T(8,128)S(1)}, f32[64,512]{1,0:T(8,128)S(1)}, u32[]{:S(2)}, u32[]{:S(2)}) collective-permute-start(f32[64,512]{1,0:T(8,128)S(1)} %get-tuple-element.142), channel_id=1, source_target_pairs={{0,8},{33,9},{2,10},{35,11},{4,12},{37,13},{6,14},{39,15},{64,72},... | collective-permute-start | bytes 393224 | tf_op jit(solution)/shard_map/ppermute | solution.py:467
  115.6 35.3 %collective-permute-start.33 = (f32[64,512]{1,0:T(8,128)S(1)}, f32[64,512]{1,0:T(8,128)S(1)}, u32[]{:S(2)}, u32[]{:S(2)}) collective-permute-start(f32[64,512]{1,0:T(8,128)S(1)} %get-tuple-element.143), channel_id=1, source_target_pairs={{0,16},{33,17},{2,18},{35,19},{4,20},{37,21},{6,22},{39,23},{64,80... | collective-permute-start | bytes 393224 | tf_op jit(solution)/shard_map/ppermute | solution.py:467
  116.3 35.3 %collective-permute-start.34 = (f32[64,512]{1,0:T(8,128)S(1)}, f32[64,512]{1,0:T(8,128)S(1)}, u32[]{:S(2)}, u32[]{:S(2)}) collective-permute-start(f32[64,512]{1,0:T(8,128)S(1)} %get-tuple-element.144), channel_id=1, source_target_pairs={{0,24},{33,25},{2,26},{35,27},{4,28},{37,29},{6,30},{39,31},{64,88... | collective-permute-start | bytes 393224 | tf_op jit(solution)/shard_map/ppermute | solution.py:467
  116.9 34.6 %collective-permute-start.35 = (f32[64,512]{1,0:T(8,128)S(1)}, f32[64,512]{1,0:T(8,128)S(1)}, u32[]{:S(2)}, u32[]{:S(2)}) collective-permute-start(f32[64,512]{1,0:T(8,128)S(1)} %get-tuple-element.145), channel_id=1, source_target_pairs={{0,32},{33,33},{2,34},{35,35},{4,36},{37,37},{6,38},{39,39},{64,96... | collective-permute-start | bytes 393224 | tf_op jit(solution)/shard_map/ppermute | solution.py:467
  149.5 2.1 %collective-permute-start.36 = (f32[64,512]{1,0:T(8,128)S(1)}, f32[64,512]{1,0:T(8,128)S(1)}, u32[]{:S(2)}, u32[]{:S(2)}) collective-permute-start(f32[64,512]{1,0:T(8,128)S(1)} %get-tuple-element.146), channel_id=1, source_target_pairs={{0,40},{33,41},{2,42},{35,43},{4,44},{37,45},{6,46},{39,47},{64,10... | collective-permute-start | bytes 393224 | tf_op jit(solution)/shard_map/ppermute | solution.py:467
  150.2 1.4 collective-permute-start.37
  150.9 0.7 collective-permute-start.38
  155.0 14.5 %collective-permute-start.39 = (f32[64,640]{1,0:T(8,128)S(1)}, f32[64,640]{1,0:T(8,128)S(1)}, u32[]{:S(2)}, u32[]{:S(2)}) collective-permute-start(f32[64,640]{1,0:T(8,128)S(1)} %get-tuple-element.151), channel_id=1, source_target_pairs={{0,1},{1,0},{2,3},{3,2},{4,5},{5,4},{6,7},{7,6},{8,9},{9,8},{10,11... | collective-permute-start | bytes 491528 | tf_op jit(solution)/shard_map/ppermute | solution.py:509
  169.5 5.5 %collective-permute-start.40 = (f32[64,640]{1,0:T(8,128)S(1)}, f32[64,640]{1,0:T(8,128)S(1)}, u32[]{:S(2)}, u32[]{:S(2)}) collective-permute-start(f32[64,640]{1,0:T(8,128)S(1)} %add.21), channel_id=1, source_target_pairs={{0,2},{1,3},{2,0},{3,1},{4,6},{5,7},{6,4},{7,5},{8,10},{9,11},{10,... | collective-permute-start | bytes 491528 | tf_op jit(solution)/shard_map/ppermute | solution.py:511
  175.1 5.9 %collective-permute-start.41 = (f32[64,640]{1,0:T(8,128)S(1)}, f32[64,640]{1,0:T(8,128)S(1)}, u32[]{:S(2)}, u32[]{:S(2)}) collective-permute-start(f32[64,640]{1,0:T(8,128)S(1)} %add.22), channel_id=1, source_target_pairs={{0,6},{1,7},{2,4},{3,5},{4,2},{5,3},{6,0},{7,1},{8,14},{9,15},{10,... | collective-permute-start | bytes 491528 | tf_op jit(solution)/shard_map/ppermute | solution.py:511
  181.0 3.2 %collective-permute-start.42 = (f32[64,640]{1,0:T(8,128)S(1)}, f32[64,640]{1,0:T(8,128)S(1)}, u32[]{:S(2)}, u32[]{:S(2)}) collective-permute-start(f32[64,640]{1,0:T(8,128)S(1)} %add.23), channel_id=1, source_target_pairs={{0,1},{1,0},{2,3},{3,2},{4,5},{5,4},{6,7},{7,6},{8,9},{9,8},{10,11... | collective-permute-start | bytes 491528 | tf_op jit(solution)/shard_map/ppermute | solution.py:512
  (1 other events, 0.7 us)

commit v2 on v1

v2 whole, which is shorter than its diff:
```python
import jax
import jax.numpy as jnp
from jax import lax
from jax.experimental import pallas as pl
from jax.experimental.pallas import tpu as pltpu
from jax.sharding import PartitionSpec as P

F32 = jnp.float32
BF16 = jnp.bfloat16
H = 0.125
CH, CELLS = 64, 512
WPAD = 640
BLK = WPAD + CELLS
RING = 8
AXES = ("layer", "dp")
ANY = pl.BlockSpec(memory_space=pl.ANY)
HBM = pl.BlockSpec(memory_space=pltpu.HBM)
VMEM = pl.BlockSpec(memory_space=pltpu.VMEM)
PARAMS = pltpu.CompilerParams(vmem_limit_bytes=40 << 20)


def split(x):
    hi = x.astype(BF16)
    return hi, (x - hi.astype(F32)).astype(BF16)


def lane_index():
    return lax.broadcasted_iota(jnp.int32, (CH, 128), 1)


def columns(x):
    return [x[:, 128 * a : 128 * (a + 1)] for a in range(4)]


def swap(x):
    parts, lane, out = columns(x), lane_index(), []
    for a in range(4):
        acc = None
        for b in range(4):
            shift = ((b - a) * 32) % 128
            part = parts[b] if shift == 0 else pltpu.roll(parts[b], shift, 1)
            acc = part if acc is None else jnp.where(lane >= 32 * b, part, acc)
        out.append(acc)
    return jnp.concatenate(out, 1)


def lhs_forward(w):
    hi = w.astype(BF16).astype(F32)
    lo = w - hi
    rows = []
    for t in range(9):
        a, b = hi[:, 64 * t : 64 * t + 64], lo[:, 64 * t : 64 * t + 64]
        rows.append(jnp.concatenate([a, a, b], 1).astype(BF16))
    return jnp.concatenate(rows, 0)


def lhs_backward(w):
    wt = w.T
    hi = wt.astype(BF16).astype(F32)
    lo = wt - hi
    return jnp.concatenate([hi, hi, lo], 1).astype(BF16)


def conv(lhs, x, sign):
    hi, lo = split(x)
    z = jnp.dot(lhs, jnp.concatenate([hi, lo, hi], 0), preferred_element_type=F32)
    lane = lane_index()
    q = lane % 32
    lower, upper, right, left = lane < 96, lane >= 32, q < 31, q > 0

    def tap(a, e, col):
        t = 3 * (sign * a + 1) + (sign * e + 1)
        return z[64 * t : 64 * t + 64, 128 * col : 128 * col + 128]

    out = []
    for col in range(4):
        s = []
        for e in (-1, 0, 1):
            if col < 3:
                up = tap(1, e, col + 1)
            else:
                up = jnp.where(lower, pltpu.roll(tap(1, e, 0), 96, 1), 0.0)
            if col > 0:
                down = tap(-1, e, col - 1)
            else:
                down = jnp.where(upper, pltpu.roll(tap(-1, e, 3), 32, 1), 0.0)
            s.append(tap(0, e, col) + up + down)
        out.append(
            s[1]
            + jnp.where(right, pltpu.roll(s[2], 127, 1), 0.0)
            + jnp.where(left, pltpu.roll(s[0], 1, 1), 0.0)
        )
    return jnp.concatenate(out, 1)


def patches(x):
    lane = lane_index()
    q = lane % 32
    lower, upper, right, left = lane < 96, lane >= 32, q < 31, q > 0
    mid = columns(x)
    base = {
        0: mid,
        1: [jnp.where(right, pltpu.roll(c, 127, 1), 0.0) for c in mid],
        -1: [jnp.where(left, pltpu.roll(c, 1, 1), 0.0) for c in mid],
    }
    hi, lo = [], []
    for a in (-1, 0, 1):
        for e in (-1, 0, 1):
            c = base[e]
            if a == 1:
                c = c[1:] + [jnp.where(lower, pltpu.roll(c[0], 96, 1), 0.0)]
            elif a == -1:
                c = [jnp.where(upper, pltpu.roll(c[3], 32, 1), 0.0)] + c[:3]
            h, l = split(jnp.concatenate(c, 1))
            hi.append(h)
            lo.append(l)
    return jnp.concatenate(hi, 0), jnp.concatenate(lo, 0)


def dot_t(a, b):
    return lax.dot_general(a, b, (((1,), (1,)), ((), ())), preferred_element_type=F32)


def correlate(term, x):
    t_hi, t_lo = split(term)
    p_hi, p_lo = patches(x)
    return dot_t(t_hi, p_hi) + dot_t(t_hi, p_lo) + dot_t(t_lo, p_hi)


def as_column(row):
    r = lax.broadcasted_iota(jnp.int32, (CH, CH), 0)
    c = lax.broadcasted_iota(jnp.int32, (CH, CH), 1)
    spread = jnp.broadcast_to(row, (CH, CH))
    return jnp.sum(jnp.where(r == c, spread, 0.0), axis=1, keepdims=True)


def place():
    layer, image = lax.axis_index("layer"), lax.axis_index("dp")
    core = image % 2
    return layer // RING, layer % RING, (RING // 2) * core, core


def start_all(copies):
    for copy in copies:
        copy.start()
    return copies


def wait_all(copies):
    for copy in copies:
        copy.wait()


def field(*lead):
    return jax.ShapeDtypeStruct((*lead, CH, CELLS), F32)


def lhs_shape(*lead):
    return jax.ShapeDtypeStruct((*lead, 9 * CH, 3 * CH), BF16)


def vmem(shape):
    return pltpu.VMEM(shape.shape, shape.dtype)


def relax_kernel(c_hbm, a_hbm, w_hbm, b_hbm, one_ref, two_ref, c_ref, a_ref, w_ref, b_ref, sems):
    copies = start_all(
        [
            pltpu.make_async_copy(source, target, sems.at[i])
            for i, (source, target) in enumerate(
                [(b_hbm, b_ref), (w_hbm, w_ref), (c_hbm, c_ref), (a_hbm, a_ref)]
            )
        ]
    )
    wait_all(copies[:3])
    c = swap(c_ref[...])
    w0, w1 = w_ref[0], w_ref[1]
    b0, b1 = as_column(b_ref[0:1]), as_column(b_ref[1:2])
    t0 = jnp.tanh(conv(lhs_forward(w0), c, 1) + b0)
    t1 = jnp.tanh(conv(lhs_forward(w1), c + H * t0, 1) + b1)
    pad = WPAD - 576
    one_ref[:, 0:576] = w0
    one_ref[:, 576:WPAD] = jnp.broadcast_to(b0, (CH, pad))
    ring, spot, _, _ = place()
    keep = jnp.where((ring == 0) & (spot == 0), 1.0, 0.0)
    one_ref[:, WPAD:BLK] = jnp.where(keep > 0.0, c + H * t0 + H * t1, H * (t1 - t0))
    two_ref[:, 0:576] = w1
    two_ref[:, 576:WPAD] = jnp.broadcast_to(b1, (CH, pad))
    wait_all(copies[3:])
    two_ref[:, WPAD:BLK] = swap(a_ref[...])


def relax(c, a, w, b):
    shape = jax.ShapeDtypeStruct((CH, BLK), F32)
    return pl.pallas_call(
        relax_kernel,
        out_shape=(shape, shape),
        in_specs=[HBM] * 4,
        scratch_shapes=[
            pltpu.VMEM(c.shape, F32),
            pltpu.VMEM(a.shape, F32),
            pltpu.VMEM(w.shape, F32),
            pltpu.VMEM(b.shape, F32),
            pltpu.SemaphoreType.DMA((4,)),
        ],
        compiler_params=pltpu.CompilerParams(vmem_limit_bytes=63 << 20),
        name="relax",
    )(c, a, w, b)


def collect(refs, target, sems, lead, part=None):
    copies = []
    for k, ref in enumerate(refs):
        j = (lead + k) % RING
        source = ref if part is None else ref.at[:, part]
        copies.append(pltpu.make_async_copy(source, target.at[j], sems.at[k]))
    return start_all(copies)


def first_kernel(*refs):
    g_refs, v_refs = refs[:RING], refs[RING : 2 * RING]
    t_ref, out_ref, g, vs, t, lhs, sems, t_sem = refs[2 * RING :]
    ring, spot, lead, _ = place()

    @pl.when((ring == 0) & (spot == lead))
    def _():
        wait_all(collect(g_refs, g, sems, lead))

        def prepare(j, carry):
            lhs[j] = lhs_forward(g[j][:, 0:576])
            return carry

        lax.fori_loop(1, RING, prepare, 0)

        def step(j, v):
            now = jnp.tanh(conv(lhs[j], v, 1) + g[j][:, 576:577])
            vs[j] = v
            t[j] = now
            return v + 2 * H * now + g[j][:, WPAD:BLK]

        out_ref[...] = lax.fori_loop(1, RING, step, g[0][:, WPAD:BLK])
        copies = [
            pltpu.make_async_copy(vs.at[(lead + k) % RING], v_refs[k], sems.at[k])
            for k in range(RING)
        ]
        copies.append(pltpu.make_async_copy(t, t_ref, t_sem))
        wait_all(start_all(copies))


def first_chain(blocks):
    out = pl.pallas_call(
        first_kernel,
        out_shape=(field(),) * RING + (field(RING), field()),
        in_specs=[ANY] * RING,
        out_specs=(ANY,) * (RING + 1) + (VMEM,),
        scratch_shapes=[
            pltpu.VMEM((RING, CH, BLK), F32),
            vmem(field(RING)),
            vmem(field(RING)),
            vmem(lhs_shape(RING)),
            pltpu.SemaphoreType.DMA((RING,)),
            pltpu.SemaphoreType.DMA,
        ],
        compiler_params=PARAMS,
        name="chain_0",
    )(*blocks)
    return out[:RING], out[RING], out[RING + 1]


def prepare_kernel(*refs):
    g_refs, outs = refs[:RING], refs[RING : RING + 2]
    g, ahead, behind, sems, out_sems = refs[RING + 2 :]
    ring, spot, lead, _ = place()

    @pl.when(spot == lead)
    def _():
        wait_all(collect(g_refs, g, sems, lead))

        def step(j, carry):
            w = g[j][:, 0:576]
            ahead[j] = lhs_forward(w)
            behind[j] = lhs_backward(w)
            return carry

        lax.fori_loop(0, RING, step, 0)
        wait_all(
            start_all(
                [
                    pltpu.make_async_copy(ahead, outs[0], out_sems.at[0]),
                    pltpu.make_async_copy(behind, outs[1], out_sems.at[1]),
                ]
            )
        )


def prepare(blocks, name):
    return pl.pallas_call(
        prepare_kernel,
        out_shape=(lhs_shape(RING), lhs_shape(RING)),
        in_specs=[ANY] * RING,
        out_specs=(ANY, ANY),
        scratch_shapes=[
            pltpu.VMEM((RING, CH, BLK), F32),
            vmem(lhs_shape(RING)),
            vmem(lhs_shape(RING)),
            pltpu.SemaphoreType.DMA((RING,)),
            pltpu.SemaphoreType.DMA((2,)),
        ],
        compiler_params=PARAMS,
        cost_estimate=pl.CostEstimate(flops=0, bytes_accessed=20 << 20, transcendentals=0),
        name=name,
    )(*blocks)


def chain_kernel(stage, *refs):
    g_refs, ahead_ref, v_ref = refs[:RING], refs[RING], refs[RING + 1]
    outs = refs[-(RING + 2 + 6) : -6]
    v_refs, t_ref, out_ref = outs[:RING], outs[RING], outs[RING + 1]
    g, vs, t, ahead, sems, ahead_sems = refs[-6:]
    ring, spot, lead, _ = place()

    @pl.when((ring == stage) & (spot == lead))
    def _():
        copies = [
            pltpu.make_async_copy(ahead_ref.at[j], ahead.at[j], ahead_sems.at[j])
            for j in range(RING)
        ]
        start_all(copies)
        wait_all(collect(g_refs, g, sems, lead))
        wait_all(copies)

        def step(j, v):
            now = jnp.tanh(conv(ahead[j], v, 1) + g[j][:, 576:577])
            vs[j] = v
            t[j] = now
            return v + 2 * H * now + g[j][:, WPAD:BLK]

        out_ref[...] = lax.fori_loop(0, RING, step, v_ref[...], unroll=2)
        copies = [
            pltpu.make_async_copy(vs.at[(lead + k) % RING], v_refs[k], sems.at[k])
            for k in range(RING)
        ]
        copies.append(pltpu.make_async_copy(t, t_ref, ahead_sems.at[0]))
        wait_all(start_all(copies))


def chain(stage, blocks, ahead, v, vs, t):
    args = [*blocks, ahead, v]
    aliases = {len(args) + k: k for k in range(RING + 1)}
    out = pl.pallas_call(
        lambda *refs: chain_kernel(stage, *refs),
        out_shape=(field(),) * RING + (field(RING), field()),
        in_specs=[ANY] * (RING + 1) + [VMEM] + [ANY] * (RING + 1),
        out_specs=(ANY,) * (RING + 1) + (VMEM,),
        scratch_shapes=[
            pltpu.VMEM((RING, CH, BLK), F32),
            vmem(field(RING)),
            vmem(field(RING)),
            vmem(lhs_shape(RING)),
            pltpu.SemaphoreType.DMA((RING,)),
            pltpu.SemaphoreType.DMA((RING,)),
        ],
        input_output_aliases=aliases,
        compiler_params=PARAMS,
        name=f"chain_{stage}",
    )(*args, *vs, t)
    return out[:RING], out[RING], out[RING + 1]


def correction(w1, v, t0, b1, a):
    t1 = jnp.tanh(conv(lhs_forward(w1), v + H * t0, 1) + b1)
    shift = H * conv(lhs_backward(w1), (1.0 - t1 * t1) * a, -1)
    s0 = 1.0 - t0 * t0
    return shift, s0 * (H * (shift - a)), (2 * H) * s0


def back_step(behind, mu, shift, part, slope):
    return mu + shift + conv(behind, slope * mu + part, -1)


def middle_kernel(last, *refs):
    two_refs, v_refs = refs[:RING], refs[RING : 2 * RING]
    near_ref, far_ref, c_ref, t_ref, ahead0_ref = refs[2 * RING : 2 * RING + 5]
    refs = refs[2 * RING + 5 :]
    outs = refs[:3]
    two, vs, t, ahead0, c, out, two_sems, v_sems, sems = refs[3:]
    ring, spot, lead, _ = place()

    @pl.when((spot == lead) & (ring < last))
    def _():
        copies = collect(two_refs, two, two_sems, lead)
        copies += collect(v_refs, vs, v_sems, lead)
        copies += start_all(
            [
                pltpu.make_async_copy(t_ref, t, sems.at[0]),
                pltpu.make_async_copy(ahead0_ref.at[0], ahead0, sems.at[1]),
                pltpu.make_async_copy(c_ref, c, sems.at[2]),
            ]
        )
        wait_all(copies)

        @pl.when(ring == 0)
        def _():
            v = swap(c[...])
            vs[0] = v
            bias = jnp.where(lead > 0, far_ref[:, 576:577], near_ref[:, 576:577])
            t[0] = jnp.tanh(conv(ahead0[...], v, 1) + bias)

        def step(j, carry):
            b1, a = two[j][:, 576:577], two[j][:, WPAD:BLK]
            got = correction(two[j][:, 0:576], vs[j], t[j], b1, a)
            for i in range(3):
                out[i, j] = got[i]
            return carry

        lax.fori_loop(0, RING, step, 0, unroll=2)
        wait_all(
            start_all([pltpu.make_async_copy(out.at[i], outs[i], sems.at[i]) for i in range(3)])
        )


def middle(last, twos, vs, ones, c, t, ahead0):
    return pl.pallas_call(
        lambda *refs: middle_kernel(last, *refs),
        out_shape=(field(RING),) * 3,
        in_specs=[ANY] * (2 * RING) + [VMEM] * 2 + [ANY] * 3,
        out_specs=(ANY,) * 3,
        scratch_shapes=[
            pltpu.VMEM((RING, CH, BLK), F32),
            vmem(field(RING)),
            vmem(field(RING)),
            vmem(lhs_shape()),
            vmem(field()),
            vmem(field(3, RING)),
            pltpu.SemaphoreType.DMA((RING,)),
            pltpu.SemaphoreType.DMA((RING,)),
            pltpu.SemaphoreType.DMA((3,)),
        ],
        compiler_params=PARAMS,
        name="middle",
    )(*twos, *vs, ones[0], ones[RING // 2], c, t, ahead0)


def turn_kernel(stage, *refs):
    one_refs, two_refs = refs[:RING], refs[RING : 2 * RING]
    lhs_refs, v_ref = refs[2 * RING : 2 * RING + 2], refs[2 * RING + 2]
    tail = 7
    v_refs = refs[-(2 * RING + 1 + tail) : -(RING + 1 + tail)]
    mu_refs = refs[-(RING + 1 + tail) : -(1 + tail)]
    out_ref = refs[-(1 + tail)]
    one, two, vs, lhs, out, sems, lhs_sems = refs[-tail:]
    ring, spot, lead, _ = place()

    @pl.when((ring == stage) & (spot == lead))
    def _():
        copies = [
            pltpu.make_async_copy(lhs_refs[i], lhs.at[i], lhs_sems.at[i]) for i in range(2)
        ]
        start_all(copies)
        late_copies = collect(two_refs, two, sems.at[1], lead)
        wait_all(collect(one_refs, one, sems.at[0], lead))
        wait_all(copies[:1])

        def ahead_step(j, v):
            now = jnp.tanh(conv(lhs[0, j], v, 1) + one[j][:, 576:577])
            vs[j] = v
            return v + 2 * H * now + one[j][:, WPAD:BLK], now

        def correct(j, v, t0):
            b1, a = two[j][:, 576:577], two[j][:, WPAD:BLK]
            got = correction(two[j][:, 0:576], v, t0, b1, a)
            for i in range(3):
                out[i, j] = got[i]

        def step(j, carry):
            v, old_v, old_t = carry
            new_v, now = ahead_step(j, v)
            correct(j - 1, old_v, old_t)
            return new_v, v, now

        start = v_ref[...]
        v, now = ahead_step(0, start)
        wait_all(late_copies)
        wait_all(copies[1:])
        _, v, now = lax.fori_loop(1, RING, step, (v, start, now))
        correct(RING - 1, v, now)
        copies = start_all(
            [
                pltpu.make_async_copy(vs.at[(lead + k) % RING], v_refs[k], sems.at[0, k])
                for k in range(RING)
            ]
        )
        wait_all(copies)

        def back(k, mu):
            j = RING - 1 - k
            vs[j] = mu
            return back_step(lhs[1, j], mu, out[0, j], out[1, j], out[2, j])

        out_ref[...] = lax.fori_loop(0, RING, back, two[RING - 1][:, WPAD:BLK], unroll=2)
        wait_all(
            start_all(
                [
                    pltpu.make_async_copy(vs.at[(lead + k) % RING], mu_refs[k], sems.at[1, k])
                    for k in range(RING)
                ]
            )
        )


def turn(stage, ones, twos, lhs, v, vs):
    args = [*ones, *twos, *lhs, v]
    aliases = {len(args) + k: k for k in range(RING)}
    out = pl.pallas_call(
        lambda *refs: turn_kernel(stage, *refs),
        out_shape=(field(),) * (2 * RING + 1),
        in_specs=[ANY] * (2 * RING + 2) + [VMEM] + [ANY] * RING,
        out_specs=(ANY,) * (2 * RING) + (VMEM,),
        scratch_shapes=[
            pltpu.VMEM((RING, CH, BLK), F32),
            pltpu.VMEM((RING, CH, BLK), F32),
            vmem(field(RING)),
            vmem(lhs_shape(2, RING)),
            vmem(field(3, RING)),
            pltpu.SemaphoreType.DMA((2, RING)),
            pltpu.SemaphoreType.DMA((2,)),
        ],
        input_output_aliases=aliases,
        compiler_params=PARAMS,
        name="turn",
    )(*args, *vs)
    return out[:RING], out[RING : 2 * RING], out[2 * RING]


def back_kernel(stage, *refs):
    part_refs, behind_ref, mu_ref = refs[:3], refs[3], refs[4]
    outs = refs[-(RING + 1 + 5) : -5]
    parts, behind, mus, sems, out_sems = refs[-5:]
    ring, spot, lead, _ = place()

    @pl.when((ring == stage) & (spot == lead))
    def _():
        copies = [pltpu.make_async_copy(part_refs[i], parts.at[i], sems.at[i]) for i in range(3)]
        copies.append(pltpu.make_async_copy(behind_ref, behind, sems.at[3]))
        wait_all(start_all(copies))

        def step(k, mu):
            j = RING - 1 - k
            mus[j] = mu
            return back_step(behind[j], mu, parts[0, j], parts[1, j], parts[2, j])

        outs[RING][...] = lax.fori_loop(0, RING, step, mu_ref[...], unroll=2)
        wait_all(
            start_all(
                [
                    pltpu.make_async_copy(mus.at[(lead + k) % RING], outs[k], out_sems.at[k])
                    for k in range(RING)
                ]
            )
        )


def back_chain(stage, parts, behind, mu, mus):
    args = [*parts, behind, mu]
    aliases = {len(args) + k: k for k in range(RING)}
    out = pl.pallas_call(
        lambda *refs: back_kernel(stage, *refs),
        out_shape=(field(),) * (RING + 1),
        in_specs=[ANY] * 4 + [VMEM] + [ANY] * RING,
        out_specs=(ANY,) * RING + (VMEM,),
        scratch_shapes=[
            vmem(field(3, RING)),
            vmem(lhs_shape(RING)),
            vmem(field(RING)),
            pltpu.SemaphoreType.DMA((4,)),
            pltpu.SemaphoreType.DMA((RING,)),
        ],
        input_output_aliases=aliases,
        compiler_params=PARAMS,
        name=f"back_{stage}",
    )(*args, *mus)
    return out[:RING], out[RING]


def fetch(refs, target, sem):
    _, spot, lead, _ = place()
    step = (spot + RING - lead) % RING
    for k in range(RING):

        @pl.when(step == k)
        def _():
            copy = pltpu.make_async_copy(refs[k], target, sem)
            copy.start()
            copy.wait()


def early_kernel(*refs):
    one_ref, two_ref, c_ref, refs = refs[0], refs[1], refs[2], refs[3:]
    v_refs = refs[:RING]
    states_ref, keep_ref, lhs_ref, v_ref, sem = refs[RING:]
    fetch(v_refs, v_ref, sem)
    ring, spot, _, _ = place()

    @pl.when((ring == 0) & (spot == 0))
    def _():
        v_ref[...] = swap(c_ref[...])

    v = v_ref[...]
    w0, w1 = one_ref[:, 0:576], two_ref[:, 0:576]
    t0 = jnp.tanh(conv(lhs_forward(w0), v, 1) + one_ref[:, 576:577])
    m = v + H * t0
    b1, a = two_ref[:, 576:577], two_ref[:, WPAD:BLK]
    t1 = jnp.tanh(conv(lhs_forward(w1), m, 1) + b1)
    s1 = 1.0 - t1 * t1
    s0 = 1.0 - t0 * t0
    lhs_ref[0] = lhs_backward(w0)
    behind = lhs_backward(w1)
    lhs_ref[1] = behind
    shift = H * conv(behind, s1 * a, -1)
    states_ref[0] = swap(m)
    slot = one_ref[:, WPAD:BLK]
    keep = jnp.where((ring == 0) & (spot == 0), 1.0, 0.0)
    states_ref[1] = swap(jnp.where(keep > 0.0, slot, v + 2 * H * t0 + slot))
    keep_ref[0] = v
    keep_ref[1] = m
    keep_ref[2] = s0
    keep_ref[3] = s1
    keep_ref[4] = shift
    keep_ref[5] = s0 * (H * (shift - a))


def early(one, two, c, vs):
    return pl.pallas_call(
        early_kernel,
        out_shape=(field(2), field(6), lhs_shape(2)),
        in_specs=[VMEM, VMEM, VMEM] + [ANY] * RING,
        scratch_shapes=[vmem(field()), pltpu.SemaphoreType.DMA],
        compiler_params=PARAMS,
        name="early",
    )(one, two, c, *vs)


def late_kernel(*refs):
    keep_ref, lhs_ref = refs[:2]
    mu_refs = refs[2 : 2 + RING]
    adjoints_ref, mine_ref, other_ref, mu_scratch, sem = refs[2 + RING :]
    fetch(mu_refs, mu_scratch, sem)
    mu = mu_scratch[...]
    s0 = keep_ref[2]
    odd_product = keep_ref[3] * mu
    odd = mu + H * conv(lhs_ref[1], odd_product, -1)
    even_term = (H / 8) * (s0 * odd)
    odd_term = (H / 8) * odd_product
    odd_grad = correlate(odd_term, keep_ref[1])
    even_grad = correlate(even_term, keep_ref[0])
    even = back_step(lhs_ref[0], mu, keep_ref[4], keep_ref[5], (2 * H) * s0)
    adjoints_ref[0] = swap(even)
    adjoints_ref[1] = swap(odd)
    pad = (CH, WPAD - 576)
    even_bias = jnp.broadcast_to(jnp.sum(even_term, axis=1, keepdims=True), pad)
    odd_bias = jnp.broadcast_to(jnp.sum(odd_term, axis=1, keepdims=True), pad)

    def write(ref, grad, bias):
        ref[:, 0:576] = grad
        ref[:, 576:WPAD] = bias

    core = place()[3]

    @pl.when(core == 0)
    def _():
        write(mine_ref, even_grad, even_bias)
        write(other_ref, odd_grad, odd_bias)

    @pl.when(core == 1)
    def _():
        write(mine_ref, odd_grad, odd_bias)
        write(other_ref, even_grad, even_bias)


def late(keep, lhs, mus):
    grad = jax.ShapeDtypeStruct((CH, WPAD), F32)
    return pl.pallas_call(
        late_kernel,
        out_shape=(field(2), grad, grad),
        in_specs=[VMEM] * 2 + [ANY] * RING,
        scratch_shapes=[vmem(field()), pltpu.SemaphoreType.DMA],
        compiler_params=PARAMS,
        name="late",
    )(keep, lhs, *mus)


def finish_kernel(mine_ref, other_ref, grad_ref, bias_ref):
    core = place()[3]
    r = lax.broadcasted_iota(jnp.int32, (CH, CH), 0)
    c = lax.broadcasted_iota(jnp.int32, (CH, CH), 1)

    def write(slot, ref):
        grad_ref[slot] = ref[:, 0:576]
        spread = jnp.broadcast_to(ref[:, 576:577], (CH, CH))
        bias_ref[slot : slot + 1] = jnp.sum(jnp.where(r == c, spread, 0.0), axis=0, keepdims=True)

    @pl.when(core == 0)
    def _():
        write(0, mine_ref)
        write(1, other_ref)

    @pl.when(core == 1)
    def _():
        write(1, mine_ref)
        write(0, other_ref)


def finish(mine, other):
    return pl.pallas_call(
        finish_kernel,
        out_shape=(
            jax.ShapeDtypeStruct((2, CH, 576), F32),
            jax.ShapeDtypeStruct((2, CH), F32),
        ),
        compiler_params=PARAMS,
        name="finish",
    )(mine, other)


def tie(*values):
    return lax.optimization_barrier(values)


NEAR = (1, 7, 2, 6, 3, 5, 4)
FAR = NEAR[::-1]


def body(coarse_guess, adjoint_guess, weights, biases):
    images = lax.axis_size("dp")
    groups = lax.axis_size("layer") // RING
    last = groups - 1

    def device(x, z, d):
        return (RING * x + z % RING) * images + d

    def lead(d):
        return (RING // 2) * (d % 2)

    everyone = [(x, d) for x in range(groups) for d in range(images)]

    def gather(value, k):
        pairs = [(device(x, lead(d) + k, d), device(x, lead(d), d)) for x, d in everyone]
        return lax.ppermute(value, AXES, pairs)

    def scatter(value, k):
        pairs = [(device(x, lead(d), d), device(x, lead(d) + k, d)) for x, d in everyone]
        return lax.ppermute(value, AXES, pairs)

    def hop(value, source, target):
        pairs = [
            (device(source, lead(d), d), device(target, lead(d), d)) for d in range(images)
        ]
        return lax.ppermute(value, AXES, pairs)

    c, a = coarse_guess[0, 0], adjoint_guess[0, 0]
    one, two = relax(c, a, weights, biases)
    ones, twos = {0: one}, {0: two}
    for k in NEAR:
        ones[k] = gather(one, k)
    ones = [ones[k] for k in range(RING)]
    vs, t, end = first_chain(ones)
    v = hop(end, 0, 1)
    ones[0] = tie(end, one)[1]
    ahead0, behind0 = prepare(ones, "prepare")
    for stage in range(1, last):
        vs, t, end = chain(stage, ones, ahead0, v, vs, t)
        v = hop(end, stage, stage + 1)
        for k in NEAR[:4] if stage == 1 else NEAR[4:]:
            twos[k] = gather(two, k)
    twos = [twos[k] for k in range(RING)]
    vs, mus, end = turn(last, ones, twos, [ahead0, behind0], v, vs)
    mu = hop(end, last, last - 1)
    c0 = lax.ppermute(
        tie(end, c)[1],
        AXES,
        [(device(0, 0, d), device(0, lead(d), d)) for d in range(images)],
    )
    parts = middle(last, twos, vs, ones, c0, t, ahead0)
    own_v = [vs[0]] + [None] * (RING - 1)
    keep = None
    for stage in range(last - 1, -1, -1):
        if stage == last - 1:
            chunk, gate = FAR[:4], parts[0]
        elif stage == last - 2:
            chunk, gate = FAR[4:], end
        else:
            chunk = ()
        for k in chunk:
            own_v[k] = scatter(tie(gate, vs[k])[1], k)
        mu, *parts = tie(mu, *parts)
        if stage == last - 2:
            states, keep, lhs = early(one, two, c, own_v)
            mu, keep = tie(mu, keep)
        mus, end = back_chain(stage, parts, behind0, mu, mus)
        if stage > 0:
            mu = hop(end, stage, stage - 1)
    own_mu = [mus[0]] + [None] * (RING - 1)
    for k in FAR:
        own_mu[k] = scatter(mus[k], k)
    adjoints, mine, other = late(keep, lhs, own_mu)
    mine = mine + lax.ppermute(other, "dp", [(i, i ^ 1) for i in range(images)])
    for flip in (2, 6):
        mine = mine + lax.ppermute(mine, "dp", [(i, i ^ flip) for i in range(images)])
    other = lax.ppermute(mine, "dp", [(i, i ^ 1) for i in range(images)])
    grad, bias = finish(mine, other)
    return states[:, None], adjoints[:, None], grad, bias


def solution(mesh):
    return jax.shard_map(
        body,
        mesh=mesh,
        in_specs=(
            P("layer", "dp", None, None),
            P("layer", "dp", None, None),
            P("layer", None, None),
            P("layer", None),
        ),
        out_specs=(
            P("layer", "dp", None, None),
            P("layer", "dp", None, None),
            P("layer", None, None),
            P("layer", None),
        ),
        check_vma=False,
    )
```

time: 187 us -> 168 us (0.90)
  waiting for transfers between devices: 80.9 us -> 59.3 us
  starting transfers between devices: 84.3 us -> 93.3 us
  Pallas kernels: 14 us -> 11.2 us
    ppermute x16 -> x14, waiting for transfers between devices: 66.8 us -> 46.9 us  [scatter(): return lax.ppermute(value, AXES, pairs)]
    ppermute x16 -> x14, starting transfers between devices: 36.9 us -> 51.3 us  [gather(): return lax.ppermute(value, AXES, pairs)]
    ppermute x1, starting transfers between devices: 13.5 us -> 7.82 us  [body(): mine = mine + lax.ppermute(other, 'dp', [(i, i ^ 1) for i in range(images)])]
    pallas_call x12 -> x13, Pallas kernels: 14 us -> 11.2 us  [the longest x1 3.02 us: relax(): pl.pallas_call(relax_kernel, out_shape=(shape, shape), in_specs=[HBM] * 4...]
    ppermute x16 -> x14, starting transfers between devices: 12 us -> 10.6 us  [scatter(): return lax.ppermute(value, AXES, pairs)]
  transfers between devices with their start and end apart: 43 -> 39, of which waited for: 8 -> 9; matrix products, arithmetic and copies ran while one was open for 0% -> 0% of each run, Pallas kernels for 3% -> 1%
where the time goes in v2:
time: 168 us; the launch traced here: 167 us
  starting transfers between devices  93.3 us (56%)
  waiting for transfers between devices  59.3 us (35%)
  Pallas kernels  11.2 us (7%)
  local copies, waits for them, and re-layouts  1.81 us (1%)
    ppermute x14, starting transfers between devices, gather(): return lax.ppermute(value, AXES, pairs)  51.3 us
    ppermute x14, waiting for transfers between devices, scatter(): return lax.ppermute(value, AXES, pairs)  46.9 us
    ppermute x1, starting transfers between devices, body(): lax.ppermute(tie(end, c)[1], AXES, [(device(0, 0, d), device(0, lead(d),...  13.2 us
    ppermute x14, starting transfers between devices, scatter(): return lax.ppermute(value, AXES, pairs)  10.6 us
    ppermute x1, starting transfers between devices, body(): mine = mine + lax.ppermute(other, 'dp', [(i, i ^ 1) for i in range(images)])  7.82 us
    ppermute x2, waiting for transfers between devices, body(): lax.ppermute(mine, 'dp', [(i, i ^ flip) for i in range(images)])  7.21 us
    ppermute x2, starting transfers between devices, body(): lax.ppermute(mine, 'dp', [(i, i ^ flip) for i in range(images)])  4.22 us
    ppermute x6, starting transfers between devices, hop(): return lax.ppermute(value, AXES, pairs)  4.01 us
  transfers between devices with their start and end apart: 39, of which 9 were waited for; matrix products, arithmetic and copies ran while one was open for 0% of the time, Pallas kernels for 1%

profile of v2, /device:TPU:1, one launch (start us, length us, event | category | flops | bytes accessed | tf_op | source)
XLA Modules:
  0.0 166.9 jit_solution(4901455515365116907)
XLA Ops:
  0.6 3.0 %relax.1 = (f32[64,1152]{1,0:T(8,128)}, f32[64,1152]{1,0:T(8,128)}) custom-call(f32[64,512]{1,0:T(8,128)} %bitcast.8, f32[64,512]{1,0:T(8,128)} %bitcast.11, f32[2,64,576]{2,1,0:T(8,128)} %w_hbm.1, f32[2,64]{1,0:T(2,128)} %b_hbm.1), custom_call_target="tpu_custom_call" | custom-call | tf_op jit(solution)/shard_map/relax/pallas_call | solution.py:195
  3.7 0.7 collective-permute-start.6
  4.3 0.7 collective-permute-start.5
  5.0 0.7 collective-permute-start.4
  5.7 11.5 %collective-permute-start.3 = (f32[64,1152]{1,0:T(8,128)}, f32[64,1152]{1,0:T(8,128)S(1)}, u32[]{:S(2)}, u32[]{:S(2)}) collective-permute-start(f32[64,1152]{1,0:T(8,128)} %get-tuple-element.118.refs_0_.refs_16_), channel_id=1, source_target_pairs={{32,0},{1,33},{34,2},{3,35},{36,4},{5,37},{38,6},{7,39},{96,64},{6... | collective-permute-start | bytes 884744 | tf_op jit(solution)/shard_map/ppermute | solution.py:748
  17.2 0.7 collective-permute-start.2
  17.9 0.7 collective-permute-start.1
  18.6 0.7 collective-permute-start
  19.3 0.7 collective-permute-start.13
  20.0 1.2 collective-permute-done.3.refs_4_.refs_17_
  21.9 1.0 copy-done
  23.0 0.7 collective-permute-start.14
  24.8 0.7 collective-permute-start.15
  25.5 31.6 %collective-permute-start.10 = (f32[64,1152]{1,0:T(8,128)S(1)}, f32[64,1152]{1,0:T(8,128)S(1)}, u32[]{:S(2)}, u32[]{:S(2)}) collective-permute-start(f32[64,1152]{1,0:T(8,128)S(1)} %copy-done.2), channel_id=1, source_target_pairs={{32,0},{1,33},{34,2},{3,35},{36,4},{5,37},{38,6},{7,39},{96,64},{6... | collective-permute-start | bytes 884744 | tf_op jit(solution)/shard_map/ppermute | solution.py:748
  57.2 0.7 collective-permute-start.9
  57.9 0.7 collective-permute-start.8
  58.6 0.7 collective-permute-start.7
  59.4 0.7 collective-permute-start.16
  61.7 13.2 %collective-permute-start.18 = (f32[64,512]{1,0:T(8,128)S(1)}, f32[64,512]{1,0:T(8,128)S(1)}, u32[]{:S(2)}, u32[]{:S(2)}) collective-permute-start(f32[64,512]{1,0:T(8,128)S(1)} %bitcast.9), channel_id=1, source_target_pairs={{0,0},{1,33},{2,2},{3,35},{4,4},{5,37},{6,6},{7,39}} | collective-permute-start | bytes 393224 | tf_op jit(solution)/shard_map/ppermute | solution.py:778
  74.9 0.7 collective-permute-start.17
  75.6 1.2 collective-permute-done.18.refs_18_
  77.0 0.7 collective-permute-start.21
  77.7 1.3 collective-permute-start.22
  79.2 0.7 collective-permute-start.26
  79.9 0.7 collective-permute-start.23
  80.5 0.7 collective-permute-start.24
  81.2 0.7 collective-permute-start.19
  81.9 18.0 %collective-permute-done.22.refs_7_ = f32[64,512]{1,0:T(8,128)S(1)} collective-permute-done((f32[64,512]{1,0:T(8,128)S(1)}, f32[64,512]{1,0:T(8,128)S(1)}, u32[]{:S(2)}, u32[]{:S(2)}) %collective-permute-start.22) | collective-permute-done | bytes 131104 | tf_op jit(solution)/shard_map/ppermute | solution.py:752
  100.5 0.7 collective-permute-start.25
  101.3 2.7 %early.1 = (f32[2,64,512]{2,1,0:T(8,128)}, f32[6,64,512]{2,1,0:T(8,128)S(1)}, bf16[2,576,192]{2,1,0:T(8,128)(2,1)S(1)}) custom-call(f32[64,1152]{1,0:T(8,128)S(1)} %copy-done.1, f32[64,1152]{1,0:T(8,128)S(1)} %copy-done.2, f32[64,512]{1,0:T(8,128)S(1)} %bitcast.10, f32[64,512]{1,0:T(8,128)S(1)} %get-tuple-element.149.refs_8_.refs_3_, ...), custom_call_target="tpu_custom_call" | custom-call | tf_op jit(solution)/shard_map/early/pallas_call | solution.py:633
  104.1 0.7 collective-permute-start.27
  104.8 0.8 back_0.1
  105.6 0.7 collective-permute-start.28
  106.3 0.7 collective-permute-start.29
  106.9 0.7 collective-permute-start.30
  107.6 1.3 collective-permute-start.31
  109.6 0.7 collective-permute-start.33
  111.0 28.9 %collective-permute-done.31.refs_6_ = f32[64,512]{1,0:T(8,128)S(1)} collective-permute-done((f32[64,512]{1,0:T(8,128)S(1)}, f32[64,512]{1,0:T(8,128)S(1)}, u32[]{:S(2)}, u32[]{:S(2)}) %collective-permute-start.31) | collective-permute-done | bytes 131104 | tf_op jit(solution)/shard_map/ppermute | solution.py:752
  139.8 2.7 %late.1 = (f32[2,64,512]{2,1,0:T(8,128)}, f32[64,640]{1,0:T(8,128)S(1)}, f32[64,640]{1,0:T(8,128)S(1)}) custom-call(f32[6,64,512]{2,1,0:T(8,128)S(1)} %get-tuple-element.186.refs_0_, bf16[2,576,192]{2,1,0:T(8,128)(2,1)S(1)} %get-tuple-element.187.refs_1_, f32[64,512]{1,0:T(8,128)S(1)} %get-tuple-element.213.refs_2_, ...), custom_call_target="tpu_custom_call" | custom-call | tf_op jit(solution)/shard_map/late/pallas_call | solution.py:682
  142.6 7.8 %collective-permute-start.35 = (f32[64,640]{1,0:T(8,128)S(1)}, f32[64,640]{1,0:T(8,128)S(1)}, u32[]{:S(2)}, u32[]{:S(2)}) collective-permute-start(f32[64,640]{1,0:T(8,128)S(1)} %get-tuple-element.223), channel_id=1, source_target_pairs={{0,1},{1,0},{2,3},{3,2},{4,5},{5,4},{6,7},{7,6},{8,9},{9,8},{10,11... | collective-permute-start | bytes 491528 | tf_op jit(solution)/shard_map/ppermute | solution.py:806
  150.4 1.0 collective-permute-done.35
  151.4 1.4 collective-permute-start.36
  152.8 4.1 %collective-permute-done.36 = f32[64,640]{1,0:T(8,128)S(1)} collective-permute-done((f32[64,640]{1,0:T(8,128)S(1)}, f32[64,640]{1,0:T(8,128)S(1)}, u32[]{:S(2)}, u32[]{:S(2)}) %collective-permute-start.36) | collective-permute-done | bytes 163872 | tf_op jit(solution)/shard_map/ppermute | solution.py:808
  157.0 2.8 %collective-permute-start.37 = (f32[64,640]{1,0:T(8,128)S(1)}, f32[64,640]{1,0:T(8,128)S(1)}, u32[]{:S(2)}, u32[]{:S(2)}) collective-permute-start(f32[64,640]{1,0:T(8,128)S(1)} %add.10), channel_id=1, source_target_pairs={{0,6},{1,7},{2,4},{3,5},{4,2},{5,3},{6,0},{7,1},{8,14},{9,15},{10,... | collective-permute-start | bytes 491528 | tf_op jit(solution)/shard_map/ppermute | solution.py:808
  159.8 3.1 %collective-permute-done.37 = f32[64,640]{1,0:T(8,128)S(1)} collective-permute-done((f32[64,640]{1,0:T(8,128)S(1)}, f32[64,640]{1,0:T(8,128)S(1)}, u32[]{:S(2)}, u32[]{:S(2)}) %collective-permute-start.37) | collective-permute-done | bytes 163872 | tf_op jit(solution)/shard_map/ppermute | solution.py:808
  162.9 2.1 %collective-permute-start.38 = (f32[64,640]{1,0:T(8,128)S(1)}, f32[64,640]{1,0:T(8,128)S(1)}, u32[]{:S(2)}, u32[]{:S(2)}) collective-permute-start(f32[64,640]{1,0:T(8,128)S(1)} %add.11.mine_ref), channel_id=1, source_target_pairs={{0,1},{1,0},{2,3},{3,2},{4,5},{5,4},{6,7},{7,6},{8,9},{9,8},{10,11... | collective-permute-start | bytes 491528 | tf_op jit(solution)/shard_map/ppermute | solution.py:809
  165.1 1.0 collective-permute-done.38.other_ref
  166.1 0.8 finish.1
  (54 shorter events, 6.2 us)
Async XLA Ops:
  3.7 14.3 %collective-permute-start.6 = (f32[64,1152]{1,0:T(8,128)}, f32[64,1152]{1,0:T(8,128)S(1)}, u32[]{:S(2)}, u32[]{:S(2)}) collective-permute-start(f32[64,1152]{1,0:T(8,128)} %get-tuple-element.118.refs_0_.refs_16_), channel_id=1, source_target_pairs={{56,0},{25,33},{58,2},{27,35},{60,4},{29,37},{62,6},{31,39},{120,6... | collective-permute-start | bytes 884744 | tf_op jit(solution)/shard_map/ppermute | solution.py:748
  4.3 14.3 %collective-permute-start.5 = (f32[64,1152]{1,0:T(8,128)}, f32[64,1152]{1,0:T(8,128)S(1)}, u32[]{:S(2)}, u32[]{:S(2)}) collective-permute-start(f32[64,1152]{1,0:T(8,128)} %get-tuple-element.118.refs_0_.refs_16_), channel_id=1, source_target_pairs={{48,0},{17,33},{50,2},{19,35},{52,4},{21,37},{54,6},{23,39},{112,6... | collective-permute-start | bytes 884744 | tf_op jit(solution)/shard_map/ppermute | solution.py:748
  5.0 14.3 %collective-permute-start.4 = (f32[64,1152]{1,0:T(8,128)}, f32[64,1152]{1,0:T(8,128)S(1)}, u32[]{:S(2)}, u32[]{:S(2)}) collective-permute-start(f32[64,1152]{1,0:T(8,128)} %get-tuple-element.118.refs_0_.refs_16_), channel_id=1, source_target_pairs={{40,0},{9,33},{42,2},{11,35},{44,4},{13,37},{46,6},{15,39},{104,64... | collective-permute-start | bytes 884744 | tf_op jit(solution)/shard_map/ppermute | solution.py:748
  5.7 15.5 %collective-permute-start.3 = (f32[64,1152]{1,0:T(8,128)}, f32[64,1152]{1,0:T(8,128)S(1)}, u32[]{:S(2)}, u32[]{:S(2)}) collective-permute-start(f32[64,1152]{1,0:T(8,128)} %get-tuple-element.118.refs_0_.refs_16_), channel_id=1, source_target_pairs={{32,0},{1,33},{34,2},{3,35},{36,4},{5,37},{38,6},{7,39},{96,64},{6... | collective-permute-start | bytes 884744 | tf_op jit(solution)/shard_map/ppermute | solution.py:748
  17.2 4.7 %collective-permute-start.2 = (f32[64,1152]{1,0:T(8,128)}, f32[64,1152]{1,0:T(8,128)S(1)}, u32[]{:S(2)}, u32[]{:S(2)}) collective-permute-start(f32[64,1152]{1,0:T(8,128)} %get-tuple-element.118.refs_0_.refs_16_), channel_id=1, source_target_pairs={{24,0},{57,33},{26,2},{59,35},{28,4},{61,37},{30,6},{63,39},{88,64... | collective-permute-start | bytes 884744 | tf_op jit(solution)/shard_map/ppermute | solution.py:748
  17.9 4.0 %collective-permute-start.1 = (f32[64,1152]{1,0:T(8,128)}, f32[64,1152]{1,0:T(8,128)S(1)}, u32[]{:S(2)}, u32[]{:S(2)}) collective-permute-start(f32[64,1152]{1,0:T(8,128)} %get-tuple-element.118.refs_0_.refs_16_), channel_id=1, source_target_pairs={{16,0},{49,33},{18,2},{51,35},{20,4},{53,37},{22,6},{55,39},{80,64... | collective-permute-start | bytes 884744 | tf_op jit(solution)/shard_map/ppermute | solution.py:748
  18.6 3.3 %collective-permute-start = (f32[64,1152]{1,0:T(8,128)}, f32[64,1152]{1,0:T(8,128)S(1)}, u32[]{:S(2)}, u32[]{:S(2)}) collective-permute-start(f32[64,1152]{1,0:T(8,128)} %get-tuple-element.118.refs_0_.refs_16_), channel_id=1, source_target_pairs={{8,0},{41,33},{10,2},{43,35},{12,4},{45,37},{14,6},{47,39},{72,64}... | collective-permute-start | bytes 884744 | tf_op jit(solution)/shard_map/ppermute | solution.py:748
  19.3 37.8 %collective-permute-start.13 = (f32[64,1152]{1,0:T(8,128)}, f32[64,1152]{1,0:T(8,128)S(1)}, u32[]{:S(2)}, u32[]{:S(2)}) collective-permute-start(f32[64,1152]{1,0:T(8,128)} %get-tuple-element.116.refs_8_.refs_0_.refs_1_), channel_id=1, source_target_pairs={{56,0},{25,33},{58,2},{27,35},{60,4},{29,37},{62,6},{31,39},{120,6... | collective-permute-start | bytes 884744 | tf_op jit(solution)/shard_map/ppermute | solution.py:748
  21.2 36.6 %collective-permute-start.12 = (f32[64,1152]{1,0:T(8,128)}, f32[64,1152]{1,0:T(8,128)S(1)}, u32[]{:S(2)}, u32[]{:S(2)}) collective-permute-start(f32[64,1152]{1,0:T(8,128)} %get-tuple-element.116.refs_8_.refs_0_.refs_1_), channel_id=1, source_target_pairs={{48,0},{17,33},{50,2},{19,35},{52,4},{21,37},{54,6},{23,39},{112,6... | collective-permute-start | bytes 884744 | tf_op jit(solution)/shard_map/ppermute | solution.py:748
  21.9 1.0 copy-start
  22.9 1.0 copy-start.2
  23.0 1.7 %collective-permute-start.14 = (f32[64,512]{1,0:T(8,128)S(1)}, f32[64,512]{1,0:T(8,128)S(1)}, u32[]{:S(2)}, u32[]{:S(2)}) collective-permute-start(f32[64,512]{1,0:T(8,128)S(1)} %get-tuple-element.117), channel_id=1, source_target_pairs={{0,64},{33,97},{2,66},{35,99},{4,68},{37,101},{6,70},{39,103}} | collective-permute-start | bytes 393224 | tf_op jit(solution)/shard_map/ppermute | solution.py:758
  23.9 35.6 %collective-permute-start.11 = (f32[64,1152]{1,0:T(8,128)S(1)}, f32[64,1152]{1,0:T(8,128)S(1)}, u32[]{:S(2)}, u32[]{:S(2)}) collective-permute-start(f32[64,1152]{1,0:T(8,128)S(1)} %copy-done.2), channel_id=1, source_target_pairs={{40,0},{9,33},{42,2},{11,35},{44,4},{13,37},{46,6},{15,39},{104,64... | collective-permute-start | bytes 884744 | tf_op jit(solution)/shard_map/ppermute | solution.py:748
  24.8 33.7 %collective-permute-start.15 = (f32[64,512]{1,0:T(8,128)S(1)}, f32[64,512]{1,0:T(8,128)S(1)}, u32[]{:S(2)}, u32[]{:S(2)}) collective-permute-start(f32[64,512]{1,0:T(8,128)S(1)} %get-tuple-element.130), channel_id=1, source_target_pairs={{64,128},{97,161},{66,130},{99,163},{68,132},{101,165},{70,134},{1... | collective-permute-start | bytes 393224 | tf_op jit(solution)/shard_map/ppermute | solution.py:758
  25.5 35.3 %collective-permute-start.10 = (f32[64,1152]{1,0:T(8,128)S(1)}, f32[64,1152]{1,0:T(8,128)S(1)}, u32[]{:S(2)}, u32[]{:S(2)}) collective-permute-start(f32[64,1152]{1,0:T(8,128)S(1)} %copy-done.2), channel_id=1, source_target_pairs={{32,0},{1,33},{34,2},{3,35},{36,4},{5,37},{38,6},{7,39},{96,64},{6... | collective-permute-start | bytes 884744 | tf_op jit(solution)/shard_map/ppermute | solution.py:748
  57.2 3.6 %collective-permute-start.9 = (f32[64,1152]{1,0:T(8,128)S(1)}, f32[64,1152]{1,0:T(8,128)S(1)}, u32[]{:S(2)}, u32[]{:S(2)}) collective-permute-start(f32[64,1152]{1,0:T(8,128)S(1)} %copy-done.2), channel_id=1, source_target_pairs={{24,0},{57,33},{26,2},{59,35},{28,4},{61,37},{30,6},{63,39},{88,64... | collective-permute-start | bytes 884744 | tf_op jit(solution)/shard_map/ppermute | solution.py:748
  57.9 2.9 %collective-permute-start.8 = (f32[64,1152]{1,0:T(8,128)S(1)}, f32[64,1152]{1,0:T(8,128)S(1)}, u32[]{:S(2)}, u32[]{:S(2)}) collective-permute-start(f32[64,1152]{1,0:T(8,128)S(1)} %copy-done.2), channel_id=1, source_target_pairs={{16,0},{49,33},{18,2},{51,35},{20,4},{53,37},{22,6},{55,39},{80,64... | collective-permute-start | bytes 884744 | tf_op jit(solution)/shard_map/ppermute | solution.py:748
  58.6 2.2 %collective-permute-start.7 = (f32[64,1152]{1,0:T(8,128)S(1)}, f32[64,1152]{1,0:T(8,128)S(1)}, u32[]{:S(2)}, u32[]{:S(2)}) collective-permute-start(f32[64,1152]{1,0:T(8,128)S(1)} %copy-done.2), channel_id=1, source_target_pairs={{8,0},{41,33},{10,2},{43,35},{12,4},{45,37},{14,6},{47,39},{72,64}... | collective-permute-start | bytes 884744 | tf_op jit(solution)/shard_map/ppermute | solution.py:748
  59.4 1.4 collective-permute-start.16
  60.8 0.9 copy-start.3
  61.7 15.1 %collective-permute-start.18 = (f32[64,512]{1,0:T(8,128)S(1)}, f32[64,512]{1,0:T(8,128)S(1)}, u32[]{:S(2)}, u32[]{:S(2)}) collective-permute-start(f32[64,512]{1,0:T(8,128)S(1)} %bitcast.9), channel_id=1, source_target_pairs={{0,0},{1,33},{2,2},{3,35},{4,4},{5,37},{6,6},{7,39}} | collective-permute-start | bytes 393224 | tf_op jit(solution)/shard_map/ppermute | solution.py:778
  74.9 4.1 %collective-permute-start.17 = (f32[64,512]{1,0:T(8,128)S(1)}, f32[64,512]{1,0:T(8,128)S(1)}, u32[]{:S(2)}, u32[]{:S(2)}) collective-permute-start(f32[64,512]{1,0:T(8,128)S(1)} %get-tuple-element.150), channel_id=1, source_target_pairs={{192,128},{225,161},{194,130},{227,163},{196,132},{229,165},{198,1... | collective-permute-start | bytes 393224 | tf_op jit(solution)/shard_map/ppermute | solution.py:758
  77.0 4.2 %collective-permute-start.21 = (f32[64,512]{1,0:T(8,128)S(1)}, f32[64,512]{1,0:T(8,128)S(1)}, u32[]{:S(2)}, u32[]{:S(2)}) collective-permute-start(f32[64,512]{1,0:T(8,128)S(1)} %get-tuple-element.178.refs_11_), channel_id=1, source_target_pairs={{0,24},{33,57},{2,26},{35,59},{4,28},{37,61},{6,30},{39,63},{64,88... | collective-permute-start | bytes 393224 | tf_op jit(solution)/shard_map/ppermute | solution.py:752
  77.7 22.2 %collective-permute-start.22 = (f32[64,512]{1,0:T(8,128)S(1)}, f32[64,512]{1,0:T(8,128)S(1)}, u32[]{:S(2)}, u32[]{:S(2)}) collective-permute-start(f32[64,512]{1,0:T(8,128)S(1)} %get-tuple-element.179.refs_12_), channel_id=1, source_target_pairs={{0,32},{33,1},{2,34},{35,3},{4,36},{37,5},{6,38},{39,7},{64,96},{9... | collective-permute-start | bytes 393224 | tf_op jit(solution)/shard_map/ppermute | solution.py:752
  79.0 22.3 %copy-start.1 = (f32[64,1152]{1,0:T(8,128)S(1)}, f32[64,1152]{1,0:T(8,128)}, u32[]{:S(2)}) copy-start(f32[64,1152]{1,0:T(8,128)} %get-tuple-element.118.refs_0_.refs_16_) | copy-start | bytes 884740
  79.2 21.4 %collective-permute-start.26 = (f32[64,512]{1,0:T(8,128)S(1)}, f32[64,512]{1,0:T(8,128)S(1)}, u32[]{:S(2)}, u32[]{:S(2)}) collective-permute-start(f32[64,512]{1,0:T(8,128)S(1)} %get-tuple-element.175), channel_id=1, source_target_pairs={{128,64},{161,97},{130,66},{163,99},{132,68},{165,101},{134,70},{1... | collective-permute-start | bytes 393224 | tf_op jit(solution)/shard_map/ppermute | solution.py:758
  79.9 21.4 %collective-permute-start.23 = (f32[64,512]{1,0:T(8,128)S(1)}, f32[64,512]{1,0:T(8,128)S(1)}, u32[]{:S(2)}, u32[]{:S(2)}) collective-permute-start(f32[64,512]{1,0:T(8,128)S(1)} %get-tuple-element.180.refs_13_), channel_id=1, source_target_pairs={{0,40},{33,9},{2,42},{35,11},{4,44},{37,13},{6,46},{39,15},{64,104... | collective-permute-start | bytes 393224 | tf_op jit(solution)/shard_map/ppermute | solution.py:752
  80.5 20.7 %collective-permute-start.24 = (f32[64,512]{1,0:T(8,128)S(1)}, f32[64,512]{1,0:T(8,128)S(1)}, u32[]{:S(2)}, u32[]{:S(2)}) collective-permute-start(f32[64,512]{1,0:T(8,128)S(1)} %get-tuple-element.181.refs_14_), channel_id=1, source_target_pairs={{0,48},{33,17},{2,50},{35,19},{4,52},{37,21},{6,54},{39,23},{64,11... | collective-permute-start | bytes 393224 | tf_op jit(solution)/shard_map/ppermute | solution.py:752
  81.2 20.0 %collective-permute-start.19 = (f32[64,512]{1,0:T(8,128)S(1)}, f32[64,512]{1,0:T(8,128)S(1)}, u32[]{:S(2)}, u32[]{:S(2)}) collective-permute-start(f32[64,512]{1,0:T(8,128)S(1)} %get-tuple-element.176.refs_9_), channel_id=1, source_target_pairs={{0,8},{33,41},{2,10},{35,43},{4,12},{37,45},{6,14},{39,47},{64,72}... | collective-permute-start | bytes 393224 | tf_op jit(solution)/shard_map/ppermute | solution.py:752
  99.9 1.4 collective-permute-start.20
  100.5 0.7 collective-permute-start.25
  104.1 0.7 collective-permute-start.27
  105.6 4.0 %collective-permute-start.28 = (f32[64,512]{1,0:T(8,128)S(1)}, f32[64,512]{1,0:T(8,128)S(1)}, u32[]{:S(2)}, u32[]{:S(2)}) collective-permute-start(f32[64,512]{1,0:T(8,128)S(1)} %get-tuple-element.214), channel_id=1, source_target_pairs={{0,8},{33,41},{2,10},{35,43},{4,12},{37,45},{6,14},{39,47},{64,72}... | collective-permute-start | bytes 393224 | tf_op jit(solution)/shard_map/ppermute | solution.py:752
  106.3 4.0 %collective-permute-start.29 = (f32[64,512]{1,0:T(8,128)S(1)}, f32[64,512]{1,0:T(8,128)S(1)}, u32[]{:S(2)}, u32[]{:S(2)}) collective-permute-start(f32[64,512]{1,0:T(8,128)S(1)} %get-tuple-element.215), channel_id=1, source_target_pairs={{0,16},{33,49},{2,18},{35,51},{4,20},{37,53},{6,22},{39,55},{64,80... | collective-permute-start | bytes 393224 | tf_op jit(solution)/shard_map/ppermute | solution.py:752
  106.9 4.0 %collective-permute-start.30 = (f32[64,512]{1,0:T(8,128)S(1)}, f32[64,512]{1,0:T(8,128)S(1)}, u32[]{:S(2)}, u32[]{:S(2)}) collective-permute-start(f32[64,512]{1,0:T(8,128)S(1)} %get-tuple-element.216), channel_id=1, source_target_pairs={{0,24},{33,57},{2,26},{35,59},{4,28},{37,61},{6,30},{39,63},{64,88... | collective-permute-start | bytes 393224 | tf_op jit(solution)/shard_map/ppermute | solution.py:752
  107.6 32.2 %collective-permute-start.31 = (f32[64,512]{1,0:T(8,128)S(1)}, f32[64,512]{1,0:T(8,128)S(1)}, u32[]{:S(2)}, u32[]{:S(2)}) collective-permute-start(f32[64,512]{1,0:T(8,128)S(1)} %get-tuple-element.217), channel_id=1, source_target_pairs={{0,32},{33,1},{2,34},{35,3},{4,36},{37,5},{6,38},{39,7},{64,96},{9... | collective-permute-start | bytes 393224 | tf_op jit(solution)/shard_map/ppermute | solution.py:752
  108.9 30.9 %collective-permute-start.32 = (f32[64,512]{1,0:T(8,128)S(1)}, f32[64,512]{1,0:T(8,128)S(1)}, u32[]{:S(2)}, u32[]{:S(2)}) collective-permute-start(f32[64,512]{1,0:T(8,128)S(1)} %get-tuple-element.218), channel_id=1, source_target_pairs={{0,40},{33,9},{2,42},{35,11},{4,44},{37,13},{6,46},{39,15},{64,104... | collective-permute-start | bytes 393224 | tf_op jit(solution)/shard_map/ppermute | solution.py:752
  109.6 30.2 %collective-permute-start.33 = (f32[64,512]{1,0:T(8,128)S(1)}, f32[64,512]{1,0:T(8,128)S(1)}, u32[]{:S(2)}, u32[]{:S(2)}) collective-permute-start(f32[64,512]{1,0:T(8,128)S(1)} %get-tuple-element.219), channel_id=1, source_target_pairs={{0,48},{33,17},{2,50},{35,19},{4,52},{37,21},{6,54},{39,23},{64,11... | collective-permute-start | bytes 393224 | tf_op jit(solution)/shard_map/ppermute | solution.py:752
  110.3 29.6 %collective-permute-start.34 = (f32[64,512]{1,0:T(8,128)S(1)}, f32[64,512]{1,0:T(8,128)S(1)}, u32[]{:S(2)}, u32[]{:S(2)}) collective-permute-start(f32[64,512]{1,0:T(8,128)S(1)} %get-tuple-element.220), channel_id=1, source_target_pairs={{0,56},{33,25},{2,58},{35,27},{4,60},{37,29},{6,62},{39,31},{64,12... | collective-permute-start | bytes 393224 | tf_op jit(solution)/shard_map/ppermute | solution.py:752
  142.6 8.8 %collective-permute-start.35 = (f32[64,640]{1,0:T(8,128)S(1)}, f32[64,640]{1,0:T(8,128)S(1)}, u32[]{:S(2)}, u32[]{:S(2)}) collective-permute-start(f32[64,640]{1,0:T(8,128)S(1)} %get-tuple-element.223), channel_id=1, source_target_pairs={{0,1},{1,0},{2,3},{3,2},{4,5},{5,4},{6,7},{7,6},{8,9},{9,8},{10,11... | collective-permute-start | bytes 491528 | tf_op jit(solution)/shard_map/ppermute | solution.py:806
  151.4 5.5 %collective-permute-start.36 = (f32[64,640]{1,0:T(8,128)S(1)}, f32[64,640]{1,0:T(8,128)S(1)}, u32[]{:S(2)}, u32[]{:S(2)}) collective-permute-start(f32[64,640]{1,0:T(8,128)S(1)} %add.9), channel_id=1, source_target_pairs={{0,2},{1,3},{2,0},{3,1},{4,6},{5,7},{6,4},{7,5},{8,10},{9,11},{10,... | collective-permute-start | bytes 491528 | tf_op jit(solution)/shard_map/ppermute | solution.py:808
  157.0 5.9 %collective-permute-start.37 = (f32[64,640]{1,0:T(8,128)S(1)}, f32[64,640]{1,0:T(8,128)S(1)}, u32[]{:S(2)}, u32[]{:S(2)}) collective-permute-start(f32[64,640]{1,0:T(8,128)S(1)} %add.10), channel_id=1, source_target_pairs={{0,6},{1,7},{2,4},{3,5},{4,2},{5,3},{6,0},{7,1},{8,14},{9,15},{10,... | collective-permute-start | bytes 491528 | tf_op jit(solution)/shard_map/ppermute | solution.py:808
  162.9 3.2 %collective-permute-start.38 = (f32[64,640]{1,0:T(8,128)S(1)}, f32[64,640]{1,0:T(8,128)S(1)}, u32[]{:S(2)}, u32[]{:S(2)}) collective-permute-start(f32[64,640]{1,0:T(8,128)S(1)} %add.11.mine_ref), channel_id=1, source_target_pairs={{0,1},{1,0},{2,3},{3,2},{4,5},{5,4},{6,7},{7,6},{8,9},{9,8},{10,11... | collective-permute-start | bytes 491528 | tf_op jit(solution)/shard_map/ppermute | solution.py:809

commit v3 on v2

--- a/solution.py
+++ b/solution.py
@@ -163,7 +163,9 @@
     return pltpu.VMEM(shape.shape, shape.dtype)
 
 
-def relax_kernel(c_hbm, a_hbm, w_hbm, b_hbm, one_ref, two_ref, c_ref, a_ref, w_ref, b_ref, sems):
+def relax_kernel(c_hbm, a_hbm, w_hbm, b_hbm, *refs):
+    outs, (c_ref, a_ref, w_ref, b_ref, sems) = refs[:6], refs[6:]
+    low_ref, high_ref, mid_ref, tau_ref, even_ref, two_ref = outs
     copies = start_all(
         [
             pltpu.make_async_copy(source, target, sems.at[i])
@@ -178,23 +180,53 @@
     b0, b1 = as_column(b_ref[0:1]), as_column(b_ref[1:2])
     t0 = jnp.tanh(conv(lhs_forward(w0), c, 1) + b0)
     t1 = jnp.tanh(conv(lhs_forward(w1), c + H * t0, 1) + b1)
-    pad = WPAD - 576
-    one_ref[:, 0:576] = w0
-    one_ref[:, 576:WPAD] = jnp.broadcast_to(b0, (CH, pad))
-    ring, spot, _, _ = place()
+    ring, spot, _, core = place()
     keep = jnp.where((ring == 0) & (spot == 0), 1.0, 0.0)
-    one_ref[:, WPAD:BLK] = jnp.where(keep > 0.0, c + H * t0 + H * t1, H * (t1 - t0))
+    tau = jnp.where(keep > 0.0, c + H * t0 + H * t1, H * (t1 - t0))
+
+    def write_tau(ref):
+        ref[:, 0:CELLS] = tau
+        ref[:, CELLS:WPAD] = jnp.broadcast_to(b0, (CH, WPAD - CELLS))
+
+    def write_even(ref):
+        ref[:, 0:576] = w0
+        ref[:, 576:WPAD] = jnp.zeros((CH, WPAD - 576), F32)
+
+    write_tau(tau_ref)
+    write_even(even_ref)
+
+    first = (core == 0) == (spot < RING // 2)
+    middle_first = (core == 0) == (spot == RING // 2)
+
+    @pl.when(first)
+    def _():
+        write_tau(low_ref)
+        write_even(high_ref)
+
+    @pl.when(jnp.logical_not(first))
+    def _():
+        write_even(low_ref)
+        write_tau(high_ref)
+
+    @pl.when(middle_first)
+    def _():
+        write_tau(mid_ref)
+
+    @pl.when(jnp.logical_not(middle_first))
+    def _():
+        write_even(mid_ref)
+
     two_ref[:, 0:576] = w1
-    two_ref[:, 576:WPAD] = jnp.broadcast_to(b1, (CH, pad))
+    two_ref[:, 576:WPAD] = jnp.broadcast_to(b1, (CH, WPAD - 576))
     wait_all(copies[3:])
     two_ref[:, WPAD:BLK] = swap(a_ref[...])
 
 
 def relax(c, a, w, b):
-    shape = jax.ShapeDtypeStruct((CH, BLK), F32)
+    short = jax.ShapeDtypeStruct((CH, WPAD), F32)
     return pl.pallas_call(
         relax_kernel,
-        out_shape=(shape, shape),
+        out_shape=(short,) * 5 + (jax.ShapeDtypeStruct((CH, BLK), F32),),
         in_specs=[HBM] * 4,
         scratch_shapes=[
             pltpu.VMEM(c.shape, F32),
@@ -208,78 +240,118 @@
     )(c, a, w, b)
 
 
-def collect(refs, target, sems, lead, part=None):
+def slots(refs, target, sems, lead):
     copies = []
     for k, ref in enumerate(refs):
         j = (lead + k) % RING
-        source = ref if part is None else ref.at[:, part]
-        copies.append(pltpu.make_async_copy(source, target.at[j], sems.at[k]))
-    return start_all(copies)
+        copies.append(pltpu.make_async_copy(ref, target.at[j], sems.at[j]))
+    return copies
+
+
+def stack_kernel(*refs):
+    block_refs, stack_ref, sems = refs[: RING - 1], refs[RING - 1], refs[RING]
+    _, spot, lead, _ = place()
+
+    @pl.when(spot == RING // 2 - lead)
+    def _():
+        wait_all(
+            start_all(
+                [
+                    pltpu.make_async_copy(block_refs[k], stack_ref.at[k], sems.at[k])
+                    for k in range(RING - 1)
+                ]
+            )
+        )
+
+
+def stack(blocks):
+    return pl.pallas_call(
+        stack_kernel,
+        out_shape=jax.ShapeDtypeStruct((RING - 1, CH, WPAD), F32),
+        in_specs=[ANY] * (RING - 1),
+        out_specs=ANY,
+        scratch_shapes=[pltpu.SemaphoreType.DMA((RING - 1,))],
+        compiler_params=PARAMS,
+        name="stack",
+    )(*blocks)
+
+
+def even_slots(own_ref, stack_ref, target, sems, lead):
+    return slots([own_ref] + [stack_ref.at[k] for k in range(RING - 1)], target, sems, lead)
 
 
 def first_kernel(*refs):
-    g_refs, v_refs = refs[:RING], refs[RING : 2 * RING]
-    t_ref, out_ref, g, vs, t, lhs, sems, t_sem = refs[2 * RING :]
+    tau_refs, own_ref, stack_ref = refs[:RING], refs[RING], refs[RING + 1]
+    vt_ref, out_ref, tau, even, vt, lhs, tau_sems, even_sems, sems = refs[RING + 2 :]
     ring, spot, lead, _ = place()
 
     @pl.when((ring == 0) & (spot == lead))
     def _():
-        wait_all(collect(g_refs, g, sems, lead))
+        copies = even_slots(own_ref, stack_ref, even, even_sems, lead)
+        copies += slots(tau_refs, tau, tau_sems, lead)
+        wait_all(start_all(copies))
 
         def prepare(j, carry):
-            lhs[j] = lhs_forward(g[j][:, 0:576])
+            lhs[j] = lhs_forward(even[j][:, 0:576])
             return carry
 
         lax.fori_loop(1, RING, prepare, 0)
 
         def step(j, v):
-            now = jnp.tanh(conv(lhs[j], v, 1) + g[j][:, 576:577])
-            vs[j] = v
-            t[j] = now
-            return v + 2 * H * now + g[j][:, WPAD:BLK]
-
-        out_ref[...] = lax.fori_loop(1, RING, step, g[0][:, WPAD:BLK])
-        copies = [
-            pltpu.make_async_copy(vs.at[(lead + k) % RING], v_refs[k], sems.at[k])
-            for k in range(RING)
-        ]
-        copies.append(pltpu.make_async_copy(t, t_ref, t_sem))
-        wait_all(start_all(copies))
-
-
-def first_chain(blocks):
-    out = pl.pallas_call(
+            now = jnp.tanh(conv(lhs[j], v, 1) + tau[j][:, CELLS : CELLS + 1])
+            vt[0, j] = v
+            vt[1, j] = now
+            start_all(
+                [pltpu.make_async_copy(vt.at[i, j], vt_ref.at[i, j], sems.at[i, j]) for i in (0, 1)]
+            )
+            return v + 2 * H * now + tau[j][:, 0:CELLS]
+
+        out_ref[...] = lax.fori_loop(1, RING, step, tau[0][:, 0:CELLS])
+        wait_all(
+            [
+                pltpu.make_async_copy(vt.at[i, j], vt_ref.at[i, j], sems.at[i, j])
+                for i in (0, 1)
+                for j in range(1, RING)
+            ]
+        )
+
+
+def first_chain(taus, own, others):
+    return pl.pallas_call(
         first_kernel,
-        out_shape=(field(),) * RING + (field(RING), field()),
-        in_specs=[ANY] * RING,
-        out_specs=(ANY,) * (RING + 1) + (VMEM,),
+        out_shape=(field(2, RING), field()),
+        in_specs=[ANY] * (RING + 2),
+        out_specs=(ANY, VMEM),
         scratch_shapes=[
-            pltpu.VMEM((RING, CH, BLK), F32),
-            vmem(field(RING)),
-            vmem(field(RING)),
+            pltpu.VMEM((RING, CH, WPAD), F32),
+            pltpu.VMEM((RING, CH, WPAD), F32),
+            vmem(field(2, RING)),
             vmem(lhs_shape(RING)),
             pltpu.SemaphoreType.DMA((RING,)),
-            pltpu.SemaphoreType.DMA,
+            pltpu.SemaphoreType.DMA((RING,)),
+            pltpu.SemaphoreType.DMA((2, RING)),
         ],
         compiler_params=PARAMS,
         name="chain_0",
-    )(*blocks)
-    return out[:RING], out[RING], out[RING + 1]
-
-
-def prepare_kernel(*refs):
-    g_refs, outs = refs[:RING], refs[RING : RING + 2]
-    g, ahead, behind, sems, out_sems = refs[RING + 2 :]
-    ring, spot, lead, _ = place()
+    )(*taus, own, others)
+
+
+def prepare_kernel(sizes, *refs):
+    block_refs, outs, work = refs[:sizes], refs[sizes : sizes + 2], refs[sizes + 2 :]
+    w, ahead, behind, sems, out_sems = work
+    _, spot, lead, _ = place()
 
     @pl.when(spot == lead)
     def _():
-        wait_all(collect(g_refs, g, sems, lead))
+        if sizes == 2:
+            copies = even_slots(block_refs[0], block_refs[1], w, sems, lead)
+        else:
+            copies = slots([r.at[:, pl.ds(0, WPAD)] for r in block_refs], w, sems, lead)
+        wait_all(start_all(copies))
 
         def step(j, carry):
-            w = g[j][:, 0:576]
-            ahead[j] = lhs_forward(w)
-            behind[j] = lhs_backward(w)
+            ahead[j] = lhs_forward(w[j][:, 0:576])
+            behind[j] = lhs_backward(w[j][:, 0:576])
             return carry
 
         lax.fori_loop(0, RING, step, 0)
@@ -295,12 +367,12 @@
 
 def prepare(blocks, name):
     return pl.pallas_call(
-        prepare_kernel,
+        lambda *refs: prepare_kernel(len(blocks), *refs),
         out_shape=(lhs_shape(RING), lhs_shape(RING)),
-        in_specs=[ANY] * RING,
+        in_specs=[ANY] * len(blocks),
         out_specs=(ANY, ANY),
         scratch_shapes=[
-            pltpu.VMEM((RING, CH, BLK), F32),
+            pltpu.VMEM((RING, CH, WPAD), F32),
             vmem(lhs_shape(RING)),
             vmem(lhs_shape(RING)),
             pltpu.SemaphoreType.DMA((RING,)),
@@ -313,63 +385,64 @@
 
 
 def chain_kernel(stage, *refs):
-    g_refs, ahead_ref, v_ref = refs[:RING], refs[RING], refs[RING + 1]
-    outs = refs[-(RING + 2 + 6) : -6]
-    v_refs, t_ref, out_ref = outs[:RING], outs[RING], outs[RING + 1]
-    g, vs, t, ahead, sems, ahead_sems = refs[-6:]
+    tau_refs, ahead_ref, v_ref = refs[:RING], refs[RING], refs[RING + 1]
+    vt_ref, out_ref, tau, vt, ahead, tau_sems, ahead_sems, sems = refs[-8:]
     ring, spot, lead, _ = place()
 
     @pl.when((ring == stage) & (spot == lead))
     def _():
-        copies = [
-            pltpu.make_async_copy(ahead_ref.at[j], ahead.at[j], ahead_sems.at[j])
-            for j in range(RING)
-        ]
-        start_all(copies)
-        wait_all(collect(g_refs, g, sems, lead))
-        wait_all(copies)
+        start_all(slots(tau_refs, tau, tau_sems, lead))
+
+        def ahead_copy(j):
+            return pltpu.make_async_copy(ahead_ref.at[j], ahead.at[j], ahead_sems.at[j])
+
+        start_all([ahead_copy(j) for j in range(RING)])
 
         def step(j, v):
-            now = jnp.tanh(conv(ahead[j], v, 1) + g[j][:, 576:577])
-            vs[j] = v
-            t[j] = now
-            return v + 2 * H * now + g[j][:, WPAD:BLK]
-
-        out_ref[...] = lax.fori_loop(0, RING, step, v_ref[...], unroll=2)
-        copies = [
-            pltpu.make_async_copy(vs.at[(lead + k) % RING], v_refs[k], sems.at[k])
-            for k in range(RING)
-        ]
-        copies.append(pltpu.make_async_copy(t, t_ref, ahead_sems.at[0]))
-        wait_all(start_all(copies))
-
-
-def chain(stage, blocks, ahead, v, vs, t):
-    args = [*blocks, ahead, v]
-    aliases = {len(args) + k: k for k in range(RING + 1)}
-    out = pl.pallas_call(
+            ahead_copy(j).wait()
+            pltpu.make_async_copy(tau_refs[0], tau.at[j], tau_sems.at[j]).wait()
+            now = jnp.tanh(conv(ahead[j], v, 1) + tau[j][:, CELLS : CELLS + 1])
+            vt[0, j] = v
+            vt[1, j] = now
+            start_all(
+                [pltpu.make_async_copy(vt.at[i, j], vt_ref.at[i, j], sems.at[i, j]) for i in (0, 1)]
+            )
+            return v + 2 * H * now + tau[j][:, 0:CELLS]
+
+        out_ref[...] = lax.fori_loop(0, RING, step, v_ref[...])
+        wait_all(
+            [
+                pltpu.make_async_copy(vt.at[i, j], vt_ref.at[i, j], sems.at[i, j])
+                for i in (0, 1)
+                for j in range(RING)
+            ]
+        )
+
+
+def chain(stage, taus, ahead, v, vt):
+    args = [*taus, ahead, v]
+    return pl.pallas_call(
         lambda *refs: chain_kernel(stage, *refs),
-        out_shape=(field(),) * RING + (field(RING), field()),
-        in_specs=[ANY] * (RING + 1) + [VMEM] + [ANY] * (RING + 1),
-        out_specs=(ANY,) * (RING + 1) + (VMEM,),
+        out_shape=(field(2, RING), field()),
+        in_specs=[ANY] * (RING + 1) + [VMEM, ANY],
+        out_specs=(ANY, VMEM),
         scratch_shapes=[
-            pltpu.VMEM((RING, CH, BLK), F32),
-            vmem(field(RING)),
-            vmem(field(RING)),
+            pltpu.VMEM((RING, CH, WPAD), F32),
+            vmem(field(2, RING)),
             vmem(lhs_shape(RING)),
             pltpu.SemaphoreType.DMA((RING,)),
             pltpu.SemaphoreType.DMA((RING,)),
+            pltpu.SemaphoreType.DMA((2, RING)),
         ],
-        input_output_aliases=aliases,
+        input_output_aliases={len(args): 0},
         compiler_params=PARAMS,
         name=f"chain_{stage}",
-    )(*args, *vs, t)
-    return out[:RING], out[RING], out[RING + 1]
-
-
-def correction(w1, v, t0, b1, a):
-    t1 = jnp.tanh(conv(lhs_forward(w1), v + H * t0, 1) + b1)
-    shift = H * conv(lhs_backward(w1), (1.0 - t1 * t1) * a, -1)
+    )(*args, vt)
+
+
+def correction(ahead, behind, v, t0, b1, a):
+    t1 = jnp.tanh(conv(ahead, v + H * t0, 1) + b1)
+    shift = H * conv(behind, (1.0 - t1 * t1) * a, -1)
     s0 = 1.0 - t0 * t0
     return shift, s0 * (H * (shift - a)), (2 * H) * s0
 
@@ -379,156 +452,157 @@
 
 
 def middle_kernel(last, *refs):
-    two_refs, v_refs = refs[:RING], refs[RING : 2 * RING]
-    near_ref, far_ref, c_ref, t_ref, ahead0_ref = refs[2 * RING : 2 * RING + 5]
-    refs = refs[2 * RING + 5 :]
-    outs = refs[:3]
-    two, vs, t, ahead0, c, out, two_sems, v_sems, sems = refs[3:]
+    two_refs, (vt_ref, ahead_ref, behind_ref) = refs[:RING], refs[RING : RING + 3]
+    outs = refs[-(RING + 3 + 7) : -7]
+    two, vt, ahead, behind, out, two_sems, sems = refs[-7:]
     ring, spot, lead, _ = place()
 
     @pl.when((spot == lead) & (ring < last))
     def _():
-        copies = collect(two_refs, two, two_sems, lead)
-        copies += collect(v_refs, vs, v_sems, lead)
+        copies = start_all(slots(two_refs, two, two_sems, lead))
         copies += start_all(
             [
-                pltpu.make_async_copy(t_ref, t, sems.at[0]),
-                pltpu.make_async_copy(ahead0_ref.at[0], ahead0, sems.at[1]),
-                pltpu.make_async_copy(c_ref, c, sems.at[2]),
+                pltpu.make_async_copy(vt_ref, vt, sems.at[0]),
+                pltpu.make_async_copy(ahead_ref, ahead, sems.at[1]),
+                pltpu.make_async_copy(behind_ref, behind, sems.at[2]),
             ]
         )
         wait_all(copies)
-
-        @pl.when(ring == 0)
-        def _():
-            v = swap(c[...])
-            vs[0] = v
-            bias = jnp.where(lead > 0, far_ref[:, 576:577], near_ref[:, 576:577])
-            t[0] = jnp.tanh(conv(ahead0[...], v, 1) + bias)
+        copies = start_all(
+            [
+                pltpu.make_async_copy(vt.at[0, (lead + k) % RING], outs[k], two_sems.at[k])
+                for k in range(RING)
+            ]
+        )
 
         def step(j, carry):
             b1, a = two[j][:, 576:577], two[j][:, WPAD:BLK]
-            got = correction(two[j][:, 0:576], vs[j], t[j], b1, a)
+            got = correction(ahead[j], behind[j], vt[0, j], vt[1, j], b1, a)
             for i in range(3):
                 out[i, j] = got[i]
             return carry
 
         lax.fori_loop(0, RING, step, 0, unroll=2)
-        wait_all(
-            start_all([pltpu.make_async_copy(out.at[i], outs[i], sems.at[i]) for i in range(3)])
-        )
-
-
-def middle(last, twos, vs, ones, c, t, ahead0):
-    return pl.pallas_call(
+        copies += start_all(
+            [pltpu.make_async_copy(out.at[i], outs[RING + i], sems.at[i]) for i in range(3)]
+        )
+        wait_all(copies)
+
+
+def middle(last, twos, vt, ahead, behind, vs):
+    args = [*twos, vt, ahead, behind]
+    out = pl.pallas_call(
         lambda *refs: middle_kernel(last, *refs),
-        out_shape=(field(RING),) * 3,
-        in_specs=[ANY] * (2 * RING) + [VMEM] * 2 + [ANY] * 3,
-        out_specs=(ANY,) * 3,
+        out_shape=(field(),) * RING + (field(RING),) * 3,
+        in_specs=[ANY] * (2 * RING + 3),
+        out_specs=(ANY,) * (RING + 3),
         scratch_shapes=[
             pltpu.VMEM((RING, CH, BLK), F32),
-            vmem(field(RING)),
-            vmem(field(RING)),
-            vmem(lhs_shape()),
-            vmem(field()),
+            vmem(field(2, RING)),
+            vmem(lhs_shape(RING)),
+            vmem(lhs_shape(RING)),
             vmem(field(3, RING)),
-            pltpu.SemaphoreType.DMA((RING,)),
             pltpu.SemaphoreType.DMA((RING,)),
             pltpu.SemaphoreType.DMA((3,)),
         ],
+        input_output_aliases={len(args) + k: k for k in range(RING)},
         compiler_params=PARAMS,
         name="middle",
-    )(*twos, *vs, ones[0], ones[RING // 2], c, t, ahead0)
+    )(*args, *vs)
+    return out[:RING], out[RING:]
 
 
 def turn_kernel(stage, *refs):
-    one_refs, two_refs = refs[:RING], refs[RING : 2 * RING]
-    lhs_refs, v_ref = refs[2 * RING : 2 * RING + 2], refs[2 * RING + 2]
-    tail = 7
-    v_refs = refs[-(2 * RING + 1 + tail) : -(RING + 1 + tail)]
-    mu_refs = refs[-(RING + 1 + tail) : -(1 + tail)]
-    out_ref = refs[-(1 + tail)]
-    one, two, vs, lhs, out, sems, lhs_sems = refs[-tail:]
+    tau_refs, two_refs = refs[:RING], refs[RING : 2 * RING]
+    lhs_refs, v_ref = refs[2 * RING : 2 * RING + 4], refs[2 * RING + 4]
+    v_refs = refs[2 * RING + 5 : 3 * RING + 5]
+    mu_refs = refs[3 * RING + 5 : 4 * RING + 5]
+    out_ref, tau, two, vs, mus, lhs, out, sems, lhs_sems = refs[4 * RING + 5 :]
     ring, spot, lead, _ = place()
 
     @pl.when((ring == stage) & (spot == lead))
     def _():
-        copies = [
-            pltpu.make_async_copy(lhs_refs[i], lhs.at[i], lhs_sems.at[i]) for i in range(2)
-        ]
-        start_all(copies)
-        late_copies = collect(two_refs, two, sems.at[1], lead)
-        wait_all(collect(one_refs, one, sems.at[0], lead))
-        wait_all(copies[:1])
+        def lhs_copy(i, j):
+            return pltpu.make_async_copy(lhs_refs[i].at[j], lhs.at[i, j], lhs_sems.at[i, j])
+
+        start_all(slots(tau_refs, tau, sems.at[0], lead))
+        start_all([lhs_copy(0, j) for j in range(RING)])
+        start_all(slots(two_refs, two, sems.at[1], lead))
+        start_all([lhs_copy(i, j) for j in range(RING) for i in (2, 3)])
+        start_all([lhs_copy(1, RING - 1 - j) for j in range(RING)])
 
         def ahead_step(j, v):
-            now = jnp.tanh(conv(lhs[0, j], v, 1) + one[j][:, 576:577])
+            lhs_copy(0, j).wait()
+            pltpu.make_async_copy(tau_refs[0], tau.at[j], sems.at[0, j]).wait()
+            now = jnp.tanh(conv(lhs[0, j], v, 1) + tau[j][:, CELLS : CELLS + 1])
             vs[j] = v
-            return v + 2 * H * now + one[j][:, WPAD:BLK], now
+            return v + 2 * H * now + tau[j][:, 0:CELLS], now
 
         def correct(j, v, t0):
             b1, a = two[j][:, 576:577], two[j][:, WPAD:BLK]
-            got = correction(two[j][:, 0:576], v, t0, b1, a)
+            got = correction(lhs[2, j], lhs[3, j], v, t0, b1, a)
             for i in range(3):
                 out[i, j] = got[i]
 
+        def arrive(j):
+            pltpu.make_async_copy(two_refs[0], two.at[j], sems.at[1, j]).wait()
+            lhs_copy(2, j).wait()
+            lhs_copy(3, j).wait()
+
         def step(j, carry):
             v, old_v, old_t = carry
+            arrive(j - 1)
             new_v, now = ahead_step(j, v)
             correct(j - 1, old_v, old_t)
             return new_v, v, now
 
         start = v_ref[...]
         v, now = ahead_step(0, start)
-        wait_all(late_copies)
-        wait_all(copies[1:])
         _, v, now = lax.fori_loop(1, RING, step, (v, start, now))
-        correct(RING - 1, v, now)
         copies = start_all(
             [
                 pltpu.make_async_copy(vs.at[(lead + k) % RING], v_refs[k], sems.at[0, k])
                 for k in range(RING)
             ]
         )
-        wait_all(copies)
+        arrive(RING - 1)
+        correct(RING - 1, v, now)
 
         def back(k, mu):
             j = RING - 1 - k
-            vs[j] = mu
+            lhs_copy(1, j).wait()
+            mus[j] = mu
             return back_step(lhs[1, j], mu, out[0, j], out[1, j], out[2, j])
 
-        out_ref[...] = lax.fori_loop(0, RING, back, two[RING - 1][:, WPAD:BLK], unroll=2)
-        wait_all(
-            start_all(
-                [
-                    pltpu.make_async_copy(vs.at[(lead + k) % RING], mu_refs[k], sems.at[1, k])
-                    for k in range(RING)
-                ]
-            )
-        )
-
-
-def turn(stage, ones, twos, lhs, v, vs):
-    args = [*ones, *twos, *lhs, v]
-    aliases = {len(args) + k: k for k in range(RING)}
+        out_ref[...] = lax.fori_loop(0, RING, back, two[RING - 1][:, WPAD:BLK])
+        copies += start_all(
+            [
+                pltpu.make_async_copy(mus.at[(lead + k) % RING], mu_refs[k], sems.at[1, k])
+                for k in range(RING)
+            ]
+        )
+        wait_all(copies)
+
+
+def turn(stage, taus, twos, lhs, v):
     out = pl.pallas_call(
         lambda *refs: turn_kernel(stage, *refs),
         out_shape=(field(),) * (2 * RING + 1),
-        in_specs=[ANY] * (2 * RING + 2) + [VMEM] + [ANY] * RING,
+        in_specs=[ANY] * (2 * RING + 4) + [VMEM],
         out_specs=(ANY,) * (2 * RING) + (VMEM,),
         scratch_shapes=[
-            pltpu.VMEM((RING, CH, BLK), F32),
+            pltpu.VMEM((RING, CH, WPAD), F32),
             pltpu.VMEM((RING, CH, BLK), F32),
             vmem(field(RING)),
-            vmem(lhs_shape(2, RING)),
+            vmem(field(RING)),
+            vmem(lhs_shape(4, RING)),
             vmem(field(3, RING)),
             pltpu.SemaphoreType.DMA((2, RING)),
-            pltpu.SemaphoreType.DMA((2,)),
+            pltpu.SemaphoreType.DMA((4, RING)),
         ],
-        input_output_aliases=aliases,
         compiler_params=PARAMS,
         name="turn",
-    )(*args, *vs)
+    )(*taus, *twos, *lhs, v)
     return out[:RING], out[RING : 2 * RING], out[2 * RING]
 
 
@@ -540,16 +614,29 @@
 
     @pl.when((ring == stage) & (spot == lead))
     def _():
-        copies = [pltpu.make_async_copy(part_refs[i], parts.at[i], sems.at[i]) for i in range(3)]
-        copies.append(pltpu.make_async_copy(behind_ref, behind, sems.at[3]))
-        wait_all(start_all(copies))
+        def copies(j):
+            return [
+                pltpu.make_async_copy(behind_ref.at[j], behind.at[j], sems.at[3, j]),
+            ] + [
+                pltpu.make_async_copy(part_refs[i].at[j], parts.at[i, j], sems.at[i, j])
+                for i in range(3)
+            ]
+
+        for j in range(RING - 1, -1, -1):
+            start_all(copies(j))
 
         def step(k, mu):
             j = RING - 1 - k
+            wait_all(copies(j))
             mus[j] = mu
             return back_step(behind[j], mu, parts[0, j], parts[1, j], parts[2, j])
 
-        outs[RING][...] = lax.fori_loop(0, RING, step, mu_ref[...], unroll=2)
+        steps = RING - 1 if stage == 0 else RING
+        end = lax.fori_loop(0, steps, step, mu_ref[...])
+        if stage == 0:
+            mus[0] = end
+            wait_all(copies(0))
+        outs[RING][...] = end
         wait_all(
             start_all(
                 [
@@ -572,7 +659,7 @@
             vmem(field(3, RING)),
             vmem(lhs_shape(RING)),
             vmem(field(RING)),
-            pltpu.SemaphoreType.DMA((4,)),
+            pltpu.SemaphoreType.DMA((4, RING)),
             pltpu.SemaphoreType.DMA((RING,)),
         ],
         input_output_aliases=aliases,
@@ -595,7 +682,7 @@
 
 
 def early_kernel(*refs):
-    one_ref, two_ref, c_ref, refs = refs[0], refs[1], refs[2], refs[3:]
+    tau_ref, even_ref, two_ref, c_ref, refs = refs[0], refs[1], refs[2], refs[3], refs[4:]
     v_refs = refs[:RING]
     states_ref, keep_ref, lhs_ref, v_ref, sem = refs[RING:]
     fetch(v_refs, v_ref, sem)
@@ -606,8 +693,8 @@
         v_ref[...] = swap(c_ref[...])
 
     v = v_ref[...]
-    w0, w1 = one_ref[:, 0:576], two_ref[:, 0:576]
-    t0 = jnp.tanh(conv(lhs_forward(w0), v, 1) + one_ref[:, 576:577])
+    w0, w1 = even_ref[:, 0:576], two_ref[:, 0:576]
+    t0 = jnp.tanh(conv(lhs_forward(w0), v, 1) + tau_ref[:, CELLS : CELLS + 1])
     m = v + H * t0
     b1, a = two_ref[:, 576:577], two_ref[:, WPAD:BLK]
     t1 = jnp.tanh(conv(lhs_forward(w1), m, 1) + b1)
@@ -618,7 +705,7 @@
     lhs_ref[1] = behind
     shift = H * conv(behind, s1 * a, -1)
     states_ref[0] = swap(m)
-    slot = one_ref[:, WPAD:BLK]
+    slot = tau_ref[:, 0:CELLS]
     keep = jnp.where((ring == 0) & (spot == 0), 1.0, 0.0)
     states_ref[1] = swap(jnp.where(keep > 0.0, slot, v + 2 * H * t0 + slot))
     keep_ref[0] = v
@@ -629,15 +716,15 @@
     keep_ref[5] = s0 * (H * (shift - a))
 
 
-def early(one, two, c, vs):
+def early(tau, even, two, c, vs):
     return pl.pallas_call(
         early_kernel,
         out_shape=(field(2), field(6), lhs_shape(2)),
-        in_specs=[VMEM, VMEM, VMEM] + [ANY] * RING,
+        in_specs=[VMEM] * 4 + [ANY] * RING,
         scratch_shapes=[vmem(field()), pltpu.SemaphoreType.DMA],
         compiler_params=PARAMS,
         name="early",
-    )(one, two, c, *vs)
+    )(tau, even, two, c, *vs)
 
 
 def late_kernel(*refs):
@@ -747,6 +834,16 @@
         pairs = [(device(x, lead(d) + k, d), device(x, lead(d), d)) for x, d in everyone]
         return lax.ppermute(value, AXES, pairs)
 
+    def gather_both(value, k):
+        pairs = [
+            (device(x, z + k, d), device(x, z, d)) for x, d in everyone for z in (0, RING // 2)
+        ]
+        return lax.ppermute(value, AXES, pairs)
+
+    def hand_over(value):
+        pairs = [(device(x, lead(d), d ^ 1), device(x, lead(d), d)) for x, d in everyone]
+        return lax.ppermute(value, AXES, pairs)
+
     def scatter(value, k):
         pairs = [(device(x, lead(d), d), device(x, lead(d) + k, d)) for x, d in everyone]
         return lax.ppermute(value, AXES, pairs)
@@ -758,43 +855,41 @@
         return lax.ppermute(value, AXES, pairs)
 
     c, a = coarse_guess[0, 0], adjoint_guess[0, 0]
-    one, two = relax(c, a, weights, biases)
-    ones, twos = {0: one}, {0: two}
+    low, high, mid, tau, even, two = relax(c, a, weights, biases)
+    taus, twos = [tau] + [None] * (RING - 1), [two] + [None] * (RING - 1)
     for k in NEAR:
-        ones[k] = gather(one, k)
-    ones = [ones[k] for k in range(RING)]
-    vs, t, end = first_chain(ones)
+        taus[k] = gather_both(mid if k == RING // 2 else low if k < RING // 2 else high, k)
+    others = hand_over(stack(taus[1:]))
+    vt, end = first_chain(taus, even, others)
     v = hop(end, 0, 1)
-    ones[0] = tie(end, one)[1]
-    ahead0, behind0 = prepare(ones, "prepare")
+    even_late = tie(end, even)[1]
+    ahead0, behind0 = prepare([even_late, others], "prepare")
+    for k in NEAR:
+        twos[k] = gather(two, k)
     for stage in range(1, last):
-        vs, t, end = chain(stage, ones, ahead0, v, vs, t)
+        vt, end = chain(stage, taus, ahead0, v, vt)
         v = hop(end, stage, stage + 1)
-        for k in NEAR[:4] if stage == 1 else NEAR[4:]:
-            twos[k] = gather(two, k)
-    twos = [twos[k] for k in range(RING)]
-    vs, mus, end = turn(last, ones, twos, [ahead0, behind0], v, vs)
+    ahead1, behind1 = prepare(twos, "prepare2")
+    vs, mus, end = turn(last, taus, twos, [ahead0, behind0, ahead1, behind1], v)
     mu = hop(end, last, last - 1)
-    c0 = lax.ppermute(
-        tie(end, c)[1],
-        AXES,
-        [(device(0, 0, d), device(0, lead(d), d)) for d in range(images)],
-    )
-    parts = middle(last, twos, vs, ones, c0, t, ahead0)
+    vs, parts = middle(last, twos, vt, ahead1, behind1, vs)
     own_v = [vs[0]] + [None] * (RING - 1)
-    keep = None
     for stage in range(last - 1, -1, -1):
         if stage == last - 1:
-            chunk, gate = FAR[:4], parts[0]
+            chunk, gate = FAR[:3], parts[0]
         elif stage == last - 2:
-            chunk, gate = FAR[4:], end
+            chunk, gate = FAR[3:], end
         else:
             chunk = ()
         for k in chunk:
             own_v[k] = scatter(tie(gate, vs[k])[1], k)
-        mu, *parts = tie(mu, *parts)
-        if stage == last - 2:
-            states, keep, lhs = early(one, two, c, own_v)
+        if stage == last - 1:
+            got = tie(mu, *parts, *[own_v[k] for k in chunk])
+            mu, parts = got[0], got[1:4]
+            for k, value in zip(chunk, got[4:]):
+                own_v[k] = value
+        if stage == 0:
+            states, keep, lhs = early(tau, even, two, c, own_v)
             mu, keep = tie(mu, keep)
         mus, end = back_chain(stage, parts, behind0, mu, mus)
         if stage > 0:

time: 168 us -> 192 us (1.14)
  waiting for transfers between devices: 59.3 us -> 98.9 us
  starting transfers between devices: 93.3 us -> 72.9 us
  Pallas kernels: 11.2 us -> 14.4 us
    ppermute x14, waiting for transfers between devices: 46.9 us -> 77.9 us  [scatter(): return lax.ppermute(value, AXES, pairs)]
    ppermute x14 -> x7, starting transfers between devices: 51.3 us -> 24.6 us  [gather(): return lax.ppermute(value, AXES, pairs)]
    ppermute x1 -> x8, waiting for transfers between devices: 1.25 us -> 11.2 us  [the longest x7 10.2 us: gather_both(): return lax.ppermute(value, AXES, pairs)]
    ppermute x1 -> x8, starting transfers between devices: 13.2 us -> 21.2 us  [the longest x7 17.5 us: gather_both(): return lax.ppermute(value, AXES, pairs)]
    pallas_call x3 -> x5, Pallas kernels: 3.21 us -> 5.18 us  [the longest x1 3.15 us: relax(): pl.pallas_call(relax_kernel, out_shape=(short,) * 5 + (jax.ShapeDtypeStru...]
  transfers between devices with their start and end apart: 39 -> 39, of which waited for: 9 -> 12; matrix products, arithmetic and copies ran while one was open for 0% -> 0% of each run, Pallas kernels for 1% -> 2%
where the time goes in v3:
time: 192 us; the launch traced here: 191 us
  waiting for transfers between devices  98.9 us (52%)
  starting transfers between devices  72.9 us (38%)
  Pallas kernels  14.4 us (8%)
  local copies, waits for them, and re-layouts  3.53 us (2%)
    ppermute x14, waiting for transfers between devices, scatter(): return lax.ppermute(value, AXES, pairs)  77.9 us
    ppermute x7, starting transfers between devices, gather(): return lax.ppermute(value, AXES, pairs)  24.6 us
    ppermute x7, starting transfers between devices, gather_both(): return lax.ppermute(value, AXES, pairs)  17.5 us
    ppermute x14, starting transfers between devices, scatter(): return lax.ppermute(value, AXES, pairs)  10.6 us
    ppermute x7, waiting for transfers between devices, gather_both(): return lax.ppermute(value, AXES, pairs)  10.2 us
    ppermute x2, waiting for transfers between devices, body(): lax.ppermute(mine, 'dp', [(i, i ^ flip) for i in range(images)])  7.22 us
    ppermute x1, starting transfers between devices, body(): mine = mine + lax.ppermute(other, 'dp', [(i, i ^ 1) for i in range(images)])  6.21 us
    ppermute x2, starting transfers between devices, body(): lax.ppermute(mine, 'dp', [(i, i ^ flip) for i in range(images)])  4.21 us
  transfers between devices with their start and end apart: 39, of which 12 were waited for; matrix products, arithmetic and copies ran while one was open for 0% of the time, Pallas kernels for 2%

profile of v3, /device:TPU:1, one launch (start us, length us, event | category | flops | bytes accessed | tf_op | source)
XLA Modules:
  0.0 191.1 jit_solution(14020413111364824415)
XLA Ops:
  0.6 3.1 %relax.1 = (f32[64,640]{1,0:T(8,128)}, f32[64,640]{1,0:T(8,128)}, f32[64,640]{1,0:T(8,128)}, f32[64,640]{1,0:T(8,128)}, f32[64,640]{1,0:T(8,128)}, /*index=5*/f32[64,1152]{1,0:T(8,128)}) custom-call(f32[64,512]{1,0:T(8,128)} %bitcast.8, f32[64,512]{1,0:T(8,128)} %bitcast.10, f32[2,64,576]{2,1,0:T(8,128)} %w_hbm.1, f32[2,64]{1,0:T(2,128)} %b_hbm.1), custom_call_target="tpu_custom_call" | custom-call | tf_op jit(solution)/shard_map/relax/pallas_call | solution.py:227
  3.8 9.8 %collective-permute-start.10 = (f32[64,640]{1,0:T(8,128)}, f32[64,640]{1,0:T(8,128)S(1)}, u32[]{:S(2)}, u32[]{:S(2)}) collective-permute-start(f32[64,640]{1,0:T(8,128)} %get-tuple-element.103), channel_id=1, source_target_pairs={{32,0},{0,32},{33,1},{1,33},{34,2},{2,34},{35,3},{3,35},{36,4},{4,... | collective-permute-start | bytes 491528 | tf_op jit(solution)/shard_map/ppermute | solution.py:841
  13.6 1.3 collective-permute-start.9
  14.9 1.3 collective-permute-start.8
  16.2 1.3 collective-permute-start.7
  17.5 1.3 collective-permute-start.13
  18.8 1.3 collective-permute-start.12
  20.1 2.2 %collective-permute-done.9.refs_2_.refs_3_ = f32[64,640]{1,0:T(8,128)S(1)} collective-permute-done((f32[64,640]{1,0:T(8,128)}, f32[64,640]{1,0:T(8,128)S(1)}, u32[]{:S(2)}, u32[]{:S(2)}) %collective-permute-start.9) | collective-permute-done | bytes 163872 | tf_op jit(solution)/shard_map/ppermute | solution.py:841
  22.3 1.3 collective-permute-start.11
  23.6 3.6 %collective-permute-done.8.refs_1_.refs_2_ = f32[64,640]{1,0:T(8,128)S(1)} collective-permute-done((f32[64,640]{1,0:T(8,128)}, f32[64,640]{1,0:T(8,128)S(1)}, u32[]{:S(2)}, u32[]{:S(2)}) %collective-permute-start.8) | collective-permute-done | bytes 163872 | tf_op jit(solution)/shard_map/ppermute | solution.py:841
  27.2 3.5 %collective-permute-done.7.refs_0_.refs_1_ = f32[64,640]{1,0:T(8,128)S(1)} collective-permute-done((f32[64,640]{1,0:T(8,128)}, f32[64,640]{1,0:T(8,128)S(1)}, u32[]{:S(2)}, u32[]{:S(2)}) %collective-permute-start.7) | collective-permute-done | bytes 163872 | tf_op jit(solution)/shard_map/ppermute | solution.py:841
  30.7 0.9 collective-permute-done.11.refs_4_.refs_5_
  31.6 1.5 stack.1
  33.1 3.7 %collective-permute-start.14 = (f32[7,64,640]{2,1,0:T(8,128)S(1)}, f32[7,64,640]{2,1,0:T(8,128)S(1)}, u32[]{:S(2)}, u32[]{:S(2)}) collective-permute-start(f32[7,64,640]{2,1,0:T(8,128)S(1)} %stack.1), channel_id=1, source_target_pairs={{1,0},{32,33},{3,2},{34,35},{5,4},{36,37},{7,6},{38,39},{65,64},{9... | collective-permute-start | bytes 3440648 | tf_op jit(solution)/shard_map/ppermute | solution.py:845
  36.8 0.7 collective-permute-start.6
  37.5 0.7 collective-permute-start.5
  38.2 1.0 collective-permute-done.14.refs_9_.refs_1_
  39.4 0.7 collective-permute-start.15
  40.6 0.7 collective-permute-start.16
  41.2 0.7 collective-permute-start.4
  41.9 20.5 %collective-permute-start.3 = (f32[64,1152]{1,0:T(8,128)S(1)}, f32[64,1152]{1,0:T(8,128)S(1)}, u32[]{:S(2)}, u32[]{:S(2)}) collective-permute-start(f32[64,1152]{1,0:T(8,128)S(1)} %copy-done.2), channel_id=1, source_target_pairs={{32,0},{1,33},{34,2},{3,35},{36,4},{5,37},{38,6},{7,39},{96,64},{6... | collective-permute-start | bytes 884744 | tf_op jit(solution)/shard_map/ppermute | solution.py:835
  62.4 0.7 collective-permute-start.2
  63.1 0.7 collective-permute-start.1
  63.8 0.7 collective-permute-start
  64.9 0.7 collective-permute-start.17
  66.2 1.4 copy-done
  68.1 1.2 copy-done.1
  69.3 1.0 copy-done.5
  70.4 0.7 collective-permute-start.21
  71.0 0.7 collective-permute-start.20
  71.7 1.3 collective-permute-start.19
  73.7 25.4 %collective-permute-done.19.refs_8_ = f32[64,512]{1,0:T(8,128)S(1)} collective-permute-done((f32[64,512]{1,0:T(8,128)S(1)}, f32[64,512]{1,0:T(8,128)S(1)}, u32[]{:S(2)}, u32[]{:S(2)}) %collective-permute-start.19) | collective-permute-done | bytes 131104 | tf_op jit(solution)/shard_map/ppermute | solution.py:849
  99.5 0.7 collective-permute-start.26
  104.0 2.7 %early.1 = (f32[2,64,512]{2,1,0:T(8,128)}, f32[6,64,512]{2,1,0:T(8,128)S(1)}, bf16[2,576,192]{2,1,0:T(8,128)(2,1)S(1)}) custom-call(f32[64,640]{1,0:T(8,128)S(1)} %copy-done.3, f32[64,640]{1,0:T(8,128)S(1)} %copy-done.6, f32[64,1152]{1,0:T(8,128)S(1)} %copy-done.2, f32[64,512]{1,0:T(8,128)S(1)} %bitcast.9, f32[64,512]{1,0:T(8,128)S(1)} %get-tuple-element.124.refs_4_, ...), custom_call_target="tpu_custom_call" | custom-call | tf_op jit(solution)/shard_map/early/pallas_call | solution.py:720
  106.7 1.0 back_0.1
  109.8 1.3 collective-permute-start.31
  111.1 0.7 collective-permute-start.32
  113.2 52.5 %collective-permute-done.31.refs_6_ = f32[64,512]{1,0:T(8,128)S(1)} collective-permute-done((f32[64,512]{1,0:T(8,128)S(1)}, f32[64,512]{1,0:T(8,128)S(1)}, u32[]{:S(2)}, u32[]{:S(2)}) %collective-permute-start.31) | collective-permute-done | bytes 131104 | tf_op jit(solution)/shard_map/ppermute | solution.py:849
  165.7 2.7 %late.1 = (f32[2,64,512]{2,1,0:T(8,128)}, f32[64,640]{1,0:T(8,128)S(1)}, f32[64,640]{1,0:T(8,128)S(1)}) custom-call(f32[6,64,512]{2,1,0:T(8,128)S(1)} %get-tuple-element.170.refs_0_, bf16[2,576,192]{2,1,0:T(8,128)(2,1)S(1)} %get-tuple-element.171.refs_1_, f32[64,512]{1,0:T(8,128)S(1)} %get-tuple-element.181.refs_2_, ...), custom_call_target="tpu_custom_call" | custom-call | tf_op jit(solution)/shard_map/late/pallas_call | solution.py:769
  168.4 6.2 %collective-permute-start.35 = (f32[64,640]{1,0:T(8,128)S(1)}, f32[64,640]{1,0:T(8,128)S(1)}, u32[]{:S(2)}, u32[]{:S(2)}) collective-permute-start(f32[64,640]{1,0:T(8,128)S(1)} %get-tuple-element.191), channel_id=1, source_target_pairs={{0,1},{1,0},{2,3},{3,2},{4,5},{5,4},{6,7},{7,6},{8,9},{9,8},{10,11... | collective-permute-start | bytes 491528 | tf_op jit(solution)/shard_map/ppermute | solution.py:901
  174.6 1.0 collective-permute-done.35
  175.7 1.4 collective-permute-start.36
  177.0 4.1 %collective-permute-done.36 = f32[64,640]{1,0:T(8,128)S(1)} collective-permute-done((f32[64,640]{1,0:T(8,128)S(1)}, f32[64,640]{1,0:T(8,128)S(1)}, u32[]{:S(2)}, u32[]{:S(2)}) %collective-permute-start.36) | collective-permute-done | bytes 163872 | tf_op jit(solution)/shard_map/ppermute | solution.py:903
  181.2 2.8 %collective-permute-start.37 = (f32[64,640]{1,0:T(8,128)S(1)}, f32[64,640]{1,0:T(8,128)S(1)}, u32[]{:S(2)}, u32[]{:S(2)}) collective-permute-start(f32[64,640]{1,0:T(8,128)S(1)} %add.10), channel_id=1, source_target_pairs={{0,6},{1,7},{2,4},{3,5},{4,2},{5,3},{6,0},{7,1},{8,14},{9,15},{10,... | collective-permute-start | bytes 491528 | tf_op jit(solution)/shard_map/ppermute | solution.py:903
  184.0 3.1 %collective-permute-done.37 = f32[64,640]{1,0:T(8,128)S(1)} collective-permute-done((f32[64,640]{1,0:T(8,128)S(1)}, f32[64,640]{1,0:T(8,128)S(1)}, u32[]{:S(2)}, u32[]{:S(2)}) %collective-permute-start.37) | collective-permute-done | bytes 163872 | tf_op jit(solution)/shard_map/ppermute | solution.py:903
  187.1 2.1 %collective-permute-start.38 = (f32[64,640]{1,0:T(8,128)S(1)}, f32[64,640]{1,0:T(8,128)S(1)}, u32[]{:S(2)}, u32[]{:S(2)}) collective-permute-start(f32[64,640]{1,0:T(8,128)S(1)} %add.11.mine_ref), channel_id=1, source_target_pairs={{0,1},{1,0},{2,3},{3,2},{4,5},{5,4},{6,7},{7,6},{8,9},{9,8},{10,11... | collective-permute-start | bytes 491528 | tf_op jit(solution)/shard_map/ppermute | solution.py:904
  189.3 1.0 collective-permute-done.38.other_ref
  190.3 0.8 finish.1
  (64 shorter events, 10.6 us)
Async XLA Ops:
  3.8 33.0 %copy-start.2 = (f32[64,1152]{1,0:T(8,128)S(1)}, f32[64,1152]{1,0:T(8,128)}, u32[]{:S(2)}) copy-start(f32[64,1152]{1,0:T(8,128)} %get-tuple-element.101.refs_0_.refs_8_.refs_2_) | copy-start | bytes 884740
  3.8 35.3 %copy-start.3 = (f32[64,640]{1,0:T(8,128)S(1)}, f32[64,640]{1,0:T(8,128)}, u32[]{:S(2)}) copy-start(f32[64,640]{1,0:T(8,128)} %get-tuple-element.99.refs_0_) | copy-start | bytes 491524
  3.8 35.3 %copy-start.6 = (f32[64,640]{1,0:T(8,128)S(1)}, f32[64,640]{1,0:T(8,128)}, u32[]{:S(2)}) copy-start(f32[64,640]{1,0:T(8,128)} %get-tuple-element.106.refs_8_.refs_0_.refs_1_) | copy-start | bytes 491524
  3.8 15.0 %collective-permute-start.10 = (f32[64,640]{1,0:T(8,128)}, f32[64,640]{1,0:T(8,128)S(1)}, u32[]{:S(2)}, u32[]{:S(2)}) collective-permute-start(f32[64,640]{1,0:T(8,128)} %get-tuple-element.103), channel_id=1, source_target_pairs={{32,0},{0,32},{33,1},{1,33},{34,2},{2,34},{35,3},{3,35},{36,4},{4,... | collective-permute-start | bytes 491528 | tf_op jit(solution)/shard_map/ppermute | solution.py:841
  13.6 8.7 %collective-permute-start.9 = (f32[64,640]{1,0:T(8,128)}, f32[64,640]{1,0:T(8,128)S(1)}, u32[]{:S(2)}, u32[]{:S(2)}) collective-permute-start(f32[64,640]{1,0:T(8,128)} %get-tuple-element.102), channel_id=1, source_target_pairs={{24,0},{56,32},{25,1},{57,33},{26,2},{58,34},{27,3},{59,35},{28,4}... | collective-permute-start | bytes 491528 | tf_op jit(solution)/shard_map/ppermute | solution.py:841
  14.9 12.3 %collective-permute-start.8 = (f32[64,640]{1,0:T(8,128)}, f32[64,640]{1,0:T(8,128)S(1)}, u32[]{:S(2)}, u32[]{:S(2)}) collective-permute-start(f32[64,640]{1,0:T(8,128)} %get-tuple-element.102), channel_id=1, source_target_pairs={{16,0},{48,32},{17,1},{49,33},{18,2},{50,34},{19,3},{51,35},{20,4}... | collective-permute-start | bytes 491528 | tf_op jit(solution)/shard_map/ppermute | solution.py:841
  16.2 14.4 %collective-permute-start.7 = (f32[64,640]{1,0:T(8,128)}, f32[64,640]{1,0:T(8,128)S(1)}, u32[]{:S(2)}, u32[]{:S(2)}) collective-permute-start(f32[64,640]{1,0:T(8,128)} %get-tuple-element.102), channel_id=1, source_target_pairs={{8,0},{40,32},{9,1},{41,33},{10,2},{42,34},{11,3},{43,35},{12,4},{... | collective-permute-start | bytes 491528 | tf_op jit(solution)/shard_map/ppermute | solution.py:841
  17.5 13.1 %collective-permute-start.13 = (f32[64,640]{1,0:T(8,128)}, f32[64,640]{1,0:T(8,128)S(1)}, u32[]{:S(2)}, u32[]{:S(2)}) collective-permute-start(f32[64,640]{1,0:T(8,128)} %get-tuple-element.104), channel_id=1, source_target_pairs={{56,0},{24,32},{57,1},{25,33},{58,2},{26,34},{59,3},{27,35},{60,4}... | collective-permute-start | bytes 491528 | tf_op jit(solution)/shard_map/ppermute | solution.py:841
  18.8 11.8 %collective-permute-start.12 = (f32[64,640]{1,0:T(8,128)}, f32[64,640]{1,0:T(8,128)S(1)}, u32[]{:S(2)}, u32[]{:S(2)}) collective-permute-start(f32[64,640]{1,0:T(8,128)} %get-tuple-element.104), channel_id=1, source_target_pairs={{48,0},{16,32},{49,1},{17,33},{50,2},{18,34},{51,3},{19,35},{52,4}... | collective-permute-start | bytes 491528 | tf_op jit(solution)/shard_map/ppermute | solution.py:841
  22.3 9.3 %collective-permute-start.11 = (f32[64,640]{1,0:T(8,128)}, f32[64,640]{1,0:T(8,128)S(1)}, u32[]{:S(2)}, u32[]{:S(2)}) collective-permute-start(f32[64,640]{1,0:T(8,128)} %get-tuple-element.104), channel_id=1, source_target_pairs={{40,0},{8,32},{41,1},{9,33},{42,2},{10,34},{43,3},{11,35},{44,4},{... | collective-permute-start | bytes 491528 | tf_op jit(solution)/shard_map/ppermute | solution.py:841
  33.1 6.0 %collective-permute-start.14 = (f32[7,64,640]{2,1,0:T(8,128)S(1)}, f32[7,64,640]{2,1,0:T(8,128)S(1)}, u32[]{:S(2)}, u32[]{:S(2)}) collective-permute-start(f32[7,64,640]{2,1,0:T(8,128)S(1)} %stack.1), channel_id=1, source_target_pairs={{1,0},{32,33},{3,2},{34,35},{5,4},{36,37},{7,6},{38,39},{65,64},{9... | collective-permute-start | bytes 3440648 | tf_op jit(solution)/shard_map/ppermute | solution.py:845
  36.8 25.6 %collective-permute-start.6 = (f32[64,1152]{1,0:T(8,128)S(1)}, f32[64,1152]{1,0:T(8,128)S(1)}, u32[]{:S(2)}, u32[]{:S(2)}) collective-permute-start(f32[64,1152]{1,0:T(8,128)S(1)} %copy-done.2), channel_id=1, source_target_pairs={{56,0},{25,33},{58,2},{27,35},{60,4},{29,37},{62,6},{31,39},{120,6... | collective-permute-start | bytes 884744 | tf_op jit(solution)/shard_map/ppermute | solution.py:835
  37.5 25.6 %collective-permute-start.5 = (f32[64,1152]{1,0:T(8,128)S(1)}, f32[64,1152]{1,0:T(8,128)S(1)}, u32[]{:S(2)}, u32[]{:S(2)}) collective-permute-start(f32[64,1152]{1,0:T(8,128)S(1)} %copy-done.2), channel_id=1, source_target_pairs={{48,0},{17,33},{50,2},{19,35},{52,4},{21,37},{54,6},{23,39},{112,6... | collective-permute-start | bytes 884744 | tf_op jit(solution)/shard_map/ppermute | solution.py:835
  39.4 0.8 collective-permute-start.15
  40.6 23.3 %collective-permute-start.16 = (f32[64,512]{1,0:T(8,128)S(1)}, f32[64,512]{1,0:T(8,128)S(1)}, u32[]{:S(2)}, u32[]{:S(2)}) collective-permute-start(f32[64,512]{1,0:T(8,128)S(1)} %get-tuple-element.109), channel_id=1, source_target_pairs={{64,128},{97,161},{66,130},{99,163},{68,132},{101,165},{70,134},{1... | collective-permute-start | bytes 393224 | tf_op jit(solution)/shard_map/ppermute | solution.py:855
  41.2 23.6 %collective-permute-start.4 = (f32[64,1152]{1,0:T(8,128)S(1)}, f32[64,1152]{1,0:T(8,128)S(1)}, u32[]{:S(2)}, u32[]{:S(2)}) collective-permute-start(f32[64,1152]{1,0:T(8,128)S(1)} %copy-done.2), channel_id=1, source_target_pairs={{40,0},{9,33},{42,2},{11,35},{44,4},{13,37},{46,6},{15,39},{104,64... | collective-permute-start | bytes 884744 | tf_op jit(solution)/shard_map/ppermute | solution.py:835
  41.9 24.2 %collective-permute-start.3 = (f32[64,1152]{1,0:T(8,128)S(1)}, f32[64,1152]{1,0:T(8,128)S(1)}, u32[]{:S(2)}, u32[]{:S(2)}) collective-permute-start(f32[64,1152]{1,0:T(8,128)S(1)} %copy-done.2), channel_id=1, source_target_pairs={{32,0},{1,33},{34,2},{3,35},{36,4},{5,37},{38,6},{7,39},{96,64},{6... | collective-permute-start | bytes 884744 | tf_op jit(solution)/shard_map/ppermute | solution.py:835
  62.4 5.2 %copy-start.4 = (f32[64,1152]{1,0:T(8,128)}, f32[64,1152]{1,0:T(8,128)S(1)}, u32[]{:S(2)}) copy-start(f32[64,1152]{1,0:T(8,128)S(1)} %collective-permute-done.6.refs_7_.refs_15_) | copy-start | bytes 884740
  62.4 3.7 %collective-permute-start.2 = (f32[64,1152]{1,0:T(8,128)S(1)}, f32[64,1152]{1,0:T(8,128)S(1)}, u32[]{:S(2)}, u32[]{:S(2)}) collective-permute-start(f32[64,1152]{1,0:T(8,128)S(1)} %copy-done.2), channel_id=1, source_target_pairs={{24,0},{57,33},{26,2},{59,35},{28,4},{61,37},{30,6},{63,39},{88,64... | collective-permute-start | bytes 884744 | tf_op jit(solution)/shard_map/ppermute | solution.py:835
  63.1 3.0 %collective-permute-start.1 = (f32[64,1152]{1,0:T(8,128)S(1)}, f32[64,1152]{1,0:T(8,128)S(1)}, u32[]{:S(2)}, u32[]{:S(2)}) collective-permute-start(f32[64,1152]{1,0:T(8,128)S(1)} %copy-done.2), channel_id=1, source_target_pairs={{16,0},{49,33},{18,2},{51,35},{20,4},{53,37},{22,6},{55,39},{80,64... | collective-permute-start | bytes 884744 | tf_op jit(solution)/shard_map/ppermute | solution.py:835
  63.8 2.3 %collective-permute-start = (f32[64,1152]{1,0:T(8,128)S(1)}, f32[64,1152]{1,0:T(8,128)S(1)}, u32[]{:S(2)}, u32[]{:S(2)}) collective-permute-start(f32[64,1152]{1,0:T(8,128)S(1)} %copy-done.2), channel_id=1, source_target_pairs={{8,0},{41,33},{10,2},{43,35},{12,4},{45,37},{14,6},{47,39},{72,64}... | collective-permute-start | bytes 884744 | tf_op jit(solution)/shard_map/ppermute | solution.py:835
  64.9 2.8 %collective-permute-start.17 = (f32[64,512]{1,0:T(8,128)S(1)}, f32[64,512]{1,0:T(8,128)S(1)}, u32[]{:S(2)}, u32[]{:S(2)}) collective-permute-start(f32[64,512]{1,0:T(8,128)S(1)} %get-tuple-element.115), channel_id=1, source_target_pairs={{128,192},{161,225},{130,194},{163,227},{132,196},{165,229},{134,1... | collective-permute-start | bytes 393224 | tf_op jit(solution)/shard_map/ppermute | solution.py:855
  66.2 1.4 copy-start
  67.6 1.7 copy-start.1
  69.3 1.0 copy-start.5
  70.4 3.3 %collective-permute-start.21 = (f32[64,512]{1,0:T(8,128)S(1)}, f32[64,512]{1,0:T(8,128)S(1)}, u32[]{:S(2)}, u32[]{:S(2)}) collective-permute-start(f32[64,512]{1,0:T(8,128)S(1)} %get-tuple-element.134), channel_id=1, source_target_pairs={{0,24},{33,57},{2,26},{35,59},{4,28},{37,61},{6,30},{39,63},{64,88... | collective-permute-start | bytes 393224 | tf_op jit(solution)/shard_map/ppermute | solution.py:849
  71.0 2.7 %collective-permute-start.20 = (f32[64,512]{1,0:T(8,128)S(1)}, f32[64,512]{1,0:T(8,128)S(1)}, u32[]{:S(2)}, u32[]{:S(2)}) collective-permute-start(f32[64,512]{1,0:T(8,128)S(1)} %get-tuple-element.132), channel_id=1, source_target_pairs={{0,40},{33,9},{2,42},{35,11},{4,44},{37,13},{6,46},{39,15},{64,104... | collective-permute-start | bytes 393224 | tf_op jit(solution)/shard_map/ppermute | solution.py:849
  71.7 27.4 %collective-permute-start.19 = (f32[64,512]{1,0:T(8,128)S(1)}, f32[64,512]{1,0:T(8,128)S(1)}, u32[]{:S(2)}, u32[]{:S(2)}) collective-permute-start(f32[64,512]{1,0:T(8,128)S(1)} %get-tuple-element.130), channel_id=1, source_target_pairs={{0,32},{33,1},{2,34},{35,3},{4,36},{37,5},{6,38},{39,7},{64,96},{9... | collective-permute-start | bytes 393224 | tf_op jit(solution)/shard_map/ppermute | solution.py:849
  73.0 26.1 %collective-permute-start.18 = (f32[64,512]{1,0:T(8,128)S(1)}, f32[64,512]{1,0:T(8,128)S(1)}, u32[]{:S(2)}, u32[]{:S(2)}) collective-permute-start(f32[64,512]{1,0:T(8,128)S(1)} %get-tuple-element.125), channel_id=1, source_target_pairs={{192,128},{225,161},{194,130},{227,163},{196,132},{229,165},{198,1... | collective-permute-start | bytes 393224 | tf_op jit(solution)/shard_map/ppermute | solution.py:855
  99.5 3.4 %collective-permute-start.26 = (f32[64,512]{1,0:T(8,128)S(1)}, f32[64,512]{1,0:T(8,128)S(1)}, u32[]{:S(2)}, u32[]{:S(2)}) collective-permute-start(f32[64,512]{1,0:T(8,128)S(1)} %get-tuple-element.147), channel_id=1, source_target_pairs={{128,64},{161,97},{130,66},{163,99},{132,68},{165,101},{134,70},{1... | collective-permute-start | bytes 393224 | tf_op jit(solution)/shard_map/ppermute | solution.py:855
  100.1 3.8 %collective-permute-start.22 = (f32[64,512]{1,0:T(8,128)S(1)}, f32[64,512]{1,0:T(8,128)S(1)}, u32[]{:S(2)}, u32[]{:S(2)}) collective-permute-start(f32[64,512]{1,0:T(8,128)S(1)} %get-tuple-element.149), channel_id=1, source_target_pairs={{0,8},{33,41},{2,10},{35,43},{4,12},{37,45},{6,14},{39,47},{64,72}... | collective-permute-start | bytes 393224 | tf_op jit(solution)/shard_map/ppermute | solution.py:849
  100.8 3.1 %collective-permute-start.23 = (f32[64,512]{1,0:T(8,128)S(1)}, f32[64,512]{1,0:T(8,128)S(1)}, u32[]{:S(2)}, u32[]{:S(2)}) collective-permute-start(f32[64,512]{1,0:T(8,128)S(1)} %get-tuple-element.151), channel_id=1, source_target_pairs={{0,16},{33,49},{2,18},{35,51},{4,20},{37,53},{6,22},{39,55},{64,80... | collective-permute-start | bytes 393224 | tf_op jit(solution)/shard_map/ppermute | solution.py:849
  101.5 2.5 %collective-permute-start.24 = (f32[64,512]{1,0:T(8,128)S(1)}, f32[64,512]{1,0:T(8,128)S(1)}, u32[]{:S(2)}, u32[]{:S(2)}) collective-permute-start(f32[64,512]{1,0:T(8,128)S(1)} %get-tuple-element.156), channel_id=1, source_target_pairs={{0,48},{33,17},{2,50},{35,19},{4,52},{37,21},{6,54},{39,23},{64,11... | collective-permute-start | bytes 393224 | tf_op jit(solution)/shard_map/ppermute | solution.py:849
  102.2 1.8 collective-permute-start.25
  102.9 1.1 copy-start.7
  103.3 3.4 %collective-permute-start.27 = (f32[64,512]{1,0:T(8,128)S(1)}, f32[64,512]{1,0:T(8,128)S(1)}, u32[]{:S(2)}, u32[]{:S(2)}) collective-permute-start(f32[64,512]{1,0:T(8,128)S(1)} %get-tuple-element.168), channel_id=1, source_target_pairs={{64,0},{97,33},{66,2},{99,35},{68,4},{101,37},{70,6},{103,39}} | collective-permute-start | bytes 393224 | tf_op jit(solution)/shard_map/ppermute | solution.py:855
  107.8 4.0 %collective-permute-start.28 = (f32[64,512]{1,0:T(8,128)S(1)}, f32[64,512]{1,0:T(8,128)S(1)}, u32[]{:S(2)}, u32[]{:S(2)}) collective-permute-start(f32[64,512]{1,0:T(8,128)S(1)} %get-tuple-element.182), channel_id=1, source_target_pairs={{0,8},{33,41},{2,10},{35,43},{4,12},{37,45},{6,14},{39,47},{64,72}... | collective-permute-start | bytes 393224 | tf_op jit(solution)/shard_map/ppermute | solution.py:849
  108.4 4.0 %collective-permute-start.29 = (f32[64,512]{1,0:T(8,128)S(1)}, f32[64,512]{1,0:T(8,128)S(1)}, u32[]{:S(2)}, u32[]{:S(2)}) collective-permute-start(f32[64,512]{1,0:T(8,128)S(1)} %get-tuple-element.183), channel_id=1, source_target_pairs={{0,16},{33,49},{2,18},{35,51},{4,20},{37,53},{6,22},{39,55},{64,80... | collective-permute-start | bytes 393224 | tf_op jit(solution)/shard_map/ppermute | solution.py:849
  109.1 4.0 %collective-permute-start.30 = (f32[64,512]{1,0:T(8,128)S(1)}, f32[64,512]{1,0:T(8,128)S(1)}, u32[]{:S(2)}, u32[]{:S(2)}) collective-permute-start(f32[64,512]{1,0:T(8,128)S(1)} %get-tuple-element.184), channel_id=1, source_target_pairs={{0,24},{33,57},{2,26},{35,59},{4,28},{37,61},{6,30},{39,63},{64,88... | collective-permute-start | bytes 393224 | tf_op jit(solution)/shard_map/ppermute | solution.py:849
  109.8 55.9 %collective-permute-start.31 = (f32[64,512]{1,0:T(8,128)S(1)}, f32[64,512]{1,0:T(8,128)S(1)}, u32[]{:S(2)}, u32[]{:S(2)}) collective-permute-start(f32[64,512]{1,0:T(8,128)S(1)} %get-tuple-element.185), channel_id=1, source_target_pairs={{0,32},{33,1},{2,34},{35,3},{4,36},{37,5},{6,38},{39,7},{64,96},{9... | collective-permute-start | bytes 393224 | tf_op jit(solution)/shard_map/ppermute | solution.py:849
  111.1 54.6 %collective-permute-start.32 = (f32[64,512]{1,0:T(8,128)S(1)}, f32[64,512]{1,0:T(8,128)S(1)}, u32[]{:S(2)}, u32[]{:S(2)}) collective-permute-start(f32[64,512]{1,0:T(8,128)S(1)} %get-tuple-element.186), channel_id=1, source_target_pairs={{0,40},{33,9},{2,42},{35,11},{4,44},{37,13},{6,46},{39,15},{64,104... | collective-permute-start | bytes 393224 | tf_op jit(solution)/shard_map/ppermute | solution.py:849
  111.8 53.9 %collective-permute-start.33 = (f32[64,512]{1,0:T(8,128)S(1)}, f32[64,512]{1,0:T(8,128)S(1)}, u32[]{:S(2)}, u32[]{:S(2)}) collective-permute-start(f32[64,512]{1,0:T(8,128)S(1)} %get-tuple-element.187), channel_id=1, source_target_pairs={{0,48},{33,17},{2,50},{35,19},{4,52},{37,21},{6,54},{39,23},{64,11... | collective-permute-start | bytes 393224 | tf_op jit(solution)/shard_map/ppermute | solution.py:849
  112.5 53.2 %collective-permute-start.34 = (f32[64,512]{1,0:T(8,128)S(1)}, f32[64,512]{1,0:T(8,128)S(1)}, u32[]{:S(2)}, u32[]{:S(2)}) collective-permute-start(f32[64,512]{1,0:T(8,128)S(1)} %get-tuple-element.188), channel_id=1, source_target_pairs={{0,56},{33,25},{2,58},{35,27},{4,60},{37,29},{6,62},{39,31},{64,12... | collective-permute-start | bytes 393224 | tf_op jit(solution)/shard_map/ppermute | solution.py:849
  168.4 7.2 %collective-permute-start.35 = (f32[64,640]{1,0:T(8,128)S(1)}, f32[64,640]{1,0:T(8,128)S(1)}, u32[]{:S(2)}, u32[]{:S(2)}) collective-permute-start(f32[64,640]{1,0:T(8,128)S(1)} %get-tuple-element.191), channel_id=1, source_target_pairs={{0,1},{1,0},{2,3},{3,2},{4,5},{5,4},{6,7},{7,6},{8,9},{9,8},{10,11... | collective-permute-start | bytes 491528 | tf_op jit(solution)/shard_map/ppermute | solution.py:901
  175.7 5.5 %collective-permute-start.36 = (f32[64,640]{1,0:T(8,128)S(1)}, f32[64,640]{1,0:T(8,128)S(1)}, u32[]{:S(2)}, u32[]{:S(2)}) collective-permute-start(f32[64,640]{1,0:T(8,128)S(1)} %add.9), channel_id=1, source_target_pairs={{0,2},{1,3},{2,0},{3,1},{4,6},{5,7},{6,4},{7,5},{8,10},{9,11},{10,... | collective-permute-start | bytes 491528 | tf_op jit(solution)/shard_map/ppermute | solution.py:903
  181.2 5.9 %collective-permute-start.37 = (f32[64,640]{1,0:T(8,128)S(1)}, f32[64,640]{1,0:T(8,128)S(1)}, u32[]{:S(2)}, u32[]{:S(2)}) collective-permute-start(f32[64,640]{1,0:T(8,128)S(1)} %add.10), channel_id=1, source_target_pairs={{0,6},{1,7},{2,4},{3,5},{4,2},{5,3},{6,0},{7,1},{8,14},{9,15},{10,... | collective-permute-start | bytes 491528 | tf_op jit(solution)/shard_map/ppermute | solution.py:903
  187.1 3.2 %collective-permute-start.38 = (f32[64,640]{1,0:T(8,128)S(1)}, f32[64,640]{1,0:T(8,128)S(1)}, u32[]{:S(2)}, u32[]{:S(2)}) collective-permute-start(f32[64,640]{1,0:T(8,128)S(1)} %add.11.mine_ref), channel_id=1, source_target_pairs={{0,1},{1,0},{2,3},{3,2},{4,5},{5,4},{6,7},{7,6},{8,9},{9,8},{10,11... | collective-permute-start | bytes 491528 | tf_op jit(solution)/shard_map/ppermute | solution.py:904

commit v4 on v3

--- a/solution.py
+++ b/solution.py
@@ -137,7 +137,7 @@
 def place():
     layer, image = lax.axis_index("layer"), lax.axis_index("dp")
     core = image % 2
-    return layer // RING, layer % RING, (RING // 2) * core, core
+    return layer // RING, layer % RING, RING // 2 - 1 + core, core
 
 
 def start_all(copies):
@@ -163,9 +163,7 @@
     return pltpu.VMEM(shape.shape, shape.dtype)
 
 
-def relax_kernel(c_hbm, a_hbm, w_hbm, b_hbm, *refs):
-    outs, (c_ref, a_ref, w_ref, b_ref, sems) = refs[:6], refs[6:]
-    low_ref, high_ref, mid_ref, tau_ref, even_ref, two_ref = outs
+def relax_kernel(c_hbm, a_hbm, w_hbm, b_hbm, one_ref, two_ref, c_ref, a_ref, w_ref, b_ref, sems):
     copies = start_all(
         [
             pltpu.make_async_copy(source, target, sems.at[i])
@@ -180,53 +178,23 @@
     b0, b1 = as_column(b_ref[0:1]), as_column(b_ref[1:2])
     t0 = jnp.tanh(conv(lhs_forward(w0), c, 1) + b0)
     t1 = jnp.tanh(conv(lhs_forward(w1), c + H * t0, 1) + b1)
-    ring, spot, _, core = place()
+    pad = WPAD - 576
+    one_ref[:, 0:576] = w0
+    one_ref[:, 576:WPAD] = jnp.broadcast_to(b0, (CH, pad))
+    ring, spot, _, _ = place()
     keep = jnp.where((ring == 0) & (spot == 0), 1.0, 0.0)
-    tau = jnp.where(keep > 0.0, c + H * t0 + H * t1, H * (t1 - t0))
-
-    def write_tau(ref):
-        ref[:, 0:CELLS] = tau
-        ref[:, CELLS:WPAD] = jnp.broadcast_to(b0, (CH, WPAD - CELLS))
-
-    def write_even(ref):
-        ref[:, 0:576] = w0
-        ref[:, 576:WPAD] = jnp.zeros((CH, WPAD - 576), F32)
-
-    write_tau(tau_ref)
-    write_even(even_ref)
-
-    first = (core == 0) == (spot < RING // 2)
-    middle_first = (core == 0) == (spot == RING // 2)
-
-    @pl.when(first)
-    def _():
-        write_tau(low_ref)
-        write_even(high_ref)
-
-    @pl.when(jnp.logical_not(first))
-    def _():
-        write_even(low_ref)
-        write_tau(high_ref)
-
-    @pl.when(middle_first)
-    def _():
-        write_tau(mid_ref)
-
-    @pl.when(jnp.logical_not(middle_first))
-    def _():
-        write_even(mid_ref)
-
+    one_ref[:, WPAD:BLK] = jnp.where(keep > 0.0, c + H * t0 + H * t1, H * (t1 - t0))
     two_ref[:, 0:576] = w1
-    two_ref[:, 576:WPAD] = jnp.broadcast_to(b1, (CH, WPAD - 576))
+    two_ref[:, 576:WPAD] = jnp.broadcast_to(b1, (CH, pad))
     wait_all(copies[3:])
     two_ref[:, WPAD:BLK] = swap(a_ref[...])
 
 
 def relax(c, a, w, b):
-    short = jax.ShapeDtypeStruct((CH, WPAD), F32)
+    shape = jax.ShapeDtypeStruct((CH, BLK), F32)
     return pl.pallas_call(
         relax_kernel,
-        out_shape=(short,) * 5 + (jax.ShapeDtypeStruct((CH, BLK), F32),),
+        out_shape=(shape, shape),
         in_specs=[HBM] * 4,
         scratch_shapes=[
             pltpu.VMEM(c.shape, F32),
@@ -240,7 +208,14 @@
     )(c, a, w, b)
 
 
-def slots(refs, target, sems, lead):
+MATRIX = pl.ds(0, WPAD)
+REST = pl.ds(CELLS, WPAD)
+BIAS = WPAD - 576
+
+
+def slots(refs, target, sems, lead, part=None):
+    if part is not None:
+        refs = [ref.at[:, part] for ref in refs]
     copies = []
     for k, ref in enumerate(refs):
         j = (lead + k) % RING
@@ -248,47 +223,31 @@
     return copies
 
 
-def stack_kernel(*refs):
-    block_refs, stack_ref, sems = refs[: RING - 1], refs[RING - 1], refs[RING]
-    _, spot, lead, _ = place()
-
-    @pl.when(spot == RING // 2 - lead)
-    def _():
-        wait_all(
-            start_all(
-                [
-                    pltpu.make_async_copy(block_refs[k], stack_ref.at[k], sems.at[k])
-                    for k in range(RING - 1)
-                ]
-            )
-        )
-
-
-def stack(blocks):
-    return pl.pallas_call(
-        stack_kernel,
-        out_shape=jax.ShapeDtypeStruct((RING - 1, CH, WPAD), F32),
-        in_specs=[ANY] * (RING - 1),
-        out_specs=ANY,
-        scratch_shapes=[pltpu.SemaphoreType.DMA((RING - 1,))],
-        compiler_params=PARAMS,
-        name="stack",
-    )(*blocks)
-
-
-def even_slots(own_ref, stack_ref, target, sems, lead):
-    return slots([own_ref] + [stack_ref.at[k] for k in range(RING - 1)], target, sems, lead)
+HALF = RING // 2
+
+
+def half(array, i):
+    return array.at[pl.ds(HALF * i, HALF)]
+
+
+def half_out(vt, vt_ref, sems, part):
+    return start_all(
+        [
+            pltpu.make_async_copy(half(vt.at[i], part), half(vt_ref.at[i], part), sems.at[i, part])
+            for i in (0, 1)
+        ]
+    )
 
 
 def first_kernel(*refs):
-    tau_refs, own_ref, stack_ref = refs[:RING], refs[RING], refs[RING + 1]
-    vt_ref, out_ref, tau, even, vt, lhs, tau_sems, even_sems, sems = refs[RING + 2 :]
+    one_refs = refs[:RING]
+    vt_ref, out_ref, tau, even, vt, lhs, tau_sems, even_sems, sems = refs[RING:]
     ring, spot, lead, _ = place()
 
     @pl.when((ring == 0) & (spot == lead))
     def _():
-        copies = even_slots(own_ref, stack_ref, even, even_sems, lead)
-        copies += slots(tau_refs, tau, tau_sems, lead)
+        copies = slots(one_refs, even, even_sems, lead, MATRIX)
+        copies += slots(one_refs, tau, tau_sems, lead, REST)
         wait_all(start_all(copies))
 
         def prepare(j, carry):
@@ -298,29 +257,22 @@
         lax.fori_loop(1, RING, prepare, 0)
 
         def step(j, v):
-            now = jnp.tanh(conv(lhs[j], v, 1) + tau[j][:, CELLS : CELLS + 1])
+            now = jnp.tanh(conv(lhs[j], v, 1) + tau[j][:, BIAS : BIAS + 1])
             vt[0, j] = v
             vt[1, j] = now
-            start_all(
-                [pltpu.make_async_copy(vt.at[i, j], vt_ref.at[i, j], sems.at[i, j]) for i in (0, 1)]
-            )
-            return v + 2 * H * now + tau[j][:, 0:CELLS]
-
-        out_ref[...] = lax.fori_loop(1, RING, step, tau[0][:, 0:CELLS])
-        wait_all(
-            [
-                pltpu.make_async_copy(vt.at[i, j], vt_ref.at[i, j], sems.at[i, j])
-                for i in (0, 1)
-                for j in range(1, RING)
-            ]
-        )
-
-
-def first_chain(taus, own, others):
+            return v + 2 * H * now + tau[j][:, WPAD - CELLS :]
+
+        v = lax.fori_loop(1, HALF, step, tau[0][:, WPAD - CELLS :])
+        copies = half_out(vt, vt_ref, sems, 0)
+        out_ref[...] = lax.fori_loop(HALF, RING, step, v)
+        wait_all(copies + half_out(vt, vt_ref, sems, 1))
+
+
+def first_chain(ones):
     return pl.pallas_call(
         first_kernel,
         out_shape=(field(2, RING), field()),
-        in_specs=[ANY] * (RING + 2),
+        in_specs=[ANY] * RING,
         out_specs=(ANY, VMEM),
         scratch_shapes=[
             pltpu.VMEM((RING, CH, WPAD), F32),
@@ -329,25 +281,21 @@
             vmem(lhs_shape(RING)),
             pltpu.SemaphoreType.DMA((RING,)),
             pltpu.SemaphoreType.DMA((RING,)),
-            pltpu.SemaphoreType.DMA((2, RING)),
+            pltpu.SemaphoreType.DMA((2, 2)),
         ],
         compiler_params=PARAMS,
         name="chain_0",
-    )(*taus, own, others)
-
-
-def prepare_kernel(sizes, *refs):
-    block_refs, outs, work = refs[:sizes], refs[sizes : sizes + 2], refs[sizes + 2 :]
-    w, ahead, behind, sems, out_sems = work
+    )(*ones)
+
+
+def prepare_kernel(*refs):
+    block_refs, outs = refs[:RING], refs[RING : RING + 2]
+    w, ahead, behind, sems, out_sems = refs[RING + 2 :]
     _, spot, lead, _ = place()
 
     @pl.when(spot == lead)
     def _():
-        if sizes == 2:
-            copies = even_slots(block_refs[0], block_refs[1], w, sems, lead)
-        else:
-            copies = slots([r.at[:, pl.ds(0, WPAD)] for r in block_refs], w, sems, lead)
-        wait_all(start_all(copies))
+        wait_all(start_all(slots(block_refs, w, sems, lead, MATRIX)))
 
         def step(j, carry):
             ahead[j] = lhs_forward(w[j][:, 0:576])
@@ -367,9 +315,9 @@
 
 def prepare(blocks, name):
     return pl.pallas_call(
-        lambda *refs: prepare_kernel(len(blocks), *refs),
+        prepare_kernel,
         out_shape=(lhs_shape(RING), lhs_shape(RING)),
-        in_specs=[ANY] * len(blocks),
+        in_specs=[ANY] * RING,
         out_specs=(ANY, ANY),
         scratch_shapes=[
             pltpu.VMEM((RING, CH, WPAD), F32),
@@ -391,32 +339,26 @@
 
     @pl.when((ring == stage) & (spot == lead))
     def _():
-        start_all(slots(tau_refs, tau, tau_sems, lead))
-
-        def ahead_copy(j):
-            return pltpu.make_async_copy(ahead_ref.at[j], ahead.at[j], ahead_sems.at[j])
-
-        start_all([ahead_copy(j) for j in range(RING)])
+        copies = start_all(slots(tau_refs, tau, tau_sems, lead, REST))
+        halves = start_all(
+            [
+                pltpu.make_async_copy(half(ahead_ref, i), half(ahead, i), ahead_sems.at[i])
+                for i in (0, 1)
+            ]
+        )
+        wait_all(copies + halves[:1])
 
         def step(j, v):
-            ahead_copy(j).wait()
-            pltpu.make_async_copy(tau_refs[0], tau.at[j], tau_sems.at[j]).wait()
-            now = jnp.tanh(conv(ahead[j], v, 1) + tau[j][:, CELLS : CELLS + 1])
+            now = jnp.tanh(conv(ahead[j], v, 1) + tau[j][:, BIAS : BIAS + 1])
             vt[0, j] = v
             vt[1, j] = now
-            start_all(
-                [pltpu.make_async_copy(vt.at[i, j], vt_ref.at[i, j], sems.at[i, j]) for i in (0, 1)]
-            )
-            return v + 2 * H * now + tau[j][:, 0:CELLS]
-
-        out_ref[...] = lax.fori_loop(0, RING, step, v_ref[...])
-        wait_all(
-            [
-                pltpu.make_async_copy(vt.at[i, j], vt_ref.at[i, j], sems.at[i, j])
-                for i in (0, 1)
-                for j in range(RING)
-            ]
-        )
+            return v + 2 * H * now + tau[j][:, WPAD - CELLS :]
+
+        v = lax.fori_loop(0, HALF, step, v_ref[...], unroll=2)
+        wait_all(halves[1:])
+        copies = half_out(vt, vt_ref, sems, 0)
+        out_ref[...] = lax.fori_loop(HALF, RING, step, v, unroll=2)
+        wait_all(copies + half_out(vt, vt_ref, sems, 1))
 
 
 def chain(stage, taus, ahead, v, vt):
@@ -431,8 +373,8 @@
             vmem(field(2, RING)),
             vmem(lhs_shape(RING)),
             pltpu.SemaphoreType.DMA((RING,)),
-            pltpu.SemaphoreType.DMA((RING,)),
-            pltpu.SemaphoreType.DMA((2, RING)),
+            pltpu.SemaphoreType.DMA((2,)),
+            pltpu.SemaphoreType.DMA((2, 2)),
         ],
         input_output_aliases={len(args): 0},
         compiler_params=PARAMS,
@@ -522,21 +464,19 @@
 
     @pl.when((ring == stage) & (spot == lead))
     def _():
-        def lhs_copy(i, j):
-            return pltpu.make_async_copy(lhs_refs[i].at[j], lhs.at[i, j], lhs_sems.at[i, j])
-
-        start_all(slots(tau_refs, tau, sems.at[0], lead))
-        start_all([lhs_copy(0, j) for j in range(RING)])
-        start_all(slots(two_refs, two, sems.at[1], lead))
-        start_all([lhs_copy(i, j) for j in range(RING) for i in (2, 3)])
-        start_all([lhs_copy(1, RING - 1 - j) for j in range(RING)])
+        copies = start_all(slots(tau_refs, tau, sems.at[0], lead, REST))
+        matrices = [
+            pltpu.make_async_copy(lhs_refs[i], lhs.at[i], lhs_sems.at[i]) for i in range(4)
+        ]
+        start_all(matrices[:1])
+        block_copies = start_all(slots(two_refs, two, sems.at[1], lead))
+        start_all(matrices[2:] + matrices[1:2])
+        wait_all(copies + matrices[:1])
 
         def ahead_step(j, v):
-            lhs_copy(0, j).wait()
-            pltpu.make_async_copy(tau_refs[0], tau.at[j], sems.at[0, j]).wait()
-            now = jnp.tanh(conv(lhs[0, j], v, 1) + tau[j][:, CELLS : CELLS + 1])
+            now = jnp.tanh(conv(lhs[0, j], v, 1) + tau[j][:, BIAS : BIAS + 1])
             vs[j] = v
-            return v + 2 * H * now + tau[j][:, 0:CELLS], now
+            return v + 2 * H * now + tau[j][:, WPAD - CELLS :], now
 
         def correct(j, v, t0):
             b1, a = two[j][:, 576:577], two[j][:, WPAD:BLK]
@@ -544,20 +484,15 @@
             for i in range(3):
                 out[i, j] = got[i]
 
-        def arrive(j):
-            pltpu.make_async_copy(two_refs[0], two.at[j], sems.at[1, j]).wait()
-            lhs_copy(2, j).wait()
-            lhs_copy(3, j).wait()
-
         def step(j, carry):
             v, old_v, old_t = carry
-            arrive(j - 1)
             new_v, now = ahead_step(j, v)
             correct(j - 1, old_v, old_t)
             return new_v, v, now
 
         start = v_ref[...]
         v, now = ahead_step(0, start)
+        wait_all(block_copies + matrices[2:])
         _, v, now = lax.fori_loop(1, RING, step, (v, start, now))
         copies = start_all(
             [
@@ -565,16 +500,15 @@
                 for k in range(RING)
             ]
         )
-        arrive(RING - 1)
         correct(RING - 1, v, now)
+        wait_all(matrices[1:2])
 
         def back(k, mu):
             j = RING - 1 - k
-            lhs_copy(1, j).wait()
             mus[j] = mu
             return back_step(lhs[1, j], mu, out[0, j], out[1, j], out[2, j])
 
-        out_ref[...] = lax.fori_loop(0, RING, back, two[RING - 1][:, WPAD:BLK])
+        out_ref[...] = lax.fori_loop(0, RING, back, two[RING - 1][:, WPAD:BLK], unroll=2)
         copies += start_all(
             [
                 pltpu.make_async_copy(mus.at[(lead + k) % RING], mu_refs[k], sems.at[1, k])
@@ -598,7 +532,7 @@
             vmem(lhs_shape(4, RING)),
             vmem(field(3, RING)),
             pltpu.SemaphoreType.DMA((2, RING)),
-            pltpu.SemaphoreType.DMA((4, RING)),
+            pltpu.SemaphoreType.DMA((4,)),
         ],
         compiler_params=PARAMS,
         name="turn",
@@ -614,28 +548,29 @@
 
     @pl.when((ring == stage) & (spot == lead))
     def _():
-        def copies(j):
+        def copies(i):
             return [
-                pltpu.make_async_copy(behind_ref.at[j], behind.at[j], sems.at[3, j]),
-            ] + [
-                pltpu.make_async_copy(part_refs[i].at[j], parts.at[i, j], sems.at[i, j])
-                for i in range(3)
+                pltpu.make_async_copy(half(source, i), half(target, i), sems.at[n, i])
+                for n, (source, target) in enumerate(
+                    [(behind_ref, behind)] + [(part_refs[p], parts.at[p]) for p in range(3)]
+                )
             ]
 
-        for j in range(RING - 1, -1, -1):
-            start_all(copies(j))
+        start_all(copies(1) + copies(0))
+        wait_all(copies(1))
 
         def step(k, mu):
             j = RING - 1 - k
-            wait_all(copies(j))
             mus[j] = mu
             return back_step(behind[j], mu, parts[0, j], parts[1, j], parts[2, j])
 
-        steps = RING - 1 if stage == 0 else RING
-        end = lax.fori_loop(0, steps, step, mu_ref[...])
+        end = lax.fori_loop(0, HALF, step, mu_ref[...], unroll=2)
+        wait_all(copies(0))
         if stage == 0:
+            end = lax.fori_loop(HALF, RING - 1, step, end)
             mus[0] = end
-            wait_all(copies(0))
+        else:
+            end = lax.fori_loop(HALF, RING, step, end, unroll=2)
         outs[RING][...] = end
         wait_all(
             start_all(
@@ -659,7 +594,7 @@
             vmem(field(3, RING)),
             vmem(lhs_shape(RING)),
             vmem(field(RING)),
-            pltpu.SemaphoreType.DMA((4, RING)),
+            pltpu.SemaphoreType.DMA((4, 2)),
             pltpu.SemaphoreType.DMA((RING,)),
         ],
         input_output_aliases=aliases,
@@ -682,7 +617,7 @@
 
 
 def early_kernel(*refs):
-    tau_ref, even_ref, two_ref, c_ref, refs = refs[0], refs[1], refs[2], refs[3], refs[4:]
+    one_ref, two_ref, c_ref, refs = refs[0], refs[1], refs[2], refs[3:]
     v_refs = refs[:RING]
     states_ref, keep_ref, lhs_ref, v_ref, sem = refs[RING:]
     fetch(v_refs, v_ref, sem)
@@ -693,8 +628,8 @@
         v_ref[...] = swap(c_ref[...])
 
     v = v_ref[...]
-    w0, w1 = even_ref[:, 0:576], two_ref[:, 0:576]
-    t0 = jnp.tanh(conv(lhs_forward(w0), v, 1) + tau_ref[:, CELLS : CELLS + 1])
+    w0, w1 = one_ref[:, 0:576], two_ref[:, 0:576]
+    t0 = jnp.tanh(conv(lhs_forward(w0), v, 1) + one_ref[:, 576:577])
     m = v + H * t0
     b1, a = two_ref[:, 576:577], two_ref[:, WPAD:BLK]
     t1 = jnp.tanh(conv(lhs_forward(w1), m, 1) + b1)
@@ -705,7 +640,7 @@
     lhs_ref[1] = behind
     shift = H * conv(behind, s1 * a, -1)
     states_ref[0] = swap(m)
-    slot = tau_ref[:, 0:CELLS]
+    slot = one_ref[:, WPAD:BLK]
     keep = jnp.where((ring == 0) & (spot == 0), 1.0, 0.0)
     states_ref[1] = swap(jnp.where(keep > 0.0, slot, v + 2 * H * t0 + slot))
     keep_ref[0] = v
@@ -716,15 +651,15 @@
     keep_ref[5] = s0 * (H * (shift - a))
 
 
-def early(tau, even, two, c, vs):
+def early(one, two, c, vs):
     return pl.pallas_call(
         early_kernel,
         out_shape=(field(2), field(6), lhs_shape(2)),
-        in_specs=[VMEM] * 4 + [ANY] * RING,
+        in_specs=[VMEM] * 3 + [ANY] * RING,
         scratch_shapes=[vmem(field()), pltpu.SemaphoreType.DMA],
         compiler_params=PARAMS,
         name="early",
-    )(tau, even, two, c, *vs)
+    )(one, two, c, *vs)
 
 
 def late_kernel(*refs):
@@ -826,22 +761,12 @@
         return (RING * x + z % RING) * images + d
 
     def lead(d):
-        return (RING // 2) * (d % 2)
+        return RING // 2 - 1 + d % 2
 
     everyone = [(x, d) for x in range(groups) for d in range(images)]
 
     def gather(value, k):
         pairs = [(device(x, lead(d) + k, d), device(x, lead(d), d)) for x, d in everyone]
-        return lax.ppermute(value, AXES, pairs)
-
-    def gather_both(value, k):
-        pairs = [
-            (device(x, z + k, d), device(x, z, d)) for x, d in everyone for z in (0, RING // 2)
-        ]
-        return lax.ppermute(value, AXES, pairs)
-
-    def hand_over(value):
-        pairs = [(device(x, lead(d), d ^ 1), device(x, lead(d), d)) for x, d in everyone]
         return lax.ppermute(value, AXES, pairs)
 
     def scatter(value, k):
@@ -855,43 +780,43 @@
         return lax.ppermute(value, AXES, pairs)
 
     c, a = coarse_guess[0, 0], adjoint_guess[0, 0]
-    low, high, mid, tau, even, two = relax(c, a, weights, biases)
-    taus, twos = [tau] + [None] * (RING - 1), [two] + [None] * (RING - 1)
+    one, two = relax(c, a, weights, biases)
+    ones, twos = [one] + [None] * (RING - 1), [two] + [None] * (RING - 1)
     for k in NEAR:
-        taus[k] = gather_both(mid if k == RING // 2 else low if k < RING // 2 else high, k)
-    others = hand_over(stack(taus[1:]))
-    vt, end = first_chain(taus, even, others)
+        ones[k] = gather(one, k)
+    vt, end = first_chain(ones)
     v = hop(end, 0, 1)
-    even_late = tie(end, even)[1]
-    ahead0, behind0 = prepare([even_late, others], "prepare")
+    ahead0, behind0 = prepare([tie(end, one)[1]] + ones[1:], "prepare")
     for k in NEAR:
         twos[k] = gather(two, k)
     for stage in range(1, last):
-        vt, end = chain(stage, taus, ahead0, v, vt)
+        vt, end = chain(stage, ones, ahead0, v, vt)
         v = hop(end, stage, stage + 1)
     ahead1, behind1 = prepare(twos, "prepare2")
-    vs, mus, end = turn(last, taus, twos, [ahead0, behind0, ahead1, behind1], v)
+    vs, mus, end = turn(last, ones, twos, [ahead0, behind0, ahead1, behind1], v)
     mu = hop(end, last, last - 1)
     vs, parts = middle(last, twos, vt, ahead1, behind1, vs)
     own_v = [vs[0]] + [None] * (RING - 1)
     for stage in range(last - 1, -1, -1):
         if stage == last - 1:
-            chunk, gate = FAR[:3], parts[0]
+            chunk, gate = FAR[:4], parts[0]
         elif stage == last - 2:
-            chunk, gate = FAR[3:], end
+            chunk, gate = FAR[4:], end
         else:
             chunk = ()
         for k in chunk:
             own_v[k] = scatter(tie(gate, vs[k])[1], k)
         if stage == last - 1:
-            got = tie(mu, *parts, *[own_v[k] for k in chunk])
-            mu, parts = got[0], got[1:4]
-            for k, value in zip(chunk, got[4:]):
-                own_v[k] = value
+            mu, *parts = tie(mu, *parts)
         if stage == 0:
-            states, keep, lhs = early(tau, even, two, c, own_v)
+            states, keep, lhs = early(one, two, c, own_v)
             mu, keep = tie(mu, keep)
         mus, end = back_chain(stage, parts, behind0, mu, mus)
+        if stage == last - 1:
+            got = tie(end, *[own_v[k] for k in chunk])
+            end = got[0]
+            for k, value in zip(chunk, got[1:]):
+                own_v[k] = value
         if stage > 0:
             mu = hop(end, stage, stage - 1)
     own_mu = [mus[0]] + [None] * (RING - 1)

time: 192 us -> 167 us (0.87)
  waiting for transfers between devices: 98.9 us -> 70.7 us
  starting transfers between devices: 72.9 us -> 79.9 us
  Pallas kernels: 14.4 us -> 11.4 us
    ppermute x7 -> x14, starting transfers between devices: 24.6 us -> 52.8 us  [gather(): return lax.ppermute(value, AXES, pairs)]
    ppermute x14, waiting for transfers between devices: 77.9 us -> 56.2 us  [scatter(): return lax.ppermute(value, AXES, pairs)]
    ppermute x8 -> x0, starting transfers between devices: 21.2 us -> none  [the longest x7 17.5 us: gather_both(): return lax.ppermute(value, AXES, pairs)]
    ppermute x8 -> x0, waiting for transfers between devices: 11.2 us -> none  [the longest x7 10.2 us: gather_both(): return lax.ppermute(value, AXES, pairs)]
    ppermute x7 -> x14, waiting for transfers between devices: 0.58 us -> 5.25 us  [gather(): return lax.ppermute(value, AXES, pairs)]
    pallas_call x4 -> x3, Pallas kernels: 4.89 us -> 3.25 us  [the longest x1 3.02 us: relax(): pl.pallas_call(relax_kernel, out_shape=(shape, shape), in_specs=[HBM] * 4...]
  transfers between devices with their start and end apart: 39 -> 38, of which waited for: 12 -> 8; matrix products, arithmetic and copies ran while one was open for 0% -> 0% of each run, Pallas kernels for 2% -> 2%
where the time goes in v4:
time: 167 us; the launch traced here: 166 us
  starting transfers between devices  79.9 us (48%)
  waiting for transfers between devices  70.7 us (42%)
  Pallas kernels  11.4 us (7%)
  local copies, waits for them, and re-layouts  3.09 us (2%)
    ppermute x14, waiting for transfers between devices, scatter(): return lax.ppermute(value, AXES, pairs)  56.2 us
    ppermute x14, starting transfers between devices, gather(): return lax.ppermute(value, AXES, pairs)  52.8 us
    ppermute x14, starting transfers between devices, scatter(): return lax.ppermute(value, AXES, pairs)  10.6 us
    ppermute x2, waiting for transfers between devices, body(): lax.ppermute(mine, 'dp', [(i, i ^ flip) for i in range(images)])  7.22 us
    ppermute x1, starting transfers between devices, body(): mine = mine + lax.ppermute(other, 'dp', [(i, i ^ 1) for i in range(images)])  5.92 us
    ppermute x14, waiting for transfers between devices, gather(): return lax.ppermute(value, AXES, pairs)  5.25 us
    ppermute x6, starting transfers between devices, hop(): return lax.ppermute(value, AXES, pairs)  4.27 us
    ppermute x2, starting transfers between devices, body(): lax.ppermute(mine, 'dp', [(i, i ^ flip) for i in range(images)])  4.21 us
  transfers between devices with their start and end apart: 38, of which 8 were waited for; matrix products, arithmetic and copies ran while one was open for 0% of the time, Pallas kernels for 2%

profile of v4, /device:TPU:1, one launch (start us, length us, event | category | flops | bytes accessed | tf_op | source)
XLA Modules:
  0.0 166.5 jit_solution(1394469837146498902)
XLA Ops:
  0.6 3.0 %relax.1 = (f32[64,1152]{1,0:T(8,128)}, f32[64,1152]{1,0:T(8,128)}) custom-call(f32[64,512]{1,0:T(8,128)} %bitcast.8, f32[64,512]{1,0:T(8,128)} %bitcast.10, f32[2,64,576]{2,1,0:T(8,128)} %w_hbm.1, f32[2,64]{1,0:T(2,128)} %b_hbm.1), custom_call_target="tpu_custom_call" | custom-call | tf_op jit(solution)/shard_map/relax/pallas_call | solution.py:195
  3.7 0.7 collective-permute-start.13
  4.3 0.7 collective-permute-start.12
  5.0 0.7 collective-permute-start.11
  5.7 11.5 %collective-permute-start.10 = (f32[64,1152]{1,0:T(8,128)}, f32[64,1152]{1,0:T(8,128)S(1)}, u32[]{:S(2)}, u32[]{:S(2)}) collective-permute-start(f32[64,1152]{1,0:T(8,128)} %get-tuple-element.100.refs_0_), channel_id=1, source_target_pairs={{56,24},{1,33},{58,26},{3,35},{60,28},{5,37},{62,30},{7,39},{120,8... | collective-permute-start | bytes 884744 | tf_op jit(solution)/shard_map/ppermute | solution.py:770
  17.2 0.7 collective-permute-start.9
  17.9 0.7 collective-permute-start.8
  18.6 0.7 collective-permute-start.7
  19.3 0.7 collective-permute-start.6
  20.0 1.6 collective-permute-done.10.refs_4_
  22.4 1.0 copy-done
  23.5 0.7 collective-permute-start.14
  24.5 0.7 collective-permute-start.15
  26.0 33.2 %collective-permute-start.3 = (f32[64,1152]{1,0:T(8,128)S(1)}, f32[64,1152]{1,0:T(8,128)S(1)}, u32[]{:S(2)}, u32[]{:S(2)}) collective-permute-start(f32[64,1152]{1,0:T(8,128)S(1)} %copy-done.4), channel_id=1, source_target_pairs={{56,24},{1,33},{58,26},{3,35},{60,28},{5,37},{62,30},{7,39},{120,8... | collective-permute-start | bytes 884744 | tf_op jit(solution)/shard_map/ppermute | solution.py:770
  59.1 0.7 collective-permute-start.2
  59.8 0.7 collective-permute-start.1
  60.5 0.7 collective-permute-start
  61.4 0.8 collective-permute-start.16
  62.2 3.6 %collective-permute-done.3.refs_4_.refs_12_ = f32[64,1152]{1,0:T(8,128)S(1)} collective-permute-done((f32[64,1152]{1,0:T(8,128)S(1)}, f32[64,1152]{1,0:T(8,128)S(1)}, u32[]{:S(2)}, u32[]{:S(2)}) %collective-permute-start.3) | collective-permute-done | bytes 294944 | tf_op jit(solution)/shard_map/ppermute | solution.py:770
  65.9 1.4 copy-done.2
  67.6 0.8 collective-permute-start.17
  69.1 0.7 collective-permute-start.21
  69.8 0.7 collective-permute-start.20
  70.5 0.7 collective-permute-start.19
  71.1 1.3 collective-permute-start.18
  72.7 34.3 %collective-permute-done.18.refs_7_ = f32[64,512]{1,0:T(8,128)S(1)} collective-permute-done((f32[64,512]{1,0:T(8,128)S(1)}, f32[64,512]{1,0:T(8,128)S(1)}, u32[]{:S(2)}, u32[]{:S(2)}) %collective-permute-start.18) | collective-permute-done | bytes 131104 | tf_op jit(solution)/shard_map/ppermute | solution.py:774
  107.6 0.7 collective-permute-start.22
  108.3 0.7 collective-permute-start.23
  108.9 0.7 collective-permute-start.24
  109.8 0.7 collective-permute-start.26
  110.5 2.7 %early.1 = (f32[2,64,512]{2,1,0:T(8,128)}, f32[6,64,512]{2,1,0:T(8,128)S(1)}, bf16[2,576,192]{2,1,0:T(8,128)(2,1)S(1)}) custom-call(f32[64,1152]{1,0:T(8,128)S(1)} %copy-done.1, f32[64,1152]{1,0:T(8,128)S(1)} %copy-done.4, f32[64,512]{1,0:T(8,128)S(1)} %bitcast.9, f32[64,512]{1,0:T(8,128)S(1)} %get-tuple-element.118.refs_3_, ...), custom_call_target="tpu_custom_call" | custom-call | tf_op jit(solution)/shard_map/early/pallas_call | solution.py:655
  113.2 0.8 back_0.1
  114.0 0.7 collective-permute-start.27
  114.7 0.7 collective-permute-start.28
  115.4 0.7 collective-permute-start.29
  116.1 1.3 collective-permute-start.30
  117.4 0.7 collective-permute-start.31
  119.4 21.9 %collective-permute-done.30.refs_6_ = f32[64,512]{1,0:T(8,128)S(1)} collective-permute-done((f32[64,512]{1,0:T(8,128)S(1)}, f32[64,512]{1,0:T(8,128)S(1)}, u32[]{:S(2)}, u32[]{:S(2)}) %collective-permute-start.30) | collective-permute-done | bytes 131104 | tf_op jit(solution)/shard_map/ppermute | solution.py:774
  141.3 2.7 %late.1 = (f32[2,64,512]{2,1,0:T(8,128)}, f32[64,640]{1,0:T(8,128)S(1)}, f32[64,640]{1,0:T(8,128)S(1)}) custom-call(f32[6,64,512]{2,1,0:T(8,128)S(1)} %get-tuple-element.166.refs_0_, bf16[2,576,192]{2,1,0:T(8,128)(2,1)S(1)} %get-tuple-element.167.refs_1_, f32[64,512]{1,0:T(8,128)S(1)} %get-tuple-element.177.refs_2_, ...), custom_call_target="tpu_custom_call" | custom-call | tf_op jit(solution)/shard_map/late/pallas_call | solution.py:704
  144.1 5.9 %collective-permute-start.34 = (f32[64,640]{1,0:T(8,128)S(1)}, f32[64,640]{1,0:T(8,128)S(1)}, u32[]{:S(2)}, u32[]{:S(2)}) collective-permute-start(f32[64,640]{1,0:T(8,128)S(1)} %get-tuple-element.187), channel_id=1, source_target_pairs={{0,1},{1,0},{2,3},{3,2},{4,5},{5,4},{6,7},{7,6},{8,9},{9,8},{10,11... | collective-permute-start | bytes 491528 | tf_op jit(solution)/shard_map/ppermute | solution.py:826
  150.0 1.0 collective-permute-done.34
  151.0 1.4 collective-permute-start.35
  152.4 4.1 %collective-permute-done.35 = f32[64,640]{1,0:T(8,128)S(1)} collective-permute-done((f32[64,640]{1,0:T(8,128)S(1)}, f32[64,640]{1,0:T(8,128)S(1)}, u32[]{:S(2)}, u32[]{:S(2)}) %collective-permute-start.35) | collective-permute-done | bytes 163872 | tf_op jit(solution)/shard_map/ppermute | solution.py:828
  156.6 2.8 %collective-permute-start.36 = (f32[64,640]{1,0:T(8,128)S(1)}, f32[64,640]{1,0:T(8,128)S(1)}, u32[]{:S(2)}, u32[]{:S(2)}) collective-permute-start(f32[64,640]{1,0:T(8,128)S(1)} %add.10), channel_id=1, source_target_pairs={{0,6},{1,7},{2,4},{3,5},{4,2},{5,3},{6,0},{7,1},{8,14},{9,15},{10,... | collective-permute-start | bytes 491528 | tf_op jit(solution)/shard_map/ppermute | solution.py:828
  159.4 3.1 %collective-permute-done.36 = f32[64,640]{1,0:T(8,128)S(1)} collective-permute-done((f32[64,640]{1,0:T(8,128)S(1)}, f32[64,640]{1,0:T(8,128)S(1)}, u32[]{:S(2)}, u32[]{:S(2)}) %collective-permute-start.36) | collective-permute-done | bytes 163872 | tf_op jit(solution)/shard_map/ppermute | solution.py:828
  162.5 2.1 %collective-permute-start.37 = (f32[64,640]{1,0:T(8,128)S(1)}, f32[64,640]{1,0:T(8,128)S(1)}, u32[]{:S(2)}, u32[]{:S(2)}) collective-permute-start(f32[64,640]{1,0:T(8,128)S(1)} %add.11.mine_ref), channel_id=1, source_target_pairs={{0,1},{1,0},{2,3},{3,2},{4,5},{5,4},{6,7},{7,6},{8,9},{9,8},{10,11... | collective-permute-start | bytes 491528 | tf_op jit(solution)/shard_map/ppermute | solution.py:829
  164.6 1.0 collective-permute-done.37.other_ref
  165.7 0.8 finish.1
  (57 shorter events, 5.6 us)
Async XLA Ops:
  3.7 14.3 %collective-permute-start.13 = (f32[64,1152]{1,0:T(8,128)}, f32[64,1152]{1,0:T(8,128)S(1)}, u32[]{:S(2)}, u32[]{:S(2)}) collective-permute-start(f32[64,1152]{1,0:T(8,128)} %get-tuple-element.100.refs_0_), channel_id=1, source_target_pairs={{16,24},{25,33},{18,26},{27,35},{20,28},{29,37},{22,30},{31,39},{8... | collective-permute-start | bytes 884744 | tf_op jit(solution)/shard_map/ppermute | solution.py:770
  4.3 14.3 %collective-permute-start.12 = (f32[64,1152]{1,0:T(8,128)}, f32[64,1152]{1,0:T(8,128)S(1)}, u32[]{:S(2)}, u32[]{:S(2)}) collective-permute-start(f32[64,1152]{1,0:T(8,128)} %get-tuple-element.100.refs_0_), channel_id=1, source_target_pairs={{8,24},{17,33},{10,26},{19,35},{12,28},{21,37},{14,30},{23,39},{72... | collective-permute-start | bytes 884744 | tf_op jit(solution)/shard_map/ppermute | solution.py:770
  5.0 14.3 %collective-permute-start.11 = (f32[64,1152]{1,0:T(8,128)}, f32[64,1152]{1,0:T(8,128)S(1)}, u32[]{:S(2)}, u32[]{:S(2)}) collective-permute-start(f32[64,1152]{1,0:T(8,128)} %get-tuple-element.100.refs_0_), channel_id=1, source_target_pairs={{0,24},{9,33},{2,26},{11,35},{4,28},{13,37},{6,30},{15,39},{64,88}... | collective-permute-start | bytes 884744 | tf_op jit(solution)/shard_map/ppermute | solution.py:770
  5.7 15.9 %collective-permute-start.10 = (f32[64,1152]{1,0:T(8,128)}, f32[64,1152]{1,0:T(8,128)S(1)}, u32[]{:S(2)}, u32[]{:S(2)}) collective-permute-start(f32[64,1152]{1,0:T(8,128)} %get-tuple-element.100.refs_0_), channel_id=1, source_target_pairs={{56,24},{1,33},{58,26},{3,35},{60,28},{5,37},{62,30},{7,39},{120,8... | collective-permute-start | bytes 884744 | tf_op jit(solution)/shard_map/ppermute | solution.py:770
  17.2 5.1 %collective-permute-start.9 = (f32[64,1152]{1,0:T(8,128)}, f32[64,1152]{1,0:T(8,128)S(1)}, u32[]{:S(2)}, u32[]{:S(2)}) collective-permute-start(f32[64,1152]{1,0:T(8,128)} %get-tuple-element.100.refs_0_), channel_id=1, source_target_pairs={{48,24},{57,33},{50,26},{59,35},{52,28},{61,37},{54,30},{63,39},{1... | collective-permute-start | bytes 884744 | tf_op jit(solution)/shard_map/ppermute | solution.py:770
  17.9 4.4 %collective-permute-start.8 = (f32[64,1152]{1,0:T(8,128)}, f32[64,1152]{1,0:T(8,128)S(1)}, u32[]{:S(2)}, u32[]{:S(2)}) collective-permute-start(f32[64,1152]{1,0:T(8,128)} %get-tuple-element.100.refs_0_), channel_id=1, source_target_pairs={{40,24},{49,33},{42,26},{51,35},{44,28},{53,37},{46,30},{55,39},{1... | collective-permute-start | bytes 884744 | tf_op jit(solution)/shard_map/ppermute | solution.py:770
  18.6 3.7 %collective-permute-start.7 = (f32[64,1152]{1,0:T(8,128)}, f32[64,1152]{1,0:T(8,128)S(1)}, u32[]{:S(2)}, u32[]{:S(2)}) collective-permute-start(f32[64,1152]{1,0:T(8,128)} %get-tuple-element.100.refs_0_), channel_id=1, source_target_pairs={{32,24},{41,33},{34,26},{43,35},{36,28},{45,37},{38,30},{47,39},{9... | collective-permute-start | bytes 884744 | tf_op jit(solution)/shard_map/ppermute | solution.py:770
  19.3 39.8 %collective-permute-start.6 = (f32[64,1152]{1,0:T(8,128)}, f32[64,1152]{1,0:T(8,128)S(1)}, u32[]{:S(2)}, u32[]{:S(2)}) collective-permute-start(f32[64,1152]{1,0:T(8,128)} %get-tuple-element.98.refs_0_.refs_8_.refs_1_), channel_id=1, source_target_pairs={{16,24},{25,33},{18,26},{27,35},{20,28},{29,37},{22,30},{31,39},{8... | collective-permute-start | bytes 884744 | tf_op jit(solution)/shard_map/ppermute | solution.py:770
  21.7 38.2 %collective-permute-start.5 = (f32[64,1152]{1,0:T(8,128)}, f32[64,1152]{1,0:T(8,128)S(1)}, u32[]{:S(2)}, u32[]{:S(2)}) collective-permute-start(f32[64,1152]{1,0:T(8,128)} %get-tuple-element.98.refs_0_.refs_8_.refs_1_), channel_id=1, source_target_pairs={{8,24},{17,33},{10,26},{19,35},{12,28},{21,37},{14,30},{23,39},{72... | collective-permute-start | bytes 884744 | tf_op jit(solution)/shard_map/ppermute | solution.py:770
  22.4 1.0 copy-start
  23.5 0.8 collective-permute-start.14
  24.3 1.0 copy-start.4
  24.5 36.0 %collective-permute-start.15 = (f32[64,512]{1,0:T(8,128)S(1)}, f32[64,512]{1,0:T(8,128)S(1)}, u32[]{:S(2)}, u32[]{:S(2)}) collective-permute-start(f32[64,512]{1,0:T(8,128)S(1)} %get-tuple-element.103), channel_id=1, source_target_pairs={{88,152},{97,161},{90,154},{99,163},{92,156},{101,165},{94,158},{1... | collective-permute-start | bytes 393224 | tf_op jit(solution)/shard_map/ppermute | solution.py:780
  25.3 36.1 %collective-permute-start.4 = (f32[64,1152]{1,0:T(8,128)S(1)}, f32[64,1152]{1,0:T(8,128)S(1)}, u32[]{:S(2)}, u32[]{:S(2)}) collective-permute-start(f32[64,1152]{1,0:T(8,128)S(1)} %copy-done.4), channel_id=1, source_target_pairs={{0,24},{9,33},{2,26},{11,35},{4,28},{13,37},{6,30},{15,39},{64,88}... | collective-permute-start | bytes 884744 | tf_op jit(solution)/shard_map/ppermute | solution.py:770
  26.0 39.8 %collective-permute-start.3 = (f32[64,1152]{1,0:T(8,128)S(1)}, f32[64,1152]{1,0:T(8,128)S(1)}, u32[]{:S(2)}, u32[]{:S(2)}) collective-permute-start(f32[64,1152]{1,0:T(8,128)S(1)} %copy-done.4), channel_id=1, source_target_pairs={{56,24},{1,33},{58,26},{3,35},{60,28},{5,37},{62,30},{7,39},{120,8... | collective-permute-start | bytes 884744 | tf_op jit(solution)/shard_map/ppermute | solution.py:770
  59.1 6.7 %collective-permute-start.2 = (f32[64,1152]{1,0:T(8,128)S(1)}, f32[64,1152]{1,0:T(8,128)S(1)}, u32[]{:S(2)}, u32[]{:S(2)}) collective-permute-start(f32[64,1152]{1,0:T(8,128)S(1)} %copy-done.4), channel_id=1, source_target_pairs={{48,24},{57,33},{50,26},{59,35},{52,28},{61,37},{54,30},{63,39},{1... | collective-permute-start | bytes 884744 | tf_op jit(solution)/shard_map/ppermute | solution.py:770
  59.8 6.0 %collective-permute-start.1 = (f32[64,1152]{1,0:T(8,128)S(1)}, f32[64,1152]{1,0:T(8,128)S(1)}, u32[]{:S(2)}, u32[]{:S(2)}) collective-permute-start(f32[64,1152]{1,0:T(8,128)S(1)} %copy-done.4), channel_id=1, source_target_pairs={{40,24},{49,33},{42,26},{51,35},{44,28},{53,37},{46,30},{55,39},{1... | collective-permute-start | bytes 884744 | tf_op jit(solution)/shard_map/ppermute | solution.py:770
  60.5 5.3 %collective-permute-start = (f32[64,1152]{1,0:T(8,128)S(1)}, f32[64,1152]{1,0:T(8,128)S(1)}, u32[]{:S(2)}, u32[]{:S(2)}) collective-permute-start(f32[64,1152]{1,0:T(8,128)S(1)} %copy-done.4), channel_id=1, source_target_pairs={{32,24},{41,33},{34,26},{43,35},{36,28},{45,37},{38,30},{47,39},{9... | collective-permute-start | bytes 884744 | tf_op jit(solution)/shard_map/ppermute | solution.py:770
  61.4 6.0 %copy-start.1 = (f32[64,1152]{1,0:T(8,128)S(1)}, f32[64,1152]{1,0:T(8,128)}, u32[]{:S(2)}) copy-start(f32[64,1152]{1,0:T(8,128)} %get-tuple-element.100.refs_0_) | copy-start | bytes 884740
  61.4 5.9 %collective-permute-start.16 = (f32[64,512]{1,0:T(8,128)S(1)}, f32[64,512]{1,0:T(8,128)S(1)}, u32[]{:S(2)}, u32[]{:S(2)}) collective-permute-start(f32[64,512]{1,0:T(8,128)S(1)} %get-tuple-element.109), channel_id=1, source_target_pairs={{152,216},{161,225},{154,218},{163,227},{156,220},{165,229},{158,2... | collective-permute-start | bytes 393224 | tf_op jit(solution)/shard_map/ppermute | solution.py:780
  65.9 1.4 copy-start.2
  67.3 1.7 %copy-start.3 = (bf16[8,576,192]{2,1,0:T(8,128)(2,1)S(1)}, bf16[8,576,192]{2,1,0:T(8,128)(2,1)}, u32[]{:S(2)}) copy-start(bf16[8,576,192]{2,1,0:T(8,128)(2,1)} %copy-done.2) | copy-start | bytes 5308420
  67.6 4.8 %collective-permute-start.17 = (f32[64,512]{1,0:T(8,128)S(1)}, f32[64,512]{1,0:T(8,128)S(1)}, u32[]{:S(2)}, u32[]{:S(2)}) collective-permute-start(f32[64,512]{1,0:T(8,128)S(1)} %get-tuple-element.119), channel_id=1, source_target_pairs={{216,152},{225,161},{218,154},{227,163},{220,156},{229,165},{222,1... | collective-permute-start | bytes 393224 | tf_op jit(solution)/shard_map/ppermute | solution.py:780
  69.1 3.5 %collective-permute-start.21 = (f32[64,512]{1,0:T(8,128)S(1)}, f32[64,512]{1,0:T(8,128)S(1)}, u32[]{:S(2)}, u32[]{:S(2)}) collective-permute-start(f32[64,512]{1,0:T(8,128)S(1)} %get-tuple-element.143), channel_id=1, source_target_pairs={{24,8},{33,17},{26,10},{35,19},{28,12},{37,21},{30,14},{39,23},{88... | collective-permute-start | bytes 393224 | tf_op jit(solution)/shard_map/ppermute | solution.py:774
  69.8 2.9 %collective-permute-start.20 = (f32[64,512]{1,0:T(8,128)S(1)}, f32[64,512]{1,0:T(8,128)S(1)}, u32[]{:S(2)}, u32[]{:S(2)}) collective-permute-start(f32[64,512]{1,0:T(8,128)S(1)} %get-tuple-element.141), channel_id=1, source_target_pairs={{24,48},{33,57},{26,50},{35,59},{28,52},{37,61},{30,54},{39,63},{8... | collective-permute-start | bytes 393224 | tf_op jit(solution)/shard_map/ppermute | solution.py:774
  70.5 2.2 %collective-permute-start.19 = (f32[64,512]{1,0:T(8,128)S(1)}, f32[64,512]{1,0:T(8,128)S(1)}, u32[]{:S(2)}, u32[]{:S(2)}) collective-permute-start(f32[64,512]{1,0:T(8,128)S(1)} %get-tuple-element.139), channel_id=1, source_target_pairs={{24,0},{33,9},{26,2},{35,11},{28,4},{37,13},{30,6},{39,15},{88,64}... | collective-permute-start | bytes 393224 | tf_op jit(solution)/shard_map/ppermute | solution.py:774
  71.1 35.8 %collective-permute-start.18 = (f32[64,512]{1,0:T(8,128)S(1)}, f32[64,512]{1,0:T(8,128)S(1)}, u32[]{:S(2)}, u32[]{:S(2)}) collective-permute-start(f32[64,512]{1,0:T(8,128)S(1)} %get-tuple-element.137), channel_id=1, source_target_pairs={{24,56},{33,1},{26,58},{35,3},{28,60},{37,5},{30,62},{39,7},{88,12... | collective-permute-start | bytes 393224 | tf_op jit(solution)/shard_map/ppermute | solution.py:774
  106.9 2.7 %collective-permute-start.25 = (f32[64,512]{1,0:T(8,128)S(1)}, f32[64,512]{1,0:T(8,128)S(1)}, u32[]{:S(2)}, u32[]{:S(2)}) collective-permute-start(f32[64,512]{1,0:T(8,128)S(1)} %get-tuple-element.144), channel_id=1, source_target_pairs={{152,88},{161,97},{154,90},{163,99},{156,92},{165,101},{158,94},{1... | collective-permute-start | bytes 393224 | tf_op jit(solution)/shard_map/ppermute | solution.py:780
  107.6 2.9 %collective-permute-start.22 = (f32[64,512]{1,0:T(8,128)S(1)}, f32[64,512]{1,0:T(8,128)S(1)}, u32[]{:S(2)}, u32[]{:S(2)}) collective-permute-start(f32[64,512]{1,0:T(8,128)S(1)} %get-tuple-element.146), channel_id=1, source_target_pairs={{24,32},{33,41},{26,34},{35,43},{28,36},{37,45},{30,38},{39,47},{8... | collective-permute-start | bytes 393224 | tf_op jit(solution)/shard_map/ppermute | solution.py:774
  108.3 2.2 %collective-permute-start.23 = (f32[64,512]{1,0:T(8,128)S(1)}, f32[64,512]{1,0:T(8,128)S(1)}, u32[]{:S(2)}, u32[]{:S(2)}) collective-permute-start(f32[64,512]{1,0:T(8,128)S(1)} %get-tuple-element.148), channel_id=1, source_target_pairs={{24,40},{33,49},{26,42},{35,51},{28,44},{37,53},{30,46},{39,55},{8... | collective-permute-start | bytes 393224 | tf_op jit(solution)/shard_map/ppermute | solution.py:774
  108.9 1.6 collective-permute-start.24
  109.6 0.9 copy-start.5
  109.8 3.4 %collective-permute-start.26 = (f32[64,512]{1,0:T(8,128)S(1)}, f32[64,512]{1,0:T(8,128)S(1)}, u32[]{:S(2)}, u32[]{:S(2)}) collective-permute-start(f32[64,512]{1,0:T(8,128)S(1)} %get-tuple-element.164), channel_id=1, source_target_pairs={{88,24},{97,33},{90,26},{99,35},{92,28},{101,37},{94,30},{103,39}} | collective-permute-start | bytes 393224 | tf_op jit(solution)/shard_map/ppermute | solution.py:780
  114.0 4.0 %collective-permute-start.27 = (f32[64,512]{1,0:T(8,128)S(1)}, f32[64,512]{1,0:T(8,128)S(1)}, u32[]{:S(2)}, u32[]{:S(2)}) collective-permute-start(f32[64,512]{1,0:T(8,128)S(1)} %get-tuple-element.178), channel_id=1, source_target_pairs={{24,32},{33,41},{26,34},{35,43},{28,36},{37,45},{30,38},{39,47},{8... | collective-permute-start | bytes 393224 | tf_op jit(solution)/shard_map/ppermute | solution.py:774
  114.7 4.0 %collective-permute-start.28 = (f32[64,512]{1,0:T(8,128)S(1)}, f32[64,512]{1,0:T(8,128)S(1)}, u32[]{:S(2)}, u32[]{:S(2)}) collective-permute-start(f32[64,512]{1,0:T(8,128)S(1)} %get-tuple-element.179), channel_id=1, source_target_pairs={{24,40},{33,49},{26,42},{35,51},{28,44},{37,53},{30,46},{39,55},{8... | collective-permute-start | bytes 393224 | tf_op jit(solution)/shard_map/ppermute | solution.py:774
  115.4 4.0 %collective-permute-start.29 = (f32[64,512]{1,0:T(8,128)S(1)}, f32[64,512]{1,0:T(8,128)S(1)}, u32[]{:S(2)}, u32[]{:S(2)}) collective-permute-start(f32[64,512]{1,0:T(8,128)S(1)} %get-tuple-element.180), channel_id=1, source_target_pairs={{24,48},{33,57},{26,50},{35,59},{28,52},{37,61},{30,54},{39,63},{8... | collective-permute-start | bytes 393224 | tf_op jit(solution)/shard_map/ppermute | solution.py:774
  116.1 25.2 %collective-permute-start.30 = (f32[64,512]{1,0:T(8,128)S(1)}, f32[64,512]{1,0:T(8,128)S(1)}, u32[]{:S(2)}, u32[]{:S(2)}) collective-permute-start(f32[64,512]{1,0:T(8,128)S(1)} %get-tuple-element.181), channel_id=1, source_target_pairs={{24,56},{33,1},{26,58},{35,3},{28,60},{37,5},{30,62},{39,7},{88,12... | collective-permute-start | bytes 393224 | tf_op jit(solution)/shard_map/ppermute | solution.py:774
  117.4 23.9 %collective-permute-start.31 = (f32[64,512]{1,0:T(8,128)S(1)}, f32[64,512]{1,0:T(8,128)S(1)}, u32[]{:S(2)}, u32[]{:S(2)}) collective-permute-start(f32[64,512]{1,0:T(8,128)S(1)} %get-tuple-element.182), channel_id=1, source_target_pairs={{24,0},{33,9},{26,2},{35,11},{28,4},{37,13},{30,6},{39,15},{88,64}... | collective-permute-start | bytes 393224 | tf_op jit(solution)/shard_map/ppermute | solution.py:774
  118.1 23.3 %collective-permute-start.32 = (f32[64,512]{1,0:T(8,128)S(1)}, f32[64,512]{1,0:T(8,128)S(1)}, u32[]{:S(2)}, u32[]{:S(2)}) collective-permute-start(f32[64,512]{1,0:T(8,128)S(1)} %get-tuple-element.183), channel_id=1, source_target_pairs={{24,8},{33,17},{26,10},{35,19},{28,12},{37,21},{30,14},{39,23},{88... | collective-permute-start | bytes 393224 | tf_op jit(solution)/shard_map/ppermute | solution.py:774
  118.8 22.6 %collective-permute-start.33 = (f32[64,512]{1,0:T(8,128)S(1)}, f32[64,512]{1,0:T(8,128)S(1)}, u32[]{:S(2)}, u32[]{:S(2)}) collective-permute-start(f32[64,512]{1,0:T(8,128)S(1)} %get-tuple-element.184), channel_id=1, source_target_pairs={{24,16},{33,25},{26,18},{35,27},{28,20},{37,29},{30,22},{39,31},{8... | collective-permute-start | bytes 393224 | tf_op jit(solution)/shard_map/ppermute | solution.py:774
  144.1 6.9 %collective-permute-start.34 = (f32[64,640]{1,0:T(8,128)S(1)}, f32[64,640]{1,0:T(8,128)S(1)}, u32[]{:S(2)}, u32[]{:S(2)}) collective-permute-start(f32[64,640]{1,0:T(8,128)S(1)} %get-tuple-element.187), channel_id=1, source_target_pairs={{0,1},{1,0},{2,3},{3,2},{4,5},{5,4},{6,7},{7,6},{8,9},{9,8},{10,11... | collective-permute-start | bytes 491528 | tf_op jit(solution)/shard_map/ppermute | solution.py:826
  151.0 5.5 %collective-permute-start.35 = (f32[64,640]{1,0:T(8,128)S(1)}, f32[64,640]{1,0:T(8,128)S(1)}, u32[]{:S(2)}, u32[]{:S(2)}) collective-permute-start(f32[64,640]{1,0:T(8,128)S(1)} %add.9), channel_id=1, source_target_pairs={{0,2},{1,3},{2,0},{3,1},{4,6},{5,7},{6,4},{7,5},{8,10},{9,11},{10,... | collective-permute-start | bytes 491528 | tf_op jit(solution)/shard_map/ppermute | solution.py:828
  156.6 5.9 %collective-permute-start.36 = (f32[64,640]{1,0:T(8,128)S(1)}, f32[64,640]{1,0:T(8,128)S(1)}, u32[]{:S(2)}, u32[]{:S(2)}) collective-permute-start(f32[64,640]{1,0:T(8,128)S(1)} %add.10), channel_id=1, source_target_pairs={{0,6},{1,7},{2,4},{3,5},{4,2},{5,3},{6,0},{7,1},{8,14},{9,15},{10,... | collective-permute-start | bytes 491528 | tf_op jit(solution)/shard_map/ppermute | solution.py:828
  162.5 3.2 %collective-permute-start.37 = (f32[64,640]{1,0:T(8,128)S(1)}, f32[64,640]{1,0:T(8,128)S(1)}, u32[]{:S(2)}, u32[]{:S(2)}) collective-permute-start(f32[64,640]{1,0:T(8,128)S(1)} %add.11.mine_ref), channel_id=1, source_target_pairs={{0,1},{1,0},{2,3},{3,2},{4,5},{5,4},{6,7},{7,6},{8,9},{9,8},{10,11... | collective-permute-start | bytes 491528 | tf_op jit(solution)/shard_map/ppermute | solution.py:829

commit v5 on v4

--- a/solution.py
+++ b/solution.py
@@ -137,7 +137,7 @@
 def place():
     layer, image = lax.axis_index("layer"), lax.axis_index("dp")
     core = image % 2
-    return layer // RING, layer % RING, RING // 2 - 1 + core, core
+    return layer // RING, layer % RING, 2 + 3 * core, core
 
 
 def start_all(copies):
@@ -548,29 +548,20 @@
 
     @pl.when((ring == stage) & (spot == lead))
     def _():
-        def copies(i):
-            return [
-                pltpu.make_async_copy(half(source, i), half(target, i), sems.at[n, i])
-                for n, (source, target) in enumerate(
-                    [(behind_ref, behind)] + [(part_refs[p], parts.at[p]) for p in range(3)]
-                )
-            ]
-
-        start_all(copies(1) + copies(0))
-        wait_all(copies(1))
+        copies = [pltpu.make_async_copy(part_refs[i], parts.at[i], sems.at[i]) for i in range(3)]
+        copies.append(pltpu.make_async_copy(behind_ref, behind, sems.at[3]))
+        wait_all(start_all(copies))
 
         def step(k, mu):
             j = RING - 1 - k
             mus[j] = mu
             return back_step(behind[j], mu, parts[0, j], parts[1, j], parts[2, j])
 
-        end = lax.fori_loop(0, HALF, step, mu_ref[...], unroll=2)
-        wait_all(copies(0))
         if stage == 0:
-            end = lax.fori_loop(HALF, RING - 1, step, end)
+            end = lax.fori_loop(0, RING - 1, step, mu_ref[...])
             mus[0] = end
         else:
-            end = lax.fori_loop(HALF, RING, step, end, unroll=2)
+            end = lax.fori_loop(0, RING, step, mu_ref[...], unroll=2)
         outs[RING][...] = end
         wait_all(
             start_all(
@@ -594,7 +585,7 @@
             vmem(field(3, RING)),
             vmem(lhs_shape(RING)),
             vmem(field(RING)),
-            pltpu.SemaphoreType.DMA((4, 2)),
+            pltpu.SemaphoreType.DMA((4,)),
             pltpu.SemaphoreType.DMA((RING,)),
         ],
         input_output_aliases=aliases,
@@ -750,6 +741,7 @@
 
 NEAR = (1, 7, 2, 6, 3, 5, 4)
 FAR = NEAR[::-1]
+EARLY = FAR[:3]
 
 
 def body(coarse_guess, adjoint_guess, weights, biases):
@@ -761,7 +753,7 @@
         return (RING * x + z % RING) * images + d
 
     def lead(d):
-        return RING // 2 - 1 + d % 2
+        return 2 + 3 * (d % 2)
 
     everyone = [(x, d) for x in range(groups) for d in range(images)]
 
@@ -790,6 +782,11 @@
     for k in NEAR:
         twos[k] = gather(two, k)
     for stage in range(1, last):
+        if stage == 1:
+            got = tie(v, *[twos[k] for k in EARLY])
+            v = got[0]
+            for k, value in zip(EARLY, got[1:]):
+                twos[k] = value
         vt, end = chain(stage, ones, ahead0, v, vt)
         v = hop(end, stage, stage + 1)
     ahead1, behind1 = prepare(twos, "prepare2")

time: 167 us -> 155 us (0.928)
  starting transfers between devices: 79.9 us -> 59.9 us
  waiting for transfers between devices: 70.7 us -> 78.9 us
    ppermute x14, starting transfers between devices: 52.8 us -> 28.7 us  [gather(): return lax.ppermute(value, AXES, pairs)]
    ppermute x14, waiting for transfers between devices: 56.2 us -> 69.5 us  [scatter(): return lax.ppermute(value, AXES, pairs)]
    ppermute x14, waiting for transfers between devices: 5.25 us -> 0.04 us  [gather(): return lax.ppermute(value, AXES, pairs)]
    ppermute x1, starting transfers between devices: 5.92 us -> 9.93 us  [body(): mine = mine + lax.ppermute(other, 'dp', [(i, i ^ 1) for i in range(images)])]
  transfers between devices with their start and end apart: 38 -> 38, of which waited for: 8 -> 6; matrix products, arithmetic and copies ran while one was open for 0% -> 0% of each run, Pallas kernels for 2% -> 2%
where the time goes in v5:
time: 155 us; the launch traced here: 154 us
  waiting for transfers between devices  78.9 us (51%)
  starting transfers between devices  59.9 us (39%)
  Pallas kernels  11.3 us (7%)
  local copies, waits for them, and re-layouts  3.1 us (2%)
    ppermute x14, waiting for transfers between devices, scatter(): return lax.ppermute(value, AXES, pairs)  69.5 us
    ppermute x14, starting transfers between devices, gather(): return lax.ppermute(value, AXES, pairs)  28.7 us
    ppermute x14, starting transfers between devices, scatter(): return lax.ppermute(value, AXES, pairs)  10.6 us
    ppermute x1, starting transfers between devices, body(): mine = mine + lax.ppermute(other, 'dp', [(i, i ^ 1) for i in range(images)])  9.93 us
    ppermute x2, waiting for transfers between devices, body(): lax.ppermute(mine, 'dp', [(i, i ^ flip) for i in range(images)])  7.22 us
    ppermute x6, starting transfers between devices, hop(): return lax.ppermute(value, AXES, pairs)  4.27 us
    ppermute x2, starting transfers between devices, body(): lax.ppermute(mine, 'dp', [(i, i ^ flip) for i in range(images)])  4.21 us
  transfers between devices with their start and end apart: 38, of which 6 were waited for; matrix products, arithmetic and copies ran while one was open for 0% of the time, Pallas kernels for 2%

profile of v5, /device:TPU:1, one launch (start us, length us, event | category | flops | bytes accessed | tf_op | source)
XLA Modules:
  0.0 154.5 jit_solution(8135914580601558857)
XLA Ops:
  0.6 3.0 %relax.1 = (f32[64,1152]{1,0:T(8,128)}, f32[64,1152]{1,0:T(8,128)}) custom-call(f32[64,512]{1,0:T(8,128)} %bitcast.8, f32[64,512]{1,0:T(8,128)} %bitcast.10, f32[2,64,576]{2,1,0:T(8,128)} %w_hbm.1, f32[2,64]{1,0:T(2,128)} %b_hbm.1), custom_call_target="tpu_custom_call" | custom-call | tf_op jit(solution)/shard_map/relax/pallas_call | solution.py:195
  3.7 0.7 collective-permute-start.8
  4.3 0.7 collective-permute-start.7
  5.0 0.7 collective-permute-start.6
  5.7 0.7 collective-permute-start.5
  6.4 11.7 %collective-permute-start.4 = (f32[64,1152]{1,0:T(8,128)}, f32[64,1152]{1,0:T(8,128)S(1)}, u32[]{:S(2)}, u32[]{:S(2)}) collective-permute-start(f32[64,1152]{1,0:T(8,128)} %get-tuple-element.107.refs_0_), channel_id=1, source_target_pairs={{40,16},{1,41},{42,18},{3,43},{44,20},{5,45},{46,22},{7,47},{104,8... | collective-permute-start | bytes 884744 | tf_op jit(solution)/shard_map/ppermute | solution.py:762
  18.1 0.7 collective-permute-start.3
  18.8 0.7 collective-permute-start.2
  19.5 8.9 %collective-permute-start.12 = (f32[64,1152]{1,0:T(8,128)}, f32[64,1152]{1,0:T(8,128)S(1)}, u32[]{:S(2)}, u32[]{:S(2)}) collective-permute-start(f32[64,1152]{1,0:T(8,128)} %get-tuple-element.102.refs_0_.refs_8_.refs_1_), channel_id=1, source_target_pairs={{40,16},{1,41},{42,18},{3,43},{44,20},{5,45},{46,22},{7,47},{104,8... | collective-permute-start | bytes 884744 | tf_op jit(solution)/shard_map/ppermute | solution.py:762
  28.4 0.7 collective-permute-start.11
  29.1 0.7 collective-permute-start.10
  29.9 1.0 copy-done
  31.0 0.7 collective-permute-start.9
  32.5 0.7 collective-permute-start.13
  33.2 0.7 collective-permute-start.1
  33.9 0.7 collective-permute-start
  34.8 0.7 collective-permute-start.15
  35.7 0.8 collective-permute-start.16
  36.7 1.4 copy-done.2
  38.3 0.8 collective-permute-start.17
  39.8 0.7 collective-permute-start.21
  40.5 1.3 collective-permute-start.20
  41.8 0.7 collective-permute-start.19
  42.5 0.7 collective-permute-start.18
  43.3 39.6 %collective-permute-done.20.refs_6_ = f32[64,512]{1,0:T(8,128)S(1)} collective-permute-done((f32[64,512]{1,0:T(8,128)S(1)}, f32[64,512]{1,0:T(8,128)S(1)}, u32[]{:S(2)}, u32[]{:S(2)}) %collective-permute-start.20) | collective-permute-done | bytes 131104 | tf_op jit(solution)/shard_map/ppermute | solution.py:766
  83.7 0.7 collective-permute-start.22
  84.3 0.7 collective-permute-start.23
  85.0 0.7 collective-permute-start.24
  85.8 0.7 collective-permute-start.26
  86.6 2.6 %early.1 = (f32[2,64,512]{2,1,0:T(8,128)}, f32[6,64,512]{2,1,0:T(8,128)S(1)}, bf16[2,576,192]{2,1,0:T(8,128)(2,1)S(1)}) custom-call(f32[64,1152]{1,0:T(8,128)S(1)} %copy-done.1, f32[64,1152]{1,0:T(8,128)S(1)} %copy-done.4, f32[64,512]{1,0:T(8,128)S(1)} %bitcast.9, f32[64,512]{1,0:T(8,128)S(1)} %get-tuple-element.126.refs_3_, ...), custom_call_target="tpu_custom_call" | custom-call | tf_op jit(solution)/shard_map/early/pallas_call | solution.py:646
  89.2 0.8 back_0.1
  90.0 0.7 collective-permute-start.27
  90.7 0.7 collective-permute-start.28
  91.4 1.3 collective-permute-start.29
  92.7 0.7 collective-permute-start.30
  93.4 0.7 collective-permute-start.31
  94.8 0.7 collective-permute-start.33
  95.4 29.9 %collective-permute-done.29.refs_5_ = f32[64,512]{1,0:T(8,128)S(1)} collective-permute-done((f32[64,512]{1,0:T(8,128)S(1)}, f32[64,512]{1,0:T(8,128)S(1)}, u32[]{:S(2)}, u32[]{:S(2)}) %collective-permute-start.29) | collective-permute-done | bytes 131104 | tf_op jit(solution)/shard_map/ppermute | solution.py:766
  125.3 2.7 %late.1 = (f32[2,64,512]{2,1,0:T(8,128)}, f32[64,640]{1,0:T(8,128)S(1)}, f32[64,640]{1,0:T(8,128)S(1)}) custom-call(f32[6,64,512]{2,1,0:T(8,128)S(1)} %get-tuple-element.174.refs_0_, bf16[2,576,192]{2,1,0:T(8,128)(2,1)S(1)} %get-tuple-element.175.refs_1_, f32[64,512]{1,0:T(8,128)S(1)} %get-tuple-element.185.refs_2_, ...), custom_call_target="tpu_custom_call" | custom-call | tf_op jit(solution)/shard_map/late/pallas_call | solution.py:695
  128.0 9.9 %collective-permute-start.34 = (f32[64,640]{1,0:T(8,128)S(1)}, f32[64,640]{1,0:T(8,128)S(1)}, u32[]{:S(2)}, u32[]{:S(2)}) collective-permute-start(f32[64,640]{1,0:T(8,128)S(1)} %get-tuple-element.195), channel_id=1, source_target_pairs={{0,1},{1,0},{2,3},{3,2},{4,5},{5,4},{6,7},{7,6},{8,9},{9,8},{10,11... | collective-permute-start | bytes 491528 | tf_op jit(solution)/shard_map/ppermute | solution.py:823
  138.0 1.0 collective-permute-done.34
  139.0 1.4 collective-permute-start.35
  140.4 4.1 %collective-permute-done.35 = f32[64,640]{1,0:T(8,128)S(1)} collective-permute-done((f32[64,640]{1,0:T(8,128)S(1)}, f32[64,640]{1,0:T(8,128)S(1)}, u32[]{:S(2)}, u32[]{:S(2)}) %collective-permute-start.35) | collective-permute-done | bytes 163872 | tf_op jit(solution)/shard_map/ppermute | solution.py:825
  144.6 2.8 %collective-permute-start.36 = (f32[64,640]{1,0:T(8,128)S(1)}, f32[64,640]{1,0:T(8,128)S(1)}, u32[]{:S(2)}, u32[]{:S(2)}) collective-permute-start(f32[64,640]{1,0:T(8,128)S(1)} %add.10), channel_id=1, source_target_pairs={{0,6},{1,7},{2,4},{3,5},{4,2},{5,3},{6,0},{7,1},{8,14},{9,15},{10,... | collective-permute-start | bytes 491528 | tf_op jit(solution)/shard_map/ppermute | solution.py:825
  147.4 3.1 %collective-permute-done.36 = f32[64,640]{1,0:T(8,128)S(1)} collective-permute-done((f32[64,640]{1,0:T(8,128)S(1)}, f32[64,640]{1,0:T(8,128)S(1)}, u32[]{:S(2)}, u32[]{:S(2)}) %collective-permute-start.36) | collective-permute-done | bytes 163872 | tf_op jit(solution)/shard_map/ppermute | solution.py:825
  150.5 2.1 %collective-permute-start.37 = (f32[64,640]{1,0:T(8,128)S(1)}, f32[64,640]{1,0:T(8,128)S(1)}, u32[]{:S(2)}, u32[]{:S(2)}) collective-permute-start(f32[64,640]{1,0:T(8,128)S(1)} %add.11.mine_ref), channel_id=1, source_target_pairs={{0,1},{1,0},{2,3},{3,2},{4,5},{5,4},{6,7},{7,6},{8,9},{9,8},{10,11... | collective-permute-start | bytes 491528 | tf_op jit(solution)/shard_map/ppermute | solution.py:826
  152.6 1.0 collective-permute-done.37.other_ref
  153.7 0.8 finish.1
  (57 shorter events, 4.2 us)
Async XLA Ops:
  3.7 14.4 %collective-permute-start.8 = (f32[64,1152]{1,0:T(8,128)}, f32[64,1152]{1,0:T(8,128)S(1)}, u32[]{:S(2)}, u32[]{:S(2)}) collective-permute-start(f32[64,1152]{1,0:T(8,128)} %get-tuple-element.107.refs_0_), channel_id=1, source_target_pairs={{8,16},{33,41},{10,18},{35,43},{12,20},{37,45},{14,22},{39,47},{72... | collective-permute-start | bytes 884744 | tf_op jit(solution)/shard_map/ppermute | solution.py:762
  4.3 14.4 %collective-permute-start.7 = (f32[64,1152]{1,0:T(8,128)}, f32[64,1152]{1,0:T(8,128)S(1)}, u32[]{:S(2)}, u32[]{:S(2)}) collective-permute-start(f32[64,1152]{1,0:T(8,128)} %get-tuple-element.107.refs_0_), channel_id=1, source_target_pairs={{0,16},{25,41},{2,18},{27,43},{4,20},{29,45},{6,22},{31,47},{64,80... | collective-permute-start | bytes 884744 | tf_op jit(solution)/shard_map/ppermute | solution.py:762
  5.0 14.4 %collective-permute-start.6 = (f32[64,1152]{1,0:T(8,128)}, f32[64,1152]{1,0:T(8,128)S(1)}, u32[]{:S(2)}, u32[]{:S(2)}) collective-permute-start(f32[64,1152]{1,0:T(8,128)} %get-tuple-element.107.refs_0_), channel_id=1, source_target_pairs={{56,16},{17,41},{58,18},{19,43},{60,20},{21,45},{62,22},{23,47},{1... | collective-permute-start | bytes 884744 | tf_op jit(solution)/shard_map/ppermute | solution.py:762
  5.7 22.7 %collective-permute-start.5 = (f32[64,1152]{1,0:T(8,128)}, f32[64,1152]{1,0:T(8,128)S(1)}, u32[]{:S(2)}, u32[]{:S(2)}) collective-permute-start(f32[64,1152]{1,0:T(8,128)} %get-tuple-element.107.refs_0_), channel_id=1, source_target_pairs={{48,16},{9,41},{50,18},{11,43},{52,20},{13,45},{54,22},{15,47},{11... | collective-permute-start | bytes 884744 | tf_op jit(solution)/shard_map/ppermute | solution.py:762
  6.4 22.7 %collective-permute-start.4 = (f32[64,1152]{1,0:T(8,128)}, f32[64,1152]{1,0:T(8,128)S(1)}, u32[]{:S(2)}, u32[]{:S(2)}) collective-permute-start(f32[64,1152]{1,0:T(8,128)} %get-tuple-element.107.refs_0_), channel_id=1, source_target_pairs={{40,16},{1,41},{42,18},{3,43},{44,20},{5,45},{46,22},{7,47},{104,8... | collective-permute-start | bytes 884744 | tf_op jit(solution)/shard_map/ppermute | solution.py:762
  18.1 11.7 %collective-permute-start.3 = (f32[64,1152]{1,0:T(8,128)}, f32[64,1152]{1,0:T(8,128)S(1)}, u32[]{:S(2)}, u32[]{:S(2)}) collective-permute-start(f32[64,1152]{1,0:T(8,128)} %get-tuple-element.107.refs_0_), channel_id=1, source_target_pairs={{32,16},{57,41},{34,18},{59,43},{36,20},{61,45},{38,22},{63,47},{9... | collective-permute-start | bytes 884744 | tf_op jit(solution)/shard_map/ppermute | solution.py:762
  18.8 11.0 %collective-permute-start.2 = (f32[64,1152]{1,0:T(8,128)}, f32[64,1152]{1,0:T(8,128)S(1)}, u32[]{:S(2)}, u32[]{:S(2)}) collective-permute-start(f32[64,1152]{1,0:T(8,128)} %get-tuple-element.107.refs_0_), channel_id=1, source_target_pairs={{24,16},{49,41},{26,18},{51,43},{28,20},{53,45},{30,22},{55,47},{8... | collective-permute-start | bytes 884744 | tf_op jit(solution)/shard_map/ppermute | solution.py:762
  19.5 13.0 %collective-permute-start.12 = (f32[64,1152]{1,0:T(8,128)}, f32[64,1152]{1,0:T(8,128)S(1)}, u32[]{:S(2)}, u32[]{:S(2)}) collective-permute-start(f32[64,1152]{1,0:T(8,128)} %get-tuple-element.102.refs_0_.refs_8_.refs_1_), channel_id=1, source_target_pairs={{40,16},{1,41},{42,18},{3,43},{44,20},{5,45},{46,22},{7,47},{104,8... | collective-permute-start | bytes 884744 | tf_op jit(solution)/shard_map/ppermute | solution.py:762
  28.4 4.7 %collective-permute-start.11 = (f32[64,1152]{1,0:T(8,128)}, f32[64,1152]{1,0:T(8,128)S(1)}, u32[]{:S(2)}, u32[]{:S(2)}) collective-permute-start(f32[64,1152]{1,0:T(8,128)} %get-tuple-element.102.refs_0_.refs_8_.refs_1_), channel_id=1, source_target_pairs={{56,16},{17,41},{58,18},{19,43},{60,20},{21,45},{62,22},{23,47},{1... | collective-permute-start | bytes 884744 | tf_op jit(solution)/shard_map/ppermute | solution.py:762
  29.1 4.7 %collective-permute-start.10 = (f32[64,1152]{1,0:T(8,128)}, f32[64,1152]{1,0:T(8,128)S(1)}, u32[]{:S(2)}, u32[]{:S(2)}) collective-permute-start(f32[64,1152]{1,0:T(8,128)} %get-tuple-element.102.refs_0_.refs_8_.refs_1_), channel_id=1, source_target_pairs={{48,16},{9,41},{50,18},{11,43},{52,20},{13,45},{54,22},{15,47},{11... | collective-permute-start | bytes 884744 | tf_op jit(solution)/shard_map/ppermute | solution.py:762
  29.8 1.0 copy-start
  30.8 1.0 copy-start.4
  31.0 3.7 %collective-permute-start.9 = (f32[64,512]{1,0:T(8,128)S(1)}, f32[64,512]{1,0:T(8,128)S(1)}, u32[]{:S(2)}, u32[]{:S(2)}) collective-permute-start(f32[64,512]{1,0:T(8,128)S(1)} %get-tuple-element.103), channel_id=1, source_target_pairs={{16,80},{41,105},{18,82},{43,107},{20,84},{45,109},{22,86},{47,111}} | collective-permute-start | bytes 393224 | tf_op jit(solution)/shard_map/ppermute | solution.py:772
  31.8 4.7 %collective-permute-start.14 = (f32[64,1152]{1,0:T(8,128)S(1)}, f32[64,1152]{1,0:T(8,128)S(1)}, u32[]{:S(2)}, u32[]{:S(2)}) collective-permute-start(f32[64,1152]{1,0:T(8,128)S(1)} %copy-done.4), channel_id=1, source_target_pairs={{8,16},{33,41},{10,18},{35,43},{12,20},{37,45},{14,22},{39,47},{72... | collective-permute-start | bytes 884744 | tf_op jit(solution)/shard_map/ppermute | solution.py:762
  32.5 4.1 %collective-permute-start.13 = (f32[64,1152]{1,0:T(8,128)S(1)}, f32[64,1152]{1,0:T(8,128)S(1)}, u32[]{:S(2)}, u32[]{:S(2)}) collective-permute-start(f32[64,1152]{1,0:T(8,128)S(1)} %copy-done.4), channel_id=1, source_target_pairs={{0,16},{25,41},{2,18},{27,43},{4,20},{29,45},{6,22},{31,47},{64,80... | collective-permute-start | bytes 884744 | tf_op jit(solution)/shard_map/ppermute | solution.py:762
  33.2 3.4 %collective-permute-start.1 = (f32[64,1152]{1,0:T(8,128)S(1)}, f32[64,1152]{1,0:T(8,128)S(1)}, u32[]{:S(2)}, u32[]{:S(2)}) collective-permute-start(f32[64,1152]{1,0:T(8,128)S(1)} %copy-done.4), channel_id=1, source_target_pairs={{32,16},{57,41},{34,18},{59,43},{36,20},{61,45},{38,22},{63,47},{9... | collective-permute-start | bytes 884744 | tf_op jit(solution)/shard_map/ppermute | solution.py:762
  33.9 2.7 %collective-permute-start = (f32[64,1152]{1,0:T(8,128)S(1)}, f32[64,1152]{1,0:T(8,128)S(1)}, u32[]{:S(2)}, u32[]{:S(2)}) collective-permute-start(f32[64,1152]{1,0:T(8,128)S(1)} %copy-done.4), channel_id=1, source_target_pairs={{24,16},{49,41},{26,18},{51,43},{28,20},{53,45},{30,22},{55,47},{8... | collective-permute-start | bytes 884744 | tf_op jit(solution)/shard_map/ppermute | solution.py:762
  34.8 0.7 collective-permute-start.15
  35.7 2.4 %copy-start.1 = (f32[64,1152]{1,0:T(8,128)S(1)}, f32[64,1152]{1,0:T(8,128)}, u32[]{:S(2)}) copy-start(f32[64,1152]{1,0:T(8,128)} %get-tuple-element.107.refs_0_) | copy-start | bytes 884740
  35.7 2.4 %collective-permute-start.16 = (f32[64,512]{1,0:T(8,128)S(1)}, f32[64,512]{1,0:T(8,128)S(1)}, u32[]{:S(2)}, u32[]{:S(2)}) collective-permute-start(f32[64,512]{1,0:T(8,128)S(1)} %get-tuple-element.117), channel_id=1, source_target_pairs={{144,208},{169,233},{146,210},{171,235},{148,212},{173,237},{150,2... | collective-permute-start | bytes 393224 | tf_op jit(solution)/shard_map/ppermute | solution.py:772
  36.7 1.4 copy-start.2
  38.1 1.7 %copy-start.3 = (bf16[8,576,192]{2,1,0:T(8,128)(2,1)S(1)}, bf16[8,576,192]{2,1,0:T(8,128)(2,1)}, u32[]{:S(2)}) copy-start(bf16[8,576,192]{2,1,0:T(8,128)(2,1)} %copy-done.2) | copy-start | bytes 5308420
  38.3 4.8 %collective-permute-start.17 = (f32[64,512]{1,0:T(8,128)S(1)}, f32[64,512]{1,0:T(8,128)S(1)}, u32[]{:S(2)}, u32[]{:S(2)}) collective-permute-start(f32[64,512]{1,0:T(8,128)S(1)} %get-tuple-element.127), channel_id=1, source_target_pairs={{208,144},{233,169},{210,146},{235,171},{212,148},{237,173},{214,1... | collective-permute-start | bytes 393224 | tf_op jit(solution)/shard_map/ppermute | solution.py:772
  39.8 3.5 %collective-permute-start.21 = (f32[64,512]{1,0:T(8,128)S(1)}, f32[64,512]{1,0:T(8,128)S(1)}, u32[]{:S(2)}, u32[]{:S(2)}) collective-permute-start(f32[64,512]{1,0:T(8,128)S(1)} %get-tuple-element.151), channel_id=1, source_target_pairs={{16,0},{41,25},{18,2},{43,27},{20,4},{45,29},{22,6},{47,31},{80,64... | collective-permute-start | bytes 393224 | tf_op jit(solution)/shard_map/ppermute | solution.py:766
  40.5 42.5 %collective-permute-start.20 = (f32[64,512]{1,0:T(8,128)S(1)}, f32[64,512]{1,0:T(8,128)S(1)}, u32[]{:S(2)}, u32[]{:S(2)}) collective-permute-start(f32[64,512]{1,0:T(8,128)S(1)} %get-tuple-element.149), channel_id=1, source_target_pairs={{16,40},{41,1},{18,42},{43,3},{20,44},{45,5},{22,46},{47,7},{80,10... | collective-permute-start | bytes 393224 | tf_op jit(solution)/shard_map/ppermute | solution.py:766
  41.8 41.2 %collective-permute-start.19 = (f32[64,512]{1,0:T(8,128)S(1)}, f32[64,512]{1,0:T(8,128)S(1)}, u32[]{:S(2)}, u32[]{:S(2)}) collective-permute-start(f32[64,512]{1,0:T(8,128)S(1)} %get-tuple-element.147), channel_id=1, source_target_pairs={{16,56},{41,17},{18,58},{43,19},{20,60},{45,21},{22,62},{47,23},{8... | collective-permute-start | bytes 393224 | tf_op jit(solution)/shard_map/ppermute | solution.py:766
  42.5 40.5 %collective-permute-start.18 = (f32[64,512]{1,0:T(8,128)S(1)}, f32[64,512]{1,0:T(8,128)S(1)}, u32[]{:S(2)}, u32[]{:S(2)}) collective-permute-start(f32[64,512]{1,0:T(8,128)S(1)} %get-tuple-element.145), channel_id=1, source_target_pairs={{16,48},{41,9},{18,50},{43,11},{20,52},{45,13},{22,54},{47,15},{80... | collective-permute-start | bytes 393224 | tf_op jit(solution)/shard_map/ppermute | solution.py:766
  83.0 2.7 %collective-permute-start.25 = (f32[64,512]{1,0:T(8,128)S(1)}, f32[64,512]{1,0:T(8,128)S(1)}, u32[]{:S(2)}, u32[]{:S(2)}) collective-permute-start(f32[64,512]{1,0:T(8,128)S(1)} %get-tuple-element.152), channel_id=1, source_target_pairs={{144,80},{169,105},{146,82},{171,107},{148,84},{173,109},{150,86},... | collective-permute-start | bytes 393224 | tf_op jit(solution)/shard_map/ppermute | solution.py:772
  83.7 2.9 %collective-permute-start.22 = (f32[64,512]{1,0:T(8,128)S(1)}, f32[64,512]{1,0:T(8,128)S(1)}, u32[]{:S(2)}, u32[]{:S(2)}) collective-permute-start(f32[64,512]{1,0:T(8,128)S(1)} %get-tuple-element.154), channel_id=1, source_target_pairs={{16,24},{41,49},{18,26},{43,51},{20,28},{45,53},{22,30},{47,55},{8... | collective-permute-start | bytes 393224 | tf_op jit(solution)/shard_map/ppermute | solution.py:766
  84.3 2.2 %collective-permute-start.23 = (f32[64,512]{1,0:T(8,128)S(1)}, f32[64,512]{1,0:T(8,128)S(1)}, u32[]{:S(2)}, u32[]{:S(2)}) collective-permute-start(f32[64,512]{1,0:T(8,128)S(1)} %get-tuple-element.156), channel_id=1, source_target_pairs={{16,32},{41,57},{18,34},{43,59},{20,36},{45,61},{22,38},{47,63},{8... | collective-permute-start | bytes 393224 | tf_op jit(solution)/shard_map/ppermute | solution.py:766
  85.0 1.5 collective-permute-start.24
  85.7 0.9 copy-start.5
  85.8 3.4 %collective-permute-start.26 = (f32[64,512]{1,0:T(8,128)S(1)}, f32[64,512]{1,0:T(8,128)S(1)}, u32[]{:S(2)}, u32[]{:S(2)}) collective-permute-start(f32[64,512]{1,0:T(8,128)S(1)} %get-tuple-element.172), channel_id=1, source_target_pairs={{80,16},{105,41},{82,18},{107,43},{84,20},{109,45},{86,22},{111,47}} | collective-permute-start | bytes 393224 | tf_op jit(solution)/shard_map/ppermute | solution.py:772
  90.0 4.0 %collective-permute-start.27 = (f32[64,512]{1,0:T(8,128)S(1)}, f32[64,512]{1,0:T(8,128)S(1)}, u32[]{:S(2)}, u32[]{:S(2)}) collective-permute-start(f32[64,512]{1,0:T(8,128)S(1)} %get-tuple-element.186), channel_id=1, source_target_pairs={{16,24},{41,49},{18,26},{43,51},{20,28},{45,53},{22,30},{47,55},{8... | collective-permute-start | bytes 393224 | tf_op jit(solution)/shard_map/ppermute | solution.py:766
  90.7 4.0 %collective-permute-start.28 = (f32[64,512]{1,0:T(8,128)S(1)}, f32[64,512]{1,0:T(8,128)S(1)}, u32[]{:S(2)}, u32[]{:S(2)}) collective-permute-start(f32[64,512]{1,0:T(8,128)S(1)} %get-tuple-element.187), channel_id=1, source_target_pairs={{16,32},{41,57},{18,34},{43,59},{20,36},{45,61},{22,38},{47,63},{8... | collective-permute-start | bytes 393224 | tf_op jit(solution)/shard_map/ppermute | solution.py:766
  91.4 33.9 %collective-permute-start.29 = (f32[64,512]{1,0:T(8,128)S(1)}, f32[64,512]{1,0:T(8,128)S(1)}, u32[]{:S(2)}, u32[]{:S(2)}) collective-permute-start(f32[64,512]{1,0:T(8,128)S(1)} %get-tuple-element.188), channel_id=1, source_target_pairs={{16,40},{41,1},{18,42},{43,3},{20,44},{45,5},{22,46},{47,7},{80,10... | collective-permute-start | bytes 393224 | tf_op jit(solution)/shard_map/ppermute | solution.py:766
  92.7 32.6 %collective-permute-start.30 = (f32[64,512]{1,0:T(8,128)S(1)}, f32[64,512]{1,0:T(8,128)S(1)}, u32[]{:S(2)}, u32[]{:S(2)}) collective-permute-start(f32[64,512]{1,0:T(8,128)S(1)} %get-tuple-element.189), channel_id=1, source_target_pairs={{16,48},{41,9},{18,50},{43,11},{20,52},{45,13},{22,54},{47,15},{80... | collective-permute-start | bytes 393224 | tf_op jit(solution)/shard_map/ppermute | solution.py:766
  93.4 31.9 %collective-permute-start.31 = (f32[64,512]{1,0:T(8,128)S(1)}, f32[64,512]{1,0:T(8,128)S(1)}, u32[]{:S(2)}, u32[]{:S(2)}) collective-permute-start(f32[64,512]{1,0:T(8,128)S(1)} %get-tuple-element.190), channel_id=1, source_target_pairs={{16,56},{41,17},{18,58},{43,19},{20,60},{45,21},{22,62},{47,23},{8... | collective-permute-start | bytes 393224 | tf_op jit(solution)/shard_map/ppermute | solution.py:766
  94.1 31.2 %collective-permute-start.32 = (f32[64,512]{1,0:T(8,128)S(1)}, f32[64,512]{1,0:T(8,128)S(1)}, u32[]{:S(2)}, u32[]{:S(2)}) collective-permute-start(f32[64,512]{1,0:T(8,128)S(1)} %get-tuple-element.191), channel_id=1, source_target_pairs={{16,0},{41,25},{18,2},{43,27},{20,4},{45,29},{22,6},{47,31},{80,64... | collective-permute-start | bytes 393224 | tf_op jit(solution)/shard_map/ppermute | solution.py:766
  94.8 30.6 %collective-permute-start.33 = (f32[64,512]{1,0:T(8,128)S(1)}, f32[64,512]{1,0:T(8,128)S(1)}, u32[]{:S(2)}, u32[]{:S(2)}) collective-permute-start(f32[64,512]{1,0:T(8,128)S(1)} %get-tuple-element.192), channel_id=1, source_target_pairs={{16,8},{41,33},{18,10},{43,35},{20,12},{45,37},{22,14},{47,39},{80... | collective-permute-start | bytes 393224 | tf_op jit(solution)/shard_map/ppermute | solution.py:766
  128.0 11.0 %collective-permute-start.34 = (f32[64,640]{1,0:T(8,128)S(1)}, f32[64,640]{1,0:T(8,128)S(1)}, u32[]{:S(2)}, u32[]{:S(2)}) collective-permute-start(f32[64,640]{1,0:T(8,128)S(1)} %get-tuple-element.195), channel_id=1, source_target_pairs={{0,1},{1,0},{2,3},{3,2},{4,5},{5,4},{6,7},{7,6},{8,9},{9,8},{10,11... | collective-permute-start | bytes 491528 | tf_op jit(solution)/shard_map/ppermute | solution.py:823
  139.0 5.5 %collective-permute-start.35 = (f32[64,640]{1,0:T(8,128)S(1)}, f32[64,640]{1,0:T(8,128)S(1)}, u32[]{:S(2)}, u32[]{:S(2)}) collective-permute-start(f32[64,640]{1,0:T(8,128)S(1)} %add.9), channel_id=1, source_target_pairs={{0,2},{1,3},{2,0},{3,1},{4,6},{5,7},{6,4},{7,5},{8,10},{9,11},{10,... | collective-permute-start | bytes 491528 | tf_op jit(solution)/shard_map/ppermute | solution.py:825
  144.6 5.9 %collective-permute-start.36 = (f32[64,640]{1,0:T(8,128)S(1)}, f32[64,640]{1,0:T(8,128)S(1)}, u32[]{:S(2)}, u32[]{:S(2)}) collective-permute-start(f32[64,640]{1,0:T(8,128)S(1)} %add.10), channel_id=1, source_target_pairs={{0,6},{1,7},{2,4},{3,5},{4,2},{5,3},{6,0},{7,1},{8,14},{9,15},{10,... | collective-permute-start | bytes 491528 | tf_op jit(solution)/shard_map/ppermute | solution.py:825
  150.5 3.2 %collective-permute-start.37 = (f32[64,640]{1,0:T(8,128)S(1)}, f32[64,640]{1,0:T(8,128)S(1)}, u32[]{:S(2)}, u32[]{:S(2)}) collective-permute-start(f32[64,640]{1,0:T(8,128)S(1)} %add.11.mine_ref), channel_id=1, source_target_pairs={{0,1},{1,0},{2,3},{3,2},{4,5},{5,4},{6,7},{7,6},{8,9},{9,8},{10,11... | collective-permute-start | bytes 491528 | tf_op jit(solution)/shard_map/ppermute | solution.py:826

commit v6 on v5

--- a/solution.py
+++ b/solution.py
@@ -742,6 +742,7 @@
 NEAR = (1, 7, 2, 6, 3, 5, 4)
 FAR = NEAR[::-1]
 EARLY = FAR[:3]
+PAIRS = ((6, 3), (2, 4), (7, 5), (1, None))
 
 
 def body(coarse_guess, adjoint_guess, weights, biases):
@@ -759,6 +760,18 @@
 
     def gather(value, k):
         pairs = [(device(x, lead(d) + k, d), device(x, lead(d), d)) for x, d in everyone]
+        return lax.ppermute(value, AXES, pairs)
+
+    def gather_pair(value, direct, helped):
+        pairs = [(device(x, lead(d) + direct, d), device(x, lead(d), d)) for x, d in everyone]
+        if helped is not None:
+            pairs += [
+                (device(x, lead(d) + helped, d), device(x, lead(d), d ^ 1)) for x, d in everyone
+            ]
+        return lax.ppermute(value, AXES, pairs)
+
+    def hand_over(value):
+        pairs = [(device(x, lead(d), d ^ 1), device(x, lead(d), d)) for x, d in everyone]
         return lax.ppermute(value, AXES, pairs)
 
     def scatter(value, k):
@@ -774,8 +787,10 @@
     c, a = coarse_guess[0, 0], adjoint_guess[0, 0]
     one, two = relax(c, a, weights, biases)
     ones, twos = [one] + [None] * (RING - 1), [two] + [None] * (RING - 1)
-    for k in NEAR:
-        ones[k] = gather(one, k)
+    for direct, helped in PAIRS:
+        ones[direct] = gather_pair(one, direct, helped)
+        if helped is not None:
+            ones[helped] = hand_over(ones[direct])
     vt, end = first_chain(ones)
     v = hop(end, 0, 1)
     ahead0, behind0 = prepare([tie(end, one)[1]] + ones[1:], "prepare")

time: 155 us -> 151 us (0.974)
  waiting for transfers between devices: 78.9 us -> 73.2 us
    ppermute x14 -> x7, starting transfers between devices: 28.7 us -> 13.6 us  [gather(): return lax.ppermute(value, AXES, pairs)]
    ppermute x0 -> x7, starting transfers between devices: none -> 14.4 us  [the longest x4 12.4 us: gather_pair(): return lax.ppermute(value, AXES, pairs)]
    ppermute x14, waiting for transfers between devices: 69.5 us -> 61.9 us  [scatter(): return lax.ppermute(value, AXES, pairs)]
    ppermute x0 -> x7, waiting for transfers between devices: none -> 1.98 us  [the longest x4 1.97 us: gather_pair(): return lax.ppermute(value, AXES, pairs)]
    ppermute x1, starting transfers between devices: 9.93 us -> 11.6 us  [body(): mine = mine + lax.ppermute(other, 'dp', [(i, i ^ 1) for i in range(images)])]
  transfers between devices with their start and end apart: 38 -> 38, of which waited for: 6 -> 7; matrix products, arithmetic and copies ran while one was open for 0% -> 0% of each run, Pallas kernels for 2% -> 2%
where the time goes in v6:
time: 151 us; the launch traced here: 150 us
  waiting for transfers between devices  73.2 us (48%)
  starting transfers between devices  61 us (40%)
  Pallas kernels  11.3 us (7%)
  local copies, waits for them, and re-layouts  3.1 us (2%)
    ppermute x14, waiting for transfers between devices, scatter(): return lax.ppermute(value, AXES, pairs)  61.9 us
    ppermute x7, starting transfers between devices, gather(): return lax.ppermute(value, AXES, pairs)  13.6 us
    ppermute x4, starting transfers between devices, gather_pair(): return lax.ppermute(value, AXES, pairs)  12.4 us
    ppermute x1, starting transfers between devices, body(): mine = mine + lax.ppermute(other, 'dp', [(i, i ^ 1) for i in range(images)])  11.6 us
    ppermute x14, starting transfers between devices, scatter(): return lax.ppermute(value, AXES, pairs)  10.6 us
    ppermute x2, waiting for transfers between devices, body(): lax.ppermute(mine, 'dp', [(i, i ^ flip) for i in range(images)])  7.21 us
    ppermute x6, starting transfers between devices, hop(): return lax.ppermute(value, AXES, pairs)  4.27 us
    ppermute x2, starting transfers between devices, body(): lax.ppermute(mine, 'dp', [(i, i ^ flip) for i in range(images)])  4.2 us
  transfers between devices with their start and end apart: 38, of which 7 were waited for; matrix products, arithmetic and copies ran while one was open for 0% of the time, Pallas kernels for 2%

profile of v6, /device:TPU:1, one launch (start us, length us, event | category | flops | bytes accessed | tf_op | source)
XLA Modules:
  0.0 149.9 jit_solution(10824156762113711505)
XLA Ops:
  0.6 3.0 %relax.1 = (f32[64,1152]{1,0:T(8,128)}, f32[64,1152]{1,0:T(8,128)}) custom-call(f32[64,512]{1,0:T(8,128)} %bitcast.8, f32[64,512]{1,0:T(8,128)} %bitcast.10, f32[2,64,576]{2,1,0:T(8,128)} %w_hbm.1, f32[2,64]{1,0:T(2,128)} %b_hbm.1), custom_call_target="tpu_custom_call" | custom-call | tf_op jit(solution)/shard_map/relax/pallas_call | solution.py:195
  3.7 0.7 collective-permute-start.7
  4.3 10.4 %collective-permute-start.4 = (f32[64,1152]{1,0:T(8,128)}, f32[64,1152]{1,0:T(8,128)S(1)}, u32[]{:S(2)}, u32[]{:S(2)}) collective-permute-start(f32[64,1152]{1,0:T(8,128)} %get-tuple-element.107.refs_0_), channel_id=1, source_target_pairs={{0,16},{25,41},{2,18},{27,43},{4,20},{29,45},{6,22},{31,47},{64,80... | collective-permute-start | bytes 884744 | tf_op jit(solution)/shard_map/ppermute | solution.py:771
  14.7 0.7 collective-permute-start.3
  15.4 0.7 collective-permute-start.2
  16.1 0.7 collective-permute-start.8
  16.8 2.0 %collective-permute-done.4.refs_6_ = f32[64,1152]{1,0:T(8,128)S(1)} collective-permute-done((f32[64,1152]{1,0:T(8,128)}, f32[64,1152]{1,0:T(8,128)S(1)}, u32[]{:S(2)}, u32[]{:S(2)}) %collective-permute-start.4) | collective-permute-done | bytes 294944 | tf_op jit(solution)/shard_map/ppermute | solution.py:771
  19.5 0.7 collective-permute-start.6
  20.1 9.6 %collective-permute-start.12 = (f32[64,1152]{1,0:T(8,128)}, f32[64,1152]{1,0:T(8,128)S(1)}, u32[]{:S(2)}, u32[]{:S(2)}) collective-permute-start(f32[64,1152]{1,0:T(8,128)} %get-tuple-element.102.refs_0_.refs_8_.refs_1_), channel_id=1, source_target_pairs={{40,16},{1,41},{42,18},{3,43},{44,20},{5,45},{46,22},{7,47},{104,8... | collective-permute-start | bytes 884744 | tf_op jit(solution)/shard_map/ppermute | solution.py:763
  29.7 0.7 collective-permute-start.11
  30.4 0.7 collective-permute-start.10
  31.2 1.0 copy-done
  32.3 0.7 collective-permute-start.9
  33.8 0.7 collective-permute-start.13
  34.5 0.7 collective-permute-start.1
  35.2 0.7 collective-permute-start
  36.1 0.7 collective-permute-start.15
  37.0 0.8 collective-permute-start.16
  38.0 1.4 copy-done.2
  39.6 0.8 collective-permute-start.17
  41.1 0.7 collective-permute-start.21
  41.8 1.3 collective-permute-start.20
  43.1 0.7 collective-permute-start.19
  43.8 0.7 collective-permute-start.18
  44.6 30.8 %collective-permute-done.20.refs_6_ = f32[64,512]{1,0:T(8,128)S(1)} collective-permute-done((f32[64,512]{1,0:T(8,128)S(1)}, f32[64,512]{1,0:T(8,128)S(1)}, u32[]{:S(2)}, u32[]{:S(2)}) %collective-permute-start.20) | collective-permute-done | bytes 131104 | tf_op jit(solution)/shard_map/ppermute | solution.py:779
  76.1 0.7 collective-permute-start.22
  76.8 0.7 collective-permute-start.23
  77.5 0.7 collective-permute-start.24
  78.3 0.7 collective-permute-start.26
  79.1 2.6 %early.1 = (f32[2,64,512]{2,1,0:T(8,128)}, f32[6,64,512]{2,1,0:T(8,128)S(1)}, bf16[2,576,192]{2,1,0:T(8,128)(2,1)S(1)}) custom-call(f32[64,1152]{1,0:T(8,128)S(1)} %copy-done.1, f32[64,1152]{1,0:T(8,128)S(1)} %copy-done.4, f32[64,512]{1,0:T(8,128)S(1)} %bitcast.9, f32[64,512]{1,0:T(8,128)S(1)} %get-tuple-element.126.refs_3_, ...), custom_call_target="tpu_custom_call" | custom-call | tf_op jit(solution)/shard_map/early/pallas_call | solution.py:646
  81.7 0.8 back_0.1
  82.5 0.7 collective-permute-start.27
  83.2 0.7 collective-permute-start.28
  83.9 1.3 collective-permute-start.29
  85.2 0.7 collective-permute-start.30
  85.9 0.7 collective-permute-start.31
  86.5 0.7 collective-permute-start.32
  87.9 31.0 %collective-permute-done.29.refs_5_ = f32[64,512]{1,0:T(8,128)S(1)} collective-permute-done((f32[64,512]{1,0:T(8,128)S(1)}, f32[64,512]{1,0:T(8,128)S(1)}, u32[]{:S(2)}, u32[]{:S(2)}) %collective-permute-start.29) | collective-permute-done | bytes 131104 | tf_op jit(solution)/shard_map/ppermute | solution.py:779
  119.0 2.7 %late.1 = (f32[2,64,512]{2,1,0:T(8,128)}, f32[64,640]{1,0:T(8,128)S(1)}, f32[64,640]{1,0:T(8,128)S(1)}) custom-call(f32[6,64,512]{2,1,0:T(8,128)S(1)} %get-tuple-element.174.refs_0_, bf16[2,576,192]{2,1,0:T(8,128)(2,1)S(1)} %get-tuple-element.175.refs_1_, f32[64,512]{1,0:T(8,128)S(1)} %get-tuple-element.185.refs_2_, ...), custom_call_target="tpu_custom_call" | custom-call | tf_op jit(solution)/shard_map/late/pallas_call | solution.py:695
  121.7 11.6 %collective-permute-start.34 = (f32[64,640]{1,0:T(8,128)S(1)}, f32[64,640]{1,0:T(8,128)S(1)}, u32[]{:S(2)}, u32[]{:S(2)}) collective-permute-start(f32[64,640]{1,0:T(8,128)S(1)} %get-tuple-element.195), channel_id=1, source_target_pairs={{0,1},{1,0},{2,3},{3,2},{4,5},{5,4},{6,7},{7,6},{8,9},{9,8},{10,11... | collective-permute-start | bytes 491528 | tf_op jit(solution)/shard_map/ppermute | solution.py:838
  133.3 1.0 collective-permute-done.34
  134.4 1.4 collective-permute-start.35
  135.8 4.1 %collective-permute-done.35 = f32[64,640]{1,0:T(8,128)S(1)} collective-permute-done((f32[64,640]{1,0:T(8,128)S(1)}, f32[64,640]{1,0:T(8,128)S(1)}, u32[]{:S(2)}, u32[]{:S(2)}) %collective-permute-start.35) | collective-permute-done | bytes 163872 | tf_op jit(solution)/shard_map/ppermute | solution.py:840
  139.9 2.8 %collective-permute-start.36 = (f32[64,640]{1,0:T(8,128)S(1)}, f32[64,640]{1,0:T(8,128)S(1)}, u32[]{:S(2)}, u32[]{:S(2)}) collective-permute-start(f32[64,640]{1,0:T(8,128)S(1)} %add.10), channel_id=1, source_target_pairs={{0,6},{1,7},{2,4},{3,5},{4,2},{5,3},{6,0},{7,1},{8,14},{9,15},{10,... | collective-permute-start | bytes 491528 | tf_op jit(solution)/shard_map/ppermute | solution.py:840
  142.7 3.1 %collective-permute-done.36 = f32[64,640]{1,0:T(8,128)S(1)} collective-permute-done((f32[64,640]{1,0:T(8,128)S(1)}, f32[64,640]{1,0:T(8,128)S(1)}, u32[]{:S(2)}, u32[]{:S(2)}) %collective-permute-start.36) | collective-permute-done | bytes 163872 | tf_op jit(solution)/shard_map/ppermute | solution.py:840
  145.9 2.1 %collective-permute-start.37 = (f32[64,640]{1,0:T(8,128)S(1)}, f32[64,640]{1,0:T(8,128)S(1)}, u32[]{:S(2)}, u32[]{:S(2)}) collective-permute-start(f32[64,640]{1,0:T(8,128)S(1)} %add.11.mine_ref), channel_id=1, source_target_pairs={{0,1},{1,0},{2,3},{3,2},{4,5},{5,4},{6,7},{7,6},{8,9},{9,8},{10,11... | collective-permute-start | bytes 491528 | tf_op jit(solution)/shard_map/ppermute | solution.py:841
  148.0 1.0 collective-permute-done.37.other_ref
  149.0 0.8 finish.1
  (57 shorter events, 4.9 us)
Async XLA Ops:
  3.7 12.5 %collective-permute-start.7 = (f32[64,1152]{1,0:T(8,128)}, f32[64,1152]{1,0:T(8,128)S(1)}, u32[]{:S(2)}, u32[]{:S(2)}) collective-permute-start(f32[64,1152]{1,0:T(8,128)} %get-tuple-element.107.refs_0_), channel_id=1, source_target_pairs={{8,16},{33,41},{10,18},{35,43},{12,20},{37,45},{14,22},{39,47},{72... | collective-permute-start | bytes 884744 | tf_op jit(solution)/shard_map/ppermute | solution.py:771
  4.3 14.4 %collective-permute-start.4 = (f32[64,1152]{1,0:T(8,128)}, f32[64,1152]{1,0:T(8,128)S(1)}, u32[]{:S(2)}, u32[]{:S(2)}) collective-permute-start(f32[64,1152]{1,0:T(8,128)} %get-tuple-element.107.refs_0_), channel_id=1, source_target_pairs={{0,16},{25,41},{2,18},{27,43},{4,20},{29,45},{6,22},{31,47},{64,80... | collective-permute-start | bytes 884744 | tf_op jit(solution)/shard_map/ppermute | solution.py:771
  14.7 4.7 %collective-permute-start.3 = (f32[64,1152]{1,0:T(8,128)}, f32[64,1152]{1,0:T(8,128)S(1)}, u32[]{:S(2)}, u32[]{:S(2)}) collective-permute-start(f32[64,1152]{1,0:T(8,128)} %get-tuple-element.107.refs_0_), channel_id=1, source_target_pairs={{32,16},{57,41},{34,18},{59,43},{36,20},{61,45},{38,22},{63,47},{9... | collective-permute-start | bytes 884744 | tf_op jit(solution)/shard_map/ppermute | solution.py:771
  15.4 14.3 %collective-permute-start.2 = (f32[64,1152]{1,0:T(8,128)}, f32[64,1152]{1,0:T(8,128)S(1)}, u32[]{:S(2)}, u32[]{:S(2)}) collective-permute-start(f32[64,1152]{1,0:T(8,128)} %get-tuple-element.107.refs_0_), channel_id=1, source_target_pairs={{24,16},{49,41},{26,18},{51,43},{28,20},{53,45},{30,22},{55,47},{8... | collective-permute-start | bytes 884744 | tf_op jit(solution)/shard_map/ppermute | solution.py:771
  16.1 14.3 %collective-permute-start.8 = (f32[64,1152]{1,0:T(8,128)S(1)}, f32[64,1152]{1,0:T(8,128)S(1)}, u32[]{:S(2)}, u32[]{:S(2)}) collective-permute-start(f32[64,1152]{1,0:T(8,128)S(1)} %collective-permute-done.7.refs_7_), channel_id=1, source_target_pairs={{17,16},{40,41},{19,18},{42,43},{21,20},{44,45},{23,22},{46,47},{8... | collective-permute-start | bytes 884744 | tf_op jit(solution)/shard_map/ppermute | solution.py:775
  18.8 12.3 %collective-permute-start.5 = (f32[64,1152]{1,0:T(8,128)S(1)}, f32[64,1152]{1,0:T(8,128)S(1)}, u32[]{:S(2)}, u32[]{:S(2)}) collective-permute-start(f32[64,1152]{1,0:T(8,128)S(1)} %collective-permute-done.4.refs_6_), channel_id=1, source_target_pairs={{17,16},{40,41},{19,18},{42,43},{21,20},{44,45},{23,22},{46,47},{8... | collective-permute-start | bytes 884744 | tf_op jit(solution)/shard_map/ppermute | solution.py:775
  19.5 11.7 %collective-permute-start.6 = (f32[64,1152]{1,0:T(8,128)S(1)}, f32[64,1152]{1,0:T(8,128)S(1)}, u32[]{:S(2)}, u32[]{:S(2)}) collective-permute-start(f32[64,1152]{1,0:T(8,128)S(1)} %collective-permute-done.3.refs_2_), channel_id=1, source_target_pairs={{17,16},{40,41},{19,18},{42,43},{21,20},{44,45},{23,22},{46,47},{8... | collective-permute-start | bytes 884744 | tf_op jit(solution)/shard_map/ppermute | solution.py:775
  20.1 13.6 %collective-permute-start.12 = (f32[64,1152]{1,0:T(8,128)}, f32[64,1152]{1,0:T(8,128)S(1)}, u32[]{:S(2)}, u32[]{:S(2)}) collective-permute-start(f32[64,1152]{1,0:T(8,128)} %get-tuple-element.102.refs_0_.refs_8_.refs_1_), channel_id=1, source_target_pairs={{40,16},{1,41},{42,18},{3,43},{44,20},{5,45},{46,22},{7,47},{104,8... | collective-permute-start | bytes 884744 | tf_op jit(solution)/shard_map/ppermute | solution.py:763
  29.7 4.7 %collective-permute-start.11 = (f32[64,1152]{1,0:T(8,128)}, f32[64,1152]{1,0:T(8,128)S(1)}, u32[]{:S(2)}, u32[]{:S(2)}) collective-permute-start(f32[64,1152]{1,0:T(8,128)} %get-tuple-element.102.refs_0_.refs_8_.refs_1_), channel_id=1, source_target_pairs={{56,16},{17,41},{58,18},{19,43},{60,20},{21,45},{62,22},{23,47},{1... | collective-permute-start | bytes 884744 | tf_op jit(solution)/shard_map/ppermute | solution.py:763
  30.4 4.7 %collective-permute-start.10 = (f32[64,1152]{1,0:T(8,128)}, f32[64,1152]{1,0:T(8,128)S(1)}, u32[]{:S(2)}, u32[]{:S(2)}) collective-permute-start(f32[64,1152]{1,0:T(8,128)} %get-tuple-element.102.refs_0_.refs_8_.refs_1_), channel_id=1, source_target_pairs={{48,16},{9,41},{50,18},{11,43},{52,20},{13,45},{54,22},{15,47},{11... | collective-permute-start | bytes 884744 | tf_op jit(solution)/shard_map/ppermute | solution.py:763
  31.1 1.0 copy-start
  32.1 1.0 copy-start.4
  32.3 3.7 %collective-permute-start.9 = (f32[64,512]{1,0:T(8,128)S(1)}, f32[64,512]{1,0:T(8,128)S(1)}, u32[]{:S(2)}, u32[]{:S(2)}) collective-permute-start(f32[64,512]{1,0:T(8,128)S(1)} %get-tuple-element.103), channel_id=1, source_target_pairs={{16,80},{41,105},{18,82},{43,107},{20,84},{45,109},{22,86},{47,111}} | collective-permute-start | bytes 393224 | tf_op jit(solution)/shard_map/ppermute | solution.py:785
  33.1 4.7 %collective-permute-start.14 = (f32[64,1152]{1,0:T(8,128)S(1)}, f32[64,1152]{1,0:T(8,128)S(1)}, u32[]{:S(2)}, u32[]{:S(2)}) collective-permute-start(f32[64,1152]{1,0:T(8,128)S(1)} %copy-done.4), channel_id=1, source_target_pairs={{8,16},{33,41},{10,18},{35,43},{12,20},{37,45},{14,22},{39,47},{72... | collective-permute-start | bytes 884744 | tf_op jit(solution)/shard_map/ppermute | solution.py:763
  33.8 4.1 %collective-permute-start.13 = (f32[64,1152]{1,0:T(8,128)S(1)}, f32[64,1152]{1,0:T(8,128)S(1)}, u32[]{:S(2)}, u32[]{:S(2)}) collective-permute-start(f32[64,1152]{1,0:T(8,128)S(1)} %copy-done.4), channel_id=1, source_target_pairs={{0,16},{25,41},{2,18},{27,43},{4,20},{29,45},{6,22},{31,47},{64,80... | collective-permute-start | bytes 884744 | tf_op jit(solution)/shard_map/ppermute | solution.py:763
  34.5 3.4 %collective-permute-start.1 = (f32[64,1152]{1,0:T(8,128)S(1)}, f32[64,1152]{1,0:T(8,128)S(1)}, u32[]{:S(2)}, u32[]{:S(2)}) collective-permute-start(f32[64,1152]{1,0:T(8,128)S(1)} %copy-done.4), channel_id=1, source_target_pairs={{32,16},{57,41},{34,18},{59,43},{36,20},{61,45},{38,22},{63,47},{9... | collective-permute-start | bytes 884744 | tf_op jit(solution)/shard_map/ppermute | solution.py:763
  35.2 2.7 %collective-permute-start = (f32[64,1152]{1,0:T(8,128)S(1)}, f32[64,1152]{1,0:T(8,128)S(1)}, u32[]{:S(2)}, u32[]{:S(2)}) collective-permute-start(f32[64,1152]{1,0:T(8,128)S(1)} %copy-done.4), channel_id=1, source_target_pairs={{24,16},{49,41},{26,18},{51,43},{28,20},{53,45},{30,22},{55,47},{8... | collective-permute-start | bytes 884744 | tf_op jit(solution)/shard_map/ppermute | solution.py:763
  36.1 0.7 collective-permute-start.15
  37.0 2.4 %copy-start.1 = (f32[64,1152]{1,0:T(8,128)S(1)}, f32[64,1152]{1,0:T(8,128)}, u32[]{:S(2)}) copy-start(f32[64,1152]{1,0:T(8,128)} %get-tuple-element.107.refs_0_) | copy-start | bytes 884740
  37.0 2.4 %collective-permute-start.16 = (f32[64,512]{1,0:T(8,128)S(1)}, f32[64,512]{1,0:T(8,128)S(1)}, u32[]{:S(2)}, u32[]{:S(2)}) collective-permute-start(f32[64,512]{1,0:T(8,128)S(1)} %get-tuple-element.117), channel_id=1, source_target_pairs={{144,208},{169,233},{146,210},{171,235},{148,212},{173,237},{150,2... | collective-permute-start | bytes 393224 | tf_op jit(solution)/shard_map/ppermute | solution.py:785
  38.0 1.4 copy-start.2
  39.4 1.7 %copy-start.3 = (bf16[8,576,192]{2,1,0:T(8,128)(2,1)S(1)}, bf16[8,576,192]{2,1,0:T(8,128)(2,1)}, u32[]{:S(2)}) copy-start(bf16[8,576,192]{2,1,0:T(8,128)(2,1)} %copy-done.2) | copy-start | bytes 5308420
  39.6 4.8 %collective-permute-start.17 = (f32[64,512]{1,0:T(8,128)S(1)}, f32[64,512]{1,0:T(8,128)S(1)}, u32[]{:S(2)}, u32[]{:S(2)}) collective-permute-start(f32[64,512]{1,0:T(8,128)S(1)} %get-tuple-element.127), channel_id=1, source_target_pairs={{208,144},{233,169},{210,146},{235,171},{212,148},{237,173},{214,1... | collective-permute-start | bytes 393224 | tf_op jit(solution)/shard_map/ppermute | solution.py:785
  41.1 3.5 %collective-permute-start.21 = (f32[64,512]{1,0:T(8,128)S(1)}, f32[64,512]{1,0:T(8,128)S(1)}, u32[]{:S(2)}, u32[]{:S(2)}) collective-permute-start(f32[64,512]{1,0:T(8,128)S(1)} %get-tuple-element.151), channel_id=1, source_target_pairs={{16,0},{41,25},{18,2},{43,27},{20,4},{45,29},{22,6},{47,31},{80,64... | collective-permute-start | bytes 393224 | tf_op jit(solution)/shard_map/ppermute | solution.py:779
  41.8 33.6 %collective-permute-start.20 = (f32[64,512]{1,0:T(8,128)S(1)}, f32[64,512]{1,0:T(8,128)S(1)}, u32[]{:S(2)}, u32[]{:S(2)}) collective-permute-start(f32[64,512]{1,0:T(8,128)S(1)} %get-tuple-element.149), channel_id=1, source_target_pairs={{16,40},{41,1},{18,42},{43,3},{20,44},{45,5},{22,46},{47,7},{80,10... | collective-permute-start | bytes 393224 | tf_op jit(solution)/shard_map/ppermute | solution.py:779
  43.1 32.3 %collective-permute-start.19 = (f32[64,512]{1,0:T(8,128)S(1)}, f32[64,512]{1,0:T(8,128)S(1)}, u32[]{:S(2)}, u32[]{:S(2)}) collective-permute-start(f32[64,512]{1,0:T(8,128)S(1)} %get-tuple-element.147), channel_id=1, source_target_pairs={{16,56},{41,17},{18,58},{43,19},{20,60},{45,21},{22,62},{47,23},{8... | collective-permute-start | bytes 393224 | tf_op jit(solution)/shard_map/ppermute | solution.py:779
  43.8 31.7 %collective-permute-start.18 = (f32[64,512]{1,0:T(8,128)S(1)}, f32[64,512]{1,0:T(8,128)S(1)}, u32[]{:S(2)}, u32[]{:S(2)}) collective-permute-start(f32[64,512]{1,0:T(8,128)S(1)} %get-tuple-element.145), channel_id=1, source_target_pairs={{16,48},{41,9},{18,50},{43,11},{20,52},{45,13},{22,54},{47,15},{80... | collective-permute-start | bytes 393224 | tf_op jit(solution)/shard_map/ppermute | solution.py:779
  75.5 2.7 %collective-permute-start.25 = (f32[64,512]{1,0:T(8,128)S(1)}, f32[64,512]{1,0:T(8,128)S(1)}, u32[]{:S(2)}, u32[]{:S(2)}) collective-permute-start(f32[64,512]{1,0:T(8,128)S(1)} %get-tuple-element.152), channel_id=1, source_target_pairs={{144,80},{169,105},{146,82},{171,107},{148,84},{173,109},{150,86},... | collective-permute-start | bytes 393224 | tf_op jit(solution)/shard_map/ppermute | solution.py:785
  76.1 2.9 %collective-permute-start.22 = (f32[64,512]{1,0:T(8,128)S(1)}, f32[64,512]{1,0:T(8,128)S(1)}, u32[]{:S(2)}, u32[]{:S(2)}) collective-permute-start(f32[64,512]{1,0:T(8,128)S(1)} %get-tuple-element.154), channel_id=1, source_target_pairs={{16,24},{41,49},{18,26},{43,51},{20,28},{45,53},{22,30},{47,55},{8... | collective-permute-start | bytes 393224 | tf_op jit(solution)/shard_map/ppermute | solution.py:779
  76.8 2.2 %collective-permute-start.23 = (f32[64,512]{1,0:T(8,128)S(1)}, f32[64,512]{1,0:T(8,128)S(1)}, u32[]{:S(2)}, u32[]{:S(2)}) collective-permute-start(f32[64,512]{1,0:T(8,128)S(1)} %get-tuple-element.156), channel_id=1, source_target_pairs={{16,32},{41,57},{18,34},{43,59},{20,36},{45,61},{22,38},{47,63},{8... | collective-permute-start | bytes 393224 | tf_op jit(solution)/shard_map/ppermute | solution.py:779
  77.5 1.5 %collective-permute-start.24 = (f32[64,512]{1,0:T(8,128)S(1)}, f32[64,512]{1,0:T(8,128)S(1)}, u32[]{:S(2)}, u32[]{:S(2)}) collective-permute-start(f32[64,512]{1,0:T(8,128)S(1)} %get-tuple-element.162), channel_id=1, source_target_pairs={{16,8},{41,33},{18,10},{43,35},{20,12},{45,37},{22,14},{47,39},{80... | collective-permute-start | bytes 393224 | tf_op jit(solution)/shard_map/ppermute | solution.py:779
  78.2 0.9 copy-start.5
  78.3 3.4 %collective-permute-start.26 = (f32[64,512]{1,0:T(8,128)S(1)}, f32[64,512]{1,0:T(8,128)S(1)}, u32[]{:S(2)}, u32[]{:S(2)}) collective-permute-start(f32[64,512]{1,0:T(8,128)S(1)} %get-tuple-element.172), channel_id=1, source_target_pairs={{80,16},{105,41},{82,18},{107,43},{84,20},{109,45},{86,22},{111,47}} | collective-permute-start | bytes 393224 | tf_op jit(solution)/shard_map/ppermute | solution.py:785
  82.5 4.0 %collective-permute-start.27 = (f32[64,512]{1,0:T(8,128)S(1)}, f32[64,512]{1,0:T(8,128)S(1)}, u32[]{:S(2)}, u32[]{:S(2)}) collective-permute-start(f32[64,512]{1,0:T(8,128)S(1)} %get-tuple-element.186), channel_id=1, source_target_pairs={{16,24},{41,49},{18,26},{43,51},{20,28},{45,53},{22,30},{47,55},{8... | collective-permute-start | bytes 393224 | tf_op jit(solution)/shard_map/ppermute | solution.py:779
  83.2 4.0 %collective-permute-start.28 = (f32[64,512]{1,0:T(8,128)S(1)}, f32[64,512]{1,0:T(8,128)S(1)}, u32[]{:S(2)}, u32[]{:S(2)}) collective-permute-start(f32[64,512]{1,0:T(8,128)S(1)} %get-tuple-element.187), channel_id=1, source_target_pairs={{16,32},{41,57},{18,34},{43,59},{20,36},{45,61},{22,38},{47,63},{8... | collective-permute-start | bytes 393224 | tf_op jit(solution)/shard_map/ppermute | solution.py:779
  83.9 35.1 %collective-permute-start.29 = (f32[64,512]{1,0:T(8,128)S(1)}, f32[64,512]{1,0:T(8,128)S(1)}, u32[]{:S(2)}, u32[]{:S(2)}) collective-permute-start(f32[64,512]{1,0:T(8,128)S(1)} %get-tuple-element.188), channel_id=1, source_target_pairs={{16,40},{41,1},{18,42},{43,3},{20,44},{45,5},{22,46},{47,7},{80,10... | collective-permute-start | bytes 393224 | tf_op jit(solution)/shard_map/ppermute | solution.py:779
  85.2 33.8 %collective-permute-start.30 = (f32[64,512]{1,0:T(8,128)S(1)}, f32[64,512]{1,0:T(8,128)S(1)}, u32[]{:S(2)}, u32[]{:S(2)}) collective-permute-start(f32[64,512]{1,0:T(8,128)S(1)} %get-tuple-element.189), channel_id=1, source_target_pairs={{16,48},{41,9},{18,50},{43,11},{20,52},{45,13},{22,54},{47,15},{80... | collective-permute-start | bytes 393224 | tf_op jit(solution)/shard_map/ppermute | solution.py:779
  85.9 33.1 %collective-permute-start.31 = (f32[64,512]{1,0:T(8,128)S(1)}, f32[64,512]{1,0:T(8,128)S(1)}, u32[]{:S(2)}, u32[]{:S(2)}) collective-permute-start(f32[64,512]{1,0:T(8,128)S(1)} %get-tuple-element.190), channel_id=1, source_target_pairs={{16,56},{41,17},{18,58},{43,19},{20,60},{45,21},{22,62},{47,23},{8... | collective-permute-start | bytes 393224 | tf_op jit(solution)/shard_map/ppermute | solution.py:779
  86.5 32.4 %collective-permute-start.32 = (f32[64,512]{1,0:T(8,128)S(1)}, f32[64,512]{1,0:T(8,128)S(1)}, u32[]{:S(2)}, u32[]{:S(2)}) collective-permute-start(f32[64,512]{1,0:T(8,128)S(1)} %get-tuple-element.191), channel_id=1, source_target_pairs={{16,0},{41,25},{18,2},{43,27},{20,4},{45,29},{22,6},{47,31},{80,64... | collective-permute-start | bytes 393224 | tf_op jit(solution)/shard_map/ppermute | solution.py:779
  87.2 31.7 %collective-permute-start.33 = (f32[64,512]{1,0:T(8,128)S(1)}, f32[64,512]{1,0:T(8,128)S(1)}, u32[]{:S(2)}, u32[]{:S(2)}) collective-permute-start(f32[64,512]{1,0:T(8,128)S(1)} %get-tuple-element.192), channel_id=1, source_target_pairs={{16,8},{41,33},{18,10},{43,35},{20,12},{45,37},{22,14},{47,39},{80... | collective-permute-start | bytes 393224 | tf_op jit(solution)/shard_map/ppermute | solution.py:779
  121.7 12.7 %collective-permute-start.34 = (f32[64,640]{1,0:T(8,128)S(1)}, f32[64,640]{1,0:T(8,128)S(1)}, u32[]{:S(2)}, u32[]{:S(2)}) collective-permute-start(f32[64,640]{1,0:T(8,128)S(1)} %get-tuple-element.195), channel_id=1, source_target_pairs={{0,1},{1,0},{2,3},{3,2},{4,5},{5,4},{6,7},{7,6},{8,9},{9,8},{10,11... | collective-permute-start | bytes 491528 | tf_op jit(solution)/shard_map/ppermute | solution.py:838
  134.4 5.5 %collective-permute-start.35 = (f32[64,640]{1,0:T(8,128)S(1)}, f32[64,640]{1,0:T(8,128)S(1)}, u32[]{:S(2)}, u32[]{:S(2)}) collective-permute-start(f32[64,640]{1,0:T(8,128)S(1)} %add.9), channel_id=1, source_target_pairs={{0,2},{1,3},{2,0},{3,1},{4,6},{5,7},{6,4},{7,5},{8,10},{9,11},{10,... | collective-permute-start | bytes 491528 | tf_op jit(solution)/shard_map/ppermute | solution.py:840
  139.9 5.9 %collective-permute-start.36 = (f32[64,640]{1,0:T(8,128)S(1)}, f32[64,640]{1,0:T(8,128)S(1)}, u32[]{:S(2)}, u32[]{:S(2)}) collective-permute-start(f32[64,640]{1,0:T(8,128)S(1)} %add.10), channel_id=1, source_target_pairs={{0,6},{1,7},{2,4},{3,5},{4,2},{5,3},{6,0},{7,1},{8,14},{9,15},{10,... | collective-permute-start | bytes 491528 | tf_op jit(solution)/shard_map/ppermute | solution.py:840
  145.9 3.2 %collective-permute-start.37 = (f32[64,640]{1,0:T(8,128)S(1)}, f32[64,640]{1,0:T(8,128)S(1)}, u32[]{:S(2)}, u32[]{:S(2)}) collective-permute-start(f32[64,640]{1,0:T(8,128)S(1)} %add.11.mine_ref), channel_id=1, source_target_pairs={{0,1},{1,0},{2,3},{3,2},{4,5},{5,4},{6,7},{7,6},{8,9},{9,8},{10,11... | collective-permute-start | bytes 491528 | tf_op jit(solution)/shard_map/ppermute | solution.py:841

commit v7 on v6

--- a/solution.py
+++ b/solution.py
@@ -459,7 +459,7 @@
     lhs_refs, v_ref = refs[2 * RING : 2 * RING + 4], refs[2 * RING + 4]
     v_refs = refs[2 * RING + 5 : 3 * RING + 5]
     mu_refs = refs[3 * RING + 5 : 4 * RING + 5]
-    out_ref, tau, two, vs, mus, lhs, out, sems, lhs_sems = refs[4 * RING + 5 :]
+    out_ref, tau, two, vs, t, mus, lhs, out, sems, lhs_sems = refs[4 * RING + 5 :]
     ring, spot, lead, _ = place()
 
     @pl.when((ring == stage) & (spot == lead))
@@ -476,31 +476,25 @@
         def ahead_step(j, v):
             now = jnp.tanh(conv(lhs[0, j], v, 1) + tau[j][:, BIAS : BIAS + 1])
             vs[j] = v
-            return v + 2 * H * now + tau[j][:, WPAD - CELLS :], now
-
-        def correct(j, v, t0):
+            t[j] = now
+            return v + 2 * H * now + tau[j][:, WPAD - CELLS :]
+
+        def correct(j, carry):
             b1, a = two[j][:, 576:577], two[j][:, WPAD:BLK]
-            got = correction(lhs[2, j], lhs[3, j], v, t0, b1, a)
+            got = correction(lhs[2, j], lhs[3, j], vs[j], t[j], b1, a)
             for i in range(3):
                 out[i, j] = got[i]
-
-        def step(j, carry):
-            v, old_v, old_t = carry
-            new_v, now = ahead_step(j, v)
-            correct(j - 1, old_v, old_t)
-            return new_v, v, now
-
-        start = v_ref[...]
-        v, now = ahead_step(0, start)
-        wait_all(block_copies + matrices[2:])
-        _, v, now = lax.fori_loop(1, RING, step, (v, start, now))
+            return carry
+
+        lax.fori_loop(0, RING, ahead_step, v_ref[...], unroll=2)
         copies = start_all(
             [
                 pltpu.make_async_copy(vs.at[(lead + k) % RING], v_refs[k], sems.at[0, k])
                 for k in range(RING)
             ]
         )
-        correct(RING - 1, v, now)
+        wait_all(block_copies + matrices[2:])
+        lax.fori_loop(0, RING, correct, 0, unroll=2)
         wait_all(matrices[1:2])
 
         def back(k, mu):
@@ -527,6 +521,7 @@
         scratch_shapes=[
             pltpu.VMEM((RING, CH, WPAD), F32),
             pltpu.VMEM((RING, CH, BLK), F32),
+            vmem(field(RING)),
             vmem(field(RING)),
             vmem(field(RING)),
             vmem(lhs_shape(4, RING)),
@@ -741,7 +736,7 @@
 
 NEAR = (1, 7, 2, 6, 3, 5, 4)
 FAR = NEAR[::-1]
-EARLY = FAR[:3]
+EARLY = FAR[:0]
 PAIRS = ((6, 3), (2, 4), (7, 5), (1, None))
 
 
@@ -797,11 +792,6 @@
     for k in NEAR:
         twos[k] = gather(two, k)
     for stage in range(1, last):
-        if stage == 1:
-            got = tie(v, *[twos[k] for k in EARLY])
-            v = got[0]
-            for k, value in zip(EARLY, got[1:]):
-                twos[k] = value
         vt, end = chain(stage, ones, ahead0, v, vt)
         v = hop(end, stage, stage + 1)
     ahead1, behind1 = prepare(twos, "prepare2")

time: 151 us -> 146 us (0.967)
  waiting for transfers between devices: 73.2 us -> 61.4 us
  starting transfers between devices: 61 us -> 67.9 us
    ppermute x14, waiting for transfers between devices: 61.9 us -> 46 us  [scatter(): return lax.ppermute(value, AXES, pairs)]
    ppermute x7, starting transfers between devices: 13.6 us -> 28.2 us  [gather(): return lax.ppermute(value, AXES, pairs)]
    ppermute x1, starting transfers between devices: 11.6 us -> 4.09 us  [body(): mine = mine + lax.ppermute(other, 'dp', [(i, i ^ 1) for i in range(images)])]
    ppermute x7, waiting for transfers between devices: 0.02 us -> 4.09 us  [gather(): return lax.ppermute(value, AXES, pairs)]
  transfers between devices with their start and end apart: 38 -> 38, of which waited for: 7 -> 8; matrix products, arithmetic and copies ran while one was open for 0% -> 0% of each run, Pallas kernels for 2% -> 3%
where the time goes in v7:
time: 146 us; the launch traced here: 145 us
  starting transfers between devices  67.9 us (47%)
  waiting for transfers between devices  61.4 us (42%)
  Pallas kernels  11.3 us (8%)
  local copies, waits for them, and re-layouts  3.12 us (2%)
    ppermute x14, waiting for transfers between devices, scatter(): return lax.ppermute(value, AXES, pairs)  46 us
    ppermute x7, starting transfers between devices, gather(): return lax.ppermute(value, AXES, pairs)  28.2 us
    ppermute x4, starting transfers between devices, gather_pair(): return lax.ppermute(value, AXES, pairs)  12.4 us
    ppermute x14, starting transfers between devices, scatter(): return lax.ppermute(value, AXES, pairs)  10.6 us
    ppermute x2, waiting for transfers between devices, body(): lax.ppermute(mine, 'dp', [(i, i ^ flip) for i in range(images)])  7.24 us
    ppermute x6, starting transfers between devices, hop(): return lax.ppermute(value, AXES, pairs)  4.27 us
    ppermute x2, starting transfers between devices, body(): lax.ppermute(mine, 'dp', [(i, i ^ flip) for i in range(images)])  4.22 us
    ppermute x7, waiting for transfers between devices, gather(): return lax.ppermute(value, AXES, pairs)  4.09 us
  transfers between devices with their start and end apart: 38, of which 8 were waited for; matrix products, arithmetic and copies ran while one was open for 0% of the time, Pallas kernels for 3%

profile of v7, /device:TPU:1, one launch (start us, length us, event | category | flops | bytes accessed | tf_op | source)
XLA Modules:
  0.0 145.0 jit_solution(6809539590419230973)
XLA Ops:
  0.6 3.0 %relax.1 = (f32[64,1152]{1,0:T(8,128)}, f32[64,1152]{1,0:T(8,128)}) custom-call(f32[64,512]{1,0:T(8,128)} %bitcast.8, f32[64,512]{1,0:T(8,128)} %bitcast.10, f32[2,64,576]{2,1,0:T(8,128)} %w_hbm.1, f32[2,64]{1,0:T(2,128)} %b_hbm.1), custom_call_target="tpu_custom_call" | custom-call | tf_op jit(solution)/shard_map/relax/pallas_call | solution.py:195
  3.7 0.7 collective-permute-start.12
  4.3 10.4 %collective-permute-start.9 = (f32[64,1152]{1,0:T(8,128)}, f32[64,1152]{1,0:T(8,128)S(1)}, u32[]{:S(2)}, u32[]{:S(2)}) collective-permute-start(f32[64,1152]{1,0:T(8,128)} %get-tuple-element.100.refs_0_), channel_id=1, source_target_pairs={{0,16},{25,41},{2,18},{27,43},{4,20},{29,45},{6,22},{31,47},{64,80... | collective-permute-start | bytes 884744 | tf_op jit(solution)/shard_map/ppermute | solution.py:766
  14.7 0.7 collective-permute-start.8
  15.4 0.7 collective-permute-start.7
  16.1 0.7 collective-permute-start.13
  16.8 2.0 %collective-permute-done.9.refs_6_ = f32[64,1152]{1,0:T(8,128)S(1)} collective-permute-done((f32[64,1152]{1,0:T(8,128)}, f32[64,1152]{1,0:T(8,128)S(1)}, u32[]{:S(2)}, u32[]{:S(2)}) %collective-permute-start.9) | collective-permute-done | bytes 294944 | tf_op jit(solution)/shard_map/ppermute | solution.py:766
  19.5 0.7 collective-permute-start.11
  20.1 0.7 collective-permute-start.6
  20.8 0.7 collective-permute-start.5
  21.6 1.0 copy-done
  22.7 0.7 collective-permute-start.14
  23.7 0.7 collective-permute-start.15
  25.2 0.7 collective-permute-start.3
  25.9 24.1 %collective-permute-start.2 = (f32[64,1152]{1,0:T(8,128)S(1)}, f32[64,1152]{1,0:T(8,128)S(1)}, u32[]{:S(2)}, u32[]{:S(2)}) collective-permute-start(f32[64,1152]{1,0:T(8,128)S(1)} %copy-done.4), channel_id=1, source_target_pairs={{40,16},{1,41},{42,18},{3,43},{44,20},{5,45},{46,22},{7,47},{104,8... | collective-permute-start | bytes 884744 | tf_op jit(solution)/shard_map/ppermute | solution.py:758
  50.0 0.7 collective-permute-start.1
  50.7 0.7 collective-permute-start
  51.5 0.8 collective-permute-start.16
  52.4 4.1 %collective-permute-done.2.refs_3_.refs_11_ = f32[64,1152]{1,0:T(8,128)S(1)} collective-permute-done((f32[64,1152]{1,0:T(8,128)S(1)}, f32[64,1152]{1,0:T(8,128)S(1)}, u32[]{:S(2)}, u32[]{:S(2)}) %collective-permute-start.2) | collective-permute-done | bytes 294944 | tf_op jit(solution)/shard_map/ppermute | solution.py:758
  56.5 1.4 copy-done.2
  58.2 0.8 collective-permute-start.17
  59.7 0.7 collective-permute-start.21
  60.4 1.3 collective-permute-start.20
  61.7 0.7 collective-permute-start.19
  62.4 0.7 collective-permute-start.18
  63.2 24.8 %collective-permute-done.20.refs_6_ = f32[64,512]{1,0:T(8,128)S(1)} collective-permute-done((f32[64,512]{1,0:T(8,128)S(1)}, f32[64,512]{1,0:T(8,128)S(1)}, u32[]{:S(2)}, u32[]{:S(2)}) %collective-permute-start.20) | collective-permute-done | bytes 131104 | tf_op jit(solution)/shard_map/ppermute | solution.py:774
  88.7 0.7 collective-permute-start.22
  89.4 0.7 collective-permute-start.23
  90.1 0.7 collective-permute-start.24
  90.9 0.7 collective-permute-start.26
  91.7 2.6 %early.1 = (f32[2,64,512]{2,1,0:T(8,128)}, f32[6,64,512]{2,1,0:T(8,128)S(1)}, bf16[2,576,192]{2,1,0:T(8,128)(2,1)S(1)}) custom-call(f32[64,1152]{1,0:T(8,128)S(1)} %copy-done.1, f32[64,1152]{1,0:T(8,128)S(1)} %copy-done.4, f32[64,512]{1,0:T(8,128)S(1)} %bitcast.9, f32[64,512]{1,0:T(8,128)S(1)} %get-tuple-element.118.refs_3_, ...), custom_call_target="tpu_custom_call" | custom-call | tf_op jit(solution)/shard_map/early/pallas_call | solution.py:641
  94.3 0.8 back_0.1
  95.8 0.7 collective-permute-start.28
  96.5 1.3 collective-permute-start.29
  97.8 0.7 collective-permute-start.30
  98.4 0.7 collective-permute-start.31
  99.8 0.7 collective-permute-start.33
  100.5 21.2 %collective-permute-done.29.refs_5_ = f32[64,512]{1,0:T(8,128)S(1)} collective-permute-done((f32[64,512]{1,0:T(8,128)S(1)}, f32[64,512]{1,0:T(8,128)S(1)}, u32[]{:S(2)}, u32[]{:S(2)}) %collective-permute-start.29) | collective-permute-done | bytes 131104 | tf_op jit(solution)/shard_map/ppermute | solution.py:774
  121.7 2.7 %late.1 = (f32[2,64,512]{2,1,0:T(8,128)}, f32[64,640]{1,0:T(8,128)S(1)}, f32[64,640]{1,0:T(8,128)S(1)}) custom-call(f32[6,64,512]{2,1,0:T(8,128)S(1)} %get-tuple-element.166.refs_0_, bf16[2,576,192]{2,1,0:T(8,128)(2,1)S(1)} %get-tuple-element.167.refs_1_, f32[64,512]{1,0:T(8,128)S(1)} %get-tuple-element.177.refs_2_, ...), custom_call_target="tpu_custom_call" | custom-call | tf_op jit(solution)/shard_map/late/pallas_call | solution.py:690
  124.4 4.1 %collective-permute-start.34 = (f32[64,640]{1,0:T(8,128)S(1)}, f32[64,640]{1,0:T(8,128)S(1)}, u32[]{:S(2)}, u32[]{:S(2)}) collective-permute-start(f32[64,640]{1,0:T(8,128)S(1)} %get-tuple-element.187), channel_id=1, source_target_pairs={{0,1},{1,0},{2,3},{3,2},{4,5},{5,4},{6,7},{7,6},{8,9},{9,8},{10,11... | collective-permute-start | bytes 491528 | tf_op jit(solution)/shard_map/ppermute | solution.py:828
  128.5 1.0 collective-permute-done.34
  129.5 1.4 collective-permute-start.35
  130.9 4.1 %collective-permute-done.35 = f32[64,640]{1,0:T(8,128)S(1)} collective-permute-done((f32[64,640]{1,0:T(8,128)S(1)}, f32[64,640]{1,0:T(8,128)S(1)}, u32[]{:S(2)}, u32[]{:S(2)}) %collective-permute-start.35) | collective-permute-done | bytes 163872 | tf_op jit(solution)/shard_map/ppermute | solution.py:830
  135.0 2.8 %collective-permute-start.36 = (f32[64,640]{1,0:T(8,128)S(1)}, f32[64,640]{1,0:T(8,128)S(1)}, u32[]{:S(2)}, u32[]{:S(2)}) collective-permute-start(f32[64,640]{1,0:T(8,128)S(1)} %add.10), channel_id=1, source_target_pairs={{0,6},{1,7},{2,4},{3,5},{4,2},{5,3},{6,0},{7,1},{8,14},{9,15},{10,... | collective-permute-start | bytes 491528 | tf_op jit(solution)/shard_map/ppermute | solution.py:830
  137.9 3.1 %collective-permute-done.36 = f32[64,640]{1,0:T(8,128)S(1)} collective-permute-done((f32[64,640]{1,0:T(8,128)S(1)}, f32[64,640]{1,0:T(8,128)S(1)}, u32[]{:S(2)}, u32[]{:S(2)}) %collective-permute-start.36) | collective-permute-done | bytes 163872 | tf_op jit(solution)/shard_map/ppermute | solution.py:830
  141.0 2.1 %collective-permute-start.37 = (f32[64,640]{1,0:T(8,128)S(1)}, f32[64,640]{1,0:T(8,128)S(1)}, u32[]{:S(2)}, u32[]{:S(2)}) collective-permute-start(f32[64,640]{1,0:T(8,128)S(1)} %add.11.mine_ref), channel_id=1, source_target_pairs={{0,1},{1,0},{2,3},{3,2},{4,5},{5,4},{6,7},{7,6},{8,9},{9,8},{10,11... | collective-permute-start | bytes 491528 | tf_op jit(solution)/shard_map/ppermute | solution.py:831
  143.2 1.0 collective-permute-done.37.other_ref
  144.2 0.8 finish.1
  (57 shorter events, 5.6 us)
Async XLA Ops:
  3.7 12.5 %collective-permute-start.12 = (f32[64,1152]{1,0:T(8,128)}, f32[64,1152]{1,0:T(8,128)S(1)}, u32[]{:S(2)}, u32[]{:S(2)}) collective-permute-start(f32[64,1152]{1,0:T(8,128)} %get-tuple-element.100.refs_0_), channel_id=1, source_target_pairs={{8,16},{33,41},{10,18},{35,43},{12,20},{37,45},{14,22},{39,47},{72... | collective-permute-start | bytes 884744 | tf_op jit(solution)/shard_map/ppermute | solution.py:766
  4.3 14.4 %collective-permute-start.9 = (f32[64,1152]{1,0:T(8,128)}, f32[64,1152]{1,0:T(8,128)S(1)}, u32[]{:S(2)}, u32[]{:S(2)}) collective-permute-start(f32[64,1152]{1,0:T(8,128)} %get-tuple-element.100.refs_0_), channel_id=1, source_target_pairs={{0,16},{25,41},{2,18},{27,43},{4,20},{29,45},{6,22},{31,47},{64,80... | collective-permute-start | bytes 884744 | tf_op jit(solution)/shard_map/ppermute | solution.py:766
  14.7 4.7 %collective-permute-start.8 = (f32[64,1152]{1,0:T(8,128)}, f32[64,1152]{1,0:T(8,128)S(1)}, u32[]{:S(2)}, u32[]{:S(2)}) collective-permute-start(f32[64,1152]{1,0:T(8,128)} %get-tuple-element.100.refs_0_), channel_id=1, source_target_pairs={{32,16},{57,41},{34,18},{59,43},{36,20},{61,45},{38,22},{63,47},{9... | collective-permute-start | bytes 884744 | tf_op jit(solution)/shard_map/ppermute | solution.py:766
  15.4 5.4 %collective-permute-start.7 = (f32[64,1152]{1,0:T(8,128)}, f32[64,1152]{1,0:T(8,128)S(1)}, u32[]{:S(2)}, u32[]{:S(2)}) collective-permute-start(f32[64,1152]{1,0:T(8,128)} %get-tuple-element.100.refs_0_), channel_id=1, source_target_pairs={{24,16},{49,41},{26,18},{51,43},{28,20},{53,45},{30,22},{55,47},{8... | collective-permute-start | bytes 884744 | tf_op jit(solution)/shard_map/ppermute | solution.py:766
  16.1 5.4 %collective-permute-start.13 = (f32[64,1152]{1,0:T(8,128)S(1)}, f32[64,1152]{1,0:T(8,128)S(1)}, u32[]{:S(2)}, u32[]{:S(2)}) collective-permute-start(f32[64,1152]{1,0:T(8,128)S(1)} %collective-permute-done.12.refs_7_), channel_id=1, source_target_pairs={{17,16},{40,41},{19,18},{42,43},{21,20},{44,45},{23,22},{46,47},{8... | collective-permute-start | bytes 884744 | tf_op jit(solution)/shard_map/ppermute | solution.py:770
  18.8 2.8 %collective-permute-start.10 = (f32[64,1152]{1,0:T(8,128)S(1)}, f32[64,1152]{1,0:T(8,128)S(1)}, u32[]{:S(2)}, u32[]{:S(2)}) collective-permute-start(f32[64,1152]{1,0:T(8,128)S(1)} %collective-permute-done.9.refs_6_), channel_id=1, source_target_pairs={{17,16},{40,41},{19,18},{42,43},{21,20},{44,45},{23,22},{46,47},{8... | collective-permute-start | bytes 884744 | tf_op jit(solution)/shard_map/ppermute | solution.py:770
  19.5 2.1 %collective-permute-start.11 = (f32[64,1152]{1,0:T(8,128)S(1)}, f32[64,1152]{1,0:T(8,128)S(1)}, u32[]{:S(2)}, u32[]{:S(2)}) collective-permute-start(f32[64,1152]{1,0:T(8,128)S(1)} %collective-permute-done.8.refs_2_), channel_id=1, source_target_pairs={{17,16},{40,41},{19,18},{42,43},{21,20},{44,45},{23,22},{46,47},{8... | collective-permute-start | bytes 884744 | tf_op jit(solution)/shard_map/ppermute | solution.py:770
  20.1 5.7 %collective-permute-start.6 = (f32[64,1152]{1,0:T(8,128)}, f32[64,1152]{1,0:T(8,128)S(1)}, u32[]{:S(2)}, u32[]{:S(2)}) collective-permute-start(f32[64,1152]{1,0:T(8,128)} %get-tuple-element.98.refs_0_.refs_8_.refs_1_), channel_id=1, source_target_pairs={{8,16},{33,41},{10,18},{35,43},{12,20},{37,45},{14,22},{39,47},{72... | collective-permute-start | bytes 884744 | tf_op jit(solution)/shard_map/ppermute | solution.py:758
  20.8 29.1 %collective-permute-start.5 = (f32[64,1152]{1,0:T(8,128)}, f32[64,1152]{1,0:T(8,128)S(1)}, u32[]{:S(2)}, u32[]{:S(2)}) collective-permute-start(f32[64,1152]{1,0:T(8,128)} %get-tuple-element.98.refs_0_.refs_8_.refs_1_), channel_id=1, source_target_pairs={{0,16},{25,41},{2,18},{27,43},{4,20},{29,45},{6,22},{31,47},{64,80... | collective-permute-start | bytes 884744 | tf_op jit(solution)/shard_map/ppermute | solution.py:758
  21.6 1.0 copy-start
  22.7 0.8 collective-permute-start.14
  23.5 1.0 copy-start.4
  23.7 27.0 %collective-permute-start.15 = (f32[64,512]{1,0:T(8,128)S(1)}, f32[64,512]{1,0:T(8,128)S(1)}, u32[]{:S(2)}, u32[]{:S(2)}) collective-permute-start(f32[64,512]{1,0:T(8,128)S(1)} %get-tuple-element.103), channel_id=1, source_target_pairs={{80,144},{105,169},{82,146},{107,171},{84,148},{109,173},{86,150},... | collective-permute-start | bytes 393224 | tf_op jit(solution)/shard_map/ppermute | solution.py:780
  24.5 27.0 %collective-permute-start.4 = (f32[64,1152]{1,0:T(8,128)S(1)}, f32[64,1152]{1,0:T(8,128)S(1)}, u32[]{:S(2)}, u32[]{:S(2)}) collective-permute-start(f32[64,1152]{1,0:T(8,128)S(1)} %copy-done.4), channel_id=1, source_target_pairs={{56,16},{17,41},{58,18},{19,43},{60,20},{21,45},{62,22},{23,47},{1... | collective-permute-start | bytes 884744 | tf_op jit(solution)/shard_map/ppermute | solution.py:758
  25.2 27.2 %collective-permute-start.3 = (f32[64,1152]{1,0:T(8,128)S(1)}, f32[64,1152]{1,0:T(8,128)S(1)}, u32[]{:S(2)}, u32[]{:S(2)}) collective-permute-start(f32[64,1152]{1,0:T(8,128)S(1)} %copy-done.4), channel_id=1, source_target_pairs={{48,16},{9,41},{50,18},{11,43},{52,20},{13,45},{54,22},{15,47},{11... | collective-permute-start | bytes 884744 | tf_op jit(solution)/shard_map/ppermute | solution.py:758
  25.9 30.6 %collective-permute-start.2 = (f32[64,1152]{1,0:T(8,128)S(1)}, f32[64,1152]{1,0:T(8,128)S(1)}, u32[]{:S(2)}, u32[]{:S(2)}) collective-permute-start(f32[64,1152]{1,0:T(8,128)S(1)} %copy-done.4), channel_id=1, source_target_pairs={{40,16},{1,41},{42,18},{3,43},{44,20},{5,45},{46,22},{7,47},{104,8... | collective-permute-start | bytes 884744 | tf_op jit(solution)/shard_map/ppermute | solution.py:758
  50.0 6.5 %collective-permute-start.1 = (f32[64,1152]{1,0:T(8,128)S(1)}, f32[64,1152]{1,0:T(8,128)S(1)}, u32[]{:S(2)}, u32[]{:S(2)}) collective-permute-start(f32[64,1152]{1,0:T(8,128)S(1)} %copy-done.4), channel_id=1, source_target_pairs={{32,16},{57,41},{34,18},{59,43},{36,20},{61,45},{38,22},{63,47},{9... | collective-permute-start | bytes 884744 | tf_op jit(solution)/shard_map/ppermute | solution.py:758
  50.7 5.8 %collective-permute-start = (f32[64,1152]{1,0:T(8,128)S(1)}, f32[64,1152]{1,0:T(8,128)S(1)}, u32[]{:S(2)}, u32[]{:S(2)}) collective-permute-start(f32[64,1152]{1,0:T(8,128)S(1)} %copy-done.4), channel_id=1, source_target_pairs={{24,16},{49,41},{26,18},{51,43},{28,20},{53,45},{30,22},{55,47},{8... | collective-permute-start | bytes 884744 | tf_op jit(solution)/shard_map/ppermute | solution.py:758
  51.5 6.4 %copy-start.1 = (f32[64,1152]{1,0:T(8,128)S(1)}, f32[64,1152]{1,0:T(8,128)}, u32[]{:S(2)}) copy-start(f32[64,1152]{1,0:T(8,128)} %get-tuple-element.100.refs_0_) | copy-start | bytes 884740
  51.5 6.4 %collective-permute-start.16 = (f32[64,512]{1,0:T(8,128)S(1)}, f32[64,512]{1,0:T(8,128)S(1)}, u32[]{:S(2)}, u32[]{:S(2)}) collective-permute-start(f32[64,512]{1,0:T(8,128)S(1)} %get-tuple-element.109), channel_id=1, source_target_pairs={{144,208},{169,233},{146,210},{171,235},{148,212},{173,237},{150,2... | collective-permute-start | bytes 393224 | tf_op jit(solution)/shard_map/ppermute | solution.py:780
  56.5 1.4 copy-start.2
  57.9 1.7 %copy-start.3 = (bf16[8,576,192]{2,1,0:T(8,128)(2,1)S(1)}, bf16[8,576,192]{2,1,0:T(8,128)(2,1)}, u32[]{:S(2)}) copy-start(bf16[8,576,192]{2,1,0:T(8,128)(2,1)} %copy-done.2) | copy-start | bytes 5308420
  58.2 4.8 %collective-permute-start.17 = (f32[64,512]{1,0:T(8,128)S(1)}, f32[64,512]{1,0:T(8,128)S(1)}, u32[]{:S(2)}, u32[]{:S(2)}) collective-permute-start(f32[64,512]{1,0:T(8,128)S(1)} %get-tuple-element.119), channel_id=1, source_target_pairs={{208,144},{233,169},{210,146},{235,171},{212,148},{237,173},{214,1... | collective-permute-start | bytes 393224 | tf_op jit(solution)/shard_map/ppermute | solution.py:780
  59.7 3.5 %collective-permute-start.21 = (f32[64,512]{1,0:T(8,128)S(1)}, f32[64,512]{1,0:T(8,128)S(1)}, u32[]{:S(2)}, u32[]{:S(2)}) collective-permute-start(f32[64,512]{1,0:T(8,128)S(1)} %get-tuple-element.143), channel_id=1, source_target_pairs={{16,0},{41,25},{18,2},{43,27},{20,4},{45,29},{22,6},{47,31},{80,64... | collective-permute-start | bytes 393224 | tf_op jit(solution)/shard_map/ppermute | solution.py:774
  60.4 27.6 %collective-permute-start.20 = (f32[64,512]{1,0:T(8,128)S(1)}, f32[64,512]{1,0:T(8,128)S(1)}, u32[]{:S(2)}, u32[]{:S(2)}) collective-permute-start(f32[64,512]{1,0:T(8,128)S(1)} %get-tuple-element.141), channel_id=1, source_target_pairs={{16,40},{41,1},{18,42},{43,3},{20,44},{45,5},{22,46},{47,7},{80,10... | collective-permute-start | bytes 393224 | tf_op jit(solution)/shard_map/ppermute | solution.py:774
  61.7 26.3 %collective-permute-start.19 = (f32[64,512]{1,0:T(8,128)S(1)}, f32[64,512]{1,0:T(8,128)S(1)}, u32[]{:S(2)}, u32[]{:S(2)}) collective-permute-start(f32[64,512]{1,0:T(8,128)S(1)} %get-tuple-element.139), channel_id=1, source_target_pairs={{16,56},{41,17},{18,58},{43,19},{20,60},{45,21},{22,62},{47,23},{8... | collective-permute-start | bytes 393224 | tf_op jit(solution)/shard_map/ppermute | solution.py:774
  62.4 25.7 %collective-permute-start.18 = (f32[64,512]{1,0:T(8,128)S(1)}, f32[64,512]{1,0:T(8,128)S(1)}, u32[]{:S(2)}, u32[]{:S(2)}) collective-permute-start(f32[64,512]{1,0:T(8,128)S(1)} %get-tuple-element.137), channel_id=1, source_target_pairs={{16,48},{41,9},{18,50},{43,11},{20,52},{45,13},{22,54},{47,15},{80... | collective-permute-start | bytes 393224 | tf_op jit(solution)/shard_map/ppermute | solution.py:774
  88.0 2.7 %collective-permute-start.25 = (f32[64,512]{1,0:T(8,128)S(1)}, f32[64,512]{1,0:T(8,128)S(1)}, u32[]{:S(2)}, u32[]{:S(2)}) collective-permute-start(f32[64,512]{1,0:T(8,128)S(1)} %get-tuple-element.144), channel_id=1, source_target_pairs={{144,80},{169,105},{146,82},{171,107},{148,84},{173,109},{150,86},... | collective-permute-start | bytes 393224 | tf_op jit(solution)/shard_map/ppermute | solution.py:780
  88.7 2.9 %collective-permute-start.22 = (f32[64,512]{1,0:T(8,128)S(1)}, f32[64,512]{1,0:T(8,128)S(1)}, u32[]{:S(2)}, u32[]{:S(2)}) collective-permute-start(f32[64,512]{1,0:T(8,128)S(1)} %get-tuple-element.146), channel_id=1, source_target_pairs={{16,24},{41,49},{18,26},{43,51},{20,28},{45,53},{22,30},{47,55},{8... | collective-permute-start | bytes 393224 | tf_op jit(solution)/shard_map/ppermute | solution.py:774
  89.4 2.2 %collective-permute-start.23 = (f32[64,512]{1,0:T(8,128)S(1)}, f32[64,512]{1,0:T(8,128)S(1)}, u32[]{:S(2)}, u32[]{:S(2)}) collective-permute-start(f32[64,512]{1,0:T(8,128)S(1)} %get-tuple-element.148), channel_id=1, source_target_pairs={{16,32},{41,57},{18,34},{43,59},{20,36},{45,61},{22,38},{47,63},{8... | collective-permute-start | bytes 393224 | tf_op jit(solution)/shard_map/ppermute | solution.py:774
  90.1 1.5 %collective-permute-start.24 = (f32[64,512]{1,0:T(8,128)S(1)}, f32[64,512]{1,0:T(8,128)S(1)}, u32[]{:S(2)}, u32[]{:S(2)}) collective-permute-start(f32[64,512]{1,0:T(8,128)S(1)} %get-tuple-element.154), channel_id=1, source_target_pairs={{16,8},{41,33},{18,10},{43,35},{20,12},{45,37},{22,14},{47,39},{80... | collective-permute-start | bytes 393224 | tf_op jit(solution)/shard_map/ppermute | solution.py:774
  90.7 0.9 copy-start.5
  90.9 3.4 %collective-permute-start.26 = (f32[64,512]{1,0:T(8,128)S(1)}, f32[64,512]{1,0:T(8,128)S(1)}, u32[]{:S(2)}, u32[]{:S(2)}) collective-permute-start(f32[64,512]{1,0:T(8,128)S(1)} %get-tuple-element.164), channel_id=1, source_target_pairs={{80,16},{105,41},{82,18},{107,43},{84,20},{109,45},{86,22},{111,47}} | collective-permute-start | bytes 393224 | tf_op jit(solution)/shard_map/ppermute | solution.py:780
  95.1 4.0 %collective-permute-start.27 = (f32[64,512]{1,0:T(8,128)S(1)}, f32[64,512]{1,0:T(8,128)S(1)}, u32[]{:S(2)}, u32[]{:S(2)}) collective-permute-start(f32[64,512]{1,0:T(8,128)S(1)} %get-tuple-element.178), channel_id=1, source_target_pairs={{16,24},{41,49},{18,26},{43,51},{20,28},{45,53},{22,30},{47,55},{8... | collective-permute-start | bytes 393224 | tf_op jit(solution)/shard_map/ppermute | solution.py:774
  95.8 4.0 %collective-permute-start.28 = (f32[64,512]{1,0:T(8,128)S(1)}, f32[64,512]{1,0:T(8,128)S(1)}, u32[]{:S(2)}, u32[]{:S(2)}) collective-permute-start(f32[64,512]{1,0:T(8,128)S(1)} %get-tuple-element.179), channel_id=1, source_target_pairs={{16,32},{41,57},{18,34},{43,59},{20,36},{45,61},{22,38},{47,63},{8... | collective-permute-start | bytes 393224 | tf_op jit(solution)/shard_map/ppermute | solution.py:774
  96.5 25.2 %collective-permute-start.29 = (f32[64,512]{1,0:T(8,128)S(1)}, f32[64,512]{1,0:T(8,128)S(1)}, u32[]{:S(2)}, u32[]{:S(2)}) collective-permute-start(f32[64,512]{1,0:T(8,128)S(1)} %get-tuple-element.180), channel_id=1, source_target_pairs={{16,40},{41,1},{18,42},{43,3},{20,44},{45,5},{22,46},{47,7},{80,10... | collective-permute-start | bytes 393224 | tf_op jit(solution)/shard_map/ppermute | solution.py:774
  97.8 23.9 %collective-permute-start.30 = (f32[64,512]{1,0:T(8,128)S(1)}, f32[64,512]{1,0:T(8,128)S(1)}, u32[]{:S(2)}, u32[]{:S(2)}) collective-permute-start(f32[64,512]{1,0:T(8,128)S(1)} %get-tuple-element.181), channel_id=1, source_target_pairs={{16,48},{41,9},{18,50},{43,11},{20,52},{45,13},{22,54},{47,15},{80... | collective-permute-start | bytes 393224 | tf_op jit(solution)/shard_map/ppermute | solution.py:774
  98.4 23.2 %collective-permute-start.31 = (f32[64,512]{1,0:T(8,128)S(1)}, f32[64,512]{1,0:T(8,128)S(1)}, u32[]{:S(2)}, u32[]{:S(2)}) collective-permute-start(f32[64,512]{1,0:T(8,128)S(1)} %get-tuple-element.182), channel_id=1, source_target_pairs={{16,56},{41,17},{18,58},{43,19},{20,60},{45,21},{22,62},{47,23},{8... | collective-permute-start | bytes 393224 | tf_op jit(solution)/shard_map/ppermute | solution.py:774
  99.1 22.5 %collective-permute-start.32 = (f32[64,512]{1,0:T(8,128)S(1)}, f32[64,512]{1,0:T(8,128)S(1)}, u32[]{:S(2)}, u32[]{:S(2)}) collective-permute-start(f32[64,512]{1,0:T(8,128)S(1)} %get-tuple-element.183), channel_id=1, source_target_pairs={{16,0},{41,25},{18,2},{43,27},{20,4},{45,29},{22,6},{47,31},{80,64... | collective-permute-start | bytes 393224 | tf_op jit(solution)/shard_map/ppermute | solution.py:774
  99.8 21.9 %collective-permute-start.33 = (f32[64,512]{1,0:T(8,128)S(1)}, f32[64,512]{1,0:T(8,128)S(1)}, u32[]{:S(2)}, u32[]{:S(2)}) collective-permute-start(f32[64,512]{1,0:T(8,128)S(1)} %get-tuple-element.184), channel_id=1, source_target_pairs={{16,8},{41,33},{18,10},{43,35},{20,12},{45,37},{22,14},{47,39},{80... | collective-permute-start | bytes 393224 | tf_op jit(solution)/shard_map/ppermute | solution.py:774
  124.4 5.1 %collective-permute-start.34 = (f32[64,640]{1,0:T(8,128)S(1)}, f32[64,640]{1,0:T(8,128)S(1)}, u32[]{:S(2)}, u32[]{:S(2)}) collective-permute-start(f32[64,640]{1,0:T(8,128)S(1)} %get-tuple-element.187), channel_id=1, source_target_pairs={{0,1},{1,0},{2,3},{3,2},{4,5},{5,4},{6,7},{7,6},{8,9},{9,8},{10,11... | collective-permute-start | bytes 491528 | tf_op jit(solution)/shard_map/ppermute | solution.py:828
  129.5 5.5 %collective-permute-start.35 = (f32[64,640]{1,0:T(8,128)S(1)}, f32[64,640]{1,0:T(8,128)S(1)}, u32[]{:S(2)}, u32[]{:S(2)}) collective-permute-start(f32[64,640]{1,0:T(8,128)S(1)} %add.9), channel_id=1, source_target_pairs={{0,2},{1,3},{2,0},{3,1},{4,6},{5,7},{6,4},{7,5},{8,10},{9,11},{10,... | collective-permute-start | bytes 491528 | tf_op jit(solution)/shard_map/ppermute | solution.py:830
  135.0 6.0 %collective-permute-start.36 = (f32[64,640]{1,0:T(8,128)S(1)}, f32[64,640]{1,0:T(8,128)S(1)}, u32[]{:S(2)}, u32[]{:S(2)}) collective-permute-start(f32[64,640]{1,0:T(8,128)S(1)} %add.10), channel_id=1, source_target_pairs={{0,6},{1,7},{2,4},{3,5},{4,2},{5,3},{6,0},{7,1},{8,14},{9,15},{10,... | collective-permute-start | bytes 491528 | tf_op jit(solution)/shard_map/ppermute | solution.py:830
  141.0 3.2 %collective-permute-start.37 = (f32[64,640]{1,0:T(8,128)S(1)}, f32[64,640]{1,0:T(8,128)S(1)}, u32[]{:S(2)}, u32[]{:S(2)}) collective-permute-start(f32[64,640]{1,0:T(8,128)S(1)} %add.11.mine_ref), channel_id=1, source_target_pairs={{0,1},{1,0},{2,3},{3,2},{4,5},{5,4},{6,7},{7,6},{8,9},{9,8},{10,11... | collective-permute-start | bytes 491528 | tf_op jit(solution)/shard_map/ppermute | solution.py:831

commit v8 on v7

--- a/solution.py
+++ b/solution.py
@@ -16,7 +16,7 @@
 ANY = pl.BlockSpec(memory_space=pl.ANY)
 HBM = pl.BlockSpec(memory_space=pltpu.HBM)
 VMEM = pl.BlockSpec(memory_space=pltpu.VMEM)
-PARAMS = pltpu.CompilerParams(vmem_limit_bytes=40 << 20)
+PARAMS = pltpu.CompilerParams(vmem_limit_bytes=28 << 20)
 
 
 def split(x):

time: 146 us -> 145 us (level)
  local copies, waits for them, and re-layouts: 3.12 us -> 1.13 us
    unnamed x12 -> x8, local copies, waits for them, and re-layouts: 3.12 us -> 1.13 us
where the time goes in v8:
time: 145 us; the launch traced here: 144 us
  starting transfers between devices  68.8 us (47%)
  waiting for transfers between devices  61.4 us (42%)
  Pallas kernels  11.5 us (8%)
    ppermute x14, waiting for transfers between devices, scatter(): return lax.ppermute(value, AXES, pairs)  46 us
    ppermute x7, starting transfers between devices, gather(): return lax.ppermute(value, AXES, pairs)  28.2 us
    ppermute x4, starting transfers between devices, gather_pair(): return lax.ppermute(value, AXES, pairs)  12.4 us
    ppermute x14, starting transfers between devices, scatter(): return lax.ppermute(value, AXES, pairs)  10.6 us
    ppermute x2, waiting for transfers between devices, body(): lax.ppermute(mine, 'dp', [(i, i ^ flip) for i in range(images)])  7.21 us
    ppermute x1, starting transfers between devices, body(): mine = mine + lax.ppermute(other, 'dp', [(i, i ^ 1) for i in range(images)])  5.1 us
    ppermute x2, starting transfers between devices, body(): lax.ppermute(mine, 'dp', [(i, i ^ flip) for i in range(images)])  4.19 us
    ppermute x6, starting transfers between devices, hop(): return lax.ppermute(value, AXES, pairs)  4.14 us
  transfers between devices with their start and end apart: 38, of which 8 were waited for; matrix products, arithmetic and copies ran while one was open for 0% of the time, Pallas kernels for 3%

profile of v8, /device:TPU:1, one launch (start us, length us, event | category | flops | bytes accessed | tf_op | source)
XLA Modules:
  0.0 144.1 jit_solution(12346322303147511737)
XLA Ops:
  0.6 3.0 %relax.1 = (f32[64,1152]{1,0:T(8,128)}, f32[64,1152]{1,0:T(8,128)}) custom-call(f32[64,512]{1,0:T(8,128)} %bitcast.8, f32[64,512]{1,0:T(8,128)} %bitcast.10, f32[2,64,576]{2,1,0:T(8,128)} %w_hbm.1, f32[2,64]{1,0:T(2,128)} %b_hbm.1), custom_call_target="tpu_custom_call" | custom-call | tf_op jit(solution)/shard_map/relax/pallas_call | solution.py:195
  3.7 0.7 collective-permute-start.12
  4.3 10.4 %collective-permute-start.9 = (f32[64,1152]{1,0:T(8,128)}, f32[64,1152]{1,0:T(8,128)S(1)}, u32[]{:S(2)}, u32[]{:S(2)}) collective-permute-start(f32[64,1152]{1,0:T(8,128)} %get-tuple-element.100.refs_0_), channel_id=1, source_target_pairs={{0,16},{25,41},{2,18},{27,43},{4,20},{29,45},{6,22},{31,47},{64,80... | collective-permute-start | bytes 884744 | tf_op jit(solution)/shard_map/ppermute | solution.py:766
  14.7 0.7 collective-permute-start.8
  15.4 0.7 collective-permute-start.7
  16.1 0.7 collective-permute-start.13
  16.8 2.0 %collective-permute-done.9.refs_6_ = f32[64,1152]{1,0:T(8,128)S(1)} collective-permute-done((f32[64,1152]{1,0:T(8,128)}, f32[64,1152]{1,0:T(8,128)S(1)}, u32[]{:S(2)}, u32[]{:S(2)}) %collective-permute-start.9) | collective-permute-done | bytes 294944 | tf_op jit(solution)/shard_map/ppermute | solution.py:766
  19.5 0.7 collective-permute-start.11
  20.1 0.7 collective-permute-start.6
  20.8 0.7 collective-permute-start.5
  21.6 1.0 copy-done
  22.7 0.7 collective-permute-start.14
  23.7 0.7 collective-permute-start.15
  25.2 0.7 collective-permute-start.3
  25.9 24.1 %collective-permute-start.2 = (f32[64,1152]{1,0:T(8,128)S(1)}, f32[64,1152]{1,0:T(8,128)S(1)}, u32[]{:S(2)}, u32[]{:S(2)}) collective-permute-start(f32[64,1152]{1,0:T(8,128)S(1)} %copy-done.2), channel_id=1, source_target_pairs={{40,16},{1,41},{42,18},{3,43},{44,20},{5,45},{46,22},{7,47},{104,8... | collective-permute-start | bytes 884744 | tf_op jit(solution)/shard_map/ppermute | solution.py:758
  50.0 0.7 collective-permute-start.1
  50.7 0.7 collective-permute-start
  51.5 0.8 collective-permute-start.16
  52.4 4.1 %collective-permute-done.2.refs_3_.refs_11_ = f32[64,1152]{1,0:T(8,128)S(1)} collective-permute-done((f32[64,1152]{1,0:T(8,128)S(1)}, f32[64,1152]{1,0:T(8,128)S(1)}, u32[]{:S(2)}, u32[]{:S(2)}) %collective-permute-start.2) | collective-permute-done | bytes 294944 | tf_op jit(solution)/shard_map/ppermute | solution.py:758
  56.8 0.7 collective-permute-start.17
  57.8 0.7 collective-permute-start.21
  58.5 1.3 collective-permute-start.20
  59.8 0.7 collective-permute-start.19
  60.5 0.7 collective-permute-start.18
  61.3 24.8 %collective-permute-done.20.refs_6_ = f32[64,512]{1,0:T(8,128)S(1)} collective-permute-done((f32[64,512]{1,0:T(8,128)S(1)}, f32[64,512]{1,0:T(8,128)S(1)}, u32[]{:S(2)}, u32[]{:S(2)}) %collective-permute-start.20) | collective-permute-done | bytes 131104 | tf_op jit(solution)/shard_map/ppermute | solution.py:774
  86.9 0.7 collective-permute-start.22
  87.5 0.7 collective-permute-start.23
  88.2 0.7 collective-permute-start.24
  89.0 0.7 collective-permute-start.26
  89.8 2.6 %early.1 = (f32[2,64,512]{2,1,0:T(8,128)}, f32[6,64,512]{2,1,0:T(8,128)S(1)}, bf16[2,576,192]{2,1,0:T(8,128)(2,1)S(1)}) custom-call(f32[64,1152]{1,0:T(8,128)S(1)} %copy-done.1, f32[64,1152]{1,0:T(8,128)S(1)} %copy-done.2, f32[64,512]{1,0:T(8,128)S(1)} %bitcast.9, f32[64,512]{1,0:T(8,128)S(1)} %get-tuple-element.118.refs_3_, ...), custom_call_target="tpu_custom_call" | custom-call | tf_op jit(solution)/shard_map/early/pallas_call | solution.py:641
  92.4 0.8 back_0.1
  93.2 0.7 collective-permute-start.27
  93.9 0.7 collective-permute-start.28
  94.6 1.3 collective-permute-start.29
  95.9 0.7 collective-permute-start.30
  96.6 0.7 collective-permute-start.31
  97.3 0.7 collective-permute-start.32
  98.6 21.2 %collective-permute-done.29.refs_5_ = f32[64,512]{1,0:T(8,128)S(1)} collective-permute-done((f32[64,512]{1,0:T(8,128)S(1)}, f32[64,512]{1,0:T(8,128)S(1)}, u32[]{:S(2)}, u32[]{:S(2)}) %collective-permute-start.29) | collective-permute-done | bytes 131104 | tf_op jit(solution)/shard_map/ppermute | solution.py:774
  119.8 2.7 %late.1 = (f32[2,64,512]{2,1,0:T(8,128)}, f32[64,640]{1,0:T(8,128)S(1)}, f32[64,640]{1,0:T(8,128)S(1)}) custom-call(f32[6,64,512]{2,1,0:T(8,128)S(1)} %get-tuple-element.166.refs_0_, bf16[2,576,192]{2,1,0:T(8,128)(2,1)S(1)} %get-tuple-element.167.refs_1_, f32[64,512]{1,0:T(8,128)S(1)} %get-tuple-element.177.refs_2_, ...), custom_call_target="tpu_custom_call" | custom-call | tf_op jit(solution)/shard_map/late/pallas_call | solution.py:690
  122.5 5.1 %collective-permute-start.34 = (f32[64,640]{1,0:T(8,128)S(1)}, f32[64,640]{1,0:T(8,128)S(1)}, u32[]{:S(2)}, u32[]{:S(2)}) collective-permute-start(f32[64,640]{1,0:T(8,128)S(1)} %get-tuple-element.187), channel_id=1, source_target_pairs={{0,1},{1,0},{2,3},{3,2},{4,5},{5,4},{6,7},{7,6},{8,9},{9,8},{10,11... | collective-permute-start | bytes 491528 | tf_op jit(solution)/shard_map/ppermute | solution.py:828
  127.6 1.0 collective-permute-done.34
  128.7 1.4 collective-permute-start.35
  130.1 4.1 %collective-permute-done.35 = f32[64,640]{1,0:T(8,128)S(1)} collective-permute-done((f32[64,640]{1,0:T(8,128)S(1)}, f32[64,640]{1,0:T(8,128)S(1)}, u32[]{:S(2)}, u32[]{:S(2)}) %collective-permute-start.35) | collective-permute-done | bytes 163872 | tf_op jit(solution)/shard_map/ppermute | solution.py:830
  134.2 2.8 %collective-permute-start.36 = (f32[64,640]{1,0:T(8,128)S(1)}, f32[64,640]{1,0:T(8,128)S(1)}, u32[]{:S(2)}, u32[]{:S(2)}) collective-permute-start(f32[64,640]{1,0:T(8,128)S(1)} %add.10), channel_id=1, source_target_pairs={{0,6},{1,7},{2,4},{3,5},{4,2},{5,3},{6,0},{7,1},{8,14},{9,15},{10,... | collective-permute-start | bytes 491528 | tf_op jit(solution)/shard_map/ppermute | solution.py:830
  137.0 3.1 %collective-permute-done.36 = f32[64,640]{1,0:T(8,128)S(1)} collective-permute-done((f32[64,640]{1,0:T(8,128)S(1)}, f32[64,640]{1,0:T(8,128)S(1)}, u32[]{:S(2)}, u32[]{:S(2)}) %collective-permute-start.36) | collective-permute-done | bytes 163872 | tf_op jit(solution)/shard_map/ppermute | solution.py:830
  140.1 2.2 %collective-permute-start.37 = (f32[64,640]{1,0:T(8,128)S(1)}, f32[64,640]{1,0:T(8,128)S(1)}, u32[]{:S(2)}, u32[]{:S(2)}) collective-permute-start(f32[64,640]{1,0:T(8,128)S(1)} %add.11.mine_ref), channel_id=1, source_target_pairs={{0,1},{1,0},{2,3},{3,2},{4,5},{5,4},{6,7},{7,6},{8,9},{9,8},{10,11... | collective-permute-start | bytes 491528 | tf_op jit(solution)/shard_map/ppermute | solution.py:831
  142.3 1.0 collective-permute-done.37.other_ref
  143.3 0.8 finish.1
  (53 shorter events, 4.5 us)
Async XLA Ops:
  3.7 12.5 %collective-permute-start.12 = (f32[64,1152]{1,0:T(8,128)}, f32[64,1152]{1,0:T(8,128)S(1)}, u32[]{:S(2)}, u32[]{:S(2)}) collective-permute-start(f32[64,1152]{1,0:T(8,128)} %get-tuple-element.100.refs_0_), channel_id=1, source_target_pairs={{8,16},{33,41},{10,18},{35,43},{12,20},{37,45},{14,22},{39,47},{72... | collective-permute-start | bytes 884744 | tf_op jit(solution)/shard_map/ppermute | solution.py:766
  4.3 14.4 %collective-permute-start.9 = (f32[64,1152]{1,0:T(8,128)}, f32[64,1152]{1,0:T(8,128)S(1)}, u32[]{:S(2)}, u32[]{:S(2)}) collective-permute-start(f32[64,1152]{1,0:T(8,128)} %get-tuple-element.100.refs_0_), channel_id=1, source_target_pairs={{0,16},{25,41},{2,18},{27,43},{4,20},{29,45},{6,22},{31,47},{64,80... | collective-permute-start | bytes 884744 | tf_op jit(solution)/shard_map/ppermute | solution.py:766
  14.7 4.7 %collective-permute-start.8 = (f32[64,1152]{1,0:T(8,128)}, f32[64,1152]{1,0:T(8,128)S(1)}, u32[]{:S(2)}, u32[]{:S(2)}) collective-permute-start(f32[64,1152]{1,0:T(8,128)} %get-tuple-element.100.refs_0_), channel_id=1, source_target_pairs={{32,16},{57,41},{34,18},{59,43},{36,20},{61,45},{38,22},{63,47},{9... | collective-permute-start | bytes 884744 | tf_op jit(solution)/shard_map/ppermute | solution.py:766
  15.4 5.4 %collective-permute-start.7 = (f32[64,1152]{1,0:T(8,128)}, f32[64,1152]{1,0:T(8,128)S(1)}, u32[]{:S(2)}, u32[]{:S(2)}) collective-permute-start(f32[64,1152]{1,0:T(8,128)} %get-tuple-element.100.refs_0_), channel_id=1, source_target_pairs={{24,16},{49,41},{26,18},{51,43},{28,20},{53,45},{30,22},{55,47},{8... | collective-permute-start | bytes 884744 | tf_op jit(solution)/shard_map/ppermute | solution.py:766
  16.1 5.4 %collective-permute-start.13 = (f32[64,1152]{1,0:T(8,128)S(1)}, f32[64,1152]{1,0:T(8,128)S(1)}, u32[]{:S(2)}, u32[]{:S(2)}) collective-permute-start(f32[64,1152]{1,0:T(8,128)S(1)} %collective-permute-done.12.refs_7_), channel_id=1, source_target_pairs={{17,16},{40,41},{19,18},{42,43},{21,20},{44,45},{23,22},{46,47},{8... | collective-permute-start | bytes 884744 | tf_op jit(solution)/shard_map/ppermute | solution.py:770
  18.8 2.8 %collective-permute-start.10 = (f32[64,1152]{1,0:T(8,128)S(1)}, f32[64,1152]{1,0:T(8,128)S(1)}, u32[]{:S(2)}, u32[]{:S(2)}) collective-permute-start(f32[64,1152]{1,0:T(8,128)S(1)} %collective-permute-done.9.refs_6_), channel_id=1, source_target_pairs={{17,16},{40,41},{19,18},{42,43},{21,20},{44,45},{23,22},{46,47},{8... | collective-permute-start | bytes 884744 | tf_op jit(solution)/shard_map/ppermute | solution.py:770
  19.5 2.1 %collective-permute-start.11 = (f32[64,1152]{1,0:T(8,128)S(1)}, f32[64,1152]{1,0:T(8,128)S(1)}, u32[]{:S(2)}, u32[]{:S(2)}) collective-permute-start(f32[64,1152]{1,0:T(8,128)S(1)} %collective-permute-done.8.refs_2_), channel_id=1, source_target_pairs={{17,16},{40,41},{19,18},{42,43},{21,20},{44,45},{23,22},{46,47},{8... | collective-permute-start | bytes 884744 | tf_op jit(solution)/shard_map/ppermute | solution.py:770
  20.1 5.7 %collective-permute-start.6 = (f32[64,1152]{1,0:T(8,128)}, f32[64,1152]{1,0:T(8,128)S(1)}, u32[]{:S(2)}, u32[]{:S(2)}) collective-permute-start(f32[64,1152]{1,0:T(8,128)} %get-tuple-element.98.refs_0_.refs_8_.refs_1_), channel_id=1, source_target_pairs={{8,16},{33,41},{10,18},{35,43},{12,20},{37,45},{14,22},{39,47},{72... | collective-permute-start | bytes 884744 | tf_op jit(solution)/shard_map/ppermute | solution.py:758
  20.8 29.1 %collective-permute-start.5 = (f32[64,1152]{1,0:T(8,128)}, f32[64,1152]{1,0:T(8,128)S(1)}, u32[]{:S(2)}, u32[]{:S(2)}) collective-permute-start(f32[64,1152]{1,0:T(8,128)} %get-tuple-element.98.refs_0_.refs_8_.refs_1_), channel_id=1, source_target_pairs={{0,16},{25,41},{2,18},{27,43},{4,20},{29,45},{6,22},{31,47},{64,80... | collective-permute-start | bytes 884744 | tf_op jit(solution)/shard_map/ppermute | solution.py:758
  21.6 1.0 copy-start
  22.7 0.8 collective-permute-start.14
  23.5 1.0 copy-start.2
  23.7 27.0 %collective-permute-start.15 = (f32[64,512]{1,0:T(8,128)S(1)}, f32[64,512]{1,0:T(8,128)S(1)}, u32[]{:S(2)}, u32[]{:S(2)}) collective-permute-start(f32[64,512]{1,0:T(8,128)S(1)} %get-tuple-element.103), channel_id=1, source_target_pairs={{80,144},{105,169},{82,146},{107,171},{84,148},{109,173},{86,150},... | collective-permute-start | bytes 393224 | tf_op jit(solution)/shard_map/ppermute | solution.py:780
  24.5 27.1 %collective-permute-start.4 = (f32[64,1152]{1,0:T(8,128)S(1)}, f32[64,1152]{1,0:T(8,128)S(1)}, u32[]{:S(2)}, u32[]{:S(2)}) collective-permute-start(f32[64,1152]{1,0:T(8,128)S(1)} %copy-done.2), channel_id=1, source_target_pairs={{56,16},{17,41},{58,18},{19,43},{60,20},{21,45},{62,22},{23,47},{1... | collective-permute-start | bytes 884744 | tf_op jit(solution)/shard_map/ppermute | solution.py:758
  25.2 27.2 %collective-permute-start.3 = (f32[64,1152]{1,0:T(8,128)S(1)}, f32[64,1152]{1,0:T(8,128)S(1)}, u32[]{:S(2)}, u32[]{:S(2)}) collective-permute-start(f32[64,1152]{1,0:T(8,128)S(1)} %copy-done.2), channel_id=1, source_target_pairs={{48,16},{9,41},{50,18},{11,43},{52,20},{13,45},{54,22},{15,47},{11... | collective-permute-start | bytes 884744 | tf_op jit(solution)/shard_map/ppermute | solution.py:758
  25.9 30.6 %collective-permute-start.2 = (f32[64,1152]{1,0:T(8,128)S(1)}, f32[64,1152]{1,0:T(8,128)S(1)}, u32[]{:S(2)}, u32[]{:S(2)}) collective-permute-start(f32[64,1152]{1,0:T(8,128)S(1)} %copy-done.2), channel_id=1, source_target_pairs={{40,16},{1,41},{42,18},{3,43},{44,20},{5,45},{46,22},{7,47},{104,8... | collective-permute-start | bytes 884744 | tf_op jit(solution)/shard_map/ppermute | solution.py:758
  50.0 6.5 %collective-permute-start.1 = (f32[64,1152]{1,0:T(8,128)S(1)}, f32[64,1152]{1,0:T(8,128)S(1)}, u32[]{:S(2)}, u32[]{:S(2)}) collective-permute-start(f32[64,1152]{1,0:T(8,128)S(1)} %copy-done.2), channel_id=1, source_target_pairs={{32,16},{57,41},{34,18},{59,43},{36,20},{61,45},{38,22},{63,47},{9... | collective-permute-start | bytes 884744 | tf_op jit(solution)/shard_map/ppermute | solution.py:758
  50.7 5.8 %collective-permute-start = (f32[64,1152]{1,0:T(8,128)S(1)}, f32[64,1152]{1,0:T(8,128)S(1)}, u32[]{:S(2)}, u32[]{:S(2)}) collective-permute-start(f32[64,1152]{1,0:T(8,128)S(1)} %copy-done.2), channel_id=1, source_target_pairs={{24,16},{49,41},{26,18},{51,43},{28,20},{53,45},{30,22},{55,47},{8... | collective-permute-start | bytes 884744 | tf_op jit(solution)/shard_map/ppermute | solution.py:758
  51.5 5.0 %copy-start.1 = (f32[64,1152]{1,0:T(8,128)S(1)}, f32[64,1152]{1,0:T(8,128)}, u32[]{:S(2)}) copy-start(f32[64,1152]{1,0:T(8,128)} %get-tuple-element.100.refs_0_) | copy-start | bytes 884740
  51.5 5.0 %collective-permute-start.16 = (f32[64,512]{1,0:T(8,128)S(1)}, f32[64,512]{1,0:T(8,128)S(1)}, u32[]{:S(2)}, u32[]{:S(2)}) collective-permute-start(f32[64,512]{1,0:T(8,128)S(1)} %get-tuple-element.109), channel_id=1, source_target_pairs={{144,208},{169,233},{146,210},{171,235},{148,212},{173,237},{150,2... | collective-permute-start | bytes 393224 | tf_op jit(solution)/shard_map/ppermute | solution.py:780
  56.8 4.4 %collective-permute-start.17 = (f32[64,512]{1,0:T(8,128)S(1)}, f32[64,512]{1,0:T(8,128)S(1)}, u32[]{:S(2)}, u32[]{:S(2)}) collective-permute-start(f32[64,512]{1,0:T(8,128)S(1)} %get-tuple-element.119), channel_id=1, source_target_pairs={{208,144},{233,169},{210,146},{235,171},{212,148},{237,173},{214,1... | collective-permute-start | bytes 393224 | tf_op jit(solution)/shard_map/ppermute | solution.py:780
  57.8 3.5 %collective-permute-start.21 = (f32[64,512]{1,0:T(8,128)S(1)}, f32[64,512]{1,0:T(8,128)S(1)}, u32[]{:S(2)}, u32[]{:S(2)}) collective-permute-start(f32[64,512]{1,0:T(8,128)S(1)} %get-tuple-element.143), channel_id=1, source_target_pairs={{16,0},{41,25},{18,2},{43,27},{20,4},{45,29},{22,6},{47,31},{80,64... | collective-permute-start | bytes 393224 | tf_op jit(solution)/shard_map/ppermute | solution.py:774
  58.5 27.7 %collective-permute-start.20 = (f32[64,512]{1,0:T(8,128)S(1)}, f32[64,512]{1,0:T(8,128)S(1)}, u32[]{:S(2)}, u32[]{:S(2)}) collective-permute-start(f32[64,512]{1,0:T(8,128)S(1)} %get-tuple-element.141), channel_id=1, source_target_pairs={{16,40},{41,1},{18,42},{43,3},{20,44},{45,5},{22,46},{47,7},{80,10... | collective-permute-start | bytes 393224 | tf_op jit(solution)/shard_map/ppermute | solution.py:774
  59.8 26.4 %collective-permute-start.19 = (f32[64,512]{1,0:T(8,128)S(1)}, f32[64,512]{1,0:T(8,128)S(1)}, u32[]{:S(2)}, u32[]{:S(2)}) collective-permute-start(f32[64,512]{1,0:T(8,128)S(1)} %get-tuple-element.139), channel_id=1, source_target_pairs={{16,56},{41,17},{18,58},{43,19},{20,60},{45,21},{22,62},{47,23},{8... | collective-permute-start | bytes 393224 | tf_op jit(solution)/shard_map/ppermute | solution.py:774
  60.5 25.7 %collective-permute-start.18 = (f32[64,512]{1,0:T(8,128)S(1)}, f32[64,512]{1,0:T(8,128)S(1)}, u32[]{:S(2)}, u32[]{:S(2)}) collective-permute-start(f32[64,512]{1,0:T(8,128)S(1)} %get-tuple-element.137), channel_id=1, source_target_pairs={{16,48},{41,9},{18,50},{43,11},{20,52},{45,13},{22,54},{47,15},{80... | collective-permute-start | bytes 393224 | tf_op jit(solution)/shard_map/ppermute | solution.py:774
  86.2 2.7 %collective-permute-start.25 = (f32[64,512]{1,0:T(8,128)S(1)}, f32[64,512]{1,0:T(8,128)S(1)}, u32[]{:S(2)}, u32[]{:S(2)}) collective-permute-start(f32[64,512]{1,0:T(8,128)S(1)} %get-tuple-element.144), channel_id=1, source_target_pairs={{144,80},{169,105},{146,82},{171,107},{148,84},{173,109},{150,86},... | collective-permute-start | bytes 393224 | tf_op jit(solution)/shard_map/ppermute | solution.py:780
  86.9 2.9 %collective-permute-start.22 = (f32[64,512]{1,0:T(8,128)S(1)}, f32[64,512]{1,0:T(8,128)S(1)}, u32[]{:S(2)}, u32[]{:S(2)}) collective-permute-start(f32[64,512]{1,0:T(8,128)S(1)} %get-tuple-element.146), channel_id=1, source_target_pairs={{16,24},{41,49},{18,26},{43,51},{20,28},{45,53},{22,30},{47,55},{8... | collective-permute-start | bytes 393224 | tf_op jit(solution)/shard_map/ppermute | solution.py:774
  87.5 2.2 %collective-permute-start.23 = (f32[64,512]{1,0:T(8,128)S(1)}, f32[64,512]{1,0:T(8,128)S(1)}, u32[]{:S(2)}, u32[]{:S(2)}) collective-permute-start(f32[64,512]{1,0:T(8,128)S(1)} %get-tuple-element.148), channel_id=1, source_target_pairs={{16,32},{41,57},{18,34},{43,59},{20,36},{45,61},{22,38},{47,63},{8... | collective-permute-start | bytes 393224 | tf_op jit(solution)/shard_map/ppermute | solution.py:774
  88.2 1.5 %collective-permute-start.24 = (f32[64,512]{1,0:T(8,128)S(1)}, f32[64,512]{1,0:T(8,128)S(1)}, u32[]{:S(2)}, u32[]{:S(2)}) collective-permute-start(f32[64,512]{1,0:T(8,128)S(1)} %get-tuple-element.154), channel_id=1, source_target_pairs={{16,8},{41,33},{18,10},{43,35},{20,12},{45,37},{22,14},{47,39},{80... | collective-permute-start | bytes 393224 | tf_op jit(solution)/shard_map/ppermute | solution.py:774
  88.9 0.9 copy-start.3
  89.0 3.4 %collective-permute-start.26 = (f32[64,512]{1,0:T(8,128)S(1)}, f32[64,512]{1,0:T(8,128)S(1)}, u32[]{:S(2)}, u32[]{:S(2)}) collective-permute-start(f32[64,512]{1,0:T(8,128)S(1)} %get-tuple-element.164), channel_id=1, source_target_pairs={{80,16},{105,41},{82,18},{107,43},{84,20},{109,45},{86,22},{111,47}} | collective-permute-start | bytes 393224 | tf_op jit(solution)/shard_map/ppermute | solution.py:780
  93.2 4.0 %collective-permute-start.27 = (f32[64,512]{1,0:T(8,128)S(1)}, f32[64,512]{1,0:T(8,128)S(1)}, u32[]{:S(2)}, u32[]{:S(2)}) collective-permute-start(f32[64,512]{1,0:T(8,128)S(1)} %get-tuple-element.178), channel_id=1, source_target_pairs={{16,24},{41,49},{18,26},{43,51},{20,28},{45,53},{22,30},{47,55},{8... | collective-permute-start | bytes 393224 | tf_op jit(solution)/shard_map/ppermute | solution.py:774
  93.9 4.0 %collective-permute-start.28 = (f32[64,512]{1,0:T(8,128)S(1)}, f32[64,512]{1,0:T(8,128)S(1)}, u32[]{:S(2)}, u32[]{:S(2)}) collective-permute-start(f32[64,512]{1,0:T(8,128)S(1)} %get-tuple-element.179), channel_id=1, source_target_pairs={{16,32},{41,57},{18,34},{43,59},{20,36},{45,61},{22,38},{47,63},{8... | collective-permute-start | bytes 393224 | tf_op jit(solution)/shard_map/ppermute | solution.py:774
  94.6 25.2 %collective-permute-start.29 = (f32[64,512]{1,0:T(8,128)S(1)}, f32[64,512]{1,0:T(8,128)S(1)}, u32[]{:S(2)}, u32[]{:S(2)}) collective-permute-start(f32[64,512]{1,0:T(8,128)S(1)} %get-tuple-element.180), channel_id=1, source_target_pairs={{16,40},{41,1},{18,42},{43,3},{20,44},{45,5},{22,46},{47,7},{80,10... | collective-permute-start | bytes 393224 | tf_op jit(solution)/shard_map/ppermute | solution.py:774
  95.9 23.9 %collective-permute-start.30 = (f32[64,512]{1,0:T(8,128)S(1)}, f32[64,512]{1,0:T(8,128)S(1)}, u32[]{:S(2)}, u32[]{:S(2)}) collective-permute-start(f32[64,512]{1,0:T(8,128)S(1)} %get-tuple-element.181), channel_id=1, source_target_pairs={{16,48},{41,9},{18,50},{43,11},{20,52},{45,13},{22,54},{47,15},{80... | collective-permute-start | bytes 393224 | tf_op jit(solution)/shard_map/ppermute | solution.py:774
  96.6 23.2 %collective-permute-start.31 = (f32[64,512]{1,0:T(8,128)S(1)}, f32[64,512]{1,0:T(8,128)S(1)}, u32[]{:S(2)}, u32[]{:S(2)}) collective-permute-start(f32[64,512]{1,0:T(8,128)S(1)} %get-tuple-element.182), channel_id=1, source_target_pairs={{16,56},{41,17},{18,58},{43,19},{20,60},{45,21},{22,62},{47,23},{8... | collective-permute-start | bytes 393224 | tf_op jit(solution)/shard_map/ppermute | solution.py:774
  97.3 22.5 %collective-permute-start.32 = (f32[64,512]{1,0:T(8,128)S(1)}, f32[64,512]{1,0:T(8,128)S(1)}, u32[]{:S(2)}, u32[]{:S(2)}) collective-permute-start(f32[64,512]{1,0:T(8,128)S(1)} %get-tuple-element.183), channel_id=1, source_target_pairs={{16,0},{41,25},{18,2},{43,27},{20,4},{45,29},{22,6},{47,31},{80,64... | collective-permute-start | bytes 393224 | tf_op jit(solution)/shard_map/ppermute | solution.py:774
  98.0 21.9 %collective-permute-start.33 = (f32[64,512]{1,0:T(8,128)S(1)}, f32[64,512]{1,0:T(8,128)S(1)}, u32[]{:S(2)}, u32[]{:S(2)}) collective-permute-start(f32[64,512]{1,0:T(8,128)S(1)} %get-tuple-element.184), channel_id=1, source_target_pairs={{16,8},{41,33},{18,10},{43,35},{20,12},{45,37},{22,14},{47,39},{80... | collective-permute-start | bytes 393224 | tf_op jit(solution)/shard_map/ppermute | solution.py:774
  122.5 6.1 %collective-permute-start.34 = (f32[64,640]{1,0:T(8,128)S(1)}, f32[64,640]{1,0:T(8,128)S(1)}, u32[]{:S(2)}, u32[]{:S(2)}) collective-permute-start(f32[64,640]{1,0:T(8,128)S(1)} %get-tuple-element.187), channel_id=1, source_target_pairs={{0,1},{1,0},{2,3},{3,2},{4,5},{5,4},{6,7},{7,6},{8,9},{9,8},{10,11... | collective-permute-start | bytes 491528 | tf_op jit(solution)/shard_map/ppermute | solution.py:828
  128.7 5.5 %collective-permute-start.35 = (f32[64,640]{1,0:T(8,128)S(1)}, f32[64,640]{1,0:T(8,128)S(1)}, u32[]{:S(2)}, u32[]{:S(2)}) collective-permute-start(f32[64,640]{1,0:T(8,128)S(1)} %add.9), channel_id=1, source_target_pairs={{0,2},{1,3},{2,0},{3,1},{4,6},{5,7},{6,4},{7,5},{8,10},{9,11},{10,... | collective-permute-start | bytes 491528 | tf_op jit(solution)/shard_map/ppermute | solution.py:830
  134.2 5.9 %collective-permute-start.36 = (f32[64,640]{1,0:T(8,128)S(1)}, f32[64,640]{1,0:T(8,128)S(1)}, u32[]{:S(2)}, u32[]{:S(2)}) collective-permute-start(f32[64,640]{1,0:T(8,128)S(1)} %add.10), channel_id=1, source_target_pairs={{0,6},{1,7},{2,4},{3,5},{4,2},{5,3},{6,0},{7,1},{8,14},{9,15},{10,... | collective-permute-start | bytes 491528 | tf_op jit(solution)/shard_map/ppermute | solution.py:830
  140.1 3.2 %collective-permute-start.37 = (f32[64,640]{1,0:T(8,128)S(1)}, f32[64,640]{1,0:T(8,128)S(1)}, u32[]{:S(2)}, u32[]{:S(2)}) collective-permute-start(f32[64,640]{1,0:T(8,128)S(1)} %add.11.mine_ref), channel_id=1, source_target_pairs={{0,1},{1,0},{2,3},{3,2},{4,5},{5,4},{6,7},{7,6},{8,9},{9,8},{10,11... | collective-permute-start | bytes 491528 | tf_op jit(solution)/shard_map/ppermute | solution.py:831

commit v9 on v8

--- a/solution.py
+++ b/solution.py
@@ -264,7 +264,7 @@
 
         v = lax.fori_loop(1, HALF, step, tau[0][:, WPAD - CELLS :])
         copies = half_out(vt, vt_ref, sems, 0)
-        out_ref[...] = lax.fori_loop(HALF, RING, step, v)
+        out_ref[...] = lax.fori_loop(HALF, RING, step, v, unroll=2)
         wait_all(copies + half_out(vt, vt_ref, sems, 1))
 
 
@@ -553,7 +553,8 @@
             return back_step(behind[j], mu, parts[0, j], parts[1, j], parts[2, j])
 
         if stage == 0:
-            end = lax.fori_loop(0, RING - 1, step, mu_ref[...])
+            end = lax.fori_loop(0, RING - 2, step, mu_ref[...], unroll=2)
+            end = step(RING - 2, end)
             mus[0] = end
         else:
             end = lax.fori_loop(0, RING, step, mu_ref[...], unroll=2)

time: 145 us -> 144 us (level)
  no operation moved by 1% of the time
where the time goes in v9:
time: 144 us
  starting transfers between devices  68.6 us (48%)
  waiting for transfers between devices  61.1 us (42%)
  Pallas kernels  11.5 us (8%)
    ppermute x14, waiting for transfers between devices, scatter(): return lax.ppermute(value, AXES, pairs)  45.7 us
    ppermute x7, starting transfers between devices, gather(): return lax.ppermute(value, AXES, pairs)  28 us
    ppermute x4, starting transfers between devices, gather_pair(): return lax.ppermute(value, AXES, pairs)  12.4 us
    ppermute x14, starting transfers between devices, scatter(): return lax.ppermute(value, AXES, pairs)  10.6 us
    ppermute x2, waiting for transfers between devices, body(): lax.ppermute(mine, 'dp', [(i, i ^ flip) for i in range(images)])  7.21 us
    ppermute x1, starting transfers between devices, body(): mine = mine + lax.ppermute(other, 'dp', [(i, i ^ 1) for i in range(images)])  5.07 us
    ppermute x2, starting transfers between devices, body(): lax.ppermute(mine, 'dp', [(i, i ^ flip) for i in range(images)])  4.19 us
    ppermute x6, starting transfers between devices, hop(): return lax.ppermute(value, AXES, pairs)  4.14 us
  transfers between devices with their start and end apart: 38, of which 8 were waited for; matrix products, arithmetic and copies ran while one was open for 0% of the time, Pallas kernels for 3%

profile of v9, /device:TPU:1, one launch (start us, length us, event | category | flops | bytes accessed | tf_op | source)
XLA Modules:
  0.0 143.6 jit_solution(11421183289404419238)
XLA Ops:
  0.6 3.0 %relax.1 = (f32[64,1152]{1,0:T(8,128)}, f32[64,1152]{1,0:T(8,128)}) custom-call(f32[64,512]{1,0:T(8,128)} %bitcast.8, f32[64,512]{1,0:T(8,128)} %bitcast.10, f32[2,64,576]{2,1,0:T(8,128)} %w_hbm.1, f32[2,64]{1,0:T(2,128)} %b_hbm.1), custom_call_target="tpu_custom_call" | custom-call | tf_op jit(solution)/shard_map/relax/pallas_call | solution.py:195
  3.7 0.7 collective-permute-start.12
  4.3 10.4 %collective-permute-start.9 = (f32[64,1152]{1,0:T(8,128)}, f32[64,1152]{1,0:T(8,128)S(1)}, u32[]{:S(2)}, u32[]{:S(2)}) collective-permute-start(f32[64,1152]{1,0:T(8,128)} %get-tuple-element.100.refs_0_), channel_id=1, source_target_pairs={{0,16},{25,41},{2,18},{27,43},{4,20},{29,45},{6,22},{31,47},{64,80... | collective-permute-start | bytes 884744 | tf_op jit(solution)/shard_map/ppermute | solution.py:767
  14.7 0.7 collective-permute-start.8
  15.4 0.7 collective-permute-start.7
  16.1 0.7 collective-permute-start.13
  16.8 2.0 %collective-permute-done.9.refs_6_ = f32[64,1152]{1,0:T(8,128)S(1)} collective-permute-done((f32[64,1152]{1,0:T(8,128)}, f32[64,1152]{1,0:T(8,128)S(1)}, u32[]{:S(2)}, u32[]{:S(2)}) %collective-permute-start.9) | collective-permute-done | bytes 294944 | tf_op jit(solution)/shard_map/ppermute | solution.py:767
  19.5 0.7 collective-permute-start.11
  20.1 0.7 collective-permute-start.6
  20.8 0.7 collective-permute-start.5
  21.6 1.0 copy-done
  22.7 0.7 collective-permute-start.14
  23.7 0.7 collective-permute-start.15
  25.2 0.7 collective-permute-start.3
  25.9 23.9 %collective-permute-start.2 = (f32[64,1152]{1,0:T(8,128)S(1)}, f32[64,1152]{1,0:T(8,128)S(1)}, u32[]{:S(2)}, u32[]{:S(2)}) collective-permute-start(f32[64,1152]{1,0:T(8,128)S(1)} %copy-done.2), channel_id=1, source_target_pairs={{40,16},{1,41},{42,18},{3,43},{44,20},{5,45},{46,22},{7,47},{104,8... | collective-permute-start | bytes 884744 | tf_op jit(solution)/shard_map/ppermute | solution.py:759
  49.8 0.7 collective-permute-start.1
  50.5 0.7 collective-permute-start
  51.4 0.8 collective-permute-start.16
  52.2 4.1 %collective-permute-done.2.refs_3_.refs_11_ = f32[64,1152]{1,0:T(8,128)S(1)} collective-permute-done((f32[64,1152]{1,0:T(8,128)S(1)}, f32[64,1152]{1,0:T(8,128)S(1)}, u32[]{:S(2)}, u32[]{:S(2)}) %collective-permute-start.2) | collective-permute-done | bytes 294944 | tf_op jit(solution)/shard_map/ppermute | solution.py:759
  56.6 0.7 collective-permute-start.17
  57.7 0.7 collective-permute-start.21
  58.3 1.3 collective-permute-start.20
  59.6 0.7 collective-permute-start.19
  60.3 0.7 collective-permute-start.18
  61.2 24.8 %collective-permute-done.20.refs_6_ = f32[64,512]{1,0:T(8,128)S(1)} collective-permute-done((f32[64,512]{1,0:T(8,128)S(1)}, f32[64,512]{1,0:T(8,128)S(1)}, u32[]{:S(2)}, u32[]{:S(2)}) %collective-permute-start.20) | collective-permute-done | bytes 131104 | tf_op jit(solution)/shard_map/ppermute | solution.py:775
  86.7 0.7 collective-permute-start.22
  87.3 0.7 collective-permute-start.23
  88.0 0.7 collective-permute-start.24
  88.9 0.7 collective-permute-start.26
  89.6 2.6 %early.1 = (f32[2,64,512]{2,1,0:T(8,128)}, f32[6,64,512]{2,1,0:T(8,128)S(1)}, bf16[2,576,192]{2,1,0:T(8,128)(2,1)S(1)}) custom-call(f32[64,1152]{1,0:T(8,128)S(1)} %copy-done.1, f32[64,1152]{1,0:T(8,128)S(1)} %copy-done.2, f32[64,512]{1,0:T(8,128)S(1)} %bitcast.9, f32[64,512]{1,0:T(8,128)S(1)} %get-tuple-element.118.refs_3_, ...), custom_call_target="tpu_custom_call" | custom-call | tf_op jit(solution)/shard_map/early/pallas_call | solution.py:642
  92.3 0.8 back_0.1
  93.1 0.7 collective-permute-start.27
  93.7 0.7 collective-permute-start.28
  94.4 1.3 collective-permute-start.29
  95.7 0.7 collective-permute-start.30
  96.4 0.7 collective-permute-start.31
  97.1 0.7 collective-permute-start.32
  98.4 20.9 %collective-permute-done.29.refs_5_ = f32[64,512]{1,0:T(8,128)S(1)} collective-permute-done((f32[64,512]{1,0:T(8,128)S(1)}, f32[64,512]{1,0:T(8,128)S(1)}, u32[]{:S(2)}, u32[]{:S(2)}) %collective-permute-start.29) | collective-permute-done | bytes 131104 | tf_op jit(solution)/shard_map/ppermute | solution.py:775
  119.3 2.7 %late.1 = (f32[2,64,512]{2,1,0:T(8,128)}, f32[64,640]{1,0:T(8,128)S(1)}, f32[64,640]{1,0:T(8,128)S(1)}) custom-call(f32[6,64,512]{2,1,0:T(8,128)S(1)} %get-tuple-element.166.refs_0_, bf16[2,576,192]{2,1,0:T(8,128)(2,1)S(1)} %get-tuple-element.167.refs_1_, f32[64,512]{1,0:T(8,128)S(1)} %get-tuple-element.177.refs_2_, ...), custom_call_target="tpu_custom_call" | custom-call | tf_op jit(solution)/shard_map/late/pallas_call | solution.py:691
  122.1 5.1 %collective-permute-start.34 = (f32[64,640]{1,0:T(8,128)S(1)}, f32[64,640]{1,0:T(8,128)S(1)}, u32[]{:S(2)}, u32[]{:S(2)}) collective-permute-start(f32[64,640]{1,0:T(8,128)S(1)} %get-tuple-element.187), channel_id=1, source_target_pairs={{0,1},{1,0},{2,3},{3,2},{4,5},{5,4},{6,7},{7,6},{8,9},{9,8},{10,11... | collective-permute-start | bytes 491528 | tf_op jit(solution)/shard_map/ppermute | solution.py:829
  127.1 1.0 collective-permute-done.34
  128.2 1.4 collective-permute-start.35
  129.6 4.1 %collective-permute-done.35 = f32[64,640]{1,0:T(8,128)S(1)} collective-permute-done((f32[64,640]{1,0:T(8,128)S(1)}, f32[64,640]{1,0:T(8,128)S(1)}, u32[]{:S(2)}, u32[]{:S(2)}) %collective-permute-start.35) | collective-permute-done | bytes 163872 | tf_op jit(solution)/shard_map/ppermute | solution.py:831
  133.7 2.8 %collective-permute-start.36 = (f32[64,640]{1,0:T(8,128)S(1)}, f32[64,640]{1,0:T(8,128)S(1)}, u32[]{:S(2)}, u32[]{:S(2)}) collective-permute-start(f32[64,640]{1,0:T(8,128)S(1)} %add.10), channel_id=1, source_target_pairs={{0,6},{1,7},{2,4},{3,5},{4,2},{5,3},{6,0},{7,1},{8,14},{9,15},{10,... | collective-permute-start | bytes 491528 | tf_op jit(solution)/shard_map/ppermute | solution.py:831
  136.5 3.1 %collective-permute-done.36 = f32[64,640]{1,0:T(8,128)S(1)} collective-permute-done((f32[64,640]{1,0:T(8,128)S(1)}, f32[64,640]{1,0:T(8,128)S(1)}, u32[]{:S(2)}, u32[]{:S(2)}) %collective-permute-start.36) | collective-permute-done | bytes 163872 | tf_op jit(solution)/shard_map/ppermute | solution.py:831
  139.6 2.2 %collective-permute-start.37 = (f32[64,640]{1,0:T(8,128)S(1)}, f32[64,640]{1,0:T(8,128)S(1)}, u32[]{:S(2)}, u32[]{:S(2)}) collective-permute-start(f32[64,640]{1,0:T(8,128)S(1)} %add.11.mine_ref), channel_id=1, source_target_pairs={{0,1},{1,0},{2,3},{3,2},{4,5},{5,4},{6,7},{7,6},{8,9},{9,8},{10,11... | collective-permute-start | bytes 491528 | tf_op jit(solution)/shard_map/ppermute | solution.py:832
  141.8 1.0 collective-permute-done.37.other_ref
  142.8 0.8 finish.1
  (53 shorter events, 4.5 us)
Async XLA Ops:
  3.7 12.5 %collective-permute-start.12 = (f32[64,1152]{1,0:T(8,128)}, f32[64,1152]{1,0:T(8,128)S(1)}, u32[]{:S(2)}, u32[]{:S(2)}) collective-permute-start(f32[64,1152]{1,0:T(8,128)} %get-tuple-element.100.refs_0_), channel_id=1, source_target_pairs={{8,16},{33,41},{10,18},{35,43},{12,20},{37,45},{14,22},{39,47},{72... | collective-permute-start | bytes 884744 | tf_op jit(solution)/shard_map/ppermute | solution.py:767
  4.3 14.4 %collective-permute-start.9 = (f32[64,1152]{1,0:T(8,128)}, f32[64,1152]{1,0:T(8,128)S(1)}, u32[]{:S(2)}, u32[]{:S(2)}) collective-permute-start(f32[64,1152]{1,0:T(8,128)} %get-tuple-element.100.refs_0_), channel_id=1, source_target_pairs={{0,16},{25,41},{2,18},{27,43},{4,20},{29,45},{6,22},{31,47},{64,80... | collective-permute-start | bytes 884744 | tf_op jit(solution)/shard_map/ppermute | solution.py:767
  14.7 4.7 %collective-permute-start.8 = (f32[64,1152]{1,0:T(8,128)}, f32[64,1152]{1,0:T(8,128)S(1)}, u32[]{:S(2)}, u32[]{:S(2)}) collective-permute-start(f32[64,1152]{1,0:T(8,128)} %get-tuple-element.100.refs_0_), channel_id=1, source_target_pairs={{32,16},{57,41},{34,18},{59,43},{36,20},{61,45},{38,22},{63,47},{9... | collective-permute-start | bytes 884744 | tf_op jit(solution)/shard_map/ppermute | solution.py:767
  15.4 5.4 %collective-permute-start.7 = (f32[64,1152]{1,0:T(8,128)}, f32[64,1152]{1,0:T(8,128)S(1)}, u32[]{:S(2)}, u32[]{:S(2)}) collective-permute-start(f32[64,1152]{1,0:T(8,128)} %get-tuple-element.100.refs_0_), channel_id=1, source_target_pairs={{24,16},{49,41},{26,18},{51,43},{28,20},{53,45},{30,22},{55,47},{8... | collective-permute-start | bytes 884744 | tf_op jit(solution)/shard_map/ppermute | solution.py:767
  16.1 5.4 %collective-permute-start.13 = (f32[64,1152]{1,0:T(8,128)S(1)}, f32[64,1152]{1,0:T(8,128)S(1)}, u32[]{:S(2)}, u32[]{:S(2)}) collective-permute-start(f32[64,1152]{1,0:T(8,128)S(1)} %collective-permute-done.12.refs_7_), channel_id=1, source_target_pairs={{17,16},{40,41},{19,18},{42,43},{21,20},{44,45},{23,22},{46,47},{8... | collective-permute-start | bytes 884744 | tf_op jit(solution)/shard_map/ppermute | solution.py:771
  18.8 2.8 %collective-permute-start.10 = (f32[64,1152]{1,0:T(8,128)S(1)}, f32[64,1152]{1,0:T(8,128)S(1)}, u32[]{:S(2)}, u32[]{:S(2)}) collective-permute-start(f32[64,1152]{1,0:T(8,128)S(1)} %collective-permute-done.9.refs_6_), channel_id=1, source_target_pairs={{17,16},{40,41},{19,18},{42,43},{21,20},{44,45},{23,22},{46,47},{8... | collective-permute-start | bytes 884744 | tf_op jit(solution)/shard_map/ppermute | solution.py:771
  19.5 2.1 %collective-permute-start.11 = (f32[64,1152]{1,0:T(8,128)S(1)}, f32[64,1152]{1,0:T(8,128)S(1)}, u32[]{:S(2)}, u32[]{:S(2)}) collective-permute-start(f32[64,1152]{1,0:T(8,128)S(1)} %collective-permute-done.8.refs_2_), channel_id=1, source_target_pairs={{17,16},{40,41},{19,18},{42,43},{21,20},{44,45},{23,22},{46,47},{8... | collective-permute-start | bytes 884744 | tf_op jit(solution)/shard_map/ppermute | solution.py:771
  20.1 5.7 %collective-permute-start.6 = (f32[64,1152]{1,0:T(8,128)}, f32[64,1152]{1,0:T(8,128)S(1)}, u32[]{:S(2)}, u32[]{:S(2)}) collective-permute-start(f32[64,1152]{1,0:T(8,128)} %get-tuple-element.98.refs_0_.refs_8_.refs_1_), channel_id=1, source_target_pairs={{8,16},{33,41},{10,18},{35,43},{12,20},{37,45},{14,22},{39,47},{72... | collective-permute-start | bytes 884744 | tf_op jit(solution)/shard_map/ppermute | solution.py:759
  20.8 28.9 %collective-permute-start.5 = (f32[64,1152]{1,0:T(8,128)}, f32[64,1152]{1,0:T(8,128)S(1)}, u32[]{:S(2)}, u32[]{:S(2)}) collective-permute-start(f32[64,1152]{1,0:T(8,128)} %get-tuple-element.98.refs_0_.refs_8_.refs_1_), channel_id=1, source_target_pairs={{0,16},{25,41},{2,18},{27,43},{4,20},{29,45},{6,22},{31,47},{64,80... | collective-permute-start | bytes 884744 | tf_op jit(solution)/shard_map/ppermute | solution.py:759
  21.6 1.0 copy-start
  22.7 0.8 collective-permute-start.14
  23.5 1.0 copy-start.2
  23.7 26.8 %collective-permute-start.15 = (f32[64,512]{1,0:T(8,128)S(1)}, f32[64,512]{1,0:T(8,128)S(1)}, u32[]{:S(2)}, u32[]{:S(2)}) collective-permute-start(f32[64,512]{1,0:T(8,128)S(1)} %get-tuple-element.103), channel_id=1, source_target_pairs={{80,144},{105,169},{82,146},{107,171},{84,148},{109,173},{86,150},... | collective-permute-start | bytes 393224 | tf_op jit(solution)/shard_map/ppermute | solution.py:781
  24.5 26.9 %collective-permute-start.4 = (f32[64,1152]{1,0:T(8,128)S(1)}, f32[64,1152]{1,0:T(8,128)S(1)}, u32[]{:S(2)}, u32[]{:S(2)}) collective-permute-start(f32[64,1152]{1,0:T(8,128)S(1)} %copy-done.2), channel_id=1, source_target_pairs={{56,16},{17,41},{58,18},{19,43},{60,20},{21,45},{62,22},{23,47},{1... | collective-permute-start | bytes 884744 | tf_op jit(solution)/shard_map/ppermute | solution.py:759
  25.2 27.0 %collective-permute-start.3 = (f32[64,1152]{1,0:T(8,128)S(1)}, f32[64,1152]{1,0:T(8,128)S(1)}, u32[]{:S(2)}, u32[]{:S(2)}) collective-permute-start(f32[64,1152]{1,0:T(8,128)S(1)} %copy-done.2), channel_id=1, source_target_pairs={{48,16},{9,41},{50,18},{11,43},{52,20},{13,45},{54,22},{15,47},{11... | collective-permute-start | bytes 884744 | tf_op jit(solution)/shard_map/ppermute | solution.py:759
  25.9 30.4 %collective-permute-start.2 = (f32[64,1152]{1,0:T(8,128)S(1)}, f32[64,1152]{1,0:T(8,128)S(1)}, u32[]{:S(2)}, u32[]{:S(2)}) collective-permute-start(f32[64,1152]{1,0:T(8,128)S(1)} %copy-done.2), channel_id=1, source_target_pairs={{40,16},{1,41},{42,18},{3,43},{44,20},{5,45},{46,22},{7,47},{104,8... | collective-permute-start | bytes 884744 | tf_op jit(solution)/shard_map/ppermute | solution.py:759
  49.8 6.5 %collective-permute-start.1 = (f32[64,1152]{1,0:T(8,128)S(1)}, f32[64,1152]{1,0:T(8,128)S(1)}, u32[]{:S(2)}, u32[]{:S(2)}) collective-permute-start(f32[64,1152]{1,0:T(8,128)S(1)} %copy-done.2), channel_id=1, source_target_pairs={{32,16},{57,41},{34,18},{59,43},{36,20},{61,45},{38,22},{63,47},{9... | collective-permute-start | bytes 884744 | tf_op jit(solution)/shard_map/ppermute | solution.py:759
  50.5 5.8 %collective-permute-start = (f32[64,1152]{1,0:T(8,128)S(1)}, f32[64,1152]{1,0:T(8,128)S(1)}, u32[]{:S(2)}, u32[]{:S(2)}) collective-permute-start(f32[64,1152]{1,0:T(8,128)S(1)} %copy-done.2), channel_id=1, source_target_pairs={{24,16},{49,41},{26,18},{51,43},{28,20},{53,45},{30,22},{55,47},{8... | collective-permute-start | bytes 884744 | tf_op jit(solution)/shard_map/ppermute | solution.py:759
  51.3 5.0 %copy-start.1 = (f32[64,1152]{1,0:T(8,128)S(1)}, f32[64,1152]{1,0:T(8,128)}, u32[]{:S(2)}) copy-start(f32[64,1152]{1,0:T(8,128)} %get-tuple-element.100.refs_0_) | copy-start | bytes 884740
  51.4 5.0 %collective-permute-start.16 = (f32[64,512]{1,0:T(8,128)S(1)}, f32[64,512]{1,0:T(8,128)S(1)}, u32[]{:S(2)}, u32[]{:S(2)}) collective-permute-start(f32[64,512]{1,0:T(8,128)S(1)} %get-tuple-element.109), channel_id=1, source_target_pairs={{144,208},{169,233},{146,210},{171,235},{148,212},{173,237},{150,2... | collective-permute-start | bytes 393224 | tf_op jit(solution)/shard_map/ppermute | solution.py:781
  56.6 4.4 %collective-permute-start.17 = (f32[64,512]{1,0:T(8,128)S(1)}, f32[64,512]{1,0:T(8,128)S(1)}, u32[]{:S(2)}, u32[]{:S(2)}) collective-permute-start(f32[64,512]{1,0:T(8,128)S(1)} %get-tuple-element.119), channel_id=1, source_target_pairs={{208,144},{233,169},{210,146},{235,171},{212,148},{237,173},{214,1... | collective-permute-start | bytes 393224 | tf_op jit(solution)/shard_map/ppermute | solution.py:781
  57.7 3.5 %collective-permute-start.21 = (f32[64,512]{1,0:T(8,128)S(1)}, f32[64,512]{1,0:T(8,128)S(1)}, u32[]{:S(2)}, u32[]{:S(2)}) collective-permute-start(f32[64,512]{1,0:T(8,128)S(1)} %get-tuple-element.143), channel_id=1, source_target_pairs={{16,0},{41,25},{18,2},{43,27},{20,4},{45,29},{22,6},{47,31},{80,64... | collective-permute-start | bytes 393224 | tf_op jit(solution)/shard_map/ppermute | solution.py:775
  58.3 27.7 %collective-permute-start.20 = (f32[64,512]{1,0:T(8,128)S(1)}, f32[64,512]{1,0:T(8,128)S(1)}, u32[]{:S(2)}, u32[]{:S(2)}) collective-permute-start(f32[64,512]{1,0:T(8,128)S(1)} %get-tuple-element.141), channel_id=1, source_target_pairs={{16,40},{41,1},{18,42},{43,3},{20,44},{45,5},{22,46},{47,7},{80,10... | collective-permute-start | bytes 393224 | tf_op jit(solution)/shard_map/ppermute | solution.py:775
  59.6 26.4 %collective-permute-start.19 = (f32[64,512]{1,0:T(8,128)S(1)}, f32[64,512]{1,0:T(8,128)S(1)}, u32[]{:S(2)}, u32[]{:S(2)}) collective-permute-start(f32[64,512]{1,0:T(8,128)S(1)} %get-tuple-element.139), channel_id=1, source_target_pairs={{16,56},{41,17},{18,58},{43,19},{20,60},{45,21},{22,62},{47,23},{8... | collective-permute-start | bytes 393224 | tf_op jit(solution)/shard_map/ppermute | solution.py:775
  60.3 25.7 %collective-permute-start.18 = (f32[64,512]{1,0:T(8,128)S(1)}, f32[64,512]{1,0:T(8,128)S(1)}, u32[]{:S(2)}, u32[]{:S(2)}) collective-permute-start(f32[64,512]{1,0:T(8,128)S(1)} %get-tuple-element.137), channel_id=1, source_target_pairs={{16,48},{41,9},{18,50},{43,11},{20,52},{45,13},{22,54},{47,15},{80... | collective-permute-start | bytes 393224 | tf_op jit(solution)/shard_map/ppermute | solution.py:775
  86.0 2.7 %collective-permute-start.25 = (f32[64,512]{1,0:T(8,128)S(1)}, f32[64,512]{1,0:T(8,128)S(1)}, u32[]{:S(2)}, u32[]{:S(2)}) collective-permute-start(f32[64,512]{1,0:T(8,128)S(1)} %get-tuple-element.144), channel_id=1, source_target_pairs={{144,80},{169,105},{146,82},{171,107},{148,84},{173,109},{150,86},... | collective-permute-start | bytes 393224 | tf_op jit(solution)/shard_map/ppermute | solution.py:781
  86.7 2.9 %collective-permute-start.22 = (f32[64,512]{1,0:T(8,128)S(1)}, f32[64,512]{1,0:T(8,128)S(1)}, u32[]{:S(2)}, u32[]{:S(2)}) collective-permute-start(f32[64,512]{1,0:T(8,128)S(1)} %get-tuple-element.146), channel_id=1, source_target_pairs={{16,24},{41,49},{18,26},{43,51},{20,28},{45,53},{22,30},{47,55},{8... | collective-permute-start | bytes 393224 | tf_op jit(solution)/shard_map/ppermute | solution.py:775
  87.3 2.2 %collective-permute-start.23 = (f32[64,512]{1,0:T(8,128)S(1)}, f32[64,512]{1,0:T(8,128)S(1)}, u32[]{:S(2)}, u32[]{:S(2)}) collective-permute-start(f32[64,512]{1,0:T(8,128)S(1)} %get-tuple-element.148), channel_id=1, source_target_pairs={{16,32},{41,57},{18,34},{43,59},{20,36},{45,61},{22,38},{47,63},{8... | collective-permute-start | bytes 393224 | tf_op jit(solution)/shard_map/ppermute | solution.py:775
  88.0 1.5 %collective-permute-start.24 = (f32[64,512]{1,0:T(8,128)S(1)}, f32[64,512]{1,0:T(8,128)S(1)}, u32[]{:S(2)}, u32[]{:S(2)}) collective-permute-start(f32[64,512]{1,0:T(8,128)S(1)} %get-tuple-element.154), channel_id=1, source_target_pairs={{16,8},{41,33},{18,10},{43,35},{20,12},{45,37},{22,14},{47,39},{80... | collective-permute-start | bytes 393224 | tf_op jit(solution)/shard_map/ppermute | solution.py:775
  88.7 0.9 copy-start.3
  88.9 3.4 %collective-permute-start.26 = (f32[64,512]{1,0:T(8,128)S(1)}, f32[64,512]{1,0:T(8,128)S(1)}, u32[]{:S(2)}, u32[]{:S(2)}) collective-permute-start(f32[64,512]{1,0:T(8,128)S(1)} %get-tuple-element.164), channel_id=1, source_target_pairs={{80,16},{105,41},{82,18},{107,43},{84,20},{109,45},{86,22},{111,47}} | collective-permute-start | bytes 393224 | tf_op jit(solution)/shard_map/ppermute | solution.py:781
  93.1 4.0 %collective-permute-start.27 = (f32[64,512]{1,0:T(8,128)S(1)}, f32[64,512]{1,0:T(8,128)S(1)}, u32[]{:S(2)}, u32[]{:S(2)}) collective-permute-start(f32[64,512]{1,0:T(8,128)S(1)} %get-tuple-element.178), channel_id=1, source_target_pairs={{16,24},{41,49},{18,26},{43,51},{20,28},{45,53},{22,30},{47,55},{8... | collective-permute-start | bytes 393224 | tf_op jit(solution)/shard_map/ppermute | solution.py:775
  93.7 4.0 %collective-permute-start.28 = (f32[64,512]{1,0:T(8,128)S(1)}, f32[64,512]{1,0:T(8,128)S(1)}, u32[]{:S(2)}, u32[]{:S(2)}) collective-permute-start(f32[64,512]{1,0:T(8,128)S(1)} %get-tuple-element.179), channel_id=1, source_target_pairs={{16,32},{41,57},{18,34},{43,59},{20,36},{45,61},{22,38},{47,63},{8... | collective-permute-start | bytes 393224 | tf_op jit(solution)/shard_map/ppermute | solution.py:775
  94.4 24.9 %collective-permute-start.29 = (f32[64,512]{1,0:T(8,128)S(1)}, f32[64,512]{1,0:T(8,128)S(1)}, u32[]{:S(2)}, u32[]{:S(2)}) collective-permute-start(f32[64,512]{1,0:T(8,128)S(1)} %get-tuple-element.180), channel_id=1, source_target_pairs={{16,40},{41,1},{18,42},{43,3},{20,44},{45,5},{22,46},{47,7},{80,10... | collective-permute-start | bytes 393224 | tf_op jit(solution)/shard_map/ppermute | solution.py:775
  95.7 23.6 %collective-permute-start.30 = (f32[64,512]{1,0:T(8,128)S(1)}, f32[64,512]{1,0:T(8,128)S(1)}, u32[]{:S(2)}, u32[]{:S(2)}) collective-permute-start(f32[64,512]{1,0:T(8,128)S(1)} %get-tuple-element.181), channel_id=1, source_target_pairs={{16,48},{41,9},{18,50},{43,11},{20,52},{45,13},{22,54},{47,15},{80... | collective-permute-start | bytes 393224 | tf_op jit(solution)/shard_map/ppermute | solution.py:775
  96.4 22.9 %collective-permute-start.31 = (f32[64,512]{1,0:T(8,128)S(1)}, f32[64,512]{1,0:T(8,128)S(1)}, u32[]{:S(2)}, u32[]{:S(2)}) collective-permute-start(f32[64,512]{1,0:T(8,128)S(1)} %get-tuple-element.182), channel_id=1, source_target_pairs={{16,56},{41,17},{18,58},{43,19},{20,60},{45,21},{22,62},{47,23},{8... | collective-permute-start | bytes 393224 | tf_op jit(solution)/shard_map/ppermute | solution.py:775
  97.1 22.3 %collective-permute-start.32 = (f32[64,512]{1,0:T(8,128)S(1)}, f32[64,512]{1,0:T(8,128)S(1)}, u32[]{:S(2)}, u32[]{:S(2)}) collective-permute-start(f32[64,512]{1,0:T(8,128)S(1)} %get-tuple-element.183), channel_id=1, source_target_pairs={{16,0},{41,25},{18,2},{43,27},{20,4},{45,29},{22,6},{47,31},{80,64... | collective-permute-start | bytes 393224 | tf_op jit(solution)/shard_map/ppermute | solution.py:775
  97.8 21.6 %collective-permute-start.33 = (f32[64,512]{1,0:T(8,128)S(1)}, f32[64,512]{1,0:T(8,128)S(1)}, u32[]{:S(2)}, u32[]{:S(2)}) collective-permute-start(f32[64,512]{1,0:T(8,128)S(1)} %get-tuple-element.184), channel_id=1, source_target_pairs={{16,8},{41,33},{18,10},{43,35},{20,12},{45,37},{22,14},{47,39},{80... | collective-permute-start | bytes 393224 | tf_op jit(solution)/shard_map/ppermute | solution.py:775
  122.1 6.1 %collective-permute-start.34 = (f32[64,640]{1,0:T(8,128)S(1)}, f32[64,640]{1,0:T(8,128)S(1)}, u32[]{:S(2)}, u32[]{:S(2)}) collective-permute-start(f32[64,640]{1,0:T(8,128)S(1)} %get-tuple-element.187), channel_id=1, source_target_pairs={{0,1},{1,0},{2,3},{3,2},{4,5},{5,4},{6,7},{7,6},{8,9},{9,8},{10,11... | collective-permute-start | bytes 491528 | tf_op jit(solution)/shard_map/ppermute | solution.py:829
  128.2 5.5 %collective-permute-start.35 = (f32[64,640]{1,0:T(8,128)S(1)}, f32[64,640]{1,0:T(8,128)S(1)}, u32[]{:S(2)}, u32[]{:S(2)}) collective-permute-start(f32[64,640]{1,0:T(8,128)S(1)} %add.9), channel_id=1, source_target_pairs={{0,2},{1,3},{2,0},{3,1},{4,6},{5,7},{6,4},{7,5},{8,10},{9,11},{10,... | collective-permute-start | bytes 491528 | tf_op jit(solution)/shard_map/ppermute | solution.py:831
  133.7 5.9 %collective-permute-start.36 = (f32[64,640]{1,0:T(8,128)S(1)}, f32[64,640]{1,0:T(8,128)S(1)}, u32[]{:S(2)}, u32[]{:S(2)}) collective-permute-start(f32[64,640]{1,0:T(8,128)S(1)} %add.10), channel_id=1, source_target_pairs={{0,6},{1,7},{2,4},{3,5},{4,2},{5,3},{6,0},{7,1},{8,14},{9,15},{10,... | collective-permute-start | bytes 491528 | tf_op jit(solution)/shard_map/ppermute | solution.py:831
  139.6 3.2 %collective-permute-start.37 = (f32[64,640]{1,0:T(8,128)S(1)}, f32[64,640]{1,0:T(8,128)S(1)}, u32[]{:S(2)}, u32[]{:S(2)}) collective-permute-start(f32[64,640]{1,0:T(8,128)S(1)} %add.11.mine_ref), channel_id=1, source_target_pairs={{0,1},{1,0},{2,3},{3,2},{4,5},{5,4},{6,7},{7,6},{8,9},{9,8},{10,11... | collective-permute-start | bytes 491528 | tf_op jit(solution)/shard_map/ppermute | solution.py:832
